TPU v7x, 32 devices: a whole 2x2x4 slice. The times are simulated.
32 devices in a mesh: rep: 8 (over y, x, core), shard: 4 (over z).
Axes of the slice: x: 2, y: 2, z: 4, core: 2. Of those that a mesh axis runs over, the one named last changes fastest.
Arguments:
- block_in: float32 [4096, 1024], P(('rep', 'shard')), may hold values from -6 to 6
- cotangent: float32 [4096, 1024], P(('rep', 'shard')), may hold values from -0.09375 to 0.09375
- segments: int32 [8, 512], P('rep'), may hold values from 0 to 3, never falling along the last dimension, each value on 1 to 224 neighbouring positions
- qkv_weight: float32 [1024, 3072], P(('rep', 'shard')), may hold values from -0.1875 to 0.1875
- out_weight: float32 [1024, 1024], P(('rep', 'shard')), may hold values from -0.75 to 0.75
- up_weight: float32 [1024, 4096], P(('rep', 'shard')), may hold values from -0.1875 to 0.1875
- down_weight: float32 [4096, 1024], P(('rep', 'shard')), may hold values from -0.09375 to 0.09375
- vectors: float32 [13, 1024], P(None, ('rep', 'shard')), may hold values from -0.9 to 1.5, as said below
- first_qkv: float32 [1024, 3072], P(('rep', 'shard')), may hold values from -1.8 to 1.8
- first_out: float32 [1024, 1024], P(('rep', 'shard')), may hold values from -1.8 to 1.8
- first_up: float32 [1024, 4096], P(('rep', 'shard')), may hold values from -1.8 to 1.8
- first_down: float32 [4096, 1024], P(('rep', 'shard')), may hold values from -1.8 to 1.8
- first_vec: float32 [13, 1024], P(None, ('rep', 'shard')), may hold values from -1.8 to 1.8
- second_qkv: float32 [1024, 3072], P(('rep', 'shard')), may hold values from 0.002 to 0.2
- second_out: float32 [1024, 1024], P(('rep', 'shard')), may hold values from 0.002 to 0.2
- second_up: float32 [1024, 4096], P(('rep', 'shard')), may hold values from 0.002 to 0.2
- second_down: float32 [4096, 1024], P(('rep', 'shard')), may hold values from 0.002 to 0.2
- second_vec: float32 [13, 1024], P(None, ('rep', 'shard')), may hold values from 0.002 to 0.2
Outputs:
- block_out: float32 [4096, 1024], P(('rep', 'shard'))
- grad_input: float32 [4096, 1024], P(('rep', 'shard'))
- grad_qkv: float32 [1024, 3072], P(('rep', 'shard'))
- grad_out: float32 [1024, 1024], P(('rep', 'shard'))
- grad_up: float32 [1024, 4096], P(('rep', 'shard'))
- grad_down: float32 [4096, 1024], P(('rep', 'shard'))
- grad_vec: float32 [13, 1024], P(None, ('rep', 'shard'))
- new_qkv: float32 [1024, 3072], P(('rep', 'shard'))
- new_out: float32 [1024, 1024], P(('rep', 'shard'))
- new_up: float32 [1024, 4096], P(('rep', 'shard'))
- new_down: float32 [4096, 1024], P(('rep', 'shard'))
- new_vec: float32 [13, 1024], P(None, ('rep', 'shard'))
- new_first_qkv: float32 [1024, 3072], P(('rep', 'shard'))
- new_first_out: float32 [1024, 1024], P(('rep', 'shard'))
- new_first_up: float32 [1024, 4096], P(('rep', 'shard'))
- new_first_down: float32 [4096, 1024], P(('rep', 'shard'))
- new_first_vec: float32 [13, 1024], P(None, ('rep', 'shard'))
- new_second_qkv: float32 [1024, 3072], P(('rep', 'shard'))
- new_second_out: float32 [1024, 1024], P(('rep', 'shard'))
- new_second_up: float32 [1024, 4096], P(('rep', 'shard'))
- new_second_down: float32 [4096, 1024], P(('rep', 'shard'))
- new_second_vec: float32 [13, 1024], P(None, ('rep', 'shard'))
Inputs may be any that keep to these rules, and one draw needn't show every extreme that they name: `segments`: in every row the segment numbers never fall; each of the 4 numbers covers 1 to 224 consecutive positions and one covers exactly 224. `vectors`: rows 0 and 2 lie in 0.5 to 1.5.
All inputs are finite; a program needn't handle non-finite values.
Results may differ from a plain program's by a relative error of at most 0.019.
The roundings to bfloat16 on the way count: a program that leaves them out, or rounds other values in their place, can miss the bound.
Values may be sent and summed in bfloat16 or wider, within the bound.
No kernel may reach another device: no remote copies, remote signals or barrier semaphores. Data moves between devices by JAX's collectives and lax.ppermute only.
A program may use at most 320 MiB of HBM per device.

v0:
```python
import jax
import jax.numpy as jnp
from jax import lax
from jax.sharding import PartitionSpec as P

D = 1024
HEADS = 16
FF = 4096
ROT = 16
STEP = 10


LN_EPS = 1e-05
BETA_ONE = 0.9
BETA_TWO = 0.95
ADAM_EPS = 1e-08
LR_MATRIX = 0.03
LR_VECTOR = 0.2
WEIGHT_DECAY = 0.01
ROPE_BASE = 10000.0
INV_ROOT_TWO = 0.7071067811865476
INV_ROOT_TAU = 0.3989422804014327


def layer_norm(values, gain, shift):
    center = values - jnp.mean(values, axis=-1, keepdims=True)
    inv_std = lax.rsqrt(jnp.mean(center * center, axis=-1, keepdims=True) + LN_EPS)
    normed = center * inv_std
    return (normed * gain + shift, normed, inv_std)


def norm_backward(upstream, normed, inv_std, gain):
    scaled = upstream * gain
    result = inv_std * (
        scaled
        - jnp.mean(scaled, axis=-1, keepdims=True)
        - normed * jnp.mean(scaled * normed, axis=-1, keepdims=True)
    )
    return (result, jnp.sum(upstream * normed, axis=0), jnp.sum(upstream, axis=0))


def rope_tables(positions):
    half_rot = ROT // 2
    freqs = ROPE_BASE ** (-(2.0 * jnp.arange(half_rot).astype(jnp.float32) / ROT))
    angles = positions.astype(jnp.float32)[:, None] * freqs[None, :]
    return (jnp.cos(angles)[:, None, :], jnp.sin(angles)[:, None, :])


def rotate(heads, cosines, sines):
    half_rot = ROT // 2
    lower = heads[..., :half_rot]
    upper = heads[..., half_rot:ROT]
    return jnp.concatenate(
        [lower * cosines - upper * sines, upper * cosines + lower * sines, heads[..., ROT:]],
        axis=-1,
    )


def unrotate(heads, cosines, sines):
    half_rot = ROT // 2
    lower = heads[..., :half_rot]
    upper = heads[..., half_rot:ROT]
    return jnp.concatenate(
        [lower * cosines + upper * sines, upper * cosines - lower * sines, heads[..., ROT:]],
        axis=-1,
    )


def gelu_value(inner):
    return 0.5 * inner * (1.0 + jax.scipy.special.erf(inner * INV_ROOT_TWO))


def gelu_slope(inner):
    return (
        0.5 * (1.0 + jax.scipy.special.erf(inner * INV_ROOT_TWO))
        + inner * jnp.exp(-0.5 * inner * inner) * INV_ROOT_TAU
    )


def adam_update(param, grad, first, second, rate, decay):
    first_new = BETA_ONE * first + (1.0 - BETA_ONE) * grad
    second_new = BETA_TWO * second + (1.0 - BETA_TWO) * grad * grad
    first_hat = first_new / (1.0 - BETA_ONE**STEP)
    second_hat = second_new / (1.0 - BETA_TWO**STEP)
    return (
        param - rate * (first_hat / (jnp.sqrt(second_hat) + ADAM_EPS) + decay * param),
        first_new,
        second_new,
    )


def contract_rows(left, right):
    return lax.dot_general(
        left, right, (((0,), (0,)), ((), ())), preferred_element_type=jnp.float32
    )


def contract_cols(left, right):
    return lax.dot_general(
        left, right, (((1,), (1,)), ((), ())), preferred_element_type=jnp.float32
    )


def shards(
    block_in,
    cotangent,
    segments,
    qkv_weight,
    out_weight,
    up_weight,
    down_weight,
    vectors,
    first_qkv,
    first_out,
    first_up,
    first_down,
    first_vec,
    second_qkv,
    second_out,
    second_up,
    second_down,
    second_vec,
):
    bf16 = jnp.bfloat16
    tok_count = block_in.shape[0]
    n_shard = lax.axis_size("shard")
    seq_len = tok_count * n_shard
    head_dim = D // HEADS
    per_row = FF // D
    own_rows = qkv_weight.shape[0]
    score_scale = head_dim ** (-0.5)
    vec_all = lax.all_gather(vectors, ("rep", "shard"), axis=1, tiled=True)
    gain_one, shift_one, gain_two, shift_two = (vec_all[0], vec_all[1], vec_all[2], vec_all[3])
    qkv_bias = vec_all[4:7].reshape(3 * D)
    out_bias = vec_all[7]
    up_bias = vec_all[8 : 8 + per_row].reshape(FF)
    down_bias = vec_all[8 + per_row]
    ln_one, normed_one, inv_one = layer_norm(block_in, gain_one, shift_one)
    ln_two, normed_two, inv_two = layer_norm(block_in, gain_two, shift_two)
    h_one = ln_one.astype(bf16)
    h_two = ln_two.astype(bf16)
    in_table = jnp.concatenate([qkv_weight.astype(bf16), up_weight.astype(bf16)], axis=1)
    out_table = jnp.concatenate(
        [out_weight.astype(bf16), down_weight.astype(bf16).reshape(own_rows, per_row * D)], axis=1
    )
    in_whole = lax.all_gather(in_table, ("rep", "shard"), axis=0, tiled=True)
    qkv_lin = jnp.dot(h_one, in_whole[:, : 3 * D], preferred_element_type=jnp.float32) + qkv_bias
    up_lin = jnp.dot(h_two, in_whole[:, 3 * D :], preferred_element_type=jnp.float32) + up_bias
    offset = lax.axis_index("shard") * tok_count
    query_pos = offset + jnp.arange(tok_count)
    key_pos = jnp.arange(seq_len)
    cosines, sines = rope_tables(query_pos)
    query16 = rotate(qkv_lin[:, :D].reshape(tok_count, HEADS, head_dim), cosines, sines).astype(
        bf16
    )
    key16 = (
        rotate(qkv_lin[:, D : 2 * D].reshape(tok_count, HEADS, head_dim), cosines, sines)
        .reshape(tok_count, D)
        .astype(bf16)
    )
    value16 = qkv_lin[:, 2 * D :].astype(bf16)
    keys_all, values_all = (
        lax.all_gather(key16, "shard", axis=0, tiled=True),
        lax.all_gather(value16, "shard", axis=0, tiled=True),
    )
    keys3 = keys_all.reshape(seq_len, HEADS, head_dim)
    values3 = values_all.reshape(seq_len, HEADS, head_dim)
    seg_row = segments[0]
    seg_query = lax.dynamic_slice_in_dim(seg_row, offset, tok_count)
    allowed = (seg_query[:, None] == seg_row[None, :]) & (key_pos[None, :] <= query_pos[:, None])
    scores = jnp.where(
        allowed[None],
        jnp.einsum("qhd,khd->hqk", query16, keys3, preferred_element_type=jnp.float32)
        * score_scale,
        -jnp.inf,
    )
    row_max = jnp.max(scores, axis=-1, keepdims=True)
    expo = jnp.exp(scores - row_max)
    row_sum = jnp.sum(expo, axis=-1, keepdims=True)
    log_total = row_max + jnp.log(row_sum)
    probs16 = (expo / row_sum).astype(bf16)
    mixed16 = (
        jnp.einsum("hqk,khd->qhd", probs16, values3, preferred_element_type=jnp.float32)
        .reshape(tok_count, D)
        .astype(bf16)
    )
    act16 = gelu_value(up_lin).astype(bf16)
    act3 = act16.reshape(tok_count, D, per_row)
    out_whole = lax.all_gather(out_table, ("rep", "shard"), axis=0, tiled=True)
    branches = jnp.dot(mixed16, out_whole[:, :D], preferred_element_type=jnp.float32)
    branches = branches + jnp.dot(
        act16, out_whole[:, D:].reshape(FF, D), preferred_element_type=jnp.float32
    )
    block_out = block_in + branches + out_bias + down_bias
    upstream16 = cotangent.astype(bf16)
    piece = lax.all_gather(out_table, ("rep", "shard"), axis=0, tiled=True)
    num_rows = piece.shape[0]
    first_part = contract_cols(upstream16, piece[:, :D])
    second_part = contract_cols(upstream16, piece[:, D:].reshape(num_rows * per_row, D)).reshape(
        tok_count, num_rows, per_row
    )
    back_table = jnp.concatenate([first_part[:, :, None], second_part], axis=2)
    d_mixed = back_table[:, :, 0]
    d_act = back_table[:, :, 1:].reshape(tok_count, FF)
    d_up = d_act * gelu_slope(up_lin)
    d_up16 = d_up.astype(bf16)
    d_mixed16 = d_mixed.astype(bf16).reshape(tok_count, HEADS, head_dim)
    row_delta = jnp.sum(
        d_mixed16.astype(jnp.float32)
        * mixed16.reshape(tok_count, HEADS, head_dim).astype(jnp.float32),
        axis=-1,
    ).T[:, :, None]
    scores_again = jnp.where(
        allowed[None],
        jnp.einsum("qhd,khd->hqk", query16, keys3, preferred_element_type=jnp.float32)
        * score_scale,
        -jnp.inf,
    )
    probs_again = jnp.exp(scores_again - log_total)
    d_probs = jnp.einsum("qhd,khd->hqk", d_mixed16, values3, preferred_element_type=jnp.float32)
    d_scores16 = (probs_again * (d_probs - row_delta) * score_scale).astype(bf16)
    probs_back16 = probs_again.astype(bf16)
    d_query = jnp.einsum("hqk,khd->qhd", d_scores16, keys3, preferred_element_type=jnp.float32)
    d_keys = jnp.einsum(
        "hqk,qhd->khd", d_scores16, query16, preferred_element_type=jnp.float32
    ).reshape(seq_len, D)
    d_values = jnp.einsum(
        "hqk,qhd->khd", probs_back16, d_mixed16, preferred_element_type=jnp.float32
    ).reshape(seq_len, D)
    own_dkeys, own_dvalues = (
        lax.psum_scatter(d_keys, "shard", scatter_dimension=0, tiled=True),
        lax.psum_scatter(d_values, "shard", scatter_dimension=0, tiled=True),
    )
    d_qkv = jnp.concatenate(
        [
            unrotate(d_query, cosines, sines).reshape(tok_count, D),
            unrotate(own_dkeys.reshape(tok_count, HEADS, head_dim), cosines, sines).reshape(
                tok_count, D
            ),
            own_dvalues,
        ],
        axis=1,
    )
    d_qkv16 = d_qkv.astype(bf16)
    piece = lax.all_gather(in_table, ("rep", "shard"), axis=0, tiled=True)
    first_part = contract_cols(d_qkv16, piece[:, : 3 * D])
    second_part = contract_cols(d_up16, piece[:, 3 * D :])
    norm_table = jnp.stack([first_part, second_part], axis=2)
    d_one = norm_table[:, :, 0]
    d_two = norm_table[:, :, 1]
    dx_one, dgain_one, dshift_one = norm_backward(d_one, normed_one, inv_one, gain_one)
    dx_two, dgain_two, dshift_two = norm_backward(d_two, normed_two, inv_two, gain_two)
    grad_input = cotangent + dx_one + dx_two
    cot_sum = jnp.sum(cotangent, axis=0)
    vec_terms = jnp.concatenate(
        [
            dgain_one[None],
            dshift_one[None],
            dgain_two[None],
            dshift_two[None],
            jnp.sum(d_qkv, axis=0).reshape(3, D),
            cot_sum[None],
            jnp.sum(d_up, axis=0).reshape(per_row, D),
            cot_sum[None],
        ],
        axis=0,
    )
    grad_vec = lax.psum_scatter(vec_terms, ("rep", "shard"), scatter_dimension=1, tiled=True)
    one_cols = h_one[:, :, None]
    two_cols = h_two[:, :, None]
    mixed_cols = mixed16[:, :, None]
    term_qkv = contract_rows(one_cols.reshape(tok_count, D), d_qkv16)
    term_up = contract_rows(two_cols.reshape(tok_count, D), d_up16)
    term_out = contract_rows(mixed_cols.reshape(tok_count, D), upstream16)
    term_down = contract_rows(act3.reshape(tok_count, D * per_row), upstream16)
    grad_table = lax.psum_scatter(
        jnp.concatenate([term_qkv, term_up, term_out, term_down.reshape(D, per_row * D)], axis=1),
        ("rep", "shard"),
        scatter_dimension=0,
        tiled=True,
    )
    grad_qkv = grad_table[:, : 3 * D]
    grad_up = grad_table[:, 3 * D : 3 * D + FF]
    grad_out = grad_table[:, 3 * D + FF : 4 * D + FF]
    grad_down = grad_table[:, 4 * D + FF :].reshape(own_rows * per_row, D)
    new_qkv, new_first_qkv, new_second_qkv = adam_update(
        qkv_weight, grad_qkv, first_qkv, second_qkv, LR_MATRIX, WEIGHT_DECAY
    )
    new_out, new_first_out, new_second_out = adam_update(
        out_weight, grad_out, first_out, second_out, LR_MATRIX, WEIGHT_DECAY
    )
    new_up, new_first_up, new_second_up = adam_update(
        up_weight, grad_up, first_up, second_up, LR_MATRIX, WEIGHT_DECAY
    )
    new_down, new_first_down, new_second_down = adam_update(
        down_weight, grad_down, first_down, second_down, LR_MATRIX, WEIGHT_DECAY
    )
    new_vec, new_first_vec, new_second_vec = adam_update(
        vectors, grad_vec, first_vec, second_vec, LR_VECTOR, 0.0
    )
    return (
        block_out,
        grad_input,
        grad_qkv,
        grad_out,
        grad_up,
        grad_down,
        grad_vec,
        new_qkv,
        new_out,
        new_up,
        new_down,
        new_vec,
        new_first_qkv,
        new_first_out,
        new_first_up,
        new_first_down,
        new_first_vec,
        new_second_qkv,
        new_second_out,
        new_second_up,
        new_second_down,
        new_second_vec,
    )


def solution(mesh):
    return jax.shard_map(
        shards,
        mesh=mesh,
        in_specs=(
            P(("rep", "shard"), None),
            P(("rep", "shard"), None),
            P("rep", None),
            P(("rep", "shard"), None),
            P(("rep", "shard"), None),
            P(("rep", "shard"), None),
            P(("rep", "shard"), None),
            P(None, ("rep", "shard")),
            P(("rep", "shard"), None),
            P(("rep", "shard"), None),
            P(("rep", "shard"), None),
            P(("rep", "shard"), None),
            P(None, ("rep", "shard")),
            P(("rep", "shard"), None),
            P(("rep", "shard"), None),
            P(("rep", "shard"), None),
            P(("rep", "shard"), None),
            P(None, ("rep", "shard")),
        ),
        out_specs=(
            P(("rep", "shard"), None),
            P(("rep", "shard"), None),
            P(("rep", "shard"), None),
            P(("rep", "shard"), None),
            P(("rep", "shard"), None),
            P(("rep", "shard"), None),
            P(None, ("rep", "shard")),
            P(("rep", "shard"), None),
            P(("rep", "shard"), None),
            P(("rep", "shard"), None),
            P(("rep", "shard"), None),
            P(None, ("rep", "shard")),
            P(("rep", "shard"), None),
            P(("rep", "shard"), None),
            P(("rep", "shard"), None),
            P(("rep", "shard"), None),
            P(None, ("rep", "shard")),
            P(("rep", "shard"), None),
            P(("rep", "shard"), None),
            P(("rep", "shard"), None),
            P(("rep", "shard"), None),
            P(None, ("rep", "shard")),
        ),
        check_vma=False,
    )
```

profile of v0, /device:TPU:0, one launch (start us, length us, event | category | flops | bytes accessed | tf_op | source)
XLA Modules:
  0.0 970.5 jit_solution(3823819101333165597)
XLA Ops:
  13.3 74.3 %all-gather = f32[32,32,13]{1,2,0:T(8,128)S(1)} all-gather(f32[1,32,13]{1,2,0:T(8,128)S(1)} %bitcast.115), channel_id=1, replica_groups=mesh['rep'=8,'shard'=4] {'rep','shard'}, dimensions={0}, use_global_device_ids=true | all-gather | bytes 54912 | tf_op jit(solution)/shard_map/all_gather | solution.py:132
  88.3 33.2 %all-gather.6.cloned.1.call-done = bf16[1024,7168]{1,0:T(8,128)(2,1)} async-done(((bf16[32,7168]{1,0:T(8,128)(2,1)}), bf16[1024,7168]{1,0:T(8,128)(2,1)}) %all-gather.6.cloned.1.call-update) | async-done | bytes 14680080 | tf_op jit(solution)/shard_map/all_gather | solution.py:146
  121.5 3.8 fusion.14
  129.9 80.1 %all-gather.12.cloned.1.call-done = bf16[1024,5120]{1,0:T(8,128)(2,1)} async-done(((bf16[32,5120]{1,0:T(8,128)(2,1)}), bf16[1024,5120]{1,0:T(8,128)(2,1)}) %all-gather.12.cloned.1.call-update) | async-done | bytes 10485776 | tf_op jit(solution)/shard_map/all_gather | solution.py:189
  210.0 2.3 fusion.45
  212.4 28.5 %all-gather.10.cloned.1.call-done = bf16[512,1024]{0,1:T(8,128)(2,1)} async-done(((bf16[128,1024]{0,1:T(8,128)(2,1)}), bf16[512,1024]{0,1:T(8,128)(2,1)}) %all-gather.10.cloned.1.call-update) | async-done | bytes 1048592 | tf_op jit(solution)/shard_map/all_gather | solution.py:163
  240.9 2.1 fusion.17
  243.0 1.9 copy-done.1
  246.2 23.0 %all-gather.8.cloned.1.call-done = bf16[512,1024]{1,0:T(8,128)(2,1)} async-done(((bf16[128,1024]{1,0:T(8,128)(2,1)}), bf16[512,1024]{1,0:T(8,128)(2,1)}) %all-gather.8.cloned.1.call-update) | async-done | bytes 1048592 | tf_op jit(solution)/shard_map/all_gather | solution.py:164
  270.7 4.5 multiply_reduce_fusion.4
  280.1 4.7 fusion.22
  285.1 8.0 slice.149
  293.0 14.0 %reshape.257 = bf16[4096,1024]{1,0:T(8,128)(2,1)} reshape(bf16[1024,4096]{1,0:T(8,128)(2,1)} %slice.149) | data formatting | bytes 16777216 | tf_op jit(solution)/shard_map/reshape | solution.py:192
  307.0 4.9 fusion.9
  312.9 4.2 fusion.82
  317.1 8.1 fusion.72
  325.2 20.3 %reshape.264 = f32[1024,4096]{1,0:T(8,128)} reshape(f32[4096,1024]{1,0:T(8,128)} %fusion.72) | data formatting | bytes 33554432 | tf_op jit(solution)/shard_map/reshape | solution.py:277
  345.5 9.7 fusion.53
  356.7 2.6 fusion.83
  361.3 1.9 pad_maximum_fusion.2
  363.2 5.9 reduce-scatter.9.cloned.1.call-done
  370.8 5.4 fusion.4
  376.2 7.5 multiply_reduce_fusion
  384.8 7.7 fusion.61
  392.5 34.0 %pad_maximum_fusion = f32[1024,12288]{1,0:T(8,128)} fusion(f32[1024,4096]{1,0:T(8,128)} %reshape.264, f32[1024,1024]{1,0:T(8,128)} %fusion.83, f32[1024,4096]{1,0:T(8,128)} %fusion.53, f32[1024,3072]{1,0:T(8,128)} %fusion.61), kind=kLoop, calls=%fused_computation | loop fusion | flops 37748736 | bytes 100663296 | tf_op jit(solution)/shard_map/concatenate | solution.py:277
  426.5 4.8 fusion.73
  431.4 3.0 fusion.42
  435.6 83.1 %reduce-scatter.13.cloned.1.call-done = f32[32,13]{1,0:T(8,128)} async-done(((f32[1024,13]{1,0:T(8,128)}), f32[32,13]{1,0:T(8,128)}) %reduce-scatter.13.cloned.1.call-update) | async-done | bytes 1680
  520.1 433.9 %reduce-scatter.11.cloned.1.call-done = f32[32,12288]{1,0:T(8,128)} async-done(((f32[1024,12288]{1,0:T(8,128)}), f32[32,12288]{1,0:T(8,128)}) %reduce-scatter.11.cloned.1.call-update) | async-done | bytes 1572880 | tf_op jit(solution)/shard_map/reduce_scatter | solution.py:276
  954.0 2.6 multiply_subtract_fusion.1
  956.8 2.9 multiply_subtract_fusion
  961.5 2.2 multiply_subtract_fusion.2
  (136 shorter events, 30.8 us)
Async XLA Ops:
  7.2 6.1 copy-start.27
  7.2 80.6 %copy-start.3 = (f32[128,1024]{1,0:T(8,128)S(1)}, f32[128,1024]{1,0:T(8,128)}, u32[]{:S(2)}) copy-start(f32[128,1024]{1,0:T(8,128)} %param.18) | copy-start | bytes 1572868
  7.2 114.3 %all-gather.6.cloned.1.call-start = ((), (), s32[]{:S(2)}) async-start(), calls=%async_computation.4 | async-start | bytes 15138816 | tf_op jit(solution)/shard_map/all_gather | solution.py:146
  10.2 199.8 %all-gather.12.cloned.1.call-start = ((), (), s32[]{:S(2)}) async-start(), calls=%async_computation.7 | async-start | bytes 10813440 | tf_op jit(solution)/shard_map/all_gather | solution.py:189
  13.2 227.7 %all-gather.10.cloned.1.call-start = ((), (), s32[]{:S(2)}) async-start(), calls=%async_computation.6 | async-start | bytes 1310720 | tf_op jit(solution)/shard_map/all_gather | solution.py:163
  125.4 4.5 copy-start.10
  127.8 141.4 %all-gather.8.cloned.1.call-start = ((), (), s32[]{:S(2)}) async-start(), calls=%async_computation.5 | async-start | bytes 1310720 | tf_op jit(solution)/shard_map/all_gather | solution.py:164
  129.7 229.7 %reduce-scatter.7.cloned.1.call-start = ((), (), s32[]{:S(2)}) async-start(), calls=%async_computation.8 | async-start | bytes 2621440 | tf_op jit(solution)/shard_map/reduce_scatter | solution.py:231
  270.7 4.5 copy-start.2
  280.1 89.0 %reduce-scatter.9.cloned.1.call-start = ((), (), s32[]{:S(2)}) async-start(), calls=%async_computation.9 | async-start | bytes 2621440 | tf_op jit(solution)/shard_map/reduce_scatter | solution.py:232
  284.8 233.8 %reduce-scatter.13.cloned.1.call-start = ((), (), s32[]{:S(2)}) async-start(), calls=%async_computation.11 | async-start | bytes 540672
  307.0 5.8 copy-start
  345.4 9.7 copy-start.5
  345.4 9.7 copy-start.6
  370.7 5.4 copy-start.14
  376.2 7.5 copy-start.19
  384.8 569.3 %reduce-scatter.11.cloned.1.call-start = ((), (), s32[]{:S(2)}) async-start(), calls=%async_computation.10 | async-start | bytes 51904512 | tf_op jit(solution)/shard_map/reduce_scatter | solution.py:276
  426.5 4.9 copy-start.16
  431.3 88.1 %copy-start.29 = (f32[13,32]{1,0:T(8,128)S(1)}, f32[13,32]{1,0:T(8,128)}, u32[]{:S(2)}) copy-start(f32[13,32]{1,0:T(8,128)} %param.30) | copy-start | bytes 4996
  431.3 88.1 %copy-start.30 = (f32[13,32]{1,0:T(8,128)S(1)}, f32[13,32]{1,0:T(8,128)}, u32[]{:S(2)}) copy-start(f32[13,32]{1,0:T(8,128)} %param.35) | copy-start | bytes 4996
  431.3 522.7 %copy-start.7 = (f32[32,4096]{1,0:T(8,128)S(1)}, f32[32,4096]{1,0:T(8,128)}, u32[]{:S(2)}) copy-start(f32[32,4096]{1,0:T(8,128)} %param.23) | copy-start | bytes 1572868
  431.4 522.7 %copy-start.17 = (f32[32,4096]{1,0:T(8,128)S(1)}, f32[32,4096]{1,0:T(8,128)}, u32[]{:S(2)}) copy-start(f32[32,4096]{1,0:T(8,128)} %param.28) | copy-start | bytes 1572868
  431.4 522.7 %copy-start.18 = (f32[32,4096]{1,0:T(8,128)S(1)}, f32[32,4096]{1,0:T(8,128)}, u32[]{:S(2)}) copy-start(f32[32,4096]{1,0:T(8,128)} %param.33) | copy-start | bytes 1572868
  434.5 522.3 %copy-start.8 = (f32[128,1024]{1,0:T(8,128)S(1)}, f32[128,1024]{1,0:T(8,128)}, u32[]{:S(2)}) copy-start(f32[128,1024]{1,0:T(8,128)} %param.24) | copy-start | bytes 1572868
  519.5 440.3 %copy-start.28 = (f32[13,32]{1,0:T(8,128)}, f32[13,32]{1,0:T(8,128)S(1)}, u32[]{:S(2)}) copy-start(f32[13,32]{1,0:T(8,128)S(1)} %copy.63) | copy-start | bytes 4996
  520.1 439.6 %copy-start.22 = (f32[32,1024]{1,0:T(8,128)S(1)}, f32[32,1024]{1,0:T(8,128)}, u32[]{:S(2)}) copy-start(f32[32,1024]{1,0:T(8,128)} %param.22) | copy-start | bytes 393220
  520.1 439.6 %copy-start.25 = (f32[32,1024]{1,0:T(8,128)S(1)}, f32[32,1024]{1,0:T(8,128)}, u32[]{:S(2)}) copy-start(f32[32,1024]{1,0:T(8,128)} %param.27) | copy-start | bytes 393220
  520.1 439.6 %copy-start.26 = (f32[32,1024]{1,0:T(8,128)S(1)}, f32[32,1024]{1,0:T(8,128)}, u32[]{:S(2)}) copy-start(f32[32,1024]{1,0:T(8,128)} %param.32) | copy-start | bytes 393220
  956.6 4.8 copy-start.12
  956.6 4.8 copy-start.23
  956.7 4.8 copy-start.24
  956.8 6.9 copy-start.9
  (8 other events, 18.0 us)
Sparse Core Ops, SparseCore 0:
  11.5 110.0 all-gather.5
  124.9 85.0 all-gather.11
  212.2 28.6 all-gather.9
  242.9 26.2 all-gather.7
  280.2 43.3 reduce-scatter.6
  325.8 43.1 reduce-scatter.8
  384.9 133.7 reduce-scatter.12
  526.2 427.7 reduce-scatter.10
where the time goes:
time: 972 us; the launch traced here: 971 us
  waiting for transfers between devices  688 us (71%)
  matrix products  79.6 us (8%)
  blocking collectives  74.3 us (8%)
  other arithmetic  58 us (6%)
  local copies, waits for them, and re-layouts  55.7 us (6%)
  between operations  14.7 us (2%)
    reduce_scatter x1, waiting for transfers between devices, shards(): lax.psum_scatter(jnp.concatenate([term_qkv, term_up, term_out, term_down....  434 us
    unnamed x9, waiting for transfers between devices  83.2 us
    all_gather x1, waiting for transfers between devices, shards(): out_whole = lax.all_gather(out_table, ('rep', 'shard'), axis=0, tiled=True)  80.1 us
    all_gather x1, blocking collectives, shards(): vec_all = lax.all_gather(vectors, ('rep', 'shard'), axis=1, tiled=True)  74.3 us
    concatenate x1, other arithmetic, shards(): jnp.concatenate([term_qkv, term_up, term_out, term_down.reshape(D, per_ro...  34 us
    all_gather x1, waiting for transfers between devices, shards(): in_whole = lax.all_gather(in_table, ('rep', 'shard'), axis=0, tiled=True)  33.2 us
    all_gather x1, waiting for transfers between devices, shards(): lax.all_gather(key16, 'shard', axis=0, tiled=True)  28.5 us
    dot_general x4, matrix products, contract_rows(): lax.dot_general(left, right, (((0,), (0,)), ((), ())), preferred_element_...  28.1 us
  transfers between devices with their start and end apart: 8, of which 7 were waited for; matrix products, arithmetic and copies ran while one was open for 15% of the time, Pallas kernels for 0%

commit v1 on v0

v1 whole, which is shorter than its diff:
```python
import jax
import jax.numpy as jnp
from jax import lax
from jax.sharding import PartitionSpec as P

D = 1024
HEADS = 16
FF = 4096
ROT = 16
STEP = 10


LN_EPS = 1e-05
BETA_ONE = 0.9
BETA_TWO = 0.95
ADAM_EPS = 1e-08
LR_MATRIX = 0.03
LR_VECTOR = 0.2
WEIGHT_DECAY = 0.01
ROPE_BASE = 10000.0
INV_ROOT_TWO = 0.7071067811865476
INV_ROOT_TAU = 0.3989422804014327


def rope_tables(positions):
    half_rot = ROT // 2
    freqs = ROPE_BASE ** (-(2.0 * jnp.arange(half_rot).astype(jnp.float32) / ROT))
    angles = positions.astype(jnp.float32)[:, None] * freqs[None, :]
    return (jnp.cos(angles)[:, None, :], jnp.sin(angles)[:, None, :])


def rotate(heads, cosines, sines):
    half_rot = ROT // 2
    lower = heads[..., :half_rot]
    upper = heads[..., half_rot:ROT]
    return jnp.concatenate(
        [lower * cosines - upper * sines, upper * cosines + lower * sines, heads[..., ROT:]],
        axis=-1,
    )


def unrotate(heads, cosines, sines):
    half_rot = ROT // 2
    lower = heads[..., :half_rot]
    upper = heads[..., half_rot:ROT]
    return jnp.concatenate(
        [lower * cosines + upper * sines, upper * cosines - lower * sines, heads[..., ROT:]],
        axis=-1,
    )


def gelu_value(inner):
    return 0.5 * inner * (1.0 + jax.scipy.special.erf(inner * INV_ROOT_TWO))


def gelu_slope(inner):
    return (
        0.5 * (1.0 + jax.scipy.special.erf(inner * INV_ROOT_TWO))
        + inner * jnp.exp(-0.5 * inner * inner) * INV_ROOT_TAU
    )


def adam_update(param, grad, first, second, rate, decay):
    first_new = BETA_ONE * first + (1.0 - BETA_ONE) * grad
    second_new = BETA_TWO * second + (1.0 - BETA_TWO) * grad * grad
    first_hat = first_new / (1.0 - BETA_ONE**STEP)
    second_hat = second_new / (1.0 - BETA_TWO**STEP)
    return (
        param - rate * (first_hat / (jnp.sqrt(second_hat) + ADAM_EPS) + decay * param),
        first_new,
        second_new,
    )


def contract_rows(left, right):
    return lax.dot_general(
        left, right, (((0,), (0,)), ((), ())), preferred_element_type=jnp.float32
    )


def contract_cols(left, right):
    return lax.dot_general(
        left, right, (((1,), (1,)), ((), ())), preferred_element_type=jnp.float32
    )


def hop(value, axis, size, mask):
    return lax.ppermute(value, axis, [(i, i ^ mask) for i in range(size)])


def pick(blocks, index, axis=0):
    return lax.dynamic_index_in_dim(blocks, index, axis, keepdims=False)


def stages(size):
    bits = size.bit_length() - 1
    found = []
    while bits > 0:
        take = 2 if bits >= 2 else 1
        bits -= take
        found.append((bits, 1 << take))
    return found


def gather_axis(own, axis, me, size):
    if size > 16:
        return lax.all_gather(own, axis)
    pieces = {0: own}
    for shift, count in stages(size):
        more = dict(pieces)
        for k in range(1, count):
            for mask, piece in pieces.items():
                more[mask ^ (k << shift)] = hop(piece, axis, size, k << shift)
        pieces = more
    whole = jnp.zeros((size,) + own.shape, own.dtype)
    for mask in range(size):
        whole = lax.dynamic_update_index_in_dim(whole, pieces[mask], me ^ mask, 0)
    return whole


def exchange_axis(blocks, axis, me, size, wire):
    got = [(0, pick(blocks, me))]
    for mask in range(1, size):
        got.append((mask, hop(pick(blocks, me ^ mask).astype(wire), axis, size, mask)))
    return got


def reduce_axis(blocks, axis, me, size, wire):
    current = blocks
    for shift, count in reversed(stages(size)):
        left = current.shape[0] // count
        view = current.reshape((left, count) + current.shape[1:])
        digit = (me >> shift) & (count - 1)
        total = pick(view, digit, 1)
        for k in range(1, count):
            sent = pick(view, digit ^ k, 1).astype(wire)
            total = total + hop(sent, axis, size, k << shift).astype(jnp.float32)
        current = total
    return current[0]


def shards(
    block_in,
    cotangent,
    segments,
    qkv_weight,
    out_weight,
    up_weight,
    down_weight,
    vectors,
    first_qkv,
    first_out,
    first_up,
    first_down,
    first_vec,
    second_qkv,
    second_out,
    second_up,
    second_down,
    second_vec,
):
    bf16 = jnp.bfloat16
    f32 = jnp.float32
    tok_count = block_in.shape[0]
    n_rep = lax.axis_size("rep")
    n_shard = lax.axis_size("shard")
    rep = lax.axis_index("rep")
    shard = lax.axis_index("shard")
    seq_len = tok_count * n_shard
    head_dim = D // HEADS
    own_heads = HEADS // n_shard
    own_feats = own_heads * head_dim
    rows = qkv_weight.shape[0]
    units = down_weight.shape[0]
    own_units = units * n_rep
    cols = vectors.shape[1]
    score_scale = head_dim ** (-0.5)

    qkv_cols = qkv_weight.astype(bf16).reshape(rows, 3, own_heads, n_shard, head_dim)
    qkv_cols = qkv_cols.transpose(3, 0, 1, 2, 4).reshape(n_shard, rows, 3 * own_feats)
    up_cols = up_weight.astype(bf16).reshape(rows, n_rep, n_shard, units)
    up_cols = up_cols.transpose(2, 0, 1, 3).reshape(n_shard, rows, own_units)
    in_cols = jnp.concatenate([qkv_cols, up_cols], axis=2)
    in_rows = jnp.zeros_like(in_cols)
    for mask, piece in exchange_axis(in_cols, "shard", shard, n_shard, bf16):
        in_rows = lax.dynamic_update_index_in_dim(in_rows, piece, shard ^ mask, 0)
    in_rows = in_rows.reshape(n_shard * rows, 3 * own_feats + own_units)

    center = block_in - jnp.mean(block_in, axis=-1, keepdims=True)
    inv_std = lax.rsqrt(jnp.mean(center * center, axis=-1, keepdims=True) + LN_EPS)
    normed = center * inv_std
    normed_seq = gather_axis(normed.astype(bf16), "shard", shard, n_shard).reshape(seq_len, D)
    normed_seq = normed_seq.astype(f32)

    vec_some = gather_axis(vectors, "shard", shard, n_shard)
    vec_all = gather_axis(vec_some, "rep", rep, n_rep)
    vec_all = vec_all.transpose(2, 0, 1, 3).reshape(vectors.shape[0], D)

    in_whole = gather_axis(in_rows, "rep", rep, n_rep).reshape(D, 3 * own_feats + own_units)
    upstream16 = gather_axis(cotangent.astype(bf16), "shard", shard, n_shard).reshape(seq_len, D)
    down_whole = gather_axis(down_weight.astype(bf16), "rep", rep, n_rep).reshape(own_units, D)
    share = head_dim // rows
    moves = []
    for device in range(n_rep * n_shard):
        head, part = device // share, device % share
        moves.append((device, ((head // n_shard) * share + part) * n_shard + head % n_shard))
    out_rows = lax.ppermute(out_weight.astype(bf16), ("rep", "shard"), moves)
    out_whole = gather_axis(out_rows, "rep", rep, n_rep).reshape(own_feats, D)

    per_row = FF // D
    gain_one, shift_one, gain_two, shift_two = (vec_all[0], vec_all[1], vec_all[2], vec_all[3])
    qkv_bias = pick(vec_all[4:7].reshape(3, own_heads, n_shard, head_dim), shard, 2).reshape(
        3 * own_feats
    )
    up_bias = pick(vec_all[8 : 8 + per_row].reshape(n_rep, n_shard, units), shard, 1).reshape(
        own_units
    )
    out_bias = vec_all[7]
    down_bias = vec_all[8 + per_row]

    h_one = (normed_seq * gain_one + shift_one).astype(bf16)
    h_two = (normed_seq * gain_two + shift_two).astype(bf16)
    qkv_whole = in_whole[:, : 3 * own_feats]
    up_whole = in_whole[:, 3 * own_feats :]
    qkv_lin = jnp.dot(h_one, qkv_whole, preferred_element_type=f32) + qkv_bias
    up_lin = jnp.dot(h_two, up_whole, preferred_element_type=f32) + up_bias

    positions = jnp.arange(seq_len)
    cosines, sines = rope_tables(positions)

    def heads_of(values):
        return values.reshape(seq_len, own_heads, head_dim)

    query16 = rotate(heads_of(qkv_lin[:, :own_feats]), cosines, sines).astype(bf16)
    key16 = rotate(heads_of(qkv_lin[:, own_feats : 2 * own_feats]), cosines, sines).astype(bf16)
    value16 = heads_of(qkv_lin[:, 2 * own_feats :]).astype(bf16)
    seg_row = segments[0]
    allowed = (seg_row[:, None] == seg_row[None, :]) & (positions[None, :] <= positions[:, None])
    scores = jnp.where(
        allowed[None],
        jnp.einsum("qhd,khd->hqk", query16, key16, preferred_element_type=f32) * score_scale,
        -jnp.inf,
    )
    row_max = jnp.max(scores, axis=-1, keepdims=True)
    expo = jnp.exp(scores - row_max)
    row_sum = jnp.sum(expo, axis=-1, keepdims=True)
    log_total = row_max + jnp.log(row_sum)
    probs16 = (expo / row_sum).astype(bf16)
    mixed16 = (
        jnp.einsum("hqk,khd->qhd", probs16, value16, preferred_element_type=f32)
        .reshape(seq_len, own_feats)
        .astype(bf16)
    )
    act16 = gelu_value(up_lin).astype(bf16)
    branches = jnp.dot(mixed16, out_whole, preferred_element_type=f32)
    branches = branches + jnp.dot(act16, down_whole, preferred_element_type=f32)
    branches = reduce_axis(
        branches.reshape(n_shard, tok_count, D), "shard", shard, n_shard, bf16
    )
    block_out = block_in + branches + out_bias + down_bias

    term_down = contract_rows(act16, upstream16)
    sum_down = reduce_axis(term_down.reshape(n_rep, units, D), "rep", rep, n_rep, bf16)
    term_out = contract_rows(mixed16, upstream16)
    sum_out = reduce_axis(term_out.reshape(n_rep, rows, D), "rep", rep, n_rep, bf16)
    grad_out = lax.ppermute(sum_out, ("rep", "shard"), [(b, a) for a, b in moves])
    grad_down = sum_down
    d_act = contract_cols(upstream16, down_whole)
    d_mixed16 = heads_of(contract_cols(upstream16, out_whole)).astype(bf16)
    d_up = d_act * gelu_slope(up_lin)
    d_up16 = d_up.astype(bf16)
    term_up = contract_rows(h_two, d_up16)
    sum_up = reduce_axis(
        term_up.reshape(n_rep, n_shard * rows, own_units), "rep", rep, n_rep, bf16
    )

    def back_rows(sums, width):
        whole = jnp.zeros((n_shard, rows, width), f32)
        blocks = sums.reshape(n_shard, rows, width)
        for mask, piece in exchange_axis(blocks, "shard", shard, n_shard, bf16):
            whole = lax.dynamic_update_index_in_dim(whole, piece.astype(f32), shard ^ mask, 0)
        return whole

    grad_up = back_rows(sum_up, own_units).reshape(n_shard, rows, n_rep, units)
    grad_up = grad_up.transpose(1, 2, 0, 3).reshape(rows, FF)

    row_delta = jnp.sum(
        d_mixed16.astype(f32) * heads_of(mixed16).astype(f32),
        axis=-1,
    ).T[:, :, None]
    probs_again = jnp.exp(scores - log_total)
    d_probs = jnp.einsum("qhd,khd->hqk", d_mixed16, value16, preferred_element_type=f32)
    d_scores16 = (probs_again * (d_probs - row_delta) * score_scale).astype(bf16)
    probs_back16 = probs_again.astype(bf16)
    d_query = jnp.einsum("hqk,khd->qhd", d_scores16, key16, preferred_element_type=f32)
    d_keys = jnp.einsum("hqk,qhd->khd", d_scores16, query16, preferred_element_type=f32)
    d_values = jnp.einsum("hqk,qhd->khd", probs_back16, d_mixed16, preferred_element_type=f32)
    d_qkv = jnp.concatenate(
        [
            unrotate(d_query, cosines, sines).reshape(seq_len, own_feats),
            unrotate(d_keys, cosines, sines).reshape(seq_len, own_feats),
            d_values.reshape(seq_len, own_feats),
        ],
        axis=1,
    )
    d_qkv16 = d_qkv.astype(bf16)
    term_qkv = contract_rows(h_one, d_qkv16)
    sum_qkv = reduce_axis(
        term_qkv.reshape(n_rep, n_shard * rows, 3 * own_feats), "rep", rep, n_rep, bf16
    )
    grad_qkv = back_rows(sum_qkv, 3 * own_feats)
    grad_qkv = grad_qkv.reshape(n_shard, rows, 3, own_heads, head_dim)
    grad_qkv = grad_qkv.transpose(1, 2, 3, 0, 4).reshape(rows, 3 * D)

    d_one = contract_cols(d_qkv16, qkv_whole)
    d_two = contract_cols(d_up16, up_whole)
    scaled = d_one * gain_one + d_two * gain_two
    scaled = reduce_axis(scaled.reshape(n_shard, tok_count, D), "shard", shard, n_shard, bf16)
    grad_input = cotangent + inv_std * (
        scaled
        - jnp.mean(scaled, axis=-1, keepdims=True)
        - normed * jnp.mean(scaled * normed, axis=-1, keepdims=True)
    )

    mine = jnp.arange(n_shard) == shard
    cot_sum = jnp.sum(cotangent, axis=0)
    bias_qkv = jnp.where(
        mine[None, None, :, None],
        jnp.sum(d_qkv, axis=0).reshape(3, own_heads, 1, head_dim),
        0.0,
    ).reshape(3, D)
    bias_up = jnp.where(
        mine[None, :, None], jnp.sum(d_up, axis=0).reshape(n_rep, 1, units), 0.0
    ).reshape(per_row, D)
    vec_terms = jnp.concatenate(
        [
            jnp.sum(d_one * normed_seq, axis=0)[None],
            jnp.sum(d_one, axis=0)[None],
            jnp.sum(d_two * normed_seq, axis=0)[None],
            jnp.sum(d_two, axis=0)[None],
            bias_qkv,
            cot_sum[None],
            bias_up,
            cot_sum[None],
        ],
        axis=0,
    )
    vec_blocks = vec_terms.reshape(vectors.shape[0], n_rep, n_shard, cols).transpose(1, 2, 0, 3)
    grad_vec = reduce_axis(
        reduce_axis(vec_blocks, "rep", rep, n_rep, f32), "shard", shard, n_shard, f32
    )

    new_qkv, new_first_qkv, new_second_qkv = adam_update(
        qkv_weight, grad_qkv, first_qkv, second_qkv, LR_MATRIX, WEIGHT_DECAY
    )
    new_out, new_first_out, new_second_out = adam_update(
        out_weight, grad_out, first_out, second_out, LR_MATRIX, WEIGHT_DECAY
    )
    new_up, new_first_up, new_second_up = adam_update(
        up_weight, grad_up, first_up, second_up, LR_MATRIX, WEIGHT_DECAY
    )
    new_down, new_first_down, new_second_down = adam_update(
        down_weight, grad_down, first_down, second_down, LR_MATRIX, WEIGHT_DECAY
    )
    new_vec, new_first_vec, new_second_vec = adam_update(
        vectors, grad_vec, first_vec, second_vec, LR_VECTOR, 0.0
    )
    return (
        block_out,
        grad_input,
        grad_qkv,
        grad_out,
        grad_up,
        grad_down,
        grad_vec,
        new_qkv,
        new_out,
        new_up,
        new_down,
        new_vec,
        new_first_qkv,
        new_first_out,
        new_first_up,
        new_first_down,
        new_first_vec,
        new_second_qkv,
        new_second_out,
        new_second_up,
        new_second_down,
        new_second_vec,
    )


def solution(mesh):
    return jax.shard_map(
        shards,
        mesh=mesh,
        in_specs=(
            P(("rep", "shard"), None),
            P(("rep", "shard"), None),
            P("rep", None),
            P(("rep", "shard"), None),
            P(("rep", "shard"), None),
            P(("rep", "shard"), None),
            P(("rep", "shard"), None),
            P(None, ("rep", "shard")),
            P(("rep", "shard"), None),
            P(("rep", "shard"), None),
            P(("rep", "shard"), None),
            P(("rep", "shard"), None),
            P(None, ("rep", "shard")),
            P(("rep", "shard"), None),
            P(("rep", "shard"), None),
            P(("rep", "shard"), None),
            P(("rep", "shard"), None),
            P(None, ("rep", "shard")),
        ),
        out_specs=(
            P(("rep", "shard"), None),
            P(("rep", "shard"), None),
            P(("rep", "shard"), None),
            P(("rep", "shard"), None),
            P(("rep", "shard"), None),
            P(("rep", "shard"), None),
            P(None, ("rep", "shard")),
            P(("rep", "shard"), None),
            P(("rep", "shard"), None),
            P(("rep", "shard"), None),
            P(("rep", "shard"), None),
            P(None, ("rep", "shard")),
            P(("rep", "shard"), None),
            P(("rep", "shard"), None),
            P(("rep", "shard"), None),
            P(("rep", "shard"), None),
            P(None, ("rep", "shard")),
            P(("rep", "shard"), None),
            P(("rep", "shard"), None),
            P(("rep", "shard"), None),
            P(("rep", "shard"), None),
            P(None, ("rep", "shard")),
        ),
        check_vma=False,
    )
```

time: 972 us -> 335 us (0.34)
  waiting for transfers between devices: 688 us -> 101 us
  starting transfers between devices: 0.51 us -> 80.6 us
  blocking collectives: 74.3 us -> 0 us
  matrix products: 79.6 us -> 41.8 us
  other arithmetic: 58 us -> 25.5 us
  local copies, waits for them, and re-layouts: 55.7 us -> 76.9 us
  between operations: 14.7 us -> 2.89 us
    reduce_scatter x3 -> x0, waiting for transfers between devices: 440 us -> none  [the longest x1 434 us: shards(): lax.psum_scatter(jnp.concatenate([term_qkv, term_up, term_out, term_down....]
    all_gather x4 -> x0, waiting for transfers between devices: 165 us -> none  [the longest x1 80.1 us: shards(): out_whole = lax.all_gather(out_table, ('rep', 'shard'), axis=0, tiled=True)]
    ppermute x0 -> x77, waiting for transfers between devices: none -> 101 us  [the longest x75 101 us: hop(): return lax.ppermute(value, axis, [(i, i ^ mask) for i in range(size)])]
    unnamed x9 -> x0, waiting for transfers between devices: 83.2 us -> none
    ppermute x0 -> x77, starting transfers between devices: none -> 80.6 us  [the longest x75 78.3 us: hop(): return lax.ppermute(value, axis, [(i, i ^ mask) for i in range(size)])]
    all_gather x1 -> x0, blocking collectives: 74.3 us -> none  [shards(): vec_all = lax.all_gather(vectors, ('rep', 'shard'), axis=1, tiled=True)]
    concatenate x4 -> x0, other arithmetic: 36.3 us -> none  [the longest x1 34 us: shards(): jnp.concatenate([term_qkv, term_up, term_out, term_down.reshape(D, per_ro...]
    reshape x6 -> x14, local copies, waits for them, and re-layouts: 34.6 us -> 6 us  [the longest x1 2.05 us: shards(): grad_up = grad_up.transpose(1, 2, 0, 3).reshape(rows, FF)]
  transfers between devices with their start and end apart: 8 -> 77, of which waited for: 7 -> 29; matrix products, arithmetic and copies ran while one was open for 15% -> 34% of each run, Pallas kernels for 0% -> 0%
where the time goes in v1:
time: 335 us; the launch traced here: 329 us
  waiting for transfers between devices  101 us (30%)
  starting transfers between devices  80.6 us (24%)
  local copies, waits for them, and re-layouts  76.9 us (23%)
  matrix products  41.8 us (12%)
  other arithmetic  25.5 us (8%)
    ppermute x75, waiting for transfers between devices, hop(): return lax.ppermute(value, axis, [(i, i ^ mask) for i in range(size)])  101 us
    ppermute x75, starting transfers between devices, hop(): return lax.ppermute(value, axis, [(i, i ^ mask) for i in range(size)])  78.3 us
    dynamic_update_slice x41, local copies, waits for them, and re-layouts, gather_axis(): whole = lax.dynamic_update_index_in_dim(whole, pieces[mask], me ^ mask, 0)  23.2 us
    dot_general x4, matrix products, contract_cols(): lax.dot_general(left, right, (((1,), (1,)), ((), ())), preferred_element_...  14.1 us
    dot_general x4, matrix products, contract_rows(): lax.dot_general(left, right, (((0,), (0,)), ((), ())), preferred_element_...  7.81 us
  transfers between devices with their start and end apart: 77, of which 29 were waited for; matrix products, arithmetic and copies ran while one was open for 34% of the time, Pallas kernels for 0%

profile of v1, /device:TPU:0, one launch (start us, length us, event | category | flops | bytes accessed | tf_op | source)
XLA Modules:
  0.0 328.8 jit_solution(10777810017864704315)
XLA Ops:
  0.7 3.1 collective-permute-start.3
  3.8 2.6 collective-permute-start.4
  11.7 3.5 %collective-permute-start.1 = (bf16[128,1024]{1,0:T(8,128)(2,1)}, bf16[128,1024]{1,0:T(8,128)(2,1)}, u32[]{:S(2)}, u32[]{:S(2)}) collective-permute-start(bf16[128,1024]{1,0:T(8,128)(2,1)} %get-tuple-element.50), channel_id=1, source_target_pairs={{0,2},{1,3},{2,0},{3,1},{4,6},{5,7},{6,4},{7,5},{8,10},{9,11},{10,... | collective-permute-start | bytes 786440 | tf_op jit(solution)/shard_map/ppermute | solution.py:88
  32.7 2.8 collective-permute-done.11
  37.0 3.8 %collective-permute-start.14 = (bf16[32,1792]{1,0:T(8,128)(2,1)}, bf16[32,1792]{1,0:T(8,128)(2,1)S(1)}, u32[]{:S(2)}, u32[]{:S(2)}) collective-permute-start(bf16[32,1792]{1,0:T(8,128)(2,1)} %get-tuple-element.91), channel_id=1, source_target_pairs={{0,2},{1,3},{2,0},{3,1},{4,6},{5,7},{6,4},{7,5},{8,10},{9,11},{10,... | collective-permute-start | bytes 344072 | tf_op jit(solution)/shard_map/ppermute | solution.py:88
  48.3 6.2 %collective-permute-done.15 = bf16[32,1792]{1,0:T(8,128)(2,1)S(1)} collective-permute-done((bf16[32,1792]{1,0:T(8,128)(2,1)}, bf16[32,1792]{1,0:T(8,128)(2,1)S(1)}, u32[]{:S(2)}, u32[]{:S(2)}) %collective-permute-start.15) | collective-permute-done | bytes 114720 | tf_op jit(solution)/shard_map/ppermute | solution.py:88
  62.3 2.8 fusion.9
  71.3 4.1 %collective-permute-done.42 = bf16[128,1024]{1,0:T(8,128)(2,1)S(1)} collective-permute-done((bf16[128,1024]{1,0:T(8,128)(2,1)}, bf16[128,1024]{1,0:T(8,128)(2,1)S(1)}, u32[]{:S(2)}, u32[]{:S(2)}) %collective-permute-start.42) | collective-permute-done | bytes 262176 | tf_op jit(solution)/shard_map/ppermute | solution.py:88
  77.0 2.3 copy.124
  92.8 11.2 %collective-permute-done.19 = bf16[128,1792]{1,0:T(8,128)(2,1)S(1)} collective-permute-done((bf16[128,1792]{1,0:T(8,128)(2,1)}, bf16[128,1792]{1,0:T(8,128)(2,1)S(1)}, u32[]{:S(2)}, u32[]{:S(2)}) %collective-permute-start.19) | collective-permute-done | bytes 458784 | tf_op jit(solution)/shard_map/ppermute | solution.py:88
  111.3 2.4 convolution_add_fusion.1
  133.5 2.8 multiply_convert_fusion.1
  143.1 3.9 %fusion.101 = (f32[1024]{0:T(1024)S(1)}, bf16[512,1024]{1,0:T(8,128)(2,1)S(1)}) fusion(f32[512,1024]{1,0:T(8,128)S(1)} %copy-done.88, f32[1024]{0:T(1024)S(1)} %bitcast.384, bf16[512,1024]{1,0:T(8,128)(2,1)S(1)} %bitcast.332, bf16[1024,1024]{1,0:T(8,128)(2,1)} %bitcast.68), kind=kOutput, calls=%fused_computation.276 | convolution fusion | flops 1080032256 | bytes 6299648 | tf_op jit(solution)/shard_map/dot_general | solution.py:82
  151.9 3.3 %fusion.30 = f32[4,2,128,1024]{3,2,1,0:T(8,128)} fusion(bf16[4,2,128,512]{3,2,1,0:T(8,128)(2,1)S(1)} %bitcast.339, bf16[512,1024]{1,0:T(8,128)(2,1)S(1)} %get-tuple-element.125), kind=kOutput, calls=%fused_computation.54 | convolution fusion | flops 1073741824 | bytes 6291456 | tf_op jit(solution)/shard_map/dot_general | solution.py:76
  157.0 4.2 %fusion.102 = f32[512,1024]{1,0:T(8,128)} fusion(bf16[512,1024]{1,0:T(8,128)(2,1)S(1)} %copy-done.29, bf16[1024,1024]{1,0:T(8,128)(2,1)} %bitcast.68), kind=kOutput, calls=%fused_computation.277 | convolution fusion | flops 1073741824 | bytes 5242880 | tf_op jit(solution)/shard_map/dot_general | solution.py:256
  164.8 4.3 %collective-permute-start.24 = (bf16[32,1024]{1,0:T(8,128)(2,1)}, bf16[32,1024]{1,0:T(8,128)(2,1)S(1)}, u32[]{:S(2)}, u32[]{:S(2)}) collective-permute-start(bf16[32,1024]{1,0:T(8,128)(2,1)} %collective-permute-done.23), channel_id=1, source_target_pairs={{0,4},{4,0},{8,12},{12,8},{16,20},{20,16},{24,28},{28,24},{1,5},{5... | collective-permute-start | bytes 196616 | tf_op jit(solution)/shard_map/ppermute | solution.py:88
  186.8 3.8 %fusion.22 = f32[512,1024]{1,0:T(8,128)} fusion(bf16[1024,1792]{1,0:T(8,128)(2,1)} %bitcast.342, f32[512,256]{1,0:T(8,128)S(1)} %copy.109, f32[512,256]{1,0:T(8,128)S(1)} %copy.108, f32[512,256]{1,0:T(8,128)S(1)} %copy.107), kind=kOutput, calls=%fused_computation.43 | convolution fusion | flops 807665664 | bytes 5242880 | tf_op jit(solution)/shard_map/dot_general | solution.py:82
  192.1 5.9 %fusion.88 = (f32[1024]{0:T(1024)S(1)}, f32[1024]{0:T(1024)S(1)}, f32[512,1024]{1,0:T(8,128)}, f32[1024]{0:T(1024)S(1)}, f32[1024]{0:T(1024)S(1)}) fusion(bf16[4,128,1024]{2,1,0:T(8,128)(2,1)} %bitcast_dynamic-update-slice_fusion.20, f32[1024]{0:T(1024)S(1)} %copy-done.72, f32[512,1024]{1,0:T(8,128)} %fusion.22, f32[1024]{0:T(1024)S(1)} %copy-done.70, ...), kind=kOutput, calls=%fused_computation.270 | convolution fusion | flops 1078980608 | bytes 8413184 | tf_op jit(solution)/shard_map/dot_general | solution.py:82
  204.8 2.3 collective-permute-start.45
  208.6 13.6 %collective-permute-done.44 = bf16[1,128,1024]{2,1,0:T(8,128)(2,1)S(1)} collective-permute-done((bf16[1,128,1024]{2,1,0:T(8,128)(2,1)S(1)}, bf16[1,128,1024]{2,1,0:T(8,128)(2,1)S(1)}, u32[]{:S(2)}, u32[]{:S(2)}) %collective-permute-start.44) | collective-permute-done | bytes 262176 | tf_op jit(solution)/shard_map/ppermute | solution.py:88
  224.3 6.1 %collective-permute-done.46 = bf16[1,128,1024]{2,1,0:T(8,128)(2,1)S(1)} collective-permute-done((bf16[1,128,1024]{2,1,0:T(8,128)(2,1)S(1)}, bf16[1,128,1024]{2,1,0:T(8,128)(2,1)S(1)}, u32[]{:S(2)}, u32[]{:S(2)}) %collective-permute-start.46) | collective-permute-done | bytes 262176 | tf_op jit(solution)/shard_map/ppermute | solution.py:88
  230.9 17.0 %collective-permute-done.39 = bf16[1,128,1024]{2,1,0:T(8,128)(2,1)S(1)} collective-permute-done((bf16[1,128,1024]{2,1,0:T(8,128)(2,1)S(1)}, bf16[1,128,1024]{2,1,0:T(8,128)(2,1)S(1)}, u32[]{:S(2)}, u32[]{:S(2)}) %collective-permute-start.39) | collective-permute-done | bytes 262176 | tf_op jit(solution)/shard_map/ppermute | solution.py:88
  255.7 2.8 fusion.34
  259.0 5.6 %collective-permute-start.74 = (f32[1,13,32]{2,0,1:T(1,128)S(1)}, f32[1,13,32]{2,0,1:T(1,128)S(1)}, u32[]{:S(2)}, u32[]{:S(2)}) collective-permute-start(f32[1,13,32]{2,0,1:T(1,128)S(1)} %get-tuple-element.113), channel_id=1, source_target_pairs={{0,1},{1,0},{2,3},{3,2},{4,5},{5,4},{6,7},{7,6},{8,9},{9,8},{10,11... | collective-permute-start | bytes 5000 | tf_op jit(solution)/shard_map/ppermute | solution.py:88
  279.1 2.8 collective-permute-done.60
  282.6 4.2 %collective-permute-done.61 = bf16[1,128,1024]{2,1,0:T(8,128)(2,1)S(1)} collective-permute-done((bf16[1,128,1024]{2,1,0:T(8,128)(2,1)S(1)}, bf16[1,128,1024]{2,1,0:T(8,128)(2,1)S(1)}, u32[]{:S(2)}, u32[]{:S(2)}) %collective-permute-start.61) | collective-permute-done | bytes 262176 | tf_op jit(solution)/shard_map/ppermute | solution.py:88
  288.2 4.2 %collective-permute-done.67 = bf16[1,128,1024]{2,1,0:T(8,128)(2,1)S(1)} collective-permute-done((bf16[1,128,1024]{2,1,0:T(8,128)(2,1)S(1)}, bf16[1,128,1024]{2,1,0:T(8,128)(2,1)S(1)}, u32[]{:S(2)}, u32[]{:S(2)}) %collective-permute-start.67) | collective-permute-done | bytes 262176 | tf_op jit(solution)/shard_map/ppermute | solution.py:88
  293.2 2.8 collective-permute-done.68
  296.0 2.3 collective-permute-start.65
  312.7 3.1 collective-permute-done.49
  316.1 3.0 collective-permute-start.52
  321.2 3.8 %collective-permute-done.53 = bf16[32,768]{1,0:T(8,128)(2,1)S(1)} collective-permute-done((bf16[32,768]{1,0:T(8,128)(2,1)S(1)}, bf16[32,768]{1,0:T(8,128)(2,1)S(1)}, u32[]{:S(2)}, u32[]{:S(2)}) %collective-permute-start.53) | collective-permute-done | bytes 49184 | tf_op jit(solution)/shard_map/ppermute | solution.py:88
  (510 shorter events, 179.4 us)
Async XLA Ops:
  0.7 23.8 %collective-permute-start.3 = (f32[13,32]{1,0:T(8,128)}, f32[13,32]{1,0:T(8,128)S(1)}, u32[]{:S(2)}, u32[]{:S(2)}) collective-permute-start(f32[13,32]{1,0:T(8,128)} %param.25), channel_id=1, source_target_pairs={{0,1},{1,0},{2,3},{3,2},{4,5},{5,4},{6,7},{7,6},{8,9},{9,8},{10,11... | collective-permute-start | bytes 5000 | tf_op jit(solution)/shard_map/ppermute | solution.py:88
  3.8 20.9 %collective-permute-start.4 = (f32[13,32]{1,0:T(8,128)}, f32[13,32]{1,0:T(8,128)S(1)}, u32[]{:S(2)}, u32[]{:S(2)}) collective-permute-start(f32[13,32]{1,0:T(8,128)} %param.25), channel_id=1, source_target_pairs={{0,2},{1,3},{2,0},{3,1},{4,6},{5,7},{6,4},{7,5},{8,10},{9,11},{10,... | collective-permute-start | bytes 5000 | tf_op jit(solution)/shard_map/ppermute | solution.py:88
  6.4 18.3 %collective-permute-start.5 = (f32[13,32]{1,0:T(8,128)}, f32[13,32]{1,0:T(8,128)S(1)}, u32[]{:S(2)}, u32[]{:S(2)}) collective-permute-start(f32[13,32]{1,0:T(8,128)} %param.25), channel_id=1, source_target_pairs={{0,3},{1,2},{2,1},{3,0},{4,7},{5,6},{6,5},{7,4},{8,11},{9,10},{10,... | collective-permute-start | bytes 5000 | tf_op jit(solution)/shard_map/ppermute | solution.py:88
  10.8 45.6 %collective-permute-start = (bf16[128,1024]{1,0:T(8,128)(2,1)}, bf16[128,1024]{1,0:T(8,128)(2,1)}, u32[]{:S(2)}, u32[]{:S(2)}) collective-permute-start(bf16[128,1024]{1,0:T(8,128)(2,1)} %get-tuple-element.50), channel_id=1, source_target_pairs={{0,1},{1,0},{2,3},{3,2},{4,5},{5,4},{6,7},{7,6},{8,9},{9,8},{10,11... | collective-permute-start | bytes 786440 | tf_op jit(solution)/shard_map/ppermute | solution.py:88
  11.7 47.1 %collective-permute-start.1 = (bf16[128,1024]{1,0:T(8,128)(2,1)}, bf16[128,1024]{1,0:T(8,128)(2,1)}, u32[]{:S(2)}, u32[]{:S(2)}) collective-permute-start(bf16[128,1024]{1,0:T(8,128)(2,1)} %get-tuple-element.50), channel_id=1, source_target_pairs={{0,2},{1,3},{2,0},{3,1},{4,6},{5,7},{6,4},{7,5},{8,10},{9,11},{10,... | collective-permute-start | bytes 786440 | tf_op jit(solution)/shard_map/ppermute | solution.py:88
  24.5 36.0 %collective-permute-start.2 = (bf16[128,1024]{1,0:T(8,128)(2,1)}, bf16[128,1024]{1,0:T(8,128)(2,1)S(1)}, u32[]{:S(2)}, u32[]{:S(2)}) collective-permute-start(bf16[128,1024]{1,0:T(8,128)(2,1)} %get-tuple-element.50), channel_id=1, source_target_pairs={{0,3},{1,2},{2,1},{3,0},{4,7},{5,6},{6,5},{7,4},{8,11},{9,10},{10,... | collective-permute-start | bytes 786440 | tf_op jit(solution)/shard_map/ppermute | solution.py:88
  47.3 17.7 %collective-permute-start.41 = (bf16[128,1024]{1,0:T(8,128)(2,1)}, bf16[128,1024]{1,0:T(8,128)(2,1)S(1)}, u32[]{:S(2)}, u32[]{:S(2)}) collective-permute-start(bf16[128,1024]{1,0:T(8,128)(2,1)} %get-tuple-element.46), channel_id=1, source_target_pairs={{0,1},{1,0},{2,3},{3,2},{4,5},{5,4},{6,7},{7,6},{8,9},{9,8},{10,11... | collective-permute-start | bytes 786440 | tf_op jit(solution)/shard_map/ppermute | solution.py:88
  54.4 21.0 %collective-permute-start.42 = (bf16[128,1024]{1,0:T(8,128)(2,1)}, bf16[128,1024]{1,0:T(8,128)(2,1)S(1)}, u32[]{:S(2)}, u32[]{:S(2)}) collective-permute-start(bf16[128,1024]{1,0:T(8,128)(2,1)} %get-tuple-element.46), channel_id=1, source_target_pairs={{0,2},{1,3},{2,0},{3,1},{4,6},{5,7},{6,4},{7,5},{8,10},{9,11},{10,... | collective-permute-start | bytes 786440 | tf_op jit(solution)/shard_map/ppermute | solution.py:88
  56.5 22.8 %collective-permute-start.43 = (bf16[128,1024]{1,0:T(8,128)(2,1)}, bf16[128,1024]{1,0:T(8,128)(2,1)}, u32[]{:S(2)}, u32[]{:S(2)}) collective-permute-start(bf16[128,1024]{1,0:T(8,128)(2,1)} %get-tuple-element.46), channel_id=1, source_target_pairs={{0,3},{1,2},{2,1},{3,0},{4,7},{5,6},{6,5},{7,4},{8,11},{9,10},{10,... | collective-permute-start | bytes 786440 | tf_op jit(solution)/shard_map/ppermute | solution.py:88
  65.0 16.2 %collective-permute-start.34 = (bf16[128,1024]{1,0:T(8,128)(2,1)}, bf16[128,1024]{1,0:T(8,128)(2,1)}, u32[]{:S(2)}, u32[]{:S(2)}) collective-permute-start(bf16[128,1024]{1,0:T(8,128)(2,1)} %get-tuple-element.48), channel_id=1, source_target_pairs={{0,16},{4,20},{8,24},{12,28},{16,0},{20,4},{24,8},{28,12},{1,17},{... | collective-permute-start | bytes 786440 | tf_op jit(solution)/shard_map/ppermute | solution.py:88
  66.6 19.6 %collective-permute-start.36 = (bf16[128,1024]{1,0:T(8,128)(2,1)}, bf16[128,1024]{1,0:T(8,128)(2,1)}, u32[]{:S(2)}, u32[]{:S(2)}) collective-permute-start(bf16[128,1024]{1,0:T(8,128)(2,1)} %get-tuple-element.48), channel_id=1, source_target_pairs={{0,24},{4,28},{8,16},{12,20},{16,8},{20,12},{24,0},{28,4},{1,25},{... | collective-permute-start | bytes 786440 | tf_op jit(solution)/shard_map/ppermute | solution.py:88
  69.7 34.9 %collective-permute-start.16 = (bf16[128,1792]{1,0:T(8,128)(2,1)}, bf16[128,1792]{1,0:T(8,128)(2,1)}, u32[]{:S(2)}, u32[]{:S(2)}) collective-permute-start(bf16[128,1792]{1,0:T(8,128)(2,1)} %bitcast.34), channel_id=1, source_target_pairs={{0,4},{4,0},{8,12},{12,8},{16,20},{20,16},{24,28},{28,24},{1,5},{5... | collective-permute-start | bytes 1376264 | tf_op jit(solution)/shard_map/ppermute | solution.py:88
  79.3 13.5 %collective-permute-start.17 = (bf16[128,1792]{1,0:T(8,128)(2,1)}, bf16[128,1792]{1,0:T(8,128)(2,1)S(1)}, u32[]{:S(2)}, u32[]{:S(2)}) collective-permute-start(bf16[128,1792]{1,0:T(8,128)(2,1)} %bitcast.34), channel_id=1, source_target_pairs={{0,8},{4,12},{8,0},{12,4},{16,24},{20,28},{24,16},{28,20},{1,9},{5... | collective-permute-start | bytes 1376264 | tf_op jit(solution)/shard_map/ppermute | solution.py:88
  81.3 22.8 %collective-permute-start.19 = (bf16[128,1792]{1,0:T(8,128)(2,1)}, bf16[128,1792]{1,0:T(8,128)(2,1)S(1)}, u32[]{:S(2)}, u32[]{:S(2)}) collective-permute-start(bf16[128,1792]{1,0:T(8,128)(2,1)} %bitcast.34), channel_id=1, source_target_pairs={{0,16},{4,20},{8,24},{12,28},{16,0},{20,4},{24,8},{28,12},{1,17},{... | collective-permute-start | bytes 1376264 | tf_op jit(solution)/shard_map/ppermute | solution.py:88
  86.2 17.8 %collective-permute-start.21 = (bf16[128,1792]{1,0:T(8,128)(2,1)}, bf16[128,1792]{1,0:T(8,128)(2,1)S(1)}, u32[]{:S(2)}, u32[]{:S(2)}) collective-permute-start(bf16[128,1792]{1,0:T(8,128)(2,1)} %bitcast.34), channel_id=1, source_target_pairs={{0,24},{4,28},{8,16},{12,20},{16,8},{20,12},{24,0},{28,4},{1,25},{... | collective-permute-start | bytes 1376264 | tf_op jit(solution)/shard_map/ppermute | solution.py:88
  92.8 14.4 %collective-permute-start.18 = (bf16[128,1792]{1,0:T(8,128)(2,1)S(1)}, bf16[128,1792]{1,0:T(8,128)(2,1)S(1)}, u32[]{:S(2)}, u32[]{:S(2)}) collective-permute-start(bf16[128,1792]{1,0:T(8,128)(2,1)S(1)} %collective-permute-done.17), channel_id=1, source_target_pairs={{0,4},{4,0},{8,12},{12,8},{16,20},{20,16},{24,28},{28,24},{1,5},{5... | collective-permute-start | bytes 1376264 | tf_op jit(solution)/shard_map/ppermute | solution.py:88
  133.5 13.5 %collective-permute-start.54 = (bf16[4,32,1024]{2,1,0:T(8,128)(2,1)}, bf16[4,32,1024]{2,1,0:T(8,128)(2,1)}, u32[]{:S(2)}, u32[]{:S(2)}) collective-permute-start(bf16[4,32,1024]{2,1,0:T(8,128)(2,1)} %fusion.58), channel_id=1, source_target_pairs={{0,4},{4,0},{8,12},{12,8},{16,20},{20,16},{24,28},{28,24},{1,5},{5... | collective-permute-start | bytes 786440 | tf_op jit(solution)/shard_map/ppermute | solution.py:88
  142.4 133.8 %collective-permute-start.66 = (bf16[4,128,1024]{2,1,0:T(8,128)(2,1)}, bf16[4,128,1024]{2,1,0:T(8,128)(2,1)}, u32[]{:S(2)}, u32[]{:S(2)}) collective-permute-start(bf16[4,128,1024]{2,1,0:T(8,128)(2,1)} %fusion.29), channel_id=1, source_target_pairs={{0,4},{4,0},{8,12},{12,8},{16,20},{20,16},{24,28},{28,24},{1,5},{5... | collective-permute-start | bytes 3145736 | tf_op jit(solution)/shard_map/ppermute | solution.py:88
  202.5 28.4 %collective-permute-start.38 = (bf16[1,128,1024]{2,1,0:T(8,128)(2,1)S(1)}, bf16[1,128,1024]{2,1,0:T(8,128)(2,1)S(1)}, u32[]{:S(2)}, u32[]{:S(2)}) collective-permute-start(bf16[1,128,1024]{2,1,0:T(8,128)(2,1)S(1)} %get-tuple-element.63), channel_id=1, source_target_pairs={{0,1},{1,0},{2,3},{3,2},{4,5},{5,4},{6,7},{7,6},{8,9},{9,8},{10,11... | collective-permute-start | bytes 786440 | tf_op jit(solution)/shard_map/ppermute | solution.py:88
  204.0 18.2 %collective-permute-start.44 = (bf16[1,128,1024]{2,1,0:T(8,128)(2,1)S(1)}, bf16[1,128,1024]{2,1,0:T(8,128)(2,1)S(1)}, u32[]{:S(2)}, u32[]{:S(2)}) collective-permute-start(bf16[1,128,1024]{2,1,0:T(8,128)(2,1)S(1)} %get-tuple-element.60), channel_id=1, source_target_pairs={{0,1},{1,0},{2,3},{3,2},{4,5},{5,4},{6,7},{7,6},{8,9},{9,8},{10,11... | collective-permute-start | bytes 786440 | tf_op jit(solution)/shard_map/ppermute | solution.py:88
  204.8 17.6 %collective-permute-start.45 = (bf16[1,128,1024]{2,1,0:T(8,128)(2,1)S(1)}, bf16[1,128,1024]{2,1,0:T(8,128)(2,1)S(1)}, u32[]{:S(2)}, u32[]{:S(2)}) collective-permute-start(bf16[1,128,1024]{2,1,0:T(8,128)(2,1)S(1)} %get-tuple-element.62), channel_id=1, source_target_pairs={{0,2},{1,3},{2,0},{3,1},{4,6},{5,7},{6,4},{7,5},{8,10},{9,11},{10,... | collective-permute-start | bytes 786440 | tf_op jit(solution)/shard_map/ppermute | solution.py:88
  207.1 23.3 %collective-permute-start.46 = (bf16[1,128,1024]{2,1,0:T(8,128)(2,1)S(1)}, bf16[1,128,1024]{2,1,0:T(8,128)(2,1)S(1)}, u32[]{:S(2)}, u32[]{:S(2)}) collective-permute-start(bf16[1,128,1024]{2,1,0:T(8,128)(2,1)S(1)} %get-tuple-element.61), channel_id=1, source_target_pairs={{0,3},{1,2},{2,1},{3,0},{4,7},{5,6},{6,5},{7,4},{8,11},{9,10},{10,... | collective-permute-start | bytes 786440 | tf_op jit(solution)/shard_map/ppermute | solution.py:88
  222.2 25.8 %collective-permute-start.39 = (bf16[1,128,1024]{2,1,0:T(8,128)(2,1)S(1)}, bf16[1,128,1024]{2,1,0:T(8,128)(2,1)S(1)}, u32[]{:S(2)}, u32[]{:S(2)}) collective-permute-start(bf16[1,128,1024]{2,1,0:T(8,128)(2,1)S(1)} %get-tuple-element.65), channel_id=1, source_target_pairs={{0,2},{1,3},{2,0},{3,1},{4,6},{5,7},{6,4},{7,5},{8,10},{9,11},{10,... | collective-permute-start | bytes 786440 | tf_op jit(solution)/shard_map/ppermute | solution.py:88
  222.4 25.6 %collective-permute-start.40 = (bf16[1,128,1024]{2,1,0:T(8,128)(2,1)S(1)}, bf16[1,128,1024]{2,1,0:T(8,128)(2,1)S(1)}, u32[]{:S(2)}, u32[]{:S(2)}) collective-permute-start(bf16[1,128,1024]{2,1,0:T(8,128)(2,1)S(1)} %get-tuple-element.64), channel_id=1, source_target_pairs={{0,3},{1,2},{2,1},{3,0},{4,7},{5,6},{6,5},{7,4},{8,11},{9,10},{10,... | collective-permute-start | bytes 786440 | tf_op jit(solution)/shard_map/ppermute | solution.py:88
  251.4 20.4 %collective-permute-start.59 = (bf16[4,128,1024]{2,1,0:T(8,128)(2,1)S(1)}, bf16[4,128,1024]{2,1,0:T(8,128)(2,1)S(1)}, u32[]{:S(2)}, u32[]{:S(2)}) collective-permute-start(bf16[4,128,1024]{2,1,0:T(8,128)(2,1)S(1)} %fusion.28), channel_id=1, source_target_pairs={{0,4},{4,0},{8,12},{12,8},{16,20},{20,16},{24,28},{28,24},{1,5},{5... | collective-permute-start | bytes 3145736 | tf_op jit(solution)/shard_map/ppermute | solution.py:88
  268.1 37.4 %collective-permute-start.47 = (bf16[4,128,768]{2,1,0:T(8,128)(2,1)}, bf16[4,128,768]{2,1,0:T(8,128)(2,1)}, u32[]{:S(2)}, u32[]{:S(2)}) collective-permute-start(bf16[4,128,768]{2,1,0:T(8,128)(2,1)} %fusion.33), channel_id=1, source_target_pairs={{0,4},{4,0},{8,12},{12,8},{16,20},{20,16},{24,28},{28,24},{1,5},{5... | collective-permute-start | bytes 2359304 | tf_op jit(solution)/shard_map/ppermute | solution.py:88
  273.7 13.1 %collective-permute-start.61 = (bf16[1,128,1024]{2,1,0:T(8,128)(2,1)S(1)}, bf16[1,128,1024]{2,1,0:T(8,128)(2,1)S(1)}, u32[]{:S(2)}, u32[]{:S(2)}) collective-permute-start(bf16[1,128,1024]{2,1,0:T(8,128)(2,1)S(1)} %get-tuple-element.59), channel_id=1, source_target_pairs={{0,16},{4,20},{8,24},{12,28},{16,0},{20,4},{24,8},{28,12},{1,17},{... | collective-permute-start | bytes 786440 | tf_op jit(solution)/shard_map/ppermute | solution.py:88
  274.4 13.4 %collective-permute-start.62 = (bf16[1,128,1024]{2,1,0:T(8,128)(2,1)S(1)}, bf16[1,128,1024]{2,1,0:T(8,128)(2,1)S(1)}, u32[]{:S(2)}, u32[]{:S(2)}) collective-permute-start(bf16[1,128,1024]{2,1,0:T(8,128)(2,1)S(1)} %get-tuple-element.58), channel_id=1, source_target_pairs={{0,24},{4,28},{8,16},{12,20},{16,8},{20,12},{24,0},{28,4},{1,25},{... | collective-permute-start | bytes 786440 | tf_op jit(solution)/shard_map/ppermute | solution.py:88
  278.0 14.4 %collective-permute-start.67 = (bf16[1,128,1024]{2,1,0:T(8,128)(2,1)S(1)}, bf16[1,128,1024]{2,1,0:T(8,128)(2,1)S(1)}, u32[]{:S(2)}, u32[]{:S(2)}) collective-permute-start(bf16[1,128,1024]{2,1,0:T(8,128)(2,1)S(1)} %get-tuple-element.54), channel_id=1, source_target_pairs={{0,8},{4,12},{8,0},{12,4},{16,24},{20,28},{24,16},{28,20},{1,9},{5... | collective-permute-start | bytes 786440 | tf_op jit(solution)/shard_map/ppermute | solution.py:88
  281.9 14.1 %collective-permute-start.68 = (bf16[1,128,1024]{2,1,0:T(8,128)(2,1)S(1)}, bf16[1,128,1024]{2,1,0:T(8,128)(2,1)S(1)}, u32[]{:S(2)}, u32[]{:S(2)}) collective-permute-start(bf16[1,128,1024]{2,1,0:T(8,128)(2,1)S(1)} %get-tuple-element.56), channel_id=1, source_target_pairs={{0,16},{4,20},{8,24},{12,28},{16,0},{20,4},{24,8},{28,12},{1,17},{... | collective-permute-start | bytes 786440 | tf_op jit(solution)/shard_map/ppermute | solution.py:88
  286.8 11.6 %collective-permute-start.69 = (bf16[1,128,1024]{2,1,0:T(8,128)(2,1)S(1)}, bf16[1,128,1024]{2,1,0:T(8,128)(2,1)S(1)}, u32[]{:S(2)}, u32[]{:S(2)}) collective-permute-start(bf16[1,128,1024]{2,1,0:T(8,128)(2,1)S(1)} %get-tuple-element.55), channel_id=1, source_target_pairs={{0,24},{4,28},{8,16},{12,20},{16,8},{20,12},{24,0},{28,4},{1,25},{... | collective-permute-start | bytes 786440 | tf_op jit(solution)/shard_map/ppermute | solution.py:88
  287.9 12.1 %collective-permute-start.63 = (bf16[32,1024]{1,0:T(8,128)(2,1)S(1)}, bf16[32,1024]{1,0:T(8,128)(2,1)S(1)}, u32[]{:S(2)}, u32[]{:S(2)}) collective-permute-start(bf16[32,1024]{1,0:T(8,128)(2,1)S(1)} %get-tuple-element.86), channel_id=1, source_target_pairs={{0,1},{1,0},{2,3},{3,2},{4,5},{5,4},{6,7},{7,6},{8,9},{9,8},{10,11... | collective-permute-start | bytes 196616 | tf_op jit(solution)/shard_map/ppermute | solution.py:88
  (135 other events, 913.6 us)

commit v2 on v1

v2 whole, which is shorter than its diff:
```python
import functools

import jax
import jax.numpy as jnp
import numpy as np
from jax import lax
from jax.experimental import pallas as pl
from jax.experimental.pallas import tpu as pltpu
from jax.sharding import PartitionSpec as P

D = 1024
HEADS = 16
HEAD = D // HEADS
FF = 4096
ROT = 16
STEP = 10
LANES = 128


LN_EPS = 1e-05
BETA_ONE = 0.9
BETA_TWO = 0.95
ADAM_EPS = 1e-08
LR_MATRIX = 0.03
LR_VECTOR = 0.2
WEIGHT_DECAY = 0.01
ROPE_BASE = 10000.0
INV_ROOT_TWO = 0.7071067811865476
INV_ROOT_TAU = 0.3989422804014327
HIDDEN = -1e30
bf16 = jnp.bfloat16
f32 = jnp.float32
TILE = 256


def adam_update(param, grad, first, second, rate, decay):
    first_new = BETA_ONE * first + (1.0 - BETA_ONE) * grad
    second_new = BETA_TWO * second + (1.0 - BETA_TWO) * grad * grad
    first_hat = first_new / (1.0 - BETA_ONE**STEP)
    second_hat = second_new / (1.0 - BETA_TWO**STEP)
    return (
        param - rate * (first_hat / (jnp.sqrt(second_hat) + ADAM_EPS) + decay * param),
        first_new,
        second_new,
    )


def contract_rows(left, right):
    return lax.dot_general(left, right, (((0,), (0,)), ((), ())), preferred_element_type=f32)


def contract_cols(left, right):
    return lax.dot_general(left, right, (((1,), (1,)), ((), ())), preferred_element_type=f32)


def plain_dot(left, right):
    return jnp.dot(left, right, preferred_element_type=f32)


def rope_lanes(seq_len):
    half = ROT // 2
    freqs = (ROPE_BASE ** (-(2.0 * np.arange(half, dtype=np.float32) / ROT))).astype(np.float32)
    angles = np.arange(seq_len, dtype=np.float32)[:, None] * freqs[None, :]
    cosines, sines = np.cos(angles), np.sin(angles)
    keep = np.ones((seq_len, HEAD), np.float32)
    up = np.zeros((seq_len, HEAD), np.float32)
    down = np.zeros((seq_len, HEAD), np.float32)
    keep[:, :half], keep[:, half:ROT] = cosines, cosines
    up[:, :half] = -sines
    down[:, half:ROT] = sines
    reps = LANES // HEAD
    return np.concatenate([np.tile(t, (1, reps)) for t in (keep, up, down)], axis=1)


def turn(values, table, sign):
    half = ROT // 2
    above = pltpu.roll(values, LANES - half, 1)
    below = pltpu.roll(values, half, 1)
    moved = above * table[:, LANES : 2 * LANES] + below * table[:, 2 * LANES :]
    return values * table[:, :LANES] + sign * moved


def params(mib):
    return pltpu.CompilerParams(vmem_limit_bytes=mib << 20)


def cost(flops, count):
    return pl.CostEstimate(flops=flops, bytes_accessed=count, transcendentals=0)


def whole_spec(shape):
    return pl.BlockSpec(shape, lambda *_: (0,) * len(shape))


def columns_body(inverse, width, order_ref, x_ref, o_ref):
    for i in range(x_ref.shape[1] // width):
        there = pl.ds(pl.multiple_of(order_ref[i] * width, LANES), width)
        here = slice(i * width, (i + 1) * width)
        if inverse:
            o_ref[:, there] = x_ref[:, here]
        else:
            o_ref[:, here] = x_ref[:, there]


def order_columns(values, order, inverse=False):
    width = values.shape[1] // order.shape[0]
    if width % LANES:
        return values
    spec = whole_spec(values.shape)
    return pl.pallas_call(
        functools.partial(columns_body, inverse, width),
        out_shape=jax.ShapeDtypeStruct(values.shape, values.dtype),
        grid_spec=pltpu.PrefetchScalarGridSpec(
            num_scalar_prefetch=1, grid=(1,), in_specs=[spec], out_specs=spec
        ),
        cost_estimate=cost(0, 2 * values.size * values.dtype.itemsize),
        name="order_columns",
    )(order, values)


def blocks_body(order_ref, x_ref, o_ref):
    for i in range(o_ref.shape[0]):
        o_ref[i] = x_ref[order_ref[i]]


def order_blocks(values, order):
    spec = whole_spec(values.shape)
    return pl.pallas_call(
        blocks_body,
        out_shape=jax.ShapeDtypeStruct(values.shape, values.dtype),
        grid_spec=pltpu.PrefetchScalarGridSpec(
            num_scalar_prefetch=1, grid=(1,), in_specs=[spec], out_specs=spec
        ),
        cost_estimate=cost(0, 2 * values.size * values.dtype.itemsize),
        name="order_blocks",
    )(order, values)


def front_body(
    width, order_ref, n_ref, vec_ref, low_ref, high_ref, bias_ref, rope_ref, h1_ref, h2_ref, qkv_ref, act_ref, slope_ref
):
    j = pl.program_id(0)

    @pl.when(j == 0)
    def _():
        normed = n_ref[...].astype(f32)
        h1_ref[...] = (normed * vec_ref[0:1, :] + vec_ref[1:2, :]).astype(bf16)
        h2_ref[...] = (normed * vec_ref[2:3, :] + vec_ref[3:4, :]).astype(bf16)

    half = low_ref.shape[0]

    def product(h_ref):
        total = plain_dot(h_ref[:, :half], low_ref[...]) + plain_dot(h_ref[:, half:], high_ref[...])
        return total + bias_ref[...]

    @pl.when(j < 2)
    def _():
        lin = product(h1_ref)
        for c in range(0, TILE, LANES):
            qkv_ref[:, c : c + LANES] = turn(lin[:, c : c + LANES], rope_ref[...], 1.0).astype(bf16)

    @pl.when(j == 2)
    def _():
        qkv_ref[...] = product(h1_ref).astype(bf16)

    @pl.when(j > 2)
    def _():
        lin = product(h2_ref)
        above = 0.5 * (1.0 + lax.erf(lin * INV_ROOT_TWO))
        act = (lin * above).astype(bf16)
        slope = above + lin * jnp.exp(-0.5 * lin * lin) * INV_ROOT_TAU
        for c in range(0, TILE, LANES):
            at = (j - 3) * TILE + c
            if width % LANES == 0:
                block = at // width
                place = order_ref[order_ref.shape[0] // 2 + block] * width
                at = place + (at - block * width)
            at = pl.ds(pl.multiple_of(at, LANES), LANES)
            act_ref[:, at] = act[:, c : c + LANES]
            slope_ref[:, at] = slope[:, c : c + LANES]


def front(orders, normed, vec, low, high, bias, rope, width):
    tokens = normed.shape[0]
    half, cols = low.shape
    tiles = cols // TILE
    gaps = D
    call = pl.pallas_call(
        functools.partial(front_body, width),
        out_shape=(
            jax.ShapeDtypeStruct((tokens, D), bf16),
            jax.ShapeDtypeStruct((tokens, D), bf16),
            jax.ShapeDtypeStruct((tokens, 3 * TILE), bf16),
            jax.ShapeDtypeStruct((tokens, cols - 3 * TILE), bf16),
            jax.ShapeDtypeStruct((tokens, cols - 3 * TILE), f32),
        ),
        grid_spec=pltpu.PrefetchScalarGridSpec(
            num_scalar_prefetch=1,
            grid=(tiles,),
            in_specs=[
                whole_spec((tokens, gaps)),
                whole_spec(vec.shape),
                pl.BlockSpec((half, TILE), lambda j, o: (0, j)),
                pl.BlockSpec((half, TILE), lambda j, o: (0, j)),
                pl.BlockSpec((1, TILE), lambda j, o: (0, j)),
                whole_spec(rope.shape),
            ],
            out_specs=(
                whole_spec((tokens, D)),
                whole_spec((tokens, D)),
                pl.BlockSpec((tokens, TILE), lambda j, o: (0, jnp.minimum(j, 2))),
                whole_spec((tokens, cols - 3 * TILE)),
                whole_spec((tokens, cols - 3 * TILE)),
            ),
        ),
        compiler_params=params(40),
        cost_estimate=cost(2 * tokens * D * cols, 12 << 20),
        name="front",
    )
    return call(orders, normed, vec, low, high, bias, rope)


def hidden_body(width, order_ref, dy_ref, out_ref, down_ref, slope_ref, dmix_ref, du_ref, sum_ref):
    dy = dy_ref[...]
    dmix_ref[...] = contract_cols(dy, out_ref[...]).astype(bf16)
    for c in range(0, down_ref.shape[0], LANES):
        du = contract_cols(dy, down_ref[c : c + LANES, :]) * slope_ref[:, c : c + LANES]
        at = c
        if width % LANES == 0:
            block = c // width
            at = pl.multiple_of(order_ref[block] * width + (c - block * width), LANES)
        at = pl.ds(at, LANES)
        du_ref[:, at] = du.astype(bf16)
        sum_ref[:, at] = jnp.sum(du, axis=0, keepdims=True)


def hidden(orders, dy, out_whole, down_whole, slope, width):
    tokens = dy.shape[0]
    feats, units = out_whole.shape[0], down_whole.shape[0]
    return pl.pallas_call(
        functools.partial(hidden_body, width),
        out_shape=(
            jax.ShapeDtypeStruct((tokens, feats), bf16),
            jax.ShapeDtypeStruct((tokens, units), bf16),
            jax.ShapeDtypeStruct((1, units), f32),
        ),
        grid_spec=pltpu.PrefetchScalarGridSpec(
            num_scalar_prefetch=1,
            grid=(1,),
            in_specs=[whole_spec(a.shape) for a in (dy, out_whole, down_whole, slope)],
            out_specs=(
                whole_spec((tokens, feats)),
                whole_spec((tokens, units)),
                whole_spec((1, units)),
            ),
        ),
        compiler_params=params(40),
        cost_estimate=cost(2 * tokens * D * (feats + units), 8 << 20),
        name="hidden",
    )(orders, dy, out_whole, down_whole, slope)


def attend_body(q_ref, k_ref, v_ref, dm_ref, mask_ref, rope_ref, mix_ref, dqkv_ref, sum_ref, dk_ref, dv_ref):
    pair = pl.program_id(0)
    tokens = q_ref.shape[0]
    chunk = LANES
    scale = HEAD ** (-0.5)
    first = lax.broadcasted_iota(jnp.int32, (chunk, LANES), 1) < HEAD
    every = lax.broadcasted_iota(jnp.int32, (tokens, LANES), 1) < HEAD
    k = k_ref[...]
    v = v_ref[...]
    pairs = pl.num_programs(0)

    def columns(part):
        return pl.ds(pl.multiple_of(part * pairs * LANES + pair * LANES, LANES), LANES)

    dq_total = jnp.zeros((1, LANES), f32)
    for c in range(0, tokens, chunk):
        rows = slice(c, c + chunk)
        q = q_ref[rows, :]
        dm = dm_ref[rows, :]
        mixes, dqs, dks, dvs = [], [], [], []
        for h in range(2):
            mine = first if h == 0 else jnp.logical_not(first)
            qh = jnp.where(mine, q, jnp.zeros_like(q))
            dmh = jnp.where(mine, dm, jnp.zeros_like(dm))
            score = contract_cols(qh, k) * scale + mask_ref[rows, :]
            expo = jnp.exp(score - jnp.max(score, axis=-1, keepdims=True))
            prob = expo * (1.0 / jnp.sum(expo, axis=-1, keepdims=True))
            prob16 = prob.astype(bf16)
            mix16 = plain_dot(prob16, v).astype(bf16)
            delta = jnp.sum(dmh.astype(f32) * mix16.astype(f32), axis=-1, keepdims=True)
            d_prob = contract_cols(dmh, v)
            ds16 = (prob * (d_prob - delta) * scale).astype(bf16)
            mixes.append(mix16)
            dqs.append(plain_dot(ds16, k))
            dks.append(contract_rows(ds16, q))
            dvs.append(contract_rows(prob16, dm))
        mix_ref[rows, :] = jnp.where(first, mixes[0], mixes[1])
        dq = turn(jnp.where(first, dqs[0], dqs[1]), rope_ref[rows, :], -1.0)
        dqkv_ref[rows, columns(0)] = dq.astype(bf16)
        dq_total = dq_total + jnp.sum(dq, axis=0, keepdims=True)
        dk = jnp.where(every, dks[0], dks[1])
        dv = jnp.where(every, dvs[0], dvs[1])
        if c == 0:
            dk_ref[...] = dk
            dv_ref[...] = dv
        else:
            dk_ref[...] += dk
            dv_ref[...] += dv
    dk = turn(dk_ref[...], rope_ref[...], -1.0)
    dv = dv_ref[...]
    dqkv_ref[:, columns(1)] = dk.astype(bf16)
    dqkv_ref[:, columns(2)] = dv.astype(bf16)
    sum_ref[:, columns(0)] = dq_total
    sum_ref[:, columns(1)] = jnp.sum(dk, axis=0, keepdims=True)
    sum_ref[:, columns(2)] = jnp.sum(dv, axis=0, keepdims=True)


def attend(qkv, d_mix, mask, rope):
    tokens, feats = d_mix.shape
    pairs = feats // LANES

    def part(first):
        return pl.BlockSpec((tokens, LANES), lambda j: (0, first * pairs + j))

    return pl.pallas_call(
        attend_body,
        out_shape=(
            jax.ShapeDtypeStruct((tokens, feats), bf16),
            jax.ShapeDtypeStruct((tokens, 3 * feats), bf16),
            jax.ShapeDtypeStruct((1, 3 * feats), f32),
        ),
        grid=(pairs,),
        in_specs=[
            part(0),
            part(1),
            part(2),
            part(0),
            whole_spec(mask.shape),
            whole_spec(rope.shape),
        ],
        out_specs=(
            pl.BlockSpec((tokens, LANES), lambda j: (0, j)),
            whole_spec((tokens, 3 * feats)),
            whole_spec((1, 3 * feats)),
        ),
        scratch_shapes=[pltpu.VMEM((tokens, LANES), f32), pltpu.VMEM((tokens, LANES), f32)],
        compiler_params=params(40),
        cost_estimate=cost(60 * tokens * tokens * feats, 6 << 20),
        name="attend",
    )(qkv, qkv, qkv, d_mix, mask, rope)


def back_body(dqkv_ref, du_ref, n_ref, vec_ref, low_ref, high_ref, sent_ref, own_ref, sum_ref):
    feats = dqkv_ref.shape[1]
    weights = jnp.where(pl.program_id(0) * 2 < pl.num_programs(0), low_ref[...], high_ref[...])
    d_one = contract_cols(dqkv_ref[...], weights[:, :feats])
    d_two = contract_cols(du_ref[...], weights[:, feats:])
    scaled = d_one * vec_ref[0:1, :] + d_two * vec_ref[2:3, :]
    sent_ref[...] = scaled.astype(bf16)
    own_ref[...] = scaled[: own_ref.shape[0], :]
    normed = n_ref[...].astype(f32)
    sum_ref[0:1, :] = jnp.sum(d_one * normed, axis=0, keepdims=True)
    sum_ref[1:2, :] = jnp.sum(d_one, axis=0, keepdims=True)
    sum_ref[2:3, :] = jnp.sum(d_two * normed, axis=0, keepdims=True)
    sum_ref[3:4, :] = jnp.sum(d_two, axis=0, keepdims=True)


def back(d_qkv, d_up, normed, vec, low, high, own_rows):
    tokens = normed.shape[0]
    half, cols = low.shape
    near = half // TILE
    return pl.pallas_call(
        back_body,
        out_shape=(
            jax.ShapeDtypeStruct((tokens, D), bf16),
            jax.ShapeDtypeStruct((own_rows, D), f32),
            jax.ShapeDtypeStruct((4, D), f32),
        ),
        grid=(2 * near,),
        in_specs=[
            whole_spec(d_qkv.shape),
            whole_spec(d_up.shape),
            pl.BlockSpec((tokens, TILE), lambda j: (0, j)),
            pl.BlockSpec((4, TILE), lambda j: (0, j)),
            pl.BlockSpec((TILE, cols), lambda j: (jnp.minimum(j, near - 1), 0)),
            pl.BlockSpec((TILE, cols), lambda j: (jnp.maximum(j - near, 0), 0)),
        ],
        out_specs=(
            pl.BlockSpec((tokens, TILE), lambda j: (0, j)),
            pl.BlockSpec((own_rows, TILE), lambda j: (0, j)),
            pl.BlockSpec((4, TILE), lambda j: (0, j)),
        ),
        compiler_params=params(40),
        cost_estimate=cost(2 * tokens * D * cols, 10 << 20),
        name="back",
    )(d_qkv, d_up, normed, vec, low, high)


def hop(value, axis, size, mask):
    return lax.ppermute(value, axis, [(i, i ^ mask) for i in range(size)])


def stages(size):
    bits = size.bit_length() - 1
    found = []
    while bits > 0:
        take = 2 if bits >= 2 else 1
        bits -= take
        found.append((bits, 1 << take))
    return found


def relative_masks(size):
    masks = np.zeros((1,), np.int32)
    for shift, count in stages(size):
        masks = np.concatenate([masks ^ (k << shift) for k in range(count)])
    return masks


def gather_halves(own, axis, size, relative):
    if not relative:
        whole = lax.all_gather(own, axis)
        return whole[: size // 2], whole[size // 2 :]
    current = own[None]
    pieces = []
    for shift, count in stages(size):
        pieces = [current] + [hop(current, axis, size, k << shift) for k in range(1, count)]
        if shift:
            current = jnp.concatenate(pieces, axis=0)
    if len(pieces) == 2:
        return pieces
    middle = len(pieces) // 2
    return jnp.concatenate(pieces[:middle]), jnp.concatenate(pieces[middle:])


def reduce_relative(keep, sent, axis, size):
    for shift, count in reversed(stages(size)):
        total = keep
        for k in range(1, count):
            total = total + hop(sent[k - 1], axis, size, k << shift).astype(f32)
        if shift == 0 and len(stages(size)) == 1:
            return total
        if total.shape[0] == 1:
            return total[0]
        upper = [c for t, c in stages(size) if t > shift][-1]
        view = total.reshape((upper, total.shape[0] // upper) + total.shape[1:])
        keep, sent = view[0], [view[k].astype(bf16) for k in range(1, upper)]
    return keep


def shards(
    block_in,
    cotangent,
    segments,
    qkv_weight,
    out_weight,
    up_weight,
    down_weight,
    vectors,
    first_qkv,
    first_out,
    first_up,
    first_down,
    first_vec,
    second_qkv,
    second_out,
    second_up,
    second_down,
    second_vec,
):
    tok_count = block_in.shape[0]
    n_rep = lax.axis_size("rep")
    n_shard = lax.axis_size("shard")
    rep = lax.axis_index("rep")
    shard = lax.axis_index("shard")
    seq_len = tok_count * n_shard
    own_heads = HEADS // n_shard
    own_feats = own_heads * HEAD
    rows = qkv_weight.shape[0]
    units = down_weight.shape[0]
    own_units = units * n_rep
    n_vec, cols = vectors.shape
    groups = own_feats // LANES
    width = D // n_rep
    relative = width % LANES == 0
    masks = relative_masks(n_rep)
    if relative:
        order = rep ^ jnp.asarray(masks)
        mask_of = rep ^ jnp.arange(n_rep, dtype=jnp.int32)
        place = jnp.sum(
            jnp.where(mask_of[:, None] == jnp.asarray(masks)[None], jnp.arange(n_rep)[None], 0), axis=1
        ).astype(jnp.int32)
    else:
        order = jnp.arange(n_rep, dtype=jnp.int32)
        place = order
    orders = jnp.concatenate([order, place]).astype(jnp.int32)
    near = shard ^ jnp.arange(n_shard, dtype=jnp.int32)

    qkv_cols = qkv_weight.astype(bf16).reshape(rows, 3 * groups, n_shard, LANES)
    up_cols = up_weight.astype(bf16).reshape(rows, n_rep, n_shard, units)
    in_cols = jnp.concatenate(
        [
            qkv_cols.transpose(2, 0, 1, 3).reshape(n_shard, rows, 3 * own_feats),
            up_cols.transpose(2, 0, 1, 3).reshape(n_shard, rows, own_units),
        ],
        axis=2,
    )
    in_cols = order_blocks(in_cols, near)
    in_rows = jnp.stack(
        [in_cols[0]] + [hop(in_cols[k], "shard", n_shard, k) for k in range(1, n_shard)]
    )
    in_rows = order_blocks(in_rows, near).reshape(n_shard * rows, 3 * own_feats + own_units)

    center = block_in - jnp.mean(block_in, axis=-1, keepdims=True)
    inv_std = lax.rsqrt(jnp.mean(center * center, axis=-1, keepdims=True) + LN_EPS)
    normed = center * inv_std
    normed_own = order_columns(normed.astype(bf16), order)
    normed_seq = jnp.concatenate(
        [normed_own] + [hop(normed_own, "shard", n_shard, k) for k in range(1, n_shard)], axis=0
    )

    vec_all = vectors
    vec_all = jnp.stack(
        [vec_all] + [hop(vec_all, "shard", n_shard, k) for k in range(1, n_shard)], axis=0
    )
    vec_low, vec_high = gather_halves(vec_all, "rep", n_rep, relative)
    vec_all = jnp.concatenate([vec_low, vec_high], axis=0).reshape(
        n_rep * n_shard, n_vec, cols
    )
    flat = jnp.arange(n_rep * n_shard, dtype=jnp.int32)
    vec_all = order_blocks(vec_all, flat ^ shard)
    norm_vec = vec_all[:, :4].transpose(1, 0, 2).reshape(4, D)
    if relative:
        vec_all = order_blocks(
            vec_all, (place[:, None] * n_shard + jnp.arange(n_shard)[None]).reshape(-1)
        )
    vec_abs = vec_all.transpose(1, 0, 2).reshape(n_vec, D)

    low, high = gather_halves(in_rows, "rep", n_rep, relative)
    low = low.reshape(D // 2, 3 * own_feats + own_units)
    high = high.reshape(D // 2, 3 * own_feats + own_units)

    dy_own = cotangent.astype(bf16)
    upstream16 = jnp.concatenate(
        [dy_own] + [hop(dy_own, "shard", n_shard, k) for k in range(1, n_shard)], axis=0
    )

    share = HEAD // rows
    pair = LANES // HEAD
    moves = []
    for device in range(n_rep * n_shard):
        head, part = device // share, device % share
        owner = (head // pair) % n_shard
        local = (head // (pair * n_shard)) * pair + head % pair
        moves.append((device, (local * share + part) * n_shard + owner))
    out_rows = lax.ppermute(out_weight.astype(bf16), ("rep", "shard"), moves)
    both_rows = jnp.concatenate([out_rows, down_weight.astype(bf16)], axis=0)
    both = jnp.concatenate(gather_halves(both_rows, "rep", n_rep, relative), axis=0)
    out_whole = both[:, :rows]
    if relative:
        out_whole = order_blocks(out_whole, place)
    out_whole = out_whole.reshape(own_feats, D)
    down_whole = both[:, rows:].reshape(own_units, D)

    per_row = FF // D
    qkv_bias = vec_abs[4:7].reshape(3 * groups, n_shard, LANES)
    up_bias = vec_abs[8 : 8 + per_row].reshape(n_rep, n_shard, units)
    bias = jnp.concatenate(
        [
            lax.dynamic_index_in_dim(qkv_bias, shard, 1, keepdims=False).reshape(1, 3 * own_feats),
            lax.dynamic_index_in_dim(up_bias, shard, 1, keepdims=False).reshape(1, own_units),
        ],
        axis=1,
    )
    rope = order_blocks(
        jnp.asarray(rope_lanes(seq_len)).reshape(n_shard, tok_count, 3 * LANES), near
    ).reshape(seq_len, 3 * LANES)
    seg_row = jnp.concatenate(
        [lax.dynamic_slice(segments[0], (near[k] * tok_count,), (tok_count,)) for k in range(n_shard)]
    )
    positions = (near[:, None] * tok_count + jnp.arange(tok_count)[None, :]).reshape(seq_len)
    allowed = (seg_row[:, None] == seg_row[None, :]) & (positions[None, :] <= positions[:, None])
    mask = jnp.where(allowed, 0.0, HIDDEN).astype(f32)

    h_one, h_two, qkv16, act16, slope = front(
        orders, normed_seq, norm_vec, low, high, bias, rope, units
    )
    d_mixed16, d_up16, up_sum = hidden(orders, upstream16, out_whole, down_whole, slope, units)
    term_half = D // 2

    def split_terms(left, right):
        keep = contract_rows(left[:, :term_half], right)
        sent = contract_rows(left[:, term_half:], right).astype(bf16)
        return keep, sent

    def reduce_rep(keep, sent, block):
        if relative:
            return reduce_relative(keep, [sent], "rep", n_rep)
        terms = jnp.concatenate([keep, sent.astype(f32)], axis=0)
        return lax.psum_scatter(terms, "rep", scatter_dimension=0, tiled=True)[0]

    up_keep, up_sent = split_terms(h_two, d_up16)
    half_rep = n_rep // 2
    sum_up = reduce_rep(
        up_keep.reshape(half_rep, n_shard * rows, own_units),
        up_sent.reshape(half_rep, n_shard * rows, own_units),
        n_shard * rows,
    )

    mixed16, d_qkv16, qkv_sum = attend(qkv16, d_mixed16, mask, rope)

    qkv_keep, qkv_sent = split_terms(h_one, d_qkv16)
    sum_qkv = reduce_rep(
        qkv_keep.reshape(half_rep, n_shard * rows, 3 * own_feats),
        qkv_sent.reshape(half_rep, n_shard * rows, 3 * own_feats),
        n_shard * rows,
    )

    scaled16, scaled_own, norm_sum = back(
        d_qkv16, d_up16, normed_seq, norm_vec, low, high, tok_count
    )
    scaled = scaled_own
    for k in range(1, n_shard):
        piece = scaled16[k * tok_count : (k + 1) * tok_count]
        scaled = scaled + hop(piece, "shard", n_shard, k).astype(f32)
    scaled = order_columns(scaled, order, inverse=True)
    grad_input = cotangent + inv_std * (
        scaled
        - jnp.mean(scaled, axis=-1, keepdims=True)
        - normed * jnp.mean(scaled * normed, axis=-1, keepdims=True)
    )

    def branch(some):
        return plain_dot(mixed16[some], out_whole) + plain_dot(act16[some], down_whole)

    block_out = block_in + branch(slice(0, tok_count)) + vec_abs[7] + vec_abs[8 + per_row]
    sent_out = branch(slice(tok_count, seq_len)).astype(bf16)
    for k in range(1, n_shard):
        piece = sent_out[(k - 1) * tok_count : k * tok_count]
        block_out = block_out + hop(piece, "shard", n_shard, k).astype(f32)

    down_keep, down_sent = split_terms(act16, upstream16)
    term_out = contract_rows(mixed16, upstream16).reshape(n_rep, rows, D)
    if relative:
        term_out = order_blocks(term_out, order)
    sum_both = reduce_rep(
        jnp.concatenate([down_keep.reshape(half_rep, units, D), term_out[:half_rep]], axis=1),
        jnp.concatenate(
            [down_sent.reshape(half_rep, units, D), term_out[half_rep:].astype(bf16)], axis=1
        ),
        units + rows,
    )
    grad_down = sum_both[:units]
    grad_out = lax.ppermute(sum_both[units:], ("rep", "shard"), [(b, a) for a, b in moves])

    def back_rows(sums):
        blocks = order_blocks(sums.reshape(n_shard, rows, sums.shape[1]), near)
        got = [blocks[0]]
        for k in range(1, n_shard):
            got.append(hop(blocks[k].astype(bf16), "shard", n_shard, k).astype(f32))
        return order_blocks(jnp.stack(got), near)

    grad_up = back_rows(sum_up).reshape(n_shard, rows, n_rep, units)
    grad_up = grad_up.transpose(1, 2, 0, 3).reshape(rows, FF)
    grad_qkv = back_rows(sum_qkv).reshape(n_shard, rows, 3 * groups, LANES)
    grad_qkv = grad_qkv.transpose(1, 2, 0, 3).reshape(rows, 3 * D)

    mine = jnp.arange(n_shard) == shard
    cot_sum = jnp.sum(cotangent, axis=0)[None]
    bias_qkv = jnp.where(
        mine[None, :, None], qkv_sum.reshape(3 * groups, 1, LANES), 0.0
    ).reshape(3, D)
    bias_up = jnp.where(
        mine[None, :, None], up_sum.reshape(n_rep, 1, units), 0.0
    ).reshape(per_row, D)
    late = jnp.concatenate([bias_qkv, cot_sum, bias_up, cot_sum], axis=0)
    late = late.reshape(n_vec - 4, n_rep * n_shard, cols).transpose(1, 0, 2)
    early = norm_sum.reshape(4, n_rep * n_shard, cols).transpose(1, 0, 2)
    late = order_blocks(late, (order[:, None] * n_shard + near[None]).reshape(-1))
    early = order_blocks(early, flat ^ shard)
    vec_terms = jnp.concatenate([early, late], axis=1)
    vec_terms = vec_terms.reshape(n_rep, n_shard, n_vec, cols).transpose(1, 0, 2, 3)
    grad_vec = vec_terms[0]
    for k in range(1, n_shard):
        grad_vec = grad_vec + hop(vec_terms[k], "shard", n_shard, k)
    if relative:
        for shift, count in reversed(stages(n_rep)):
            view = grad_vec.reshape((count, grad_vec.shape[0] // count) + grad_vec.shape[1:])
            grad_vec = view[0]
            for k in range(1, count):
                grad_vec = grad_vec + hop(view[k], "rep", n_rep, k << shift)
        grad_vec = grad_vec[0]
    else:
        grad_vec = lax.psum_scatter(grad_vec, "rep", scatter_dimension=0, tiled=True)[0]

    new_qkv, new_first_qkv, new_second_qkv = adam_update(
        qkv_weight, grad_qkv, first_qkv, second_qkv, LR_MATRIX, WEIGHT_DECAY
    )
    new_out, new_first_out, new_second_out = adam_update(
        out_weight, grad_out, first_out, second_out, LR_MATRIX, WEIGHT_DECAY
    )
    new_up, new_first_up, new_second_up = adam_update(
        up_weight, grad_up, first_up, second_up, LR_MATRIX, WEIGHT_DECAY
    )
    new_down, new_first_down, new_second_down = adam_update(
        down_weight, grad_down, first_down, second_down, LR_MATRIX, WEIGHT_DECAY
    )
    new_vec, new_first_vec, new_second_vec = adam_update(
        vectors, grad_vec, first_vec, second_vec, LR_VECTOR, 0.0
    )
    return (
        block_out,
        grad_input,
        grad_qkv,
        grad_out,
        grad_up,
        grad_down,
        grad_vec,
        new_qkv,
        new_out,
        new_up,
        new_down,
        new_vec,
        new_first_qkv,
        new_first_out,
        new_first_up,
        new_first_down,
        new_first_vec,
        new_second_qkv,
        new_second_out,
        new_second_up,
        new_second_down,
        new_second_vec,
    )


def solution(mesh):
    return jax.shard_map(
        shards,
        mesh=mesh,
        in_specs=(
            P(("rep", "shard"), None),
            P(("rep", "shard"), None),
            P("rep", None),
            P(("rep", "shard"), None),
            P(("rep", "shard"), None),
            P(("rep", "shard"), None),
            P(("rep", "shard"), None),
            P(None, ("rep", "shard")),
            P(("rep", "shard"), None),
            P(("rep", "shard"), None),
            P(("rep", "shard"), None),
            P(("rep", "shard"), None),
            P(None, ("rep", "shard")),
            P(("rep", "shard"), None),
            P(("rep", "shard"), None),
            P(("rep", "shard"), None),
            P(("rep", "shard"), None),
            P(None, ("rep", "shard")),
        ),
        out_specs=(
            P(("rep", "shard"), None),
            P(("rep", "shard"), None),
            P(("rep", "shard"), None),
            P(("rep", "shard"), None),
            P(("rep", "shard"), None),
            P(("rep", "shard"), None),
            P(None, ("rep", "shard")),
            P(("rep", "shard"), None),
            P(("rep", "shard"), None),
            P(("rep", "shard"), None),
            P(("rep", "shard"), None),
            P(None, ("rep", "shard")),
            P(("rep", "shard"), None),
            P(("rep", "shard"), None),
            P(("rep", "shard"), None),
            P(("rep", "shard"), None),
            P(None, ("rep", "shard")),
            P(("rep", "shard"), None),
            P(("rep", "shard"), None),
            P(("rep", "shard"), None),
            P(("rep", "shard"), None),
            P(None, ("rep", "shard")),
        ),
        check_vma=False,
    )
```

time: 335 us -> 324 us (0.967)
  the two profiles are of different devices: /device:TPU:0 before, /device:TPU:2 now
where the time goes in v2:
time: 324 us; the launch traced here: 322 us
  waiting for transfers between devices  85.8 us (26%)
  starting transfers between devices  82.5 us (25%)
  Pallas kernels  65.3 us (20%)
  other arithmetic  40.6 us (13%)
  local copies, waits for them, and re-layouts  24.2 us (7%)
  matrix products  19.1 us (6%)
  between operations  4.36 us (1%)
    ppermute x55, waiting for transfers between devices, hop(): return lax.ppermute(value, axis, [(i, i ^ mask) for i in range(size)])  78.5 us
    ppermute x55, starting transfers between devices, hop(): return lax.ppermute(value, axis, [(i, i ^ mask) for i in range(size)])  76.5 us
    pallas_call x13, Pallas kernels, order_blocks(): pl.pallas_call(blocks_body, out_shape=jax.ShapeDtypeStruct(values.shape,...  32.3 us
    dot_general x7, matrix products, contract_rows(): lax.dot_general(left, right, (((0,), (0,)), ((), ())), preferred_element_...  13.4 us
    pallas_call x1, Pallas kernels, attend(): pl.pallas_call(attend_body, out_shape=(jax.ShapeDtypeStruct((tokens, feat...  11.7 us
    pallas_call x1, Pallas kernels, front(): return call(orders, normed, vec, low, high, bias, rope)  7.88 us
    another operation x5, other arithmetic  7.51 us
    ppermute x1, waiting for transfers between devices, shards(): lax.ppermute(sum_both[units:], ('rep', 'shard'), [(b, a) for a, b in moves])  7.27 us
  transfers between devices with their start and end apart: 57, of which 26 were waited for; matrix products, arithmetic and copies ran while one was open for 18% of the time, Pallas kernels for 10%

profile of v2, /device:TPU:2, one launch (start us, length us, event | category | flops | bytes accessed | tf_op | source)
XLA Modules:
  0.0 321.8 jit_solution(9822231164997616204)
XLA Ops:
  0.7 3.7 %collective-permute-start.5 = (f32[13,32]{1,0:T(8,128)}, f32[13,32]{1,0:T(8,128)S(1)}, u32[]{:S(2)}, u32[]{:S(2)}) collective-permute-start(f32[13,32]{1,0:T(8,128)} %param.27), channel_id=1, source_target_pairs={{0,3},{1,2},{2,1},{3,0},{4,7},{5,6},{6,5},{7,4},{8,11},{9,10},{10,... | collective-permute-start | bytes 5000 | tf_op jit(solution)/shard_map/ppermute | solution.py:402
  6.0 4.0 %collective-permute-start.20 = (bf16[32,1024]{1,0:T(8,128)(2,1)S(1)}, bf16[32,1024]{1,0:T(8,128)(2,1)S(1)}, u32[]{:S(2)}, u32[]{:S(2)}) collective-permute-start(bf16[32,1024]{1,0:T(8,128)(2,1)S(1)} %convert_element_type.146), channel_id=1, source_target_pairs={{0,0},{1,4},{2,8},{3,12},{4,1},{5,5},{6,9},{7,13},{8,2},{9,6},{10,... | collective-permute-start | bytes 196616 | tf_op jit(solution)/shard_map/ppermute | solution.py:558
  13.3 2.6 order_blocks.14
  28.8 2.7 order_blocks.17
  39.3 4.4 %collective-permute-done.11 = bf16[32,1792]{1,0:T(8,128)(2,1)S(1)} collective-permute-done((bf16[32,1792]{1,0:T(8,128)(2,1)S(1)}, bf16[32,1792]{1,0:T(8,128)(2,1)S(1)}, u32[]{:S(2)}, u32[]{:S(2)}) %collective-permute-start.11) | collective-permute-done | bytes 114720 | tf_op jit(solution)/shard_map/ppermute | solution.py:402
  50.6 2.7 collective-permute-start.2
  64.4 5.0 %collective-permute-done.14 = bf16[1,128,1792]{2,1,0:T(8,128)(2,1)} collective-permute-done((bf16[1,128,1792]{2,1,0:T(8,128)(2,1)}, bf16[1,128,1792]{2,1,0:T(8,128)(2,1)}, u32[]{:S(2)}, u32[]{:S(2)}) %collective-permute-start.14) | collective-permute-done | bytes 458784 | tf_op jit(solution)/shard_map/ppermute | solution.py:402
  71.7 2.6 pad_maximum_fusion
  74.3 4.3 %collective-permute-done.21 = bf16[1,160,1024]{2,1,0:T(8,128)(2,1)S(1)} collective-permute-done((bf16[1,160,1024]{2,1,0:T(8,128)(2,1)S(1)}, bf16[1,160,1024]{2,1,0:T(8,128)(2,1)S(1)}, u32[]{:S(2)}, u32[]{:S(2)}) %collective-permute-start.21) | collective-permute-done | bytes 327712 | tf_op jit(solution)/shard_map/ppermute | solution.py:402
  85.5 4.3 %collective-permute-start.19 = (bf16[128,1024]{1,0:T(8,128)(2,1)S(1)}, bf16[128,1024]{1,0:T(8,128)(2,1)S(1)}, u32[]{:S(2)}, u32[]{:S(2)}) collective-permute-start(bf16[128,1024]{1,0:T(8,128)(2,1)S(1)} %get-tuple-element.93), channel_id=1, source_target_pairs={{0,3},{1,2},{2,1},{3,0},{4,7},{5,6},{6,5},{7,4},{8,11},{9,10},{10,... | collective-permute-start | bytes 786440 | tf_op jit(solution)/shard_map/ppermute | solution.py:402
  90.0 4.7 %collective-permute-start.17 = (bf16[128,1024]{1,0:T(8,128)(2,1)S(1)}, bf16[128,1024]{1,0:T(8,128)(2,1)}, u32[]{:S(2)}, u32[]{:S(2)}) collective-permute-start(bf16[128,1024]{1,0:T(8,128)(2,1)S(1)} %get-tuple-element.93), channel_id=1, source_target_pairs={{0,1},{1,0},{2,3},{3,2},{4,5},{5,4},{6,7},{7,6},{8,9},{9,8},{10,11... | collective-permute-start | bytes 786440 | tf_op jit(solution)/shard_map/ppermute | solution.py:402
  98.0 14.1 %collective-permute-done.18 = bf16[128,1024]{1,0:T(8,128)(2,1)S(1)} collective-permute-done((bf16[128,1024]{1,0:T(8,128)(2,1)S(1)}, bf16[128,1024]{1,0:T(8,128)(2,1)S(1)}, u32[]{:S(2)}, u32[]{:S(2)}) %collective-permute-start.18) | collective-permute-done | bytes 262176 | tf_op jit(solution)/shard_map/ppermute | solution.py:402
  116.5 2.5 order_blocks.18
  121.4 7.9 %front.1 = (bf16[512,1024]{1,0:T(8,128)(2,1)S(1)}, bf16[512,1024]{1,0:T(8,128)(2,1)S(1)}, bf16[512,768]{1,0:T(8,128)(2,1)S(1)}, bf16[512,1024]{1,0:T(8,128)(2,1)S(1)}, f32[512,1024]{1,0:T(8,128)S(1)}) custom-call(s32[16]{0:T(128)S(1)} %pad_add_fusion.1.order_ref, bf16[512,1024]{1,0:T(8,128)(2,1)S(1)} %copy-done.3, f32[4,1024]{1,0:T(4,128)S(1)} %reshape.329.vec_ref, ...), custom_call_target="tpu_custom_call" | custom-call | flops 1879048192 | bytes 12582912 | tf_op jit(solution)/shard_map/front/pallas_call | solution.py:220
  135.4 3.2 hidden.1
  142.3 11.7 %attend.1 = (bf16[512,256]{1,0:T(8,128)(2,1)S(1)}, bf16[512,768]{1,0:T(8,128)(2,1)S(1)}, f32[1,768]{1,0:T(1,128)S(1)}) custom-call(bf16[512,768]{1,0:T(8,128)(2,1)S(1)} %get-tuple-element.36.q_ref.k_ref.v_ref, bf16[512,768]{1,0:T(8,128)(2,1)S(1)} %get-tuple-element.36.q_ref.k_ref.v_ref, bf16[512,768]{1,0:T(8,128)(2,1)S(1)} %get-tuple-element.36.q_ref.k_ref.v_ref, ...), custom_call_target="tpu_custom_call" | custom-call | flops 4026531840 | bytes 6291456 | tf_op jit(solution)/shard_map/attend/pallas_call | solution.py:327
  156.7 5.2 %back.1 = (bf16[512,1024]{1,0:T(8,128)(2,1)S(1)}, f32[128,1024]{1,0:T(8,128)S(1)}, f32[4,1024]{1,0:T(4,128)S(1)}) custom-call(bf16[512,768]{1,0:T(8,128)(2,1)S(1)} %get-tuple-element.41.dqkv_ref, bf16[512,1024]{1,0:T(8,128)(2,1)S(1)} %get-tuple-element.42.du_ref, bf16[512,1024]{1,0:T(8,128)(2,1)S(1)} %copy-done.4, f32[4,1024]{1,0:T(4,128)S(1)} %reshape.329.vec_ref, ...), custom_call_target="tpu_custom_call" | custom-call | flops 1879048192 | bytes 10485760 | tf_op jit(solution)/shard_map/back/pallas_call | solution.py:374
  171.4 3.7 %collective-permute-start.52 = (f32[8,13,32]{2,1,0:T(8,128)S(1)}, f32[8,13,32]{2,1,0:T(8,128)S(1)}, u32[]{:S(2)}, u32[]{:S(2)}) collective-permute-start(f32[8,13,32]{2,1,0:T(8,128)S(1)} %get-tuple-element.99), channel_id=1, source_target_pairs={{0,3},{1,2},{2,1},{3,0},{4,7},{5,6},{6,5},{7,4},{8,11},{9,10},{10,... | collective-permute-start | bytes 39944 | tf_op jit(solution)/shard_map/ppermute | solution.py:402
  189.0 2.9 order_blocks.21
  199.8 6.9 %collective-permute-start.25 = (bf16[128,1024]{1,0:T(8,128)(2,1)}, bf16[128,1024]{1,0:T(8,128)(2,1)}, u32[]{:S(2)}, u32[]{:S(2)}) collective-permute-start(bf16[128,1024]{1,0:T(8,128)(2,1)} %get-tuple-element.89), channel_id=1, source_target_pairs={{0,1},{1,0},{2,3},{3,2},{4,5},{5,4},{6,7},{7,6},{8,9},{9,8},{10,11... | collective-permute-start | bytes 786440 | tf_op jit(solution)/shard_map/ppermute | solution.py:402
  206.8 15.7 %collective-permute-done.29 = bf16[128,1024]{1,0:T(8,128)(2,1)S(1)} collective-permute-done((bf16[128,1024]{1,0:T(8,128)(2,1)}, bf16[128,1024]{1,0:T(8,128)(2,1)S(1)}, u32[]{:S(2)}, u32[]{:S(2)}) %collective-permute-start.29) | collective-permute-done | bytes 262176 | tf_op jit(solution)/shard_map/ppermute | solution.py:402
  225.7 2.6 order_columns.3
  229.7 3.1 collective-permute-done.26
  238.9 5.2 %collective-permute-done.34 = bf16[1,128,768]{2,1,0:T(8,128)(2,1)S(1)} collective-permute-done((bf16[1,128,768]{2,1,0:T(8,128)(2,1)S(1)}, bf16[1,128,768]{2,1,0:T(8,128)(2,1)S(1)}, u32[]{:S(2)}, u32[]{:S(2)}) %collective-permute-start.34) | collective-permute-done | bytes 196640 | tf_op jit(solution)/shard_map/ppermute | solution.py:402
  250.5 2.5 collective-permute-start.37
  270.5 5.4 %collective-permute-done.46 = bf16[1,128,1024]{2,1,0:T(8,128)(2,1)S(1)} collective-permute-done((bf16[1,128,1024]{2,1,0:T(8,128)(2,1)S(1)}, bf16[1,128,1024]{2,1,0:T(8,128)(2,1)S(1)}, u32[]{:S(2)}, u32[]{:S(2)}) %collective-permute-start.46) | collective-permute-done | bytes 262176 | tf_op jit(solution)/shard_map/ppermute | solution.py:402
  276.0 3.3 %collective-permute-done.45 = bf16[1,128,1024]{2,1,0:T(8,128)(2,1)S(1)} collective-permute-done((bf16[1,128,1024]{2,1,0:T(8,128)(2,1)S(1)}, bf16[1,128,1024]{2,1,0:T(8,128)(2,1)S(1)}, u32[]{:S(2)}, u32[]{:S(2)}) %collective-permute-start.45) | collective-permute-done | bytes 262176 | tf_op jit(solution)/shard_map/ppermute | solution.py:402
  280.2 2.5 order_blocks.22
  286.3 3.3 %fusion.51 = (bf16[4,160,1024]{2,1,0:T(8,128)(2,1)S(1)}, f32[4,160,1024]{2,1,0:T(8,128)}) fusion(bf16[4,160,1024]{2,1,0:T(8,128)(2,1)} %collective-permute-done.38, f32[4,32,1024]{2,1,0:T(8,128)S(1)} %slice-done, f32[4,128,1024]{2,1,0:T(8,128)S(1)} %bitcast.160), kind=kLoop, calls=%fused_computation.160 | loop fusion | flops 2621440 | bytes 7864320 | tf_op jit(solution)/shard_map/convert.14
  296.1 3.5 %collective-permute-done.48 = bf16[32,1024]{1,0:T(8,128)(2,1)S(1)} collective-permute-done((bf16[32,1024]{1,0:T(8,128)(2,1)S(1)}, bf16[32,1024]{1,0:T(8,128)(2,1)S(1)}, u32[]{:S(2)}, u32[]{:S(2)}) %collective-permute-start.48) | collective-permute-done | bytes 65568 | tf_op jit(solution)/shard_map/ppermute | solution.py:402
  300.5 2.5 order_blocks.23
  313.1 7.3 %collective-permute-done.42 = f32[32,1024]{1,0:T(8,128)S(1)} collective-permute-done((f32[32,1024]{1,0:T(8,128)S(1)}, f32[32,1024]{1,0:T(8,128)S(1)}, u32[]{:S(2)}, u32[]{:S(2)}) %collective-permute-start.42) | collective-permute-done | bytes 131104 | tf_op jit(solution)/shard_map/ppermute | solution.py:656
  (358 shorter events, 161.3 us)
Async XLA Ops:
  0.7 31.6 %collective-permute-start.5 = (f32[13,32]{1,0:T(8,128)}, f32[13,32]{1,0:T(8,128)S(1)}, u32[]{:S(2)}, u32[]{:S(2)}) collective-permute-start(f32[13,32]{1,0:T(8,128)} %param.27), channel_id=1, source_target_pairs={{0,3},{1,2},{2,1},{3,0},{4,7},{5,6},{6,5},{7,4},{8,11},{9,10},{10,... | collective-permute-start | bytes 5000 | tf_op jit(solution)/shard_map/ppermute | solution.py:402
  4.3 27.9 %collective-permute-start.4 = (f32[13,32]{1,0:T(8,128)}, f32[13,32]{1,0:T(8,128)S(1)}, u32[]{:S(2)}, u32[]{:S(2)}) collective-permute-start(f32[13,32]{1,0:T(8,128)} %param.27), channel_id=1, source_target_pairs={{0,2},{1,3},{2,0},{3,1},{4,6},{5,7},{6,4},{7,5},{8,10},{9,11},{10,... | collective-permute-start | bytes 5000 | tf_op jit(solution)/shard_map/ppermute | solution.py:402
  4.3 27.9 %collective-permute-start.3 = (f32[13,32]{1,0:T(8,128)}, f32[13,32]{1,0:T(8,128)S(1)}, u32[]{:S(2)}, u32[]{:S(2)}) collective-permute-start(f32[13,32]{1,0:T(8,128)} %param.27), channel_id=1, source_target_pairs={{0,1},{1,0},{2,3},{3,2},{4,5},{5,4},{6,7},{7,6},{8,9},{9,8},{10,11... | collective-permute-start | bytes 5000 | tf_op jit(solution)/shard_map/ppermute | solution.py:402
  6.0 54.8 %collective-permute-start.20 = (bf16[32,1024]{1,0:T(8,128)(2,1)S(1)}, bf16[32,1024]{1,0:T(8,128)(2,1)S(1)}, u32[]{:S(2)}, u32[]{:S(2)}) collective-permute-start(bf16[32,1024]{1,0:T(8,128)(2,1)S(1)} %convert_element_type.146), channel_id=1, source_target_pairs={{0,0},{1,4},{2,8},{3,12},{4,1},{5,5},{6,9},{7,13},{8,2},{9,6},{10,... | collective-permute-start | bytes 196616 | tf_op jit(solution)/shard_map/ppermute | solution.py:558
  17.0 22.3 %collective-permute-start.12 = (bf16[32,1792]{1,0:T(8,128)(2,1)S(1)}, bf16[32,1792]{1,0:T(8,128)(2,1)S(1)}, u32[]{:S(2)}, u32[]{:S(2)}) collective-permute-start(bf16[32,1792]{1,0:T(8,128)(2,1)S(1)} %get-tuple-element.95), channel_id=1, source_target_pairs={{0,3},{1,2},{2,1},{3,0},{4,7},{5,6},{6,5},{7,4},{8,11},{9,10},{10,... | collective-permute-start | bytes 344072 | tf_op jit(solution)/shard_map/ppermute | solution.py:402
  47.1 15.8 %collective-permute-start.15 = (bf16[1,128,1792]{2,1,0:T(8,128)(2,1)}, bf16[1,128,1792]{2,1,0:T(8,128)(2,1)S(1)}, u32[]{:S(2)}, u32[]{:S(2)}) collective-permute-start(bf16[1,128,1792]{2,1,0:T(8,128)(2,1)} %bitcast.167), channel_id=1, source_target_pairs={{0,24},{4,28},{8,16},{12,20},{16,8},{20,12},{24,0},{28,4},{1,25},{... | collective-permute-start | bytes 1376264 | tf_op jit(solution)/shard_map/ppermute | solution.py:402
  48.7 20.8 %collective-permute-start.14 = (bf16[1,128,1792]{2,1,0:T(8,128)(2,1)}, bf16[1,128,1792]{2,1,0:T(8,128)(2,1)}, u32[]{:S(2)}, u32[]{:S(2)}) collective-permute-start(bf16[1,128,1792]{2,1,0:T(8,128)(2,1)} %bitcast.168), channel_id=1, source_target_pairs={{0,16},{4,20},{8,24},{12,28},{16,0},{20,4},{24,8},{28,12},{1,17},{... | collective-permute-start | bytes 1376264 | tf_op jit(solution)/shard_map/ppermute | solution.py:402
  49.1 22.6 %collective-permute-start.13 = (bf16[1,128,1792]{2,1,0:T(8,128)(2,1)}, bf16[1,128,1792]{2,1,0:T(8,128)(2,1)}, u32[]{:S(2)}, u32[]{:S(2)}) collective-permute-start(bf16[1,128,1792]{2,1,0:T(8,128)(2,1)} %bitcast.169), channel_id=1, source_target_pairs={{0,8},{4,12},{8,0},{12,4},{16,24},{20,28},{24,16},{28,20},{1,9},{5... | collective-permute-start | bytes 1376264 | tf_op jit(solution)/shard_map/ppermute | solution.py:402
  50.6 34.8 %collective-permute-start.2 = (bf16[128,1024]{1,0:T(8,128)(2,1)S(1)}, bf16[128,1024]{1,0:T(8,128)(2,1)}, u32[]{:S(2)}, u32[]{:S(2)}) collective-permute-start(bf16[128,1024]{1,0:T(8,128)(2,1)S(1)} %copy-done.27), channel_id=1, source_target_pairs={{0,3},{1,2},{2,1},{3,0},{4,7},{5,6},{6,5},{7,4},{8,11},{9,10},{10,... | collective-permute-start | bytes 786440 | tf_op jit(solution)/shard_map/ppermute | solution.py:402
  60.9 17.7 %collective-permute-start.21 = (bf16[1,160,1024]{2,1,0:T(8,128)(2,1)S(1)}, bf16[1,160,1024]{2,1,0:T(8,128)(2,1)S(1)}, u32[]{:S(2)}, u32[]{:S(2)}) collective-permute-start(bf16[1,160,1024]{2,1,0:T(8,128)(2,1)S(1)} %maximum_bitcast_fusion), channel_id=1, source_target_pairs={{0,8},{4,12},{8,0},{12,4},{16,24},{20,28},{24,16},{28,20},{1,9},{5... | collective-permute-start | bytes 983048 | tf_op jit(solution)/shard_map/ppermute | solution.py:402
  62.9 17.1 %collective-permute-start.22 = (bf16[1,160,1024]{2,1,0:T(8,128)(2,1)S(1)}, bf16[1,160,1024]{2,1,0:T(8,128)(2,1)S(1)}, u32[]{:S(2)}, u32[]{:S(2)}) collective-permute-start(bf16[1,160,1024]{2,1,0:T(8,128)(2,1)S(1)} %maximum_bitcast_fusion), channel_id=1, source_target_pairs={{0,16},{4,20},{8,24},{12,28},{16,0},{20,4},{24,8},{28,12},{1,17},{... | collective-permute-start | bytes 983048 | tf_op jit(solution)/shard_map/ppermute | solution.py:402
  69.5 13.8 %collective-permute-start.23 = (bf16[1,160,1024]{2,1,0:T(8,128)(2,1)S(1)}, bf16[1,160,1024]{2,1,0:T(8,128)(2,1)S(1)}, u32[]{:S(2)}, u32[]{:S(2)}) collective-permute-start(bf16[1,160,1024]{2,1,0:T(8,128)(2,1)S(1)} %maximum_bitcast_fusion), channel_id=1, source_target_pairs={{0,24},{4,28},{8,16},{12,20},{16,8},{20,12},{24,0},{28,4},{1,25},{... | collective-permute-start | bytes 983048 | tf_op jit(solution)/shard_map/ppermute | solution.py:402
  74.3 44.8 %collective-permute-start.16 = (bf16[4,128,1792]{2,1,0:T(8,128)(2,1)}, bf16[4,128,1792]{2,1,0:T(8,128)(2,1)}, u32[]{:S(2)}, u32[]{:S(2)}) collective-permute-start(bf16[4,128,1792]{2,1,0:T(8,128)(2,1)} %pad_maximum_fusion), channel_id=1, source_target_pairs={{0,4},{4,0},{8,12},{12,8},{16,20},{20,16},{24,28},{28,24},{1,5},{5... | collective-permute-start | bytes 5505032 | tf_op jit(solution)/shard_map/ppermute | solution.py:402
  84.5 29.6 %collective-permute-start.24 = (bf16[4,160,1024]{2,1,0:T(8,128)(2,1)}, bf16[4,160,1024]{2,1,0:T(8,128)(2,1)}, u32[]{:S(2)}, u32[]{:S(2)}) collective-permute-start(bf16[4,160,1024]{2,1,0:T(8,128)(2,1)} %pad_maximum_fusion.1), channel_id=1, source_target_pairs={{0,4},{4,0},{8,12},{12,8},{16,20},{20,16},{24,28},{28,24},{1,5},{5... | collective-permute-start | bytes 3932168 | tf_op jit(solution)/shard_map/ppermute | solution.py:402
  85.5 12.5 %collective-permute-start.19 = (bf16[128,1024]{1,0:T(8,128)(2,1)S(1)}, bf16[128,1024]{1,0:T(8,128)(2,1)S(1)}, u32[]{:S(2)}, u32[]{:S(2)}) collective-permute-start(bf16[128,1024]{1,0:T(8,128)(2,1)S(1)} %get-tuple-element.93), channel_id=1, source_target_pairs={{0,3},{1,2},{2,1},{3,0},{4,7},{5,6},{6,5},{7,4},{8,11},{9,10},{10,... | collective-permute-start | bytes 786440 | tf_op jit(solution)/shard_map/ppermute | solution.py:402
  90.0 22.1 %collective-permute-start.18 = (bf16[128,1024]{1,0:T(8,128)(2,1)S(1)}, bf16[128,1024]{1,0:T(8,128)(2,1)S(1)}, u32[]{:S(2)}, u32[]{:S(2)}) collective-permute-start(bf16[128,1024]{1,0:T(8,128)(2,1)S(1)} %get-tuple-element.93), channel_id=1, source_target_pairs={{0,2},{1,3},{2,0},{3,1},{4,6},{5,7},{6,4},{7,5},{8,10},{9,11},{10,... | collective-permute-start | bytes 786440 | tf_op jit(solution)/shard_map/ppermute | solution.py:402
  90.0 22.8 %collective-permute-start.17 = (bf16[128,1024]{1,0:T(8,128)(2,1)S(1)}, bf16[128,1024]{1,0:T(8,128)(2,1)}, u32[]{:S(2)}, u32[]{:S(2)}) collective-permute-start(bf16[128,1024]{1,0:T(8,128)(2,1)S(1)} %get-tuple-element.93), channel_id=1, source_target_pairs={{0,1},{1,0},{2,3},{3,2},{4,5},{5,4},{6,7},{7,6},{8,9},{9,8},{10,11... | collective-permute-start | bytes 786440 | tf_op jit(solution)/shard_map/ppermute | solution.py:402
  182.1 12.5 %collective-permute-start.56 = (f32[1,13,32]{2,1,0:T(8,128)S(1)}, f32[1,13,32]{2,1,0:T(8,128)S(1)}, u32[]{:S(2)}, u32[]{:S(2)}) collective-permute-start(f32[1,13,32]{2,1,0:T(8,128)S(1)} %get-tuple-element.108), channel_id=1, source_target_pairs={{0,24},{4,28},{8,16},{12,20},{16,8},{20,12},{24,0},{28,4},{1,25},{... | collective-permute-start | bytes 5000 | tf_op jit(solution)/shard_map/ppermute | solution.py:402
  184.6 15.3 %collective-permute-start.30 = (bf16[128,1024]{1,0:T(8,128)(2,1)}, bf16[128,1024]{1,0:T(8,128)(2,1)S(1)}, u32[]{:S(2)}, u32[]{:S(2)}) collective-permute-start(bf16[128,1024]{1,0:T(8,128)(2,1)} %get-tuple-element.84), channel_id=1, source_target_pairs={{0,3},{1,2},{2,1},{3,0},{4,7},{5,6},{6,5},{7,4},{8,11},{9,10},{10,... | collective-permute-start | bytes 786440 | tf_op jit(solution)/shard_map/ppermute | solution.py:402
  187.1 35.4 %collective-permute-start.29 = (bf16[128,1024]{1,0:T(8,128)(2,1)}, bf16[128,1024]{1,0:T(8,128)(2,1)S(1)}, u32[]{:S(2)}, u32[]{:S(2)}) collective-permute-start(bf16[128,1024]{1,0:T(8,128)(2,1)} %get-tuple-element.85), channel_id=1, source_target_pairs={{0,2},{1,3},{2,0},{3,1},{4,6},{5,7},{6,4},{7,5},{8,10},{9,11},{10,... | collective-permute-start | bytes 786440 | tf_op jit(solution)/shard_map/ppermute | solution.py:402
  187.1 36.1 %collective-permute-start.28 = (bf16[128,1024]{1,0:T(8,128)(2,1)}, bf16[128,1024]{1,0:T(8,128)(2,1)}, u32[]{:S(2)}, u32[]{:S(2)}) collective-permute-start(bf16[128,1024]{1,0:T(8,128)(2,1)} %get-tuple-element.83), channel_id=1, source_target_pairs={{0,1},{1,0},{2,3},{3,2},{4,5},{5,4},{6,7},{7,6},{8,9},{9,8},{10,11... | collective-permute-start | bytes 786440 | tf_op jit(solution)/shard_map/ppermute | solution.py:402
  196.7 32.9 %collective-permute-start.27 = (bf16[128,1024]{1,0:T(8,128)(2,1)}, bf16[128,1024]{1,0:T(8,128)(2,1)}, u32[]{:S(2)}, u32[]{:S(2)}) collective-permute-start(bf16[128,1024]{1,0:T(8,128)(2,1)} %get-tuple-element.90), channel_id=1, source_target_pairs={{0,3},{1,2},{2,1},{3,0},{4,7},{5,6},{6,5},{7,4},{8,11},{9,10},{10,... | collective-permute-start | bytes 786440 | tf_op jit(solution)/shard_map/ppermute | solution.py:402
  199.2 33.6 %collective-permute-start.26 = (bf16[128,1024]{1,0:T(8,128)(2,1)}, bf16[128,1024]{1,0:T(8,128)(2,1)}, u32[]{:S(2)}, u32[]{:S(2)}) collective-permute-start(bf16[128,1024]{1,0:T(8,128)(2,1)} %get-tuple-element.91), channel_id=1, source_target_pairs={{0,2},{1,3},{2,0},{3,1},{4,6},{5,7},{6,4},{7,5},{8,10},{9,11},{10,... | collective-permute-start | bytes 786440 | tf_op jit(solution)/shard_map/ppermute | solution.py:402
  199.8 32.9 %collective-permute-start.25 = (bf16[128,1024]{1,0:T(8,128)(2,1)}, bf16[128,1024]{1,0:T(8,128)(2,1)}, u32[]{:S(2)}, u32[]{:S(2)}) collective-permute-start(bf16[128,1024]{1,0:T(8,128)(2,1)} %get-tuple-element.89), channel_id=1, source_target_pairs={{0,1},{1,0},{2,3},{3,2},{4,5},{5,4},{6,7},{7,6},{8,9},{9,8},{10,11... | collective-permute-start | bytes 786440 | tf_op jit(solution)/shard_map/ppermute | solution.py:402
  223.2 11.8 %collective-permute-start.31 = (bf16[4,128,768]{2,1,0:T(8,128)(2,1)}, bf16[4,128,768]{2,1,0:T(8,128)(2,1)S(1)}, u32[]{:S(2)}, u32[]{:S(2)}) collective-permute-start(bf16[4,128,768]{2,1,0:T(8,128)(2,1)} %bitcast.35), channel_id=1, source_target_pairs={{0,4},{4,0},{8,12},{12,8},{16,20},{20,16},{24,28},{28,24},{1,5},{5... | collective-permute-start | bytes 2359304 | tf_op jit(solution)/shard_map/ppermute | solution.py:402
  223.2 63.1 %collective-permute-start.38 = (bf16[4,160,1024]{2,1,0:T(8,128)(2,1)}, bf16[4,160,1024]{2,1,0:T(8,128)(2,1)}, u32[]{:S(2)}, u32[]{:S(2)}) collective-permute-start(bf16[4,160,1024]{2,1,0:T(8,128)(2,1)} %pad_maximum_fusion.2), channel_id=1, source_target_pairs={{0,4},{4,0},{8,12},{12,8},{16,20},{20,16},{24,28},{28,24},{1,5},{5... | collective-permute-start | bytes 3932168 | tf_op jit(solution)/shard_map/ppermute | solution.py:402
  229.6 34.2 %collective-permute-start.43 = (bf16[4,128,1024]{2,1,0:T(8,128)(2,1)}, bf16[4,128,1024]{2,1,0:T(8,128)(2,1)}, u32[]{:S(2)}, u32[]{:S(2)}) collective-permute-start(bf16[4,128,1024]{2,1,0:T(8,128)(2,1)} %bitcast.195), channel_id=1, source_target_pairs={{0,4},{4,0},{8,12},{12,8},{16,20},{20,16},{24,28},{28,24},{1,5},{5... | collective-permute-start | bytes 3145736 | tf_op jit(solution)/shard_map/ppermute | solution.py:402
  266.9 12.3 %collective-permute-start.45 = (bf16[1,128,1024]{2,1,0:T(8,128)(2,1)S(1)}, bf16[1,128,1024]{2,1,0:T(8,128)(2,1)S(1)}, u32[]{:S(2)}, u32[]{:S(2)}) collective-permute-start(bf16[1,128,1024]{2,1,0:T(8,128)(2,1)S(1)} %get-tuple-element.82), channel_id=1, source_target_pairs={{0,16},{4,20},{8,24},{12,28},{16,0},{20,4},{24,8},{28,12},{1,17},{... | collective-permute-start | bytes 786440 | tf_op jit(solution)/shard_map/ppermute | solution.py:402
  267.7 11.5 %collective-permute-start.44 = (bf16[1,128,1024]{2,1,0:T(8,128)(2,1)S(1)}, bf16[1,128,1024]{2,1,0:T(8,128)(2,1)S(1)}, u32[]{:S(2)}, u32[]{:S(2)}) collective-permute-start(bf16[1,128,1024]{2,1,0:T(8,128)(2,1)S(1)} %get-tuple-element.80), channel_id=1, source_target_pairs={{0,8},{4,12},{8,0},{12,4},{16,24},{20,28},{24,16},{28,20},{1,9},{5... | collective-permute-start | bytes 786440 | tf_op jit(solution)/shard_map/ppermute | solution.py:402
  290.6 15.8 %collective-permute-start.41 = (bf16[1,160,1024]{2,1,0:T(8,128)(2,1)}, bf16[1,160,1024]{2,1,0:T(8,128)(2,1)S(1)}, u32[]{:S(2)}, u32[]{:S(2)}) collective-permute-start(bf16[1,160,1024]{2,1,0:T(8,128)(2,1)} %get-tuple-element.78), channel_id=1, source_target_pairs={{0,24},{4,28},{8,16},{12,20},{16,8},{20,12},{24,0},{28,4},{1,25},{... | collective-permute-start | bytes 983048 | tf_op jit(solution)/shard_map/ppermute | solution.py:402
  291.9 16.2 %collective-permute-start.40 = (bf16[1,160,1024]{2,1,0:T(8,128)(2,1)}, bf16[1,160,1024]{2,1,0:T(8,128)(2,1)S(1)}, u32[]{:S(2)}, u32[]{:S(2)}) collective-permute-start(bf16[1,160,1024]{2,1,0:T(8,128)(2,1)} %get-tuple-element.79), channel_id=1, source_target_pairs={{0,16},{4,20},{8,24},{12,28},{16,0},{20,4},{24,8},{28,12},{1,17},{... | collective-permute-start | bytes 983048 | tf_op jit(solution)/shard_map/ppermute | solution.py:402
  292.5 15.6 %collective-permute-start.39 = (bf16[1,160,1024]{2,1,0:T(8,128)(2,1)}, bf16[1,160,1024]{2,1,0:T(8,128)(2,1)}, u32[]{:S(2)}, u32[]{:S(2)}) collective-permute-start(bf16[1,160,1024]{2,1,0:T(8,128)(2,1)} %get-tuple-element.77), channel_id=1, source_target_pairs={{0,8},{4,12},{8,0},{12,4},{16,24},{20,28},{24,16},{28,20},{1,9},{5... | collective-permute-start | bytes 983048 | tf_op jit(solution)/shard_map/ppermute | solution.py:402
  (82 other events, 751.1 us)

commit v3 on v1

--- a/solution.py
+++ b/solution.py
@@ -1,13 +1,18 @@
 import jax
 import jax.numpy as jnp
+import numpy as np
 from jax import lax
+from jax.experimental import pallas as pl
+from jax.experimental.pallas import tpu as pltpu
 from jax.sharding import PartitionSpec as P
 
 D = 1024
 HEADS = 16
+HEAD = D // HEADS
 FF = 4096
 ROT = 16
 STEP = 10
+LANES = 128
 
 
 LN_EPS = 1e-05
@@ -20,44 +25,10 @@
 ROPE_BASE = 10000.0
 INV_ROOT_TWO = 0.7071067811865476
 INV_ROOT_TAU = 0.3989422804014327
-
-
-def rope_tables(positions):
-    half_rot = ROT // 2
-    freqs = ROPE_BASE ** (-(2.0 * jnp.arange(half_rot).astype(jnp.float32) / ROT))
-    angles = positions.astype(jnp.float32)[:, None] * freqs[None, :]
-    return (jnp.cos(angles)[:, None, :], jnp.sin(angles)[:, None, :])
-
-
-def rotate(heads, cosines, sines):
-    half_rot = ROT // 2
-    lower = heads[..., :half_rot]
-    upper = heads[..., half_rot:ROT]
-    return jnp.concatenate(
-        [lower * cosines - upper * sines, upper * cosines + lower * sines, heads[..., ROT:]],
-        axis=-1,
-    )
-
-
-def unrotate(heads, cosines, sines):
-    half_rot = ROT // 2
-    lower = heads[..., :half_rot]
-    upper = heads[..., half_rot:ROT]
-    return jnp.concatenate(
-        [lower * cosines + upper * sines, upper * cosines - lower * sines, heads[..., ROT:]],
-        axis=-1,
-    )
-
-
-def gelu_value(inner):
-    return 0.5 * inner * (1.0 + jax.scipy.special.erf(inner * INV_ROOT_TWO))
-
-
-def gelu_slope(inner):
-    return (
-        0.5 * (1.0 + jax.scipy.special.erf(inner * INV_ROOT_TWO))
-        + inner * jnp.exp(-0.5 * inner * inner) * INV_ROOT_TAU
-    )
+HIDDEN = -1e30
+bf16 = jnp.bfloat16
+f32 = jnp.float32
+TILE = 256
 
 
 def adam_update(param, grad, first, second, rate, decay):
@@ -73,14 +44,87 @@
 
 
 def contract_rows(left, right):
-    return lax.dot_general(
-        left, right, (((0,), (0,)), ((), ())), preferred_element_type=jnp.float32
-    )
+    return lax.dot_general(left, right, (((0,), (0,)), ((), ())), preferred_element_type=f32)
 
 
 def contract_cols(left, right):
-    return lax.dot_general(
-        left, right, (((1,), (1,)), ((), ())), preferred_element_type=jnp.float32
+    return lax.dot_general(left, right, (((1,), (1,)), ((), ())), preferred_element_type=f32)
+
+
+def plain_dot(left, right):
+    return jnp.dot(left, right, preferred_element_type=f32)
+
+
+def rope_lanes(seq_len):
+    half = ROT // 2
+    freqs = (ROPE_BASE ** (-(2.0 * np.arange(half, dtype=np.float32) / ROT))).astype(np.float32)
+    angles = np.arange(seq_len, dtype=np.float32)[:, None] * freqs[None, :]
+    cosines, sines = np.cos(angles), np.sin(angles)
+    keep = np.ones((seq_len, HEAD), np.float32)
+    up = np.zeros((seq_len, HEAD), np.float32)
+    down = np.zeros((seq_len, HEAD), np.float32)
+    keep[:, :half], keep[:, half:ROT] = cosines, cosines
+    up[:, :half] = -sines
+    down[:, half:ROT] = sines
+    reps = LANES // HEAD
+    return np.concatenate([np.tile(t, (1, reps)) for t in (keep, up, down)], axis=1)
+
+
+def turn(values, table, sign):
+    half = ROT // 2
+    above = pltpu.roll(values, LANES - half, 1)
+    below = pltpu.roll(values, half, 1)
+    moved = above * table[:, LANES : 2 * LANES] + below * table[:, 2 * LANES :]
+    return values * table[:, :LANES] + sign * moved
+
+
+def params(mib):
+    return pltpu.CompilerParams(vmem_limit_bytes=mib << 20)
+
+
+def cost(flops, count):
+    return pl.CostEstimate(flops=flops, bytes_accessed=count, transcendentals=0)
+
+
+def whole_spec(shape):
+    return pl.BlockSpec(shape, lambda *_: (0,) * len(shape))
+
+
+def rope_tables(positions):
+    half_rot = ROT // 2
+    freqs = ROPE_BASE ** (-(2.0 * jnp.arange(half_rot).astype(jnp.float32) / ROT))
+    angles = positions.astype(jnp.float32)[:, None] * freqs[None, :]
+    return (jnp.cos(angles)[:, None, :], jnp.sin(angles)[:, None, :])
+
+
+def rotate(heads, cosines, sines):
+    half_rot = ROT // 2
+    lower = heads[..., :half_rot]
+    upper = heads[..., half_rot:ROT]
+    return jnp.concatenate(
+        [lower * cosines - upper * sines, upper * cosines + lower * sines, heads[..., ROT:]],
+        axis=-1,
+    )
+
+
+def unrotate(heads, cosines, sines):
+    half_rot = ROT // 2
+    lower = heads[..., :half_rot]
+    upper = heads[..., half_rot:ROT]
+    return jnp.concatenate(
+        [lower * cosines + upper * sines, upper * cosines - lower * sines, heads[..., ROT:]],
+        axis=-1,
+    )
+
+
+def gelu_value(inner):
+    return 0.5 * inner * (1.0 + jax.scipy.special.erf(inner * INV_ROOT_TWO))
+
+
+def gelu_slope(inner):
+    return (
+        0.5 * (1.0 + jax.scipy.special.erf(inner * INV_ROOT_TWO))
+        + inner * jnp.exp(-0.5 * inner * inner) * INV_ROOT_TAU
     )
 
 
@@ -139,7 +183,7 @@
     return current[0]
 
 
-def shards(
+def general(
     block_in,
     cotangent,
     segments,
@@ -159,8 +203,6 @@
     second_down,
     second_vec,
 ):
-    bf16 = jnp.bfloat16
-    f32 = jnp.float32
     tok_count = block_in.shape[0]
     n_rep = lax.axis_size("rep")
     n_shard = lax.axis_size("shard")
@@ -391,9 +433,696 @@
     )
 
 
+def single(body, outs, prefetch, ins, flops, name, scratch=(), mib=48):
+    shapes = tuple(jax.ShapeDtypeStruct(s, d) for s, d in outs)
+    moved = sum(a.size * a.dtype.itemsize for a in ins)
+    moved += sum(s.size * s.dtype.itemsize for s in shapes)
+    return pl.pallas_call(
+        body,
+        out_shape=shapes,
+        grid_spec=pltpu.PrefetchScalarGridSpec(
+            num_scalar_prefetch=1,
+            grid=(1,),
+            in_specs=[whole_spec(a.shape) for a in ins],
+            out_specs=tuple(whole_spec(s.shape) for s in shapes),
+            scratch_shapes=list(scratch),
+        ),
+        compiler_params=params(mib),
+        cost_estimate=cost(flops, moved),
+        name=name,
+    )(prefetch, *ins)
+
+
+def lane_block(index):
+    return pl.ds(pl.multiple_of(index * LANES, LANES), LANES)
+
+
+def row_block(index, size):
+    return pl.ds(pl.multiple_of(index * size, size), size)
+
+
+N_REP = 8
+N_SHARD = 4
+ORDER = 0
+PLACE = N_REP
+NEAR = 2 * N_REP
+SHARD = NEAR + N_SHARD
+QKV = 3 * TILE
+UP = D
+OUT = TILE
+
+
+def pack_body(s_ref, qkv_ref, up_ref, vec_ref, *outs):
+    for k in range(N_SHARD):
+        t = s_ref[NEAR + k]
+        o_ref = outs[k]
+        for c in range(QKV // LANES):
+            o_ref[:, c * LANES : (c + 1) * LANES] = qkv_ref[:, lane_block(c * N_SHARD + t)].astype(bf16)
+        for c in range(UP // LANES):
+            at = QKV + c * LANES
+            o_ref[:, at : at + LANES] = up_ref[:, lane_block(c * N_SHARD + t)].astype(bf16)
+        o_ref[:, QKV + UP :] = vec_ref[...]
+
+
+def norm_body(s_ref, x_ref, o_ref, n_ref):
+    x = x_ref[...]
+    center = x - jnp.mean(x, axis=-1, keepdims=True)
+    inv_std = lax.rsqrt(jnp.mean(center * center, axis=-1, keepdims=True) + LN_EPS)
+    n_ref[...] = center * inv_std
+    for i in range(N_REP):
+        o_ref[:, i * LANES : (i + 1) * LANES] = n_ref[:, lane_block(s_ref[ORDER + i])].astype(bf16)
+
+
+def join_body(s_ref, *refs):
+    out_ref, o_ref = refs[N_SHARD], refs[N_SHARD + 1]
+    rows = out_ref.shape[0]
+    for k in range(N_SHARD):
+        at = row_block(s_ref[NEAR + k], rows)
+        o_ref[at, : QKV + UP] = refs[k][:, : QKV + UP]
+        o_ref[at, QKV + UP + OUT :] = refs[k][:, QKV + UP :]
+    for c in range(D // OUT):
+        o_ref[c * rows : (c + 1) * rows, QKV + UP : QKV + UP + OUT] = out_ref[:, c * OUT : (c + 1) * OUT]
+
+
+def bias_places(s_ref):
+    shard = s_ref[SHARD]
+    found = []
+    for c in range(QKV // LANES):
+        found.append((4 + c // 2, s_ref[PLACE + (c % 2) * N_SHARD + shard], c * LANES))
+    for c in range(UP // LANES):
+        found.append((8 + c // 2, s_ref[PLACE + (c % 2) * N_SHARD + shard], QKV + c * LANES))
+    return found
+
+
+def front_body(s_ref, *refs):
+    n_refs, refs = refs[:N_SHARD], refs[N_SHARD:]
+    w_refs, refs = refs[:N_REP], refs[N_REP:]
+    v_refs, refs = refs[:N_REP], refs[N_REP:]
+    rope_ref, h1_ref, h2_ref, qkv_ref, act_ref, slope_ref, vec_ref, last_ref, bias_ref = refs
+    j = pl.program_id(0)
+    rows = n_refs[0].shape[0]
+
+    @pl.when(j == 0)
+    def _():
+        for i in range(N_REP):
+            parts = v_refs[i][...].astype(f32).T
+            vec_ref[:, i * LANES : (i + 1) * LANES] = (parts[0:16] + parts[16:32]) + parts[32:48]
+        for k in range(N_SHARD):
+            normed = n_refs[k][...].astype(f32)
+            at = slice(k * rows, (k + 1) * rows)
+            h1_ref[at, :] = (normed * vec_ref[0:1, :] + vec_ref[1:2, :]).astype(bf16)
+            h2_ref[at, :] = (normed * vec_ref[2:3, :] + vec_ref[3:4, :]).astype(bf16)
+        for row, block, at in bias_places(s_ref):
+            bias_ref[at // TILE, 0:1, at % TILE : at % TILE + LANES] = vec_ref[row : row + 1, lane_block(block)]
+        both = vec_ref[7:8, :] + vec_ref[12:13, :]
+        for i in range(N_REP):
+            last_ref[0:1, lane_block(s_ref[ORDER + i])] = both[:, i * LANES : (i + 1) * LANES]
+
+    def product(h_ref):
+        total = bias_ref[j, 0:1, :]
+        for i in range(0, N_REP, 2):
+            weights = jnp.concatenate([w_refs[i][...], w_refs[i + 1][...]], axis=0)
+            total = total + plain_dot(h_ref[:, i * LANES : (i + 2) * LANES], weights)
+        return total
+
+    @pl.when(j < 2)
+    def _():
+        lin = product(h1_ref)
+        for c in range(0, TILE, LANES):
+            qkv_ref[:, c : c + LANES] = turn(lin[:, c : c + LANES], rope_ref[...], 1.0).astype(bf16)
+
+    @pl.when(j == 2)
+    def _():
+        qkv_ref[...] = product(h1_ref).astype(bf16)
+
+    @pl.when(j > 2)
+    def _():
+        lin = product(h2_ref)
+        above = 0.5 * (1.0 + lax.erf(lin * INV_ROOT_TWO))
+        act = (lin * above).astype(bf16)
+        slope = above + lin * jnp.exp(-0.5 * lin * lin) * INV_ROOT_TAU
+        for c in range(2):
+            at = lane_block(s_ref[PLACE + (j - 3) * 2 + c])
+            act_ref[:, at] = act[:, c * LANES : (c + 1) * LANES]
+            slope_ref[:, at] = slope[:, c * LANES : (c + 1) * LANES]
+
+
+def front(scalars, normed, pieces, rope):
+    tokens = rope.shape[0]
+    block = pieces[0].shape[0]
+    shapes = (
+        ((tokens, D), bf16),
+        ((tokens, D), bf16),
+        ((tokens, QKV), bf16),
+        ((tokens, UP), bf16),
+        ((tokens, UP), f32),
+        ((16, D), f32),
+        ((8, D), f32),
+    )
+    specs = [whole_spec(s) for s, _ in shapes]
+    specs[2] = pl.BlockSpec((tokens, TILE), lambda j, s: (0, jnp.minimum(j, 2)))
+    return pl.pallas_call(
+        front_body,
+        out_shape=tuple(jax.ShapeDtypeStruct(s, d) for s, d in shapes),
+        grid_spec=pltpu.PrefetchScalarGridSpec(
+            num_scalar_prefetch=1,
+            grid=((QKV + UP) // TILE,),
+            in_specs=[whole_spec(n.shape) for n in normed]
+            + [pl.BlockSpec((block, TILE), lambda j, s: (0, j))] * N_REP
+            + [pl.BlockSpec((block, LANES), lambda j, s: (0, (QKV + UP + OUT) // LANES))] * N_REP
+            + [whole_spec(rope.shape)],
+            out_specs=tuple(specs),
+            scratch_shapes=[pltpu.VMEM(((QKV + UP) // TILE, 8, TILE), f32)],
+        ),
+        compiler_params=params(40),
+        cost_estimate=cost(2 * tokens * D * (QKV + UP), 14 << 20),
+        name="front",
+    )(scalars, *normed, *pieces, *pieces, rope)
+
+
+def hidden_body(s_ref, *refs):
+    dy_refs, refs = refs[:N_SHARD], refs[N_SHARD:]
+    out_refs, refs = refs[:N_REP], refs[N_REP:]
+    down_refs, refs = refs[:N_REP], refs[N_REP:]
+    slope_ref, seq_ref, whole_ref, dmix_ref, du_ref, sum_ref = refs
+    tokens = dy_refs[0].shape[0]
+    for k in range(N_SHARD):
+        seq_ref[k * tokens : (k + 1) * tokens, :] = dy_refs[k][...]
+    chunks = D // OUT
+    rows = out_refs[0].shape[0] // chunks
+    for i in range(N_REP):
+        at = row_block(s_ref[ORDER + i], rows)
+        for c in range(chunks):
+            whole_ref[at, c * OUT : (c + 1) * OUT] = out_refs[i][c * rows : (c + 1) * rows, :]
+    dy = seq_ref[...]
+    dmix_ref[...] = contract_cols(dy, whole_ref[...]).astype(bf16)
+    for i in range(N_REP):
+        du = contract_cols(dy, down_refs[i][...]) * slope_ref[:, i * LANES : (i + 1) * LANES]
+        at = lane_block(s_ref[ORDER + i])
+        du_ref[:, at] = du.astype(bf16)
+        sum_ref[0:1, at] = jnp.sum(du, axis=0, keepdims=True)
+
+
+def hidden(scalars, dys, pieces, downs, slope):
+    tokens = slope.shape[0]
+    block = pieces[0].shape[0]
+    shapes = (
+        ((tokens, D), bf16),
+        ((OUT, D), bf16),
+        ((tokens, OUT), bf16),
+        ((tokens, UP), bf16),
+        ((8, UP), f32),
+    )
+    return pl.pallas_call(
+        hidden_body,
+        out_shape=tuple(jax.ShapeDtypeStruct(s, d) for s, d in shapes),
+        grid_spec=pltpu.PrefetchScalarGridSpec(
+            num_scalar_prefetch=1,
+            grid=(1,),
+            in_specs=[whole_spec(a.shape) for a in dys]
+            + [pl.BlockSpec((block, OUT), lambda j, s: (0, (QKV + UP) // OUT))] * N_REP
+            + [whole_spec(a.shape) for a in downs]
+            + [whole_spec(slope.shape)],
+            out_specs=tuple(whole_spec(s) for s, _ in shapes),
+        ),
+        compiler_params=params(40),
+        cost_estimate=cost(2 * tokens * D * (OUT + UP), 9 << 20),
+        name="hidden",
+    )(scalars, *dys, *pieces, *downs, slope)
+
+
+def attend_body(q_ref, k_ref, v_ref, dm_ref, mask_ref, rope_ref, mix_ref, dqkv_ref, sum_ref, dk_ref, dv_ref):
+    pair = pl.program_id(0)
+    tokens = q_ref.shape[0]
+    chunk = LANES
+    scale = HEAD ** (-0.5)
+    first = lax.broadcasted_iota(jnp.int32, (chunk, LANES), 1) < HEAD
+    every = lax.broadcasted_iota(jnp.int32, (tokens, LANES), 1) < HEAD
+    k = k_ref[...]
+    v = v_ref[...]
+    pairs = pl.num_programs(0)
+
+    def columns(part):
+        return pl.ds(pl.multiple_of(part * pairs * LANES + pair * LANES, LANES), LANES)
+
+    dq_total = jnp.zeros((1, LANES), f32)
+    for c in range(0, tokens, chunk):
+        rows = slice(c, c + chunk)
+        q = q_ref[rows, :]
+        dm = dm_ref[rows, :]
+        mixes, dqs, dks, dvs = [], [], [], []
+        for h in range(2):
+            mine = first if h == 0 else jnp.logical_not(first)
+            qh = jnp.where(mine, q, jnp.zeros_like(q))
+            dmh = jnp.where(mine, dm, jnp.zeros_like(dm))
+            score = contract_cols(qh, k) * scale + mask_ref[rows, :]
+            expo = jnp.exp(score - jnp.max(score, axis=-1, keepdims=True))
+            prob = expo * (1.0 / jnp.sum(expo, axis=-1, keepdims=True))
+            prob16 = prob.astype(bf16)
+            mix16 = plain_dot(prob16, v).astype(bf16)
+            delta = jnp.sum(dmh.astype(f32) * mix16.astype(f32), axis=-1, keepdims=True)
+            d_prob = contract_cols(dmh, v)
+            ds16 = (prob * (d_prob - delta) * scale).astype(bf16)
+            mixes.append(mix16)
+            dqs.append(plain_dot(ds16, k))
+            dks.append(contract_rows(ds16, q))
+            dvs.append(contract_rows(prob16, dm))
+        mix_ref[rows, :] = jnp.where(first, mixes[0], mixes[1])
+        dq = turn(jnp.where(first, dqs[0], dqs[1]), rope_ref[rows, :], -1.0)
+        dqkv_ref[rows, columns(0)] = dq.astype(bf16)
+        dq_total = dq_total + jnp.sum(dq, axis=0, keepdims=True)
+        dk = jnp.where(every, dks[0], dks[1])
+        dv = jnp.where(every, dvs[0], dvs[1])
+        if c == 0:
+            dk_ref[...] = dk
+            dv_ref[...] = dv
+        else:
+            dk_ref[...] += dk
+            dv_ref[...] += dv
+    dk = turn(dk_ref[...], rope_ref[...], -1.0)
+    dv = dv_ref[...]
+    dqkv_ref[:, columns(1)] = dk.astype(bf16)
+    dqkv_ref[:, columns(2)] = dv.astype(bf16)
+    sum_ref[:, columns(0)] = dq_total
+    sum_ref[:, columns(1)] = jnp.sum(dk, axis=0, keepdims=True)
+    sum_ref[:, columns(2)] = jnp.sum(dv, axis=0, keepdims=True)
+
+
+def attend(qkv, d_mix, mask, rope):
+    tokens, feats = d_mix.shape
+    pairs = feats // LANES
+
+    def part(first):
+        return pl.BlockSpec((tokens, LANES), lambda j: (0, first * pairs + j))
+
+    return pl.pallas_call(
+        attend_body,
+        out_shape=(
+            jax.ShapeDtypeStruct((tokens, feats), bf16),
+            jax.ShapeDtypeStruct((tokens, 3 * feats), bf16),
+            jax.ShapeDtypeStruct((1, 3 * feats), f32),
+        ),
+        grid=(pairs,),
+        in_specs=[
+            part(0),
+            part(1),
+            part(2),
+            part(0),
+            whole_spec(mask.shape),
+            whole_spec(rope.shape),
+        ],
+        out_specs=(
+            pl.BlockSpec((tokens, LANES), lambda j: (0, j)),
+            whole_spec((tokens, 3 * feats)),
+            whole_spec((1, 3 * feats)),
+        ),
+        scratch_shapes=[pltpu.VMEM((tokens, LANES), f32), pltpu.VMEM((tokens, LANES), f32)],
+        compiler_params=params(40),
+        cost_estimate=cost(60 * tokens * tokens * feats, 6 << 20),
+        name="attend",
+    )(qkv, qkv, qkv, d_mix, mask, rope)
+
+
+def back_body(s_ref, dqkv_ref, du_ref, vec_ref, *refs):
+    n_refs, refs = refs[:N_SHARD], refs[N_SHARD:]
+    w_refs, refs = refs[:N_REP], refs[N_REP:]
+    own_ref, sent_refs, sum_ref = refs[0], refs[1:N_SHARD], refs[N_SHARD]
+    rows = n_refs[0].shape[0]
+    for i in range(0, N_REP, 2):
+        cols = slice(i * LANES, (i + 2) * LANES)
+        weights = jnp.concatenate([w_refs[i][:, : QKV + UP], w_refs[i + 1][:, : QKV + UP]], axis=0)
+        d_one = contract_cols(dqkv_ref[...], weights[:, :QKV])
+        d_two = contract_cols(du_ref[...], weights[:, QKV:])
+        scaled = d_one * vec_ref[0:1, cols] + d_two * vec_ref[2:3, cols]
+        own_ref[:, cols] = scaled[:rows]
+        sums = [jnp.sum(d, axis=0, keepdims=True) for d in (d_one, d_two)]
+        turned = [jnp.zeros_like(sums[0])] * 2
+        for k in range(N_SHARD):
+            at = slice(k * rows, (k + 1) * rows)
+            if k:
+                sent_refs[k - 1][:, cols] = scaled[at].astype(bf16)
+            normed = n_refs[k][:, cols].astype(f32)
+            turned = [
+                t + jnp.sum(d[at] * normed, axis=0, keepdims=True)
+                for t, d in zip(turned, (d_one, d_two))
+            ]
+        sum_ref[0:1, cols] = turned[0]
+        sum_ref[1:2, cols] = sums[0]
+        sum_ref[2:3, cols] = turned[1]
+        sum_ref[3:4, cols] = sums[1]
+
+
+def branch_body(s_ref, mix_ref, act_ref, out_ref, last_ref, x_ref, *refs):
+    down_refs, refs = refs[:N_REP], refs[N_REP:]
+    own_ref, sent_refs = refs[0], refs[1:]
+    rows = x_ref.shape[0]
+    total = plain_dot(mix_ref[...], out_ref[...])
+    for i in range(0, N_REP, 2):
+        weights = jnp.concatenate([down_refs[i][...], down_refs[i + 1][...]], axis=0)
+        total = total + plain_dot(act_ref[:, i * LANES : (i + 2) * LANES], weights)
+    own_ref[...] = x_ref[...] + total[:rows] + last_ref[0:1, :]
+    for k in range(1, N_SHARD):
+        sent_refs[k - 1][...] = total[k * rows : (k + 1) * rows].astype(bf16)
+
+
+def terms_body(
+    s_ref, h_ref, dqkv_ref, mix_ref, dy_ref, norm_ref, qkv_sum_ref, up_sum_ref, cot_ref, keep_ref, sent_ref, vec_ref, g_ref
+):
+    half = keep_ref.shape[0]
+    keep_ref[:, :QKV] = contract_rows(h_ref[:, :half], dqkv_ref[...])
+    sent_ref[:, :QKV] = contract_rows(h_ref[:, half:], dqkv_ref[...]).astype(bf16)
+    g_ref[...] = contract_rows(mix_ref[...], dy_ref[...])
+    vec_ref[...] = jnp.zeros_like(vec_ref)
+    vec_ref[0:4, :] = norm_ref[0:4, :]
+    for row, block, at in bias_places(s_ref):
+        ref, at = (qkv_sum_ref, at) if at < QKV else (up_sum_ref, at - QKV)
+        vec_ref[row : row + 1, lane_block(block)] = ref[0:1, at : at + LANES]
+    rows = OUT // N_REP
+    for i in range(N_REP):
+        here = slice(i * LANES, (i + 1) * LANES)
+        cot = cot_ref[0:1, lane_block(s_ref[ORDER + i])]
+        vec_ref[7:8, here] = cot
+        vec_ref[12:13, here] = cot
+        ref = keep_ref if i < N_REP // 2 else sent_ref
+        base = i * LANES % half
+        found = g_ref[row_block(s_ref[ORDER + i], rows), :]
+        for c in range(D // OUT):
+            ref[base + c * rows : base + (c + 1) * rows, QKV : QKV + OUT] = found[
+                :, c * OUT : (c + 1) * OUT
+            ].astype(ref.dtype)
+        ref[base : base + LANES, QKV + OUT :] = vec_ref[:, here].T.astype(ref.dtype)
+
+
+def fold_body(s_ref, *refs):
+    up_refs, refs = refs[:4], refs[4:]
+    qkv_refs, refs = refs[:4], refs[4:]
+    own_ref, sent_refs, out_ref, up_sum, qkv_sum = refs[0], refs[1:4], refs[4], refs[5], refs[6]
+    for some, total in ((up_refs, up_sum), (qkv_refs, qkv_sum)):
+        total[...] = some[0][...] + some[1][...].astype(f32) + some[2][...].astype(f32) + some[3][...].astype(f32)
+    rows = own_ref.shape[0]
+    for k in range(N_SHARD):
+        at = row_block(s_ref[NEAR + k], rows)
+        ref = own_ref if k == 0 else sent_refs[k - 1]
+        ref[:, :QKV] = qkv_sum[at, :QKV].astype(ref.dtype)
+        ref[:, QKV : QKV + UP] = up_sum[at, :].astype(ref.dtype)
+        ref[:, QKV + UP :] = qkv_sum[at, QKV + OUT :].astype(ref.dtype)
+    for c in range(D // OUT):
+        out_ref[:, c * OUT : (c + 1) * OUT] = qkv_sum[c * rows : (c + 1) * rows, QKV : QKV + OUT]
+
+
+def adam_body(s_ref, *refs):
+    got, refs = refs[:N_SHARD], refs[N_SHARD:]
+    states, refs = (refs[0:3], refs[3:6]), refs[6:]
+    results, refs = (refs[0:4], refs[4:8]), refs[8:]
+    vec_ref, all_ref = refs
+    for k in range(N_SHARD):
+        all_ref[k] = got[k][...].astype(f32)
+    vec_ref[...] = sum(all_ref[k, :, QKV + UP :] for k in range(N_SHARD))
+    first = 0
+    for state, result in zip(states, results):
+        for c in range(state[0].shape[1] // (N_SHARD * LANES)):
+            for t in range(N_SHARD):
+                grad = all_ref[s_ref[NEAR + t], :, first : first + LANES]
+                at = slice((c * N_SHARD + t) * LANES, (c * N_SHARD + t + 1) * LANES)
+                result[0][:, at] = grad
+                new = adam_update(
+                    state[0][:, at], grad, state[1][:, at], state[2][:, at], LR_MATRIX, WEIGHT_DECAY
+                )
+                for ref, value in zip(result[1:], new):
+                    ref[:, at] = value
+            first += LANES
+
+
+def finish_body(s_ref, own_ref, r1_ref, r2_ref, r3_ref, x_ref, cot_ref, o_ref, e_ref):
+    total = own_ref[...] + r1_ref[...].astype(f32) + r2_ref[...].astype(f32) + r3_ref[...].astype(f32)
+    for i in range(N_REP):
+        e_ref[:, lane_block(s_ref[ORDER + i])] = total[:, i * LANES : (i + 1) * LANES]
+    x = x_ref[...]
+    center = x - jnp.mean(x, axis=-1, keepdims=True)
+    inv_std = lax.rsqrt(jnp.mean(center * center, axis=-1, keepdims=True) + LN_EPS)
+    normed = center * inv_std
+    scaled = e_ref[...]
+    o_ref[...] = cot_ref[...] + inv_std * (
+        scaled
+        - jnp.mean(scaled, axis=-1, keepdims=True)
+        - normed * jnp.mean(scaled * normed, axis=-1, keepdims=True)
+    )
+
+
+def to_shards(values):
+    return [hop(values[k - 1], "shard", N_SHARD, k) for k in range(1, N_SHARD)]
+
+
+def to_chips(values):
+    return [hop(values[k - 1], "rep", N_REP, 2 * k) for k in range(1, 4)]
+
+
+def gather_chips(own):
+    near = [own] + to_chips([own] * 3)
+    return near + [hop(piece, "rep", N_REP, 1) for piece in near]
+
+
+def sum_rep(keep, sent):
+    got = hop(sent, "rep", N_REP, 1)
+    parts = [keep[k] + got[k].astype(f32) for k in range(4)]
+    return [parts[0]] + to_chips([part.astype(bf16) for part in parts[1:]])
+
+
+def after(value, *others):
+    return lax.optimization_barrier((value,) + others)[0]
+
+
+def shards(
+    block_in,
+    cotangent,
+    segments,
+    qkv_weight,
+    out_weight,
+    up_weight,
+    down_weight,
+    vectors,
+    first_qkv,
+    first_out,
+    first_up,
+    first_down,
+    first_vec,
+    second_qkv,
+    second_out,
+    second_up,
+    second_down,
+    second_vec,
+):
+    tok_count = block_in.shape[0]
+    rep = lax.axis_index("rep")
+    shard = lax.axis_index("shard")
+    seq_len = tok_count * N_SHARD
+    rows = qkv_weight.shape[0]
+    units = down_weight.shape[0]
+    n_vec, cols = vectors.shape
+    masks = np.array([0, 2, 4, 6, 1, 3, 5, 7], np.int32)
+    spots = np.argsort(masks)
+    device = np.arange(N_REP)
+    places = spots[device[:, None] ^ device[None, :]].astype(np.int32)
+    orders = (device[:, None] ^ masks[None, :]).astype(np.int32)
+    near = shard ^ jnp.arange(N_SHARD, dtype=jnp.int32)
+    table = jnp.asarray(np.concatenate([orders, places], axis=1))
+    scalars = jnp.concatenate(
+        [lax.dynamic_index_in_dim(table, rep, 0, keepdims=False), near, shard[None]]
+    ).astype(jnp.int32)
+
+    vec_t = vectors.T
+    high = lax.reduce_precision(vec_t, 8, 7)
+    middle = lax.reduce_precision(vec_t - high, 8, 7)
+    low = (vec_t - high) - middle
+    gap = jnp.zeros((cols, 16 - n_vec), f32)
+    vec16 = jnp.concatenate(
+        [high, gap, middle, gap, low, gap, jnp.zeros((cols, LANES - 48), f32)], axis=1
+    ).astype(bf16)
+
+    share = HEAD // rows
+    pair = LANES // HEAD
+    moves = []
+    for at in range(N_REP * N_SHARD):
+        head, part = at // share, at % share
+        owner = (head // pair) % N_SHARD
+        local = (head // (pair * N_SHARD)) * pair + head % pair
+        moves.append((at, (local * share + part) * N_SHARD + owner))
+
+    own_cols = [((rows, QKV + UP + LANES), bf16)] * N_SHARD
+    packed = single(pack_body, own_cols, scalars, [qkv_weight, up_weight, vec16], 0, "pack")
+    got_cols = to_shards(packed[1:])
+    out_rows = lax.ppermute(out_weight.astype(bf16), ("rep", "shard"), moves)
+    (normed_own,) = single(
+        norm_body,
+        [((tok_count, D), bf16)],
+        scalars,
+        [block_in],
+        0,
+        "norm",
+        [pltpu.VMEM((tok_count, D), f32)],
+    )
+    downs = gather_chips(down_weight.astype(bf16))
+    (in_rows,) = single(
+        join_body,
+        [((N_SHARD * rows, QKV + UP + OUT + LANES), bf16)],
+        scalars,
+        [packed[0], *got_cols, out_rows],
+        0,
+        "join",
+    )
+    normed = [normed_own] + to_shards([normed_own] * 3)
+    pieces = gather_chips(in_rows)
+    dy_own = cotangent.astype(bf16)
+    dys = [dy_own] + to_shards([dy_own] * 3)
+
+    rope_parts = jnp.asarray(rope_lanes(seq_len)).reshape(N_SHARD, tok_count, 3 * LANES)
+    rope = jnp.concatenate(
+        [lax.dynamic_index_in_dim(rope_parts, near[k], 0, keepdims=False) for k in range(N_SHARD)]
+    )
+    seg_row = jnp.concatenate(
+        [lax.dynamic_slice(segments[0], (near[k] * tok_count,), (tok_count,)) for k in range(N_SHARD)]
+    )
+    positions = (near[:, None] * tok_count + jnp.arange(tok_count)[None, :]).reshape(seq_len)
+    allowed = (seg_row[:, None] == seg_row[None, :]) & (positions[None, :] <= positions[:, None])
+    mask = jnp.where(allowed, 0.0, HIDDEN).astype(f32)
+
+    h_one, h_two, qkv16, act16, slope, vec_rel, last = front(scalars, normed, pieces, rope)
+    dy_seq, out_whole, d_mixed16, d_up16, up_sum = hidden(scalars, dys, pieces, downs, slope)
+    half = D // 2
+
+    def split_terms(left, right):
+        keep = contract_rows(left[:, :half], right).reshape(4, LANES, D)
+        sent = contract_rows(left[:, half:], right).astype(bf16).reshape(4, LANES, D)
+        return keep, sent
+
+    down_parts = sum_rep(*split_terms(act16, dy_seq))
+    up_parts = sum_rep(*split_terms(h_two, d_up16))
+
+    mixed16, d_qkv16, qkv_sum = attend(qkv16, d_mixed16, mask, rope)
+
+    block16 = ((tok_count, D), bf16)
+    block32 = ((tok_count, D), f32)
+    size = 2 * seq_len * D
+    out_own, *out_sent = single(
+        branch_body,
+        [block32, block16, block16, block16],
+        scalars,
+        [mixed16, act16, out_whole, last, block_in, *downs],
+        size * (OUT + UP),
+        "branch",
+    )
+    e_own, *e_sent, norm_sum = single(
+        back_body,
+        [block32, block16, block16, block16, ((8, D), f32)],
+        scalars,
+        [d_qkv16, d_up16, vec_rel, *normed, *pieces],
+        size * (QKV + UP),
+        "back",
+    )
+    out_got = to_shards(out_sent)
+    e_got = to_shards(e_sent)
+    cot_sum = jnp.sum(cotangent, axis=0, keepdims=True)
+    wide = QKV + OUT + LANES
+    qkv_keep, qkv_sent = single(
+        terms_body,
+        [((half, wide), f32), ((half, wide), bf16)],
+        scalars,
+        [h_one, d_qkv16, mixed16, dy_seq, norm_sum, qkv_sum, up_sum, cot_sum],
+        size * (QKV + OUT),
+        "terms",
+        [pltpu.VMEM((LANES, D), f32), pltpu.VMEM((OUT, D), f32)],
+    )
+    qkv_parts = sum_rep(qkv_keep.reshape(4, LANES, wide), qkv_sent.reshape(4, LANES, wide))
+    narrow = (rows, QKV + UP + LANES)
+    g_own, g1, g2, g3, out_sum = single(
+        fold_body,
+        [(narrow, f32), (narrow, bf16), (narrow, bf16), (narrow, bf16), ((rows, D), f32)],
+        scalars,
+        [*up_parts, *qkv_parts],
+        0,
+        "fold",
+        [pltpu.VMEM((LANES, UP), f32), pltpu.VMEM((LANES, wide), f32)],
+    )
+    g_got = to_shards([g1, g2, g3])
+    grad_out = lax.ppermute(out_sum, ("rep", "shard"), [(b, a) for a, b in moves])
+    block_out = out_own + out_got[0].astype(f32) + out_got[1].astype(f32) + out_got[2].astype(f32)
+    grad_down = (
+        down_parts[0]
+        + down_parts[1].astype(f32)
+        + down_parts[2].astype(f32)
+        + down_parts[3].astype(f32)
+    )
+    (grad_input,) = single(
+        finish_body,
+        [block32],
+        scalars,
+        [e_own, *e_got, block_in, cotangent],
+        0,
+        "finish",
+        [pltpu.VMEM((tok_count, D), f32)],
+    )
+    qkv_shape = (qkv_weight.shape, f32)
+    up_shape = (up_weight.shape, f32)
+    (
+        grad_qkv,
+        new_qkv,
+        new_first_qkv,
+        new_second_qkv,
+        grad_up,
+        new_up,
+        new_first_up,
+        new_second_up,
+        vec_sum,
+    ) = single(
+        adam_body,
+        [qkv_shape] * 4 + [up_shape] * 4 + [((rows, LANES), f32)],
+        scalars,
+        [g_own, *g_got, qkv_weight, first_qkv, second_qkv, up_weight, first_up, second_up],
+        0,
+        "adam",
+        [pltpu.VMEM((N_SHARD,) + narrow, f32)],
+    )
+    grad_vec = vec_sum[:, :n_vec].T
+
+    new_out, new_first_out, new_second_out = adam_update(
+        out_weight, grad_out, first_out, second_out, LR_MATRIX, WEIGHT_DECAY
+    )
+    new_down, new_first_down, new_second_down = adam_update(
+        down_weight, grad_down, first_down, second_down, LR_MATRIX, WEIGHT_DECAY
+    )
+    new_vec, new_first_vec, new_second_vec = adam_update(
+        vectors, grad_vec, first_vec, second_vec, LR_VECTOR, 0.0
+    )
+    return (
+        block_out,
+        grad_input,
+        grad_qkv,
+        grad_out,
+        grad_up,
+        grad_down,
+        grad_vec,
+        new_qkv,
+        new_out,
+        new_up,
+        new_down,
+        new_vec,
+        new_first_qkv,
+        new_first_out,
+        new_first_up,
+        new_first_down,
+        new_first_vec,
+        new_second_qkv,
+        new_second_out,
+        new_second_up,
+        new_second_down,
+        new_second_vec,
+    )
+
+
 def solution(mesh):
+    aligned = mesh.shape["rep"] == N_REP and mesh.shape["shard"] == N_SHARD
     return jax.shard_map(
-        shards,
+        shards if aligned else general,
         mesh=mesh,
         in_specs=(
             P(("rep", "shard"), None),

time: 335 us -> 248 us (0.74); the launches traced: 329 us -> 247 us
  local copies, waits for them, and re-layouts: 76.9 us -> 19.3 us
  Pallas kernels: 0 us -> 44 us
  matrix products: 41.8 us -> 5.12 us
  starting transfers between devices: 80.6 us -> 58.2 us
  other arithmetic: 25.5 us -> 9.94 us
  between operations: 2.89 us -> 12 us
    pallas_call x0 -> x12, Pallas kernels: none -> 44 us  [the longest x9 19.2 us: single(): pl.pallas_call(body, out_shape=shapes, grid_spec=pltpu.PrefetchScalarGrid...]
    dot_general x14 -> x0, matrix products: 34 us -> none  [the longest x4 14.1 us: contract_cols(): lax.dot_general(left, right, (((1,), (1,)), ((), ())), preferred_element_...]
    dynamic_update_slice x46 -> x0, local copies, waits for them, and re-layouts: 25.2 us -> none  [the longest x41 23.2 us: gather_axis(): whole = lax.dynamic_update_index_in_dim(whole, pieces[mask], me ^ mask, 0)]
    ppermute x75 -> x44, starting transfers between devices: 78.3 us -> 56.7 us  [hop(): return lax.ppermute(value, axis, [(i, i ^ mask) for i in range(size)])]
    slice x13 -> x1, local copies, waits for them, and re-layouts: 11.1 us -> 0.59 us  [shards(): near[k]]
    unnamed x186 -> x150, local copies, waits for them, and re-layouts: 6.62 us -> 16.1 us
    broadcast_in_dim x21 -> x2, local copies, waits for them, and re-layouts: 6.41 us -> 0.01 us  [the longest x1 0.01 us: shards(): gap = jnp.zeros((cols, 16 - n_vec), f32)]
    reshape x14 -> x0, local copies, waits for them, and re-layouts: 6 us -> none  [the longest x1 2.05 us: shards(): grad_up = grad_up.transpose(1, 2, 0, 3).reshape(rows, FF)]
  transfers between devices with their start and end apart: 77 -> 46, of which waited for: 29 -> 9; matrix products, arithmetic and copies ran while one was open for 34% -> 7% of each run, Pallas kernels for 0% -> 16%
where the time goes in v3:
time: 248 us; the launch traced here: 247 us
  waiting for transfers between devices  98.3 us (40%)
  starting transfers between devices  58.2 us (23%)
  Pallas kernels  44 us (18%)
  local copies, waits for them, and re-layouts  19.3 us (8%)
  between operations  12 us (5%)
  other arithmetic  9.94 us (4%)
  matrix products  5.12 us (2%)
    ppermute x44, waiting for transfers between devices, hop(): return lax.ppermute(value, axis, [(i, i ^ mask) for i in range(size)])  98.3 us
    ppermute x44, starting transfers between devices, hop(): return lax.ppermute(value, axis, [(i, i ^ mask) for i in range(size)])  56.7 us
    pallas_call x9, Pallas kernels, single(): pl.pallas_call(body, out_shape=shapes, grid_spec=pltpu.PrefetchScalarGrid...  19.2 us
    unnamed x150, local copies, waits for them, and re-layouts  16.1 us
    pallas_call x1, Pallas kernels, attend(): pl.pallas_call(attend_body, out_shape=(jax.ShapeDtypeStruct((tokens, feat...  12 us
    pallas_call x1, Pallas kernels, front(): pl.pallas_call(front_body, out_shape=tuple((jax.ShapeDtypeStruct(s, d) fo...  8.38 us
    dot_general x4, matrix products, contract_rows(): lax.dot_general(left, right, (((0,), (0,)), ((), ())), preferred_element_...  5.12 us
  transfers between devices with their start and end apart: 46, of which 9 were waited for; matrix products, arithmetic and copies ran while one was open for 7% of the time, Pallas kernels for 16%

profile of v3, /device:TPU:0, one launch (start us, length us, event | category | flops | bytes accessed | tf_op | source)
XLA Modules:
  0.0 246.8 jit_solution(18103671729686716489)
XLA Ops:
  5.1 3.1 %collective-permute-start.3 = (bf16[32,1920]{1,0:T(8,128)(2,1)S(1)}, bf16[32,1920]{1,0:T(8,128)(2,1)S(1)}, u32[]{:S(2)}, u32[]{:S(2)}) collective-permute-start(bf16[32,1920]{1,0:T(8,128)(2,1)S(1)} %get-tuple-element.67), channel_id=1, source_target_pairs={{0,1},{1,0},{2,3},{3,2},{4,5},{5,4},{6,7},{7,6},{8,9},{9,8},{10,11... | collective-permute-start | bytes 368648 | tf_op jit(solution)/shard_map/ppermute | solution.py:132
  11.7 2.5 %collective-permute-start = (bf16[128,1024]{1,0:T(8,128)(2,1)S(1)}, bf16[128,1024]{1,0:T(8,128)(2,1)S(1)}, u32[]{:S(2)}, u32[]{:S(2)}) collective-permute-start(bf16[128,1024]{1,0:T(8,128)(2,1)S(1)} %norm.1.refs_0_), channel_id=1, source_target_pairs={{0,1},{1,0},{2,3},{3,2},{4,5},{5,4},{6,7},{7,6},{8,9},{9,8},{10,11... | collective-permute-start | bytes 786440 | tf_op jit(solution)/shard_map/ppermute | solution.py:132
  14.2 3.3 %collective-permute-start.1 = (bf16[128,1024]{1,0:T(8,128)(2,1)S(1)}, bf16[128,1024]{1,0:T(8,128)(2,1)S(1)}, u32[]{:S(2)}, u32[]{:S(2)}) collective-permute-start(bf16[128,1024]{1,0:T(8,128)(2,1)S(1)} %norm.1.refs_0_), channel_id=1, source_target_pairs={{0,2},{1,3},{2,0},{3,1},{4,6},{5,7},{6,4},{7,5},{8,10},{9,11},{10,... | collective-permute-start | bytes 786440 | tf_op jit(solution)/shard_map/ppermute | solution.py:132
  18.4 2.0 collective-permute-start.4
  21.5 28.0 %collective-permute-done.4.refs_2_ = bf16[32,1920]{1,0:T(8,128)(2,1)S(1)} collective-permute-done((bf16[32,1920]{1,0:T(8,128)(2,1)S(1)}, bf16[32,1920]{1,0:T(8,128)(2,1)S(1)}, u32[]{:S(2)}, u32[]{:S(2)}) %collective-permute-start.4) | collective-permute-done | bytes 122912 | tf_op jit(solution)/shard_map/ppermute | solution.py:132
  50.2 2.5 %collective-permute-start.7 = (bf16[128,2176]{1,0:T(8,128)(2,1)S(1)}, bf16[128,2176]{1,0:T(8,128)(2,1)S(1)}, u32[]{:S(2)}, u32[]{:S(2)}) collective-permute-start(bf16[128,2176]{1,0:T(8,128)(2,1)S(1)} %join.1.refs_4_.refs_12_), channel_id=1, source_target_pairs={{0,8},{4,12},{8,0},{12,4},{16,24},{20,28},{24,16},{28,20},{1,9},{5... | collective-permute-start | bytes 1671176 | tf_op jit(solution)/shard_map/ppermute | solution.py:132
  55.0 2.9 %collective-permute-start.15 = (bf16[128,1024]{1,0:T(8,128)(2,1)S(1)}, bf16[128,1024]{1,0:T(8,128)(2,1)}, u32[]{:S(2)}, u32[]{:S(2)}) collective-permute-start(bf16[128,1024]{1,0:T(8,128)(2,1)S(1)} %get-tuple-element.180.refs_0_), channel_id=1, source_target_pairs={{0,2},{1,3},{2,0},{3,1},{4,6},{5,7},{6,4},{7,5},{8,10},{9,11},{10,... | collective-permute-start | bytes 786440 | tf_op jit(solution)/shard_map/ppermute | solution.py:132
  75.0 6.4 %collective-permute-done.17.refs_13_.refs_1_ = bf16[128,1024]{1,0:T(8,128)(2,1)} collective-permute-done((bf16[128,1024]{1,0:T(8,128)(2,1)S(1)}, bf16[128,1024]{1,0:T(8,128)(2,1)}, u32[]{:S(2)}, u32[]{:S(2)}) %collective-permute-start.17) | collective-permute-done | bytes 262176 | tf_op jit(solution)/shard_map/ppermute | solution.py:132
  82.7 2.4 collective-permute-start.19
  86.1 5.6 %collective-permute-done.19.refs_15_.refs_3_ = bf16[128,1024]{1,0:T(8,128)(2,1)S(1)} collective-permute-done((bf16[128,1024]{1,0:T(8,128)(2,1)S(1)}, bf16[128,1024]{1,0:T(8,128)(2,1)S(1)}, u32[]{:S(2)}, u32[]{:S(2)}) %collective-permute-start.19) | collective-permute-done | bytes 262176 | tf_op jit(solution)/shard_map/ppermute | solution.py:132
  91.7 2.1 collective-permute-start.16
  94.9 8.4 %front.1 = (bf16[512,1024]{1,0:T(8,128)(2,1)S(1)}, bf16[512,1024]{1,0:T(8,128)(2,1)S(1)}, bf16[512,768]{1,0:T(8,128)(2,1)S(1)}, bf16[512,1024]{1,0:T(8,128)(2,1)...) custom-call(s32[21]{0:T(128)S(1)} %pad_add_fusion.1.s_ref, ...), custom_call_target="tpu_custom_call" | custom-call | flops 1879048192 | bytes 14680064 | tf_op jit(solution)/shard_map/front/pallas_call | solution.py:584
  105.7 4.4 %hidden.1 = (bf16[512,1024]{1,0:T(8,128)(2,1)S(1)}, bf16[256,1024]{1,0:T(8,128)(2,1)S(1)}, bf16[512,256]{1,0:T(8,128)(2,1)S(1)}, bf16[512,1024]{1,0:T(8,128)(2,1)S(1)}, f32[8,1024]{1,0:T(8,128)S(1)}) custom-call(s32[21]{0:T(128)S(1)} %pad_add_fusion.1.s_ref, bf16[128,1024]{1,0:T(8,128)(2,1)S(1)} %copy-done.15, ...), custom_call_target="tpu_custom_call" | custom-call | flops 1342177280 | bytes 9437184 | tf_op jit(solution)/shard_map/hidden/pallas_call | solution.py:636
  110.1 1.8 convolution_convert_fusion.1
  112.1 12.0 %attend.1 = (bf16[512,256]{1,0:T(8,128)(2,1)S(1)}, bf16[512,768]{1,0:T(8,128)(2,1)S(1)}, f32[1,768]{1,0:T(1,128)S(1)}) custom-call(bf16[512,768]{1,0:T(8,128)(2,1)S(1)} %get-tuple-element.70.q_ref.k_ref.v_ref, bf16[512,768]{1,0:T(8,128)(2,1)S(1)} %get-tuple-element.70.q_ref.k_ref.v_ref, bf16[512,768]{1,0:T(8,128)(2,1)S(1)} %get-tuple-element.70.q_ref.k_ref.v_ref, ...), custom_call_target="tpu_custom_call" | custom-call | flops 4026531840 | bytes 6291456 | tf_op jit(solution)/shard_map/attend/pallas_call | solution.py:718
  124.9 4.7 %back.1 = (f32[128,1024]{1,0:T(8,128)S(1)}, bf16[128,1024]{1,0:T(8,128)(2,1)S(1)}, bf16[128,1024]{1,0:T(8,128)(2,1)S(1)}, bf16[128,1024]{1,0:T(8,128)(2,1)S(1)}, f32[8,1024]{1,0:T(8,128)S(1)}) custom-call(s32[21]{0:T(128)S(1)} %pad_add_fusion.1.s_ref, bf16[512,768]{1,0:T(8,128)(2,1)} %copy-done.25, bf16[512,1024]{1,0:T(8,128)(2,1)} %copy-done.2, ...), custom_call_target="tpu_custom_call" | custom-call | flops 1879048192 | bytes 8749056 | tf_op jit(solution)/shard_map/back/pallas_call | solution.py:440
  130.5 3.7 %terms.1 = (f32[512,1152]{1,0:T(8,128)}, bf16[512,1152]{1,0:T(8,128)(2,1)}) custom-call(s32[21]{0:T(128)S(1)} %pad_add_fusion.1.s_ref, bf16[512,1024]{1,0:T(8,128)(2,1)S(1)} %get-tuple-element.89.h_ref, bf16[512,768]{1,0:T(8,128)(2,1)S(1)} %copy-done.26, bf16[512,256]{1,0:T(8,128)(2,1)S(1)} %get-tuple-element.73.mix_ref, ...), custom_call_target="tpu_custom_call" | custom-call | flops 1073741824 | bytes 6757376 | tf_op jit(solution)/shard_map/terms/pallas_call | solution.py:440
  138.8 3.0 %branch.1 = (f32[128,1024]{1,0:T(8,128)S(1)}, bf16[128,1024]{1,0:T(8,128)(2,1)S(1)}, bf16[128,1024]{1,0:T(8,128)(2,1)S(1)}, bf16[128,1024]{1,0:T(8,128)(2,1)S(1)}) custom-call(s32[21]{0:T(128)S(1)} %pad_add_fusion.1.s_ref, bf16[512,256]{1,0:T(8,128)(2,1)S(1)} %copy-done.58, bf16[512,1024]{1,0:T(8,128)(2,1)S(1)} %copy-done.32, ...), custom_call_target="tpu_custom_call" | custom-call | flops 1342177280 | bytes 5799936 | tf_op jit(solution)/shard_map/branch/pallas_call | solution.py:440
  141.8 1.8 collective-permute-start.26
  143.7 2.0 collective-permute-start.27
  150.7 1.8 collective-permute-start.29
  154.1 5.4 %collective-permute-start.25 = (bf16[128,1024]{1,0:T(8,128)(2,1)S(1)}, bf16[128,1024]{1,0:T(8,128)(2,1)S(1)}, u32[]{:S(2)}, u32[]{:S(2)}) collective-permute-start(bf16[128,1024]{1,0:T(8,128)(2,1)S(1)} %get-tuple-element.79), channel_id=1, source_target_pairs={{0,2},{1,3},{2,0},{3,1},{4,6},{5,7},{6,4},{7,5},{8,10},{9,11},{10,... | collective-permute-start | bytes 786440 | tf_op jit(solution)/shard_map/ppermute | solution.py:132
  159.4 20.8 %collective-permute-done.28.r2_ref = bf16[128,1024]{1,0:T(8,128)(2,1)S(1)} collective-permute-done((bf16[128,1024]{1,0:T(8,128)(2,1)S(1)}, bf16[128,1024]{1,0:T(8,128)(2,1)S(1)}, u32[]{:S(2)}, u32[]{:S(2)}) %collective-permute-start.28) | collective-permute-done | bytes 262176 | tf_op jit(solution)/shard_map/ppermute | solution.py:132
  183.0 1.9 finish.1
  185.0 6.4 %collective-permute-done.25 = bf16[128,1024]{1,0:T(8,128)(2,1)S(1)} collective-permute-done((bf16[128,1024]{1,0:T(8,128)(2,1)S(1)}, bf16[128,1024]{1,0:T(8,128)(2,1)S(1)}, u32[]{:S(2)}, u32[]{:S(2)}) %collective-permute-start.25) | collective-permute-done | bytes 262176 | tf_op jit(solution)/shard_map/ppermute | solution.py:132
  196.6 15.9 %collective-permute-done.32.refs_2_ = bf16[128,1024]{1,0:T(8,128)(2,1)S(1)} collective-permute-done((bf16[128,1024]{1,0:T(8,128)(2,1)S(1)}, bf16[128,1024]{1,0:T(8,128)(2,1)S(1)}, u32[]{:S(2)}, u32[]{:S(2)}) %collective-permute-start.32) | collective-permute-done | bytes 262176 | tf_op jit(solution)/shard_map/ppermute | solution.py:132
  212.5 2.6 %collective-permute-start.45 = (bf16[128,1024]{1,0:T(8,128)(2,1)S(1)}, bf16[128,1024]{1,0:T(8,128)(2,1)S(1)}, u32[]{:S(2)}, u32[]{:S(2)}) collective-permute-start(bf16[128,1024]{1,0:T(8,128)(2,1)S(1)} %get-tuple-element.169), channel_id=1, source_target_pairs={{0,24},{4,28},{8,16},{12,20},{16,8},{20,12},{24,0},{28,4},{1,25},{... | collective-permute-start | bytes 786440 | tf_op jit(solution)/shard_map/ppermute | solution.py:132
  216.9 7.5 %collective-permute-done.36.refs_6_ = bf16[128,1152]{1,0:T(8,128)(2,1)S(1)} collective-permute-done((bf16[128,1152]{1,0:T(8,128)(2,1)S(1)}, bf16[128,1152]{1,0:T(8,128)(2,1)S(1)}, u32[]{:S(2)}, u32[]{:S(2)}) %collective-permute-start.36) | collective-permute-done | bytes 294944 | tf_op jit(solution)/shard_map/ppermute | solution.py:132
  225.5 2.3 collective-permute-start.39
  227.8 2.2 collective-permute-start.40
  232.4 7.4 %collective-permute-done.39.refs_2_ = bf16[32,1920]{1,0:T(8,128)(2,1)S(1)} collective-permute-done((bf16[32,1920]{1,0:T(8,128)(2,1)S(1)}, bf16[32,1920]{1,0:T(8,128)(2,1)S(1)}, u32[]{:S(2)}, u32[]{:S(2)}) %collective-permute-start.39) | collective-permute-done | bytes 122912 | tf_op jit(solution)/shard_map/ppermute | solution.py:132
  239.8 2.8 %adam.1 = (f32[32,3072]{1,0:T(8,128)}, f32[32,3072]{1,0:T(8,128)}, f32[32,3072]{1,0:T(8,128)}, f32[32,3072]{1,0:T(8,128)}, f32[32,4096]{1,0:T(8,128)}, /*index=5...) custom-call(s32[21]{0:T(128)S(1)} %pad_add_fusion.1.s_ref, ...), custom_call_target="tpu_custom_call" | custom-call | bytes 7053312 | tf_op jit(solution)/shard_map/adam/pallas_call | solution.py:440
  (252 shorter events, 55.3 us)
Async XLA Ops:
  5.1 15.2 %collective-permute-start.3 = (bf16[32,1920]{1,0:T(8,128)(2,1)S(1)}, bf16[32,1920]{1,0:T(8,128)(2,1)S(1)}, u32[]{:S(2)}, u32[]{:S(2)}) collective-permute-start(bf16[32,1920]{1,0:T(8,128)(2,1)S(1)} %get-tuple-element.67), channel_id=1, source_target_pairs={{0,1},{1,0},{2,3},{3,2},{4,5},{5,4},{6,7},{7,6},{8,9},{9,8},{10,11... | collective-permute-start | bytes 368648 | tf_op jit(solution)/shard_map/ppermute | solution.py:132
  11.7 41.0 %collective-permute-start = (bf16[128,1024]{1,0:T(8,128)(2,1)S(1)}, bf16[128,1024]{1,0:T(8,128)(2,1)S(1)}, u32[]{:S(2)}, u32[]{:S(2)}) collective-permute-start(bf16[128,1024]{1,0:T(8,128)(2,1)S(1)} %norm.1.refs_0_), channel_id=1, source_target_pairs={{0,1},{1,0},{2,3},{3,2},{4,5},{5,4},{6,7},{7,6},{8,9},{9,8},{10,11... | collective-permute-start | bytes 786440 | tf_op jit(solution)/shard_map/ppermute | solution.py:132
  14.2 40.0 %collective-permute-start.1 = (bf16[128,1024]{1,0:T(8,128)(2,1)S(1)}, bf16[128,1024]{1,0:T(8,128)(2,1)S(1)}, u32[]{:S(2)}, u32[]{:S(2)}) collective-permute-start(bf16[128,1024]{1,0:T(8,128)(2,1)S(1)} %norm.1.refs_0_), channel_id=1, source_target_pairs={{0,2},{1,3},{2,0},{3,1},{4,6},{5,7},{6,4},{7,5},{8,10},{9,11},{10,... | collective-permute-start | bytes 786440 | tf_op jit(solution)/shard_map/ppermute | solution.py:132
  17.5 36.8 %collective-permute-start.2 = (bf16[128,1024]{1,0:T(8,128)(2,1)S(1)}, bf16[128,1024]{1,0:T(8,128)(2,1)S(1)}, u32[]{:S(2)}, u32[]{:S(2)}) collective-permute-start(bf16[128,1024]{1,0:T(8,128)(2,1)S(1)} %norm.1.refs_0_), channel_id=1, source_target_pairs={{0,3},{1,2},{2,1},{3,0},{4,7},{5,6},{6,5},{7,4},{8,11},{9,10},{10,... | collective-permute-start | bytes 786440 | tf_op jit(solution)/shard_map/ppermute | solution.py:132
  18.4 31.1 %collective-permute-start.4 = (bf16[32,1920]{1,0:T(8,128)(2,1)S(1)}, bf16[32,1920]{1,0:T(8,128)(2,1)S(1)}, u32[]{:S(2)}, u32[]{:S(2)}) collective-permute-start(bf16[32,1920]{1,0:T(8,128)(2,1)S(1)} %get-tuple-element.68), channel_id=1, source_target_pairs={{0,2},{1,3},{2,0},{3,1},{4,6},{5,7},{6,4},{7,5},{8,10},{9,11},{10,... | collective-permute-start | bytes 368648 | tf_op jit(solution)/shard_map/ppermute | solution.py:132
  20.4 29.2 %collective-permute-start.5 = (bf16[32,1920]{1,0:T(8,128)(2,1)S(1)}, bf16[32,1920]{1,0:T(8,128)(2,1)S(1)}, u32[]{:S(2)}, u32[]{:S(2)}) collective-permute-start(bf16[32,1920]{1,0:T(8,128)(2,1)S(1)} %get-tuple-element.69), channel_id=1, source_target_pairs={{0,3},{1,2},{2,1},{3,0},{4,7},{5,6},{6,5},{7,4},{8,11},{9,10},{10,... | collective-permute-start | bytes 368648 | tf_op jit(solution)/shard_map/ppermute | solution.py:132
  49.5 12.8 %collective-permute-start.14 = (bf16[128,1024]{1,0:T(8,128)(2,1)S(1)}, bf16[128,1024]{1,0:T(8,128)(2,1)}, u32[]{:S(2)}, u32[]{:S(2)}) collective-permute-start(bf16[128,1024]{1,0:T(8,128)(2,1)S(1)} %get-tuple-element.180.refs_0_), channel_id=1, source_target_pairs={{0,1},{1,0},{2,3},{3,2},{4,5},{5,4},{6,7},{7,6},{8,9},{9,8},{10,11... | collective-permute-start | bytes 786440 | tf_op jit(solution)/shard_map/ppermute | solution.py:132
  50.2 31.2 %collective-permute-start.7 = (bf16[128,2176]{1,0:T(8,128)(2,1)S(1)}, bf16[128,2176]{1,0:T(8,128)(2,1)S(1)}, u32[]{:S(2)}, u32[]{:S(2)}) collective-permute-start(bf16[128,2176]{1,0:T(8,128)(2,1)S(1)} %join.1.refs_4_.refs_12_), channel_id=1, source_target_pairs={{0,8},{4,12},{8,0},{12,4},{16,24},{20,28},{24,16},{28,20},{1,9},{5... | collective-permute-start | bytes 1671176 | tf_op jit(solution)/shard_map/ppermute | solution.py:132
  52.7 29.2 %collective-permute-start.8 = (bf16[128,2176]{1,0:T(8,128)(2,1)S(1)}, bf16[128,2176]{1,0:T(8,128)(2,1)S(1)}, u32[]{:S(2)}, u32[]{:S(2)}) collective-permute-start(bf16[128,2176]{1,0:T(8,128)(2,1)S(1)} %join.1.refs_4_.refs_12_), channel_id=1, source_target_pairs={{0,16},{4,20},{8,24},{12,28},{16,0},{20,4},{24,8},{28,12},{1,17},{... | collective-permute-start | bytes 1671176 | tf_op jit(solution)/shard_map/ppermute | solution.py:132
  54.2 27.8 %collective-permute-start.9 = (bf16[128,2176]{1,0:T(8,128)(2,1)S(1)}, bf16[128,2176]{1,0:T(8,128)(2,1)S(1)}, u32[]{:S(2)}, u32[]{:S(2)}) collective-permute-start(bf16[128,2176]{1,0:T(8,128)(2,1)S(1)} %join.1.refs_4_.refs_12_), channel_id=1, source_target_pairs={{0,24},{4,28},{8,16},{12,20},{16,8},{20,12},{24,0},{28,4},{1,25},{... | collective-permute-start | bytes 1671176 | tf_op jit(solution)/shard_map/ppermute | solution.py:132
  55.0 18.4 %collective-permute-start.15 = (bf16[128,1024]{1,0:T(8,128)(2,1)S(1)}, bf16[128,1024]{1,0:T(8,128)(2,1)}, u32[]{:S(2)}, u32[]{:S(2)}) collective-permute-start(bf16[128,1024]{1,0:T(8,128)(2,1)S(1)} %get-tuple-element.180.refs_0_), channel_id=1, source_target_pairs={{0,2},{1,3},{2,0},{3,1},{4,6},{5,7},{6,4},{7,5},{8,10},{9,11},{10,... | collective-permute-start | bytes 786440 | tf_op jit(solution)/shard_map/ppermute | solution.py:132
  62.2 19.1 %collective-permute-start.17 = (bf16[128,1024]{1,0:T(8,128)(2,1)S(1)}, bf16[128,1024]{1,0:T(8,128)(2,1)}, u32[]{:S(2)}, u32[]{:S(2)}) collective-permute-start(bf16[128,1024]{1,0:T(8,128)(2,1)S(1)} %convert_element_type.135.refs_12_.refs_0_), channel_id=1, source_target_pairs={{0,8},{4,12},{8,0},{12,4},{16,24},{20,28},{24,16},{28,20},{1,9},{5... | collective-permute-start | bytes 786440 | tf_op jit(solution)/shard_map/ppermute | solution.py:132
  91.7 12.7 %collective-permute-start.16 = (bf16[128,1024]{1,0:T(8,128)(2,1)S(1)}, bf16[128,1024]{1,0:T(8,128)(2,1)S(1)}, u32[]{:S(2)}, u32[]{:S(2)}) collective-permute-start(bf16[128,1024]{1,0:T(8,128)(2,1)S(1)} %get-tuple-element.180.refs_0_), channel_id=1, source_target_pairs={{0,3},{1,2},{2,1},{3,0},{4,7},{5,6},{6,5},{7,4},{8,11},{9,10},{10,... | collective-permute-start | bytes 786440 | tf_op jit(solution)/shard_map/ppermute | solution.py:132
  112.0 36.9 %collective-permute-start.30 = (bf16[4,128,1024]{2,1,0:T(8,128)(2,1)}, bf16[4,128,1024]{2,1,0:T(8,128)(2,1)}, u32[]{:S(2)}, u32[]{:S(2)}) collective-permute-start(bf16[4,128,1024]{2,1,0:T(8,128)(2,1)} %bitcast.16), channel_id=1, source_target_pairs={{0,4},{4,0},{8,12},{12,8},{16,20},{20,16},{24,28},{28,24},{1,5},{5... | collective-permute-start | bytes 3145736 | tf_op jit(solution)/shard_map/ppermute | solution.py:132
  134.2 16.4 %collective-permute-start.34 = (bf16[4,128,1152]{2,1,0:T(8,128)(2,1)}, bf16[4,128,1152]{2,1,0:T(8,128)(2,1)}, u32[]{:S(2)}, u32[]{:S(2)}) collective-permute-start(bf16[4,128,1152]{2,1,0:T(8,128)(2,1)} %bitcast.22), channel_id=1, source_target_pairs={{0,4},{4,0},{8,12},{12,8},{16,20},{20,16},{24,28},{28,24},{1,5},{5... | collective-permute-start | bytes 3538952 | tf_op jit(solution)/shard_map/ppermute | solution.py:132
  143.7 15.8 %collective-permute-start.27 = (bf16[128,1024]{1,0:T(8,128)(2,1)S(1)}, bf16[128,1024]{1,0:T(8,128)(2,1)S(1)}, u32[]{:S(2)}, u32[]{:S(2)}) collective-permute-start(bf16[128,1024]{1,0:T(8,128)(2,1)S(1)} %copy-done.54), channel_id=1, source_target_pairs={{0,1},{1,0},{2,3},{3,2},{4,5},{5,4},{6,7},{7,6},{8,9},{9,8},{10,11... | collective-permute-start | bytes 786440 | tf_op jit(solution)/shard_map/ppermute | solution.py:132
  145.6 34.6 %collective-permute-start.28 = (bf16[128,1024]{1,0:T(8,128)(2,1)S(1)}, bf16[128,1024]{1,0:T(8,128)(2,1)S(1)}, u32[]{:S(2)}, u32[]{:S(2)}) collective-permute-start(bf16[128,1024]{1,0:T(8,128)(2,1)S(1)} %copy-done.52), channel_id=1, source_target_pairs={{0,2},{1,3},{2,0},{3,1},{4,6},{5,7},{6,4},{7,5},{8,10},{9,11},{10,... | collective-permute-start | bytes 786440 | tf_op jit(solution)/shard_map/ppermute | solution.py:132
  148.9 45.7 %collective-permute-start.42 = (bf16[4,128,1024]{2,1,0:T(8,128)(2,1)}, bf16[4,128,1024]{2,1,0:T(8,128)(2,1)S(1)}, u32[]{:S(2)}, u32[]{:S(2)}) collective-permute-start(bf16[4,128,1024]{2,1,0:T(8,128)(2,1)} %bitcast.27), channel_id=1, source_target_pairs={{0,4},{4,0},{8,12},{12,8},{16,20},{20,16},{24,28},{28,24},{1,5},{5... | collective-permute-start | bytes 3145736 | tf_op jit(solution)/shard_map/ppermute | solution.py:132
  150.7 31.2 %collective-permute-start.29 = (bf16[128,1024]{1,0:T(8,128)(2,1)S(1)}, bf16[128,1024]{1,0:T(8,128)(2,1)S(1)}, u32[]{:S(2)}, u32[]{:S(2)}) collective-permute-start(bf16[128,1024]{1,0:T(8,128)(2,1)S(1)} %copy-done.50), channel_id=1, source_target_pairs={{0,3},{1,2},{2,1},{3,0},{4,7},{5,6},{6,5},{7,4},{8,11},{9,10},{10,... | collective-permute-start | bytes 786440 | tf_op jit(solution)/shard_map/ppermute | solution.py:132
  154.1 37.3 %collective-permute-start.25 = (bf16[128,1024]{1,0:T(8,128)(2,1)S(1)}, bf16[128,1024]{1,0:T(8,128)(2,1)S(1)}, u32[]{:S(2)}, u32[]{:S(2)}) collective-permute-start(bf16[128,1024]{1,0:T(8,128)(2,1)S(1)} %get-tuple-element.79), channel_id=1, source_target_pairs={{0,2},{1,3},{2,0},{3,1},{4,6},{5,7},{6,4},{7,5},{8,10},{9,11},{10,... | collective-permute-start | bytes 786440 | tf_op jit(solution)/shard_map/ppermute | solution.py:132
  159.4 33.4 %collective-permute-start.24 = (bf16[128,1024]{1,0:T(8,128)(2,1)S(1)}, bf16[128,1024]{1,0:T(8,128)(2,1)S(1)}, u32[]{:S(2)}, u32[]{:S(2)}) collective-permute-start(bf16[128,1024]{1,0:T(8,128)(2,1)S(1)} %get-tuple-element.78), channel_id=1, source_target_pairs={{0,1},{1,0},{2,3},{3,2},{4,5},{5,4},{6,7},{7,6},{8,9},{9,8},{10,11... | collective-permute-start | bytes 786440 | tf_op jit(solution)/shard_map/ppermute | solution.py:132
  180.2 15.8 %collective-permute-start.31 = (bf16[128,1024]{1,0:T(8,128)(2,1)S(1)}, bf16[128,1024]{1,0:T(8,128)(2,1)S(1)}, u32[]{:S(2)}, u32[]{:S(2)}) collective-permute-start(bf16[128,1024]{1,0:T(8,128)(2,1)S(1)} %get-tuple-element.173), channel_id=1, source_target_pairs={{0,8},{4,12},{8,0},{12,4},{16,24},{20,28},{24,16},{28,20},{1,9},{5... | collective-permute-start | bytes 786440 | tf_op jit(solution)/shard_map/ppermute | solution.py:132
  181.9 33.7 %collective-permute-start.35 = (bf16[128,1152]{1,0:T(8,128)(2,1)S(1)}, bf16[128,1152]{1,0:T(8,128)(2,1)S(1)}, u32[]{:S(2)}, u32[]{:S(2)}) collective-permute-start(bf16[128,1152]{1,0:T(8,128)(2,1)S(1)} %get-tuple-element.166), channel_id=1, source_target_pairs={{0,8},{4,12},{8,0},{12,4},{16,24},{20,28},{24,16},{28,20},{1,9},{5... | collective-permute-start | bytes 884744 | tf_op jit(solution)/shard_map/ppermute | solution.py:132
  191.4 21.1 %collective-permute-start.32 = (bf16[128,1024]{1,0:T(8,128)(2,1)S(1)}, bf16[128,1024]{1,0:T(8,128)(2,1)S(1)}, u32[]{:S(2)}, u32[]{:S(2)}) collective-permute-start(bf16[128,1024]{1,0:T(8,128)(2,1)S(1)} %get-tuple-element.172), channel_id=1, source_target_pairs={{0,16},{4,20},{8,24},{12,28},{16,0},{20,4},{24,8},{28,12},{1,17},{... | collective-permute-start | bytes 786440 | tf_op jit(solution)/shard_map/ppermute | solution.py:132
  192.8 22.3 %collective-permute-start.33 = (bf16[128,1024]{1,0:T(8,128)(2,1)S(1)}, bf16[128,1024]{1,0:T(8,128)(2,1)S(1)}, u32[]{:S(2)}, u32[]{:S(2)}) collective-permute-start(bf16[128,1024]{1,0:T(8,128)(2,1)S(1)} %get-tuple-element.171), channel_id=1, source_target_pairs={{0,24},{4,28},{8,16},{12,20},{16,8},{20,12},{24,0},{28,4},{1,25},{... | collective-permute-start | bytes 786440 | tf_op jit(solution)/shard_map/ppermute | solution.py:132
  194.5 29.9 %collective-permute-start.36 = (bf16[128,1152]{1,0:T(8,128)(2,1)S(1)}, bf16[128,1152]{1,0:T(8,128)(2,1)S(1)}, u32[]{:S(2)}, u32[]{:S(2)}) collective-permute-start(bf16[128,1152]{1,0:T(8,128)(2,1)S(1)} %get-tuple-element.165), channel_id=1, source_target_pairs={{0,16},{4,20},{8,24},{12,28},{16,0},{20,4},{24,8},{28,12},{1,17},{... | collective-permute-start | bytes 884744 | tf_op jit(solution)/shard_map/ppermute | solution.py:132
  196.0 28.4 %collective-permute-start.37 = (bf16[128,1152]{1,0:T(8,128)(2,1)S(1)}, bf16[128,1152]{1,0:T(8,128)(2,1)S(1)}, u32[]{:S(2)}, u32[]{:S(2)}) collective-permute-start(bf16[128,1152]{1,0:T(8,128)(2,1)S(1)} %get-tuple-element.164), channel_id=1, source_target_pairs={{0,24},{4,28},{8,16},{12,20},{16,8},{20,12},{24,0},{28,4},{1,25},{... | collective-permute-start | bytes 884744 | tf_op jit(solution)/shard_map/ppermute | solution.py:132
  212.5 15.3 %collective-permute-start.45 = (bf16[128,1024]{1,0:T(8,128)(2,1)S(1)}, bf16[128,1024]{1,0:T(8,128)(2,1)S(1)}, u32[]{:S(2)}, u32[]{:S(2)}) collective-permute-start(bf16[128,1024]{1,0:T(8,128)(2,1)S(1)} %get-tuple-element.169), channel_id=1, source_target_pairs={{0,24},{4,28},{8,16},{12,20},{16,8},{20,12},{24,0},{28,4},{1,25},{... | collective-permute-start | bytes 786440 | tf_op jit(solution)/shard_map/ppermute | solution.py:132
  215.1 14.9 %collective-permute-start.44 = (bf16[128,1024]{1,0:T(8,128)(2,1)S(1)}, bf16[128,1024]{1,0:T(8,128)(2,1)S(1)}, u32[]{:S(2)}, u32[]{:S(2)}) collective-permute-start(bf16[128,1024]{1,0:T(8,128)(2,1)S(1)} %get-tuple-element.170), channel_id=1, source_target_pairs={{0,16},{4,20},{8,24},{12,28},{16,0},{20,4},{24,8},{28,12},{1,17},{... | collective-permute-start | bytes 786440 | tf_op jit(solution)/shard_map/ppermute | solution.py:132
  215.6 14.3 %collective-permute-start.43 = (bf16[128,1024]{1,0:T(8,128)(2,1)S(1)}, bf16[128,1024]{1,0:T(8,128)(2,1)S(1)}, u32[]{:S(2)}, u32[]{:S(2)}) collective-permute-start(bf16[128,1024]{1,0:T(8,128)(2,1)S(1)} %get-tuple-element.168), channel_id=1, source_target_pairs={{0,8},{4,12},{8,0},{12,4},{16,24},{20,28},{24,16},{28,20},{1,9},{5... | collective-permute-start | bytes 786440 | tf_op jit(solution)/shard_map/ppermute | solution.py:132
  225.5 14.3 %collective-permute-start.39 = (bf16[32,1920]{1,0:T(8,128)(2,1)S(1)}, bf16[32,1920]{1,0:T(8,128)(2,1)S(1)}, u32[]{:S(2)}, u32[]{:S(2)}) collective-permute-start(bf16[32,1920]{1,0:T(8,128)(2,1)S(1)} %get-tuple-element.98), channel_id=1, source_target_pairs={{0,2},{1,3},{2,0},{3,1},{4,6},{5,7},{6,4},{7,5},{8,10},{9,11},{10,... | collective-permute-start | bytes 368648 | tf_op jit(solution)/shard_map/ppermute | solution.py:132
  231.6 13.8 %collective-permute-start.41 = (f32[32,1024]{1,0:T(8,128)S(1)}, f32[32,1024]{1,0:T(8,128)S(1)}, u32[]{:S(2)}, u32[]{:S(2)}) collective-permute-start(f32[32,1024]{1,0:T(8,128)S(1)} %get-tuple-element.101), channel_id=1, source_target_pairs={{0,0},{4,1},{8,2},{12,3},{1,4},{5,5},{9,6},{13,7},{2,8},{6,9},{10,... | collective-permute-start | bytes 393224 | tf_op jit(solution)/shard_map/ppermute | solution.py:1047
  (85 other events, 925.4 us)

commit v4 on v3

--- a/solution.py
+++ b/solution.py
@@ -82,8 +82,8 @@
     return pltpu.CompilerParams(vmem_limit_bytes=mib << 20)
 
 
-def cost(flops, count):
-    return pl.CostEstimate(flops=flops, bytes_accessed=count, transcendentals=0)
+def cost(micros):
+    return pl.CostEstimate(flops=int(micros * 1.15e9), bytes_accessed=1 << 20, transcendentals=0)
 
 
 def whole_spec(shape):
@@ -433,10 +433,8 @@
     )
 
 
-def single(body, outs, prefetch, ins, flops, name, scratch=(), mib=48):
+def single(body, outs, prefetch, ins, micros, name, scratch=(), mib=48):
     shapes = tuple(jax.ShapeDtypeStruct(s, d) for s, d in outs)
-    moved = sum(a.size * a.dtype.itemsize for a in ins)
-    moved += sum(s.size * s.dtype.itemsize for s in shapes)
     return pl.pallas_call(
         body,
         out_shape=shapes,
@@ -448,7 +446,7 @@
             scratch_shapes=list(scratch),
         ),
         compiler_params=params(mib),
-        cost_estimate=cost(flops, moved),
+        cost_estimate=cost(micros),
         name=name,
     )(prefetch, *ins)
 
@@ -472,7 +470,16 @@
 OUT = TILE
 
 
-def pack_body(s_ref, qkv_ref, up_ref, vec_ref, *outs):
+def pack_body(s_ref, qkv_ref, up_ref, vec_ref, *refs):
+    outs, turn_ref = refs[:-1], refs[-1]
+    count, cols = vec_ref.shape
+    turn_ref[...] = jnp.zeros_like(turn_ref)
+    vec = vec_ref[...]
+    for i in range(3):
+        part = vec.astype(bf16).astype(f32)
+        turn_ref[16 * i : 16 * i + count, :cols] = part
+        vec = vec - part
+    vec16 = turn_ref[...].T[:cols, :].astype(bf16)
     for k in range(N_SHARD):
         t = s_ref[NEAR + k]
         o_ref = outs[k]
@@ -481,7 +488,7 @@
         for c in range(UP // LANES):
             at = QKV + c * LANES
             o_ref[:, at : at + LANES] = up_ref[:, lane_block(c * N_SHARD + t)].astype(bf16)
-        o_ref[:, QKV + UP :] = vec_ref[...]
+        o_ref[:, QKV + UP :] = vec16
 
 
 def norm_body(s_ref, x_ref, o_ref, n_ref):
@@ -518,7 +525,8 @@
     n_refs, refs = refs[:N_SHARD], refs[N_SHARD:]
     w_refs, refs = refs[:N_REP], refs[N_REP:]
     v_refs, refs = refs[:N_REP], refs[N_REP:]
-    rope_ref, h1_ref, h2_ref, qkv_ref, act_ref, slope_ref, vec_ref, last_ref, bias_ref = refs
+    out_refs, refs = refs[:N_REP], refs[N_REP:]
+    rope_ref, whole_ref, h1_ref, h2_ref, qkv_ref, act_ref, slope_ref, vec_ref, last_ref, bias_ref = refs
     j = pl.program_id(0)
     rows = n_refs[0].shape[0]
 
@@ -537,6 +545,12 @@
         both = vec_ref[7:8, :] + vec_ref[12:13, :]
         for i in range(N_REP):
             last_ref[0:1, lane_block(s_ref[ORDER + i])] = both[:, i * LANES : (i + 1) * LANES]
+        chunks = D // OUT
+        size = out_refs[0].shape[0] // chunks
+        for i in range(N_REP):
+            at = row_block(s_ref[ORDER + i], size)
+            for c in range(chunks):
+                whole_ref[at, c * OUT : (c + 1) * OUT] = out_refs[i][c * size : (c + 1) * size, :]
 
     def product(h_ref):
         total = bias_ref[j, 0:1, :]
@@ -571,6 +585,7 @@
     tokens = rope.shape[0]
     block = pieces[0].shape[0]
     shapes = (
+        ((OUT, D), bf16),
         ((tokens, D), bf16),
         ((tokens, D), bf16),
         ((tokens, QKV), bf16),
@@ -580,7 +595,7 @@
         ((8, D), f32),
     )
     specs = [whole_spec(s) for s, _ in shapes]
-    specs[2] = pl.BlockSpec((tokens, TILE), lambda j, s: (0, jnp.minimum(j, 2)))
+    specs[3] = pl.BlockSpec((tokens, TILE), lambda j, s: (0, jnp.minimum(j, 2)))
     return pl.pallas_call(
         front_body,
         out_shape=tuple(jax.ShapeDtypeStruct(s, d) for s, d in shapes),
@@ -590,30 +605,24 @@
             in_specs=[whole_spec(n.shape) for n in normed]
             + [pl.BlockSpec((block, TILE), lambda j, s: (0, j))] * N_REP
             + [pl.BlockSpec((block, LANES), lambda j, s: (0, (QKV + UP + OUT) // LANES))] * N_REP
+            + [pl.BlockSpec((block, OUT), lambda j, s: (0, (QKV + UP) // OUT))] * N_REP
             + [whole_spec(rope.shape)],
             out_specs=tuple(specs),
             scratch_shapes=[pltpu.VMEM(((QKV + UP) // TILE, 8, TILE), f32)],
         ),
         compiler_params=params(40),
-        cost_estimate=cost(2 * tokens * D * (QKV + UP), 14 << 20),
+        cost_estimate=cost(9),
         name="front",
-    )(scalars, *normed, *pieces, *pieces, rope)
+    )(scalars, *normed, *pieces, *pieces, *pieces, rope)
 
 
 def hidden_body(s_ref, *refs):
-    dy_refs, refs = refs[:N_SHARD], refs[N_SHARD:]
-    out_refs, refs = refs[:N_REP], refs[N_REP:]
+    dy_ref, refs = refs[0], refs[1:]
     down_refs, refs = refs[:N_REP], refs[N_REP:]
-    slope_ref, seq_ref, whole_ref, dmix_ref, du_ref, sum_ref = refs
-    tokens = dy_refs[0].shape[0]
+    slope_ref, whole_ref, seq_ref, dmix_ref, du_ref, sum_ref = refs
+    tokens = dy_ref.shape[0] // N_SHARD
     for k in range(N_SHARD):
-        seq_ref[k * tokens : (k + 1) * tokens, :] = dy_refs[k][...]
-    chunks = D // OUT
-    rows = out_refs[0].shape[0] // chunks
-    for i in range(N_REP):
-        at = row_block(s_ref[ORDER + i], rows)
-        for c in range(chunks):
-            whole_ref[at, c * OUT : (c + 1) * OUT] = out_refs[i][c * rows : (c + 1) * rows, :]
+        seq_ref[k * tokens : (k + 1) * tokens, :] = dy_ref[row_block(s_ref[NEAR + k], tokens), :]
     dy = seq_ref[...]
     dmix_ref[...] = contract_cols(dy, whole_ref[...]).astype(bf16)
     for i in range(N_REP):
@@ -623,71 +632,61 @@
         sum_ref[0:1, at] = jnp.sum(du, axis=0, keepdims=True)
 
 
-def hidden(scalars, dys, pieces, downs, slope):
-    tokens = slope.shape[0]
-    block = pieces[0].shape[0]
-    shapes = (
-        ((tokens, D), bf16),
-        ((OUT, D), bf16),
-        ((tokens, OUT), bf16),
-        ((tokens, UP), bf16),
-        ((8, UP), f32),
-    )
-    return pl.pallas_call(
-        hidden_body,
-        out_shape=tuple(jax.ShapeDtypeStruct(s, d) for s, d in shapes),
-        grid_spec=pltpu.PrefetchScalarGridSpec(
-            num_scalar_prefetch=1,
-            grid=(1,),
-            in_specs=[whole_spec(a.shape) for a in dys]
-            + [pl.BlockSpec((block, OUT), lambda j, s: (0, (QKV + UP) // OUT))] * N_REP
-            + [whole_spec(a.shape) for a in downs]
-            + [whole_spec(slope.shape)],
-            out_specs=tuple(whole_spec(s) for s, _ in shapes),
-        ),
-        compiler_params=params(40),
-        cost_estimate=cost(2 * tokens * D * (OUT + UP), 9 << 20),
-        name="hidden",
-    )(scalars, *dys, *pieces, *downs, slope)
-
-
-def attend_body(q_ref, k_ref, v_ref, dm_ref, mask_ref, rope_ref, mix_ref, dqkv_ref, sum_ref, dk_ref, dv_ref):
+def weigh(q, k, mask):
+    score = contract_cols(q, k) * (HEAD ** (-0.5)) + mask
+    expo = jnp.exp(score - jnp.max(score, axis=-1, keepdims=True))
+    return expo * (1.0 / jnp.sum(expo, axis=-1, keepdims=True))
+
+
+def only(values, mine):
+    return jnp.where(mine, values, jnp.zeros_like(values))
+
+
+def mix_body(q_ref, k_ref, v_ref, mask_ref, mix_ref):
+    first = lax.broadcasted_iota(jnp.int32, (LANES, LANES), 1) < HEAD
+    k = k_ref[...]
+    v = v_ref[...]
+    for c in range(0, q_ref.shape[0], LANES):
+        rows = slice(c, c + LANES)
+        q = q_ref[rows, :]
+        mixes = []
+        for mine in (first, jnp.logical_not(first)):
+            prob = weigh(only(q, mine), k, mask_ref[rows, :])
+            mixes.append(plain_dot(prob.astype(bf16), v))
+        mix_ref[rows, :] = jnp.where(first, mixes[0], mixes[1]).astype(bf16)
+
+
+def attend_body(
+    q_ref, k_ref, v_ref, dm_ref, mix_ref, mask_ref, rope_ref, dqkv_ref, sum_ref, dk_ref, dv_ref
+):
     pair = pl.program_id(0)
     tokens = q_ref.shape[0]
-    chunk = LANES
     scale = HEAD ** (-0.5)
-    first = lax.broadcasted_iota(jnp.int32, (chunk, LANES), 1) < HEAD
+    first = lax.broadcasted_iota(jnp.int32, (LANES, LANES), 1) < HEAD
     every = lax.broadcasted_iota(jnp.int32, (tokens, LANES), 1) < HEAD
     k = k_ref[...]
     v = v_ref[...]
     pairs = pl.num_programs(0)
 
     def columns(part):
-        return pl.ds(pl.multiple_of(part * pairs * LANES + pair * LANES, LANES), LANES)
+        return lane_block(part * pairs + pair)
 
     dq_total = jnp.zeros((1, LANES), f32)
-    for c in range(0, tokens, chunk):
-        rows = slice(c, c + chunk)
+    for c in range(0, tokens, LANES):
+        rows = slice(c, c + LANES)
         q = q_ref[rows, :]
         dm = dm_ref[rows, :]
-        mixes, dqs, dks, dvs = [], [], [], []
-        for h in range(2):
-            mine = first if h == 0 else jnp.logical_not(first)
-            qh = jnp.where(mine, q, jnp.zeros_like(q))
-            dmh = jnp.where(mine, dm, jnp.zeros_like(dm))
-            score = contract_cols(qh, k) * scale + mask_ref[rows, :]
-            expo = jnp.exp(score - jnp.max(score, axis=-1, keepdims=True))
-            prob = expo * (1.0 / jnp.sum(expo, axis=-1, keepdims=True))
-            prob16 = prob.astype(bf16)
-            mix16 = plain_dot(prob16, v).astype(bf16)
-            delta = jnp.sum(dmh.astype(f32) * mix16.astype(f32), axis=-1, keepdims=True)
+        mix = mix_ref[rows, :].astype(f32)
+        dqs, dks, dvs = [], [], []
+        for mine in (first, jnp.logical_not(first)):
+            dmh = only(dm, mine)
+            prob = weigh(only(q, mine), k, mask_ref[rows, :])
+            delta = jnp.sum(dmh.astype(f32) * mix, axis=-1, keepdims=True)
             d_prob = contract_cols(dmh, v)
             ds16 = (prob * (d_prob - delta) * scale).astype(bf16)
-            mixes.append(mix16)
             dqs.append(plain_dot(ds16, k))
             dks.append(contract_rows(ds16, q))
-            dvs.append(contract_rows(prob16, dm))
-        mix_ref[rows, :] = jnp.where(first, mixes[0], mixes[1])
+            dvs.append(contract_rows(prob.astype(bf16), dm))
         dq = turn(jnp.where(first, dqs[0], dqs[1]), rope_ref[rows, :], -1.0)
         dqkv_ref[rows, columns(0)] = dq.astype(bf16)
         dq_total = dq_total + jnp.sum(dq, axis=0, keepdims=True)
@@ -708,39 +707,43 @@
     sum_ref[:, columns(2)] = jnp.sum(dv, axis=0, keepdims=True)
 
 
-def attend(qkv, d_mix, mask, rope):
-    tokens, feats = d_mix.shape
-    pairs = feats // LANES
-
-    def part(first):
-        return pl.BlockSpec((tokens, LANES), lambda j: (0, first * pairs + j))
-
+def pair_spec(tokens, first):
+    return pl.BlockSpec((tokens, LANES), lambda j: (0, first + j))
+
+
+def mix_heads(qkv, mask):
+    tokens = qkv.shape[0]
+    pairs = OUT // LANES
+    return pl.pallas_call(
+        mix_body,
+        out_shape=jax.ShapeDtypeStruct((tokens, OUT), bf16),
+        grid=(pairs,),
+        in_specs=[pair_spec(tokens, i * pairs) for i in range(3)] + [whole_spec(mask.shape)],
+        out_specs=pair_spec(tokens, 0),
+        compiler_params=params(24),
+        cost_estimate=cost(6),
+        name="mix_heads",
+    )(qkv, qkv, qkv, mask)
+
+
+def attend_back(qkv, d_mix, mixed, mask, rope):
+    tokens = qkv.shape[0]
+    pairs = OUT // LANES
     return pl.pallas_call(
         attend_body,
         out_shape=(
-            jax.ShapeDtypeStruct((tokens, feats), bf16),
-            jax.ShapeDtypeStruct((tokens, 3 * feats), bf16),
-            jax.ShapeDtypeStruct((1, 3 * feats), f32),
+            jax.ShapeDtypeStruct((tokens, QKV), bf16),
+            jax.ShapeDtypeStruct((1, QKV), f32),
         ),
         grid=(pairs,),
-        in_specs=[
-            part(0),
-            part(1),
-            part(2),
-            part(0),
-            whole_spec(mask.shape),
-            whole_spec(rope.shape),
-        ],
-        out_specs=(
-            pl.BlockSpec((tokens, LANES), lambda j: (0, j)),
-            whole_spec((tokens, 3 * feats)),
-            whole_spec((1, 3 * feats)),
-        ),
+        in_specs=[pair_spec(tokens, i * pairs) for i in range(3)]
+        + [pair_spec(tokens, 0), pair_spec(tokens, 0), whole_spec(mask.shape), whole_spec(rope.shape)],
+        out_specs=(whole_spec((tokens, QKV)), whole_spec((1, QKV))),
         scratch_shapes=[pltpu.VMEM((tokens, LANES), f32), pltpu.VMEM((tokens, LANES), f32)],
-        compiler_params=params(40),
-        cost_estimate=cost(60 * tokens * tokens * feats, 6 << 20),
-        name="attend",
-    )(qkv, qkv, qkv, d_mix, mask, rope)
+        compiler_params=params(32),
+        cost_estimate=cost(11),
+        name="attend_back",
+    )(qkv, qkv, qkv, d_mix, mixed, mask, rope)
 
 
 def back_body(s_ref, dqkv_ref, du_ref, vec_ref, *refs):
@@ -772,17 +775,16 @@
         sum_ref[3:4, cols] = sums[1]
 
 
-def branch_body(s_ref, mix_ref, act_ref, out_ref, last_ref, x_ref, *refs):
-    down_refs, refs = refs[:N_REP], refs[N_REP:]
-    own_ref, sent_refs = refs[0], refs[1:]
-    rows = x_ref.shape[0]
+def branch_body(s_ref, mix_ref, act_ref, out_ref, *refs):
+    down_refs, total_ref = refs[:N_REP], refs[N_REP]
     total = plain_dot(mix_ref[...], out_ref[...])
     for i in range(0, N_REP, 2):
         weights = jnp.concatenate([down_refs[i][...], down_refs[i + 1][...]], axis=0)
         total = total + plain_dot(act_ref[:, i * LANES : (i + 2) * LANES], weights)
-    own_ref[...] = x_ref[...] + total[:rows] + last_ref[0:1, :]
-    for k in range(1, N_SHARD):
-        sent_refs[k - 1][...] = total[k * rows : (k + 1) * rows].astype(bf16)
+    rows = total.shape[0] // N_SHARD
+    for k in range(N_SHARD):
+        at = row_block(s_ref[NEAR + k], rows)
+        total_ref[at, :] = total[k * rows : (k + 1) * rows].astype(bf16)
 
 
 def terms_body(
@@ -832,12 +834,20 @@
 
 def adam_body(s_ref, *refs):
     got, refs = refs[:N_SHARD], refs[N_SHARD:]
-    states, refs = (refs[0:3], refs[3:6]), refs[6:]
-    results, refs = (refs[0:4], refs[4:8]), refs[8:]
-    vec_ref, all_ref = refs
+    states, vec_state, refs = (refs[0:3], refs[3:6]), refs[6:9], refs[9:]
+    results, vec_result, refs = (refs[0:4], refs[4:8]), refs[8:12], refs[12:]
+    all_ref, turn_ref = refs
     for k in range(N_SHARD):
         all_ref[k] = got[k][...].astype(f32)
-    vec_ref[...] = sum(all_ref[k, :, QKV + UP :] for k in range(N_SHARD))
+    count, cols = vec_state[0].shape
+    turn_ref[...] = jnp.zeros_like(turn_ref)
+    turn_ref[:cols, :] = sum(all_ref[k, :, QKV + UP :] for k in range(N_SHARD))
+    turn_ref[...] = turn_ref[...].T
+    grad = turn_ref[:count, :cols]
+    vec_result[0][...] = grad
+    new = adam_update(vec_state[0][...], grad, vec_state[1][...], vec_state[2][...], LR_VECTOR, 0.0)
+    for ref, value in zip(vec_result[1:], new):
+        ref[...] = value
     first = 0
     for state, result in zip(states, results):
         for c in range(state[0].shape[1] // (N_SHARD * LANES)):
@@ -882,10 +892,12 @@
     return near + [hop(piece, "rep", N_REP, 1) for piece in near]
 
 
-def sum_rep(keep, sent):
-    got = hop(sent, "rep", N_REP, 1)
+def sum_rep(keep, got, *earlier):
     parts = [keep[k] + got[k].astype(f32) for k in range(4)]
-    return [parts[0]] + to_chips([part.astype(bf16) for part in parts[1:]])
+    sent = [part.astype(bf16) for part in parts[1:]]
+    if earlier:
+        sent = [after(part, *earlier) for part in sent]
+    return [parts[0]] + to_chips(sent)
 
 
 def after(value, *others):
@@ -930,15 +942,6 @@
         [lax.dynamic_index_in_dim(table, rep, 0, keepdims=False), near, shard[None]]
     ).astype(jnp.int32)
 
-    vec_t = vectors.T
-    high = lax.reduce_precision(vec_t, 8, 7)
-    middle = lax.reduce_precision(vec_t - high, 8, 7)
-    low = (vec_t - high) - middle
-    gap = jnp.zeros((cols, 16 - n_vec), f32)
-    vec16 = jnp.concatenate(
-        [high, gap, middle, gap, low, gap, jnp.zeros((cols, LANES - 48), f32)], axis=1
-    ).astype(bf16)
-
     share = HEAD // rows
     pair = LANES // HEAD
     moves = []
@@ -949,31 +952,42 @@
         moves.append((at, (local * share + part) * N_SHARD + owner))
 
     own_cols = [((rows, QKV + UP + LANES), bf16)] * N_SHARD
-    packed = single(pack_body, own_cols, scalars, [qkv_weight, up_weight, vec16], 0, "pack")
+    square = pltpu.VMEM((LANES, LANES), f32)
+    packed = single(
+        pack_body, own_cols, scalars, [qkv_weight, up_weight, vectors], 1, "pack", [square]
+    )
     got_cols = to_shards(packed[1:])
     out_rows = lax.ppermute(out_weight.astype(bf16), ("rep", "shard"), moves)
+    down_own = down_weight.astype(bf16)
+    late_down = after(down_own, out_rows, got_cols[0])
+    downs = [
+        down_own,
+        hop(down_own, "rep", N_REP, 2),
+        hop(late_down, "rep", N_REP, 4),
+    ]
     (normed_own,) = single(
         norm_body,
         [((tok_count, D), bf16)],
         scalars,
         [block_in],
-        0,
+        1,
         "norm",
         [pltpu.VMEM((tok_count, D), f32)],
     )
-    downs = gather_chips(down_weight.astype(bf16))
     (in_rows,) = single(
         join_body,
         [((N_SHARD * rows, QKV + UP + OUT + LANES), bf16)],
         scalars,
-        [packed[0], *got_cols, out_rows],
-        0,
+        [packed[0], *got_cols[:2], after(got_cols[2], normed_own), out_rows],
+        1,
         "join",
     )
-    normed = [normed_own] + to_shards([normed_own] * 3)
+    in_rows = after(in_rows, *downs[1:])
+    normed = [normed_own] + to_shards([after(normed_own, *got_cols)] * 3)
     pieces = gather_chips(in_rows)
-    dy_own = cotangent.astype(bf16)
-    dys = [dy_own] + to_shards([dy_own] * 3)
+    downs.append(hop(after(down_own, *pieces[1:4]), "rep", N_REP, 6))
+    downs = downs + [hop(piece, "rep", N_REP, 1) for piece in downs]
+    dy_all = lax.all_gather(cotangent.astype(bf16), "shard", axis=0, tiled=True)
 
     rope_parts = jnp.asarray(rope_lanes(seq_len)).reshape(N_SHARD, tok_count, 3 * LANES)
     rope = jnp.concatenate(
@@ -986,40 +1000,53 @@
     allowed = (seg_row[:, None] == seg_row[None, :]) & (positions[None, :] <= positions[:, None])
     mask = jnp.where(allowed, 0.0, HIDDEN).astype(f32)
 
-    h_one, h_two, qkv16, act16, slope, vec_rel, last = front(scalars, normed, pieces, rope)
-    dy_seq, out_whole, d_mixed16, d_up16, up_sum = hidden(scalars, dys, pieces, downs, slope)
-    half = D // 2
-
-    def split_terms(left, right):
-        keep = contract_rows(left[:, :half], right).reshape(4, LANES, D)
-        sent = contract_rows(left[:, half:], right).astype(bf16).reshape(4, LANES, D)
-        return keep, sent
-
-    down_parts = sum_rep(*split_terms(act16, dy_seq))
-    up_parts = sum_rep(*split_terms(h_two, d_up16))
-
-    mixed16, d_qkv16, qkv_sum = attend(qkv16, d_mixed16, mask, rope)
-
+    out_whole, h_one, h_two, qkv16, act16, slope, vec_rel, last = front(
+        scalars, normed, pieces, rope
+    )
     block16 = ((tok_count, D), bf16)
     block32 = ((tok_count, D), f32)
-    size = 2 * seq_len * D
-    out_own, *out_sent = single(
+    half = D // 2
+    dy_seq, d_mixed16, d_up16, up_sum = single(
+        hidden_body,
+        [((seq_len, D), bf16), ((seq_len, OUT), bf16), ((seq_len, UP), bf16), ((8, UP), f32)],
+        scalars,
+        [dy_all, *downs, slope, out_whole],
+        4,
+        "hidden",
+    )
+
+    def split_terms(left, right):
+        sent = contract_rows(left[:, half:], right).astype(bf16).reshape(4, LANES, D)
+        got = hop(sent, "rep", N_REP, 1)
+        keep = contract_rows(left[:, :half], right).reshape(4, LANES, D)
+        return keep, got
+
+    down_keep, down_got = split_terms(act16, dy_seq)
+    up_keep, up_got = split_terms(h_two, d_up16)
+    down_parts = sum_rep(down_keep, down_got)
+    up_parts = sum_rep(up_keep, up_got, *down_parts[1:])
+    mixed16 = mix_heads(after(qkv16, down_got, up_got), mask)
+    (branches,) = single(
         branch_body,
-        [block32, block16, block16, block16],
+        [((seq_len, D), bf16)],
         scalars,
-        [mixed16, act16, out_whole, last, block_in, *downs],
-        size * (OUT + UP),
+        [mixed16, act16, out_whole, *downs],
+        3,
         "branch",
     )
+    d_mixed16 = after(d_mixed16, branches, *down_parts[1:])
+    branches = lax.psum_scatter(branches, "shard", scatter_dimension=0, tiled=True)
+    d_qkv16, qkv_sum = attend_back(qkv16, d_mixed16, mixed16, mask, rope)
+    d_qkv16 = after(d_qkv16, *up_parts[1:])
+
     e_own, *e_sent, norm_sum = single(
         back_body,
         [block32, block16, block16, block16, ((8, D), f32)],
         scalars,
         [d_qkv16, d_up16, vec_rel, *normed, *pieces],
-        size * (QKV + UP),
+        5,
         "back",
     )
-    out_got = to_shards(out_sent)
     e_got = to_shards(e_sent)
     cot_sum = jnp.sum(cotangent, axis=0, keepdims=True)
     wide = QKV + OUT + LANES
@@ -1028,24 +1055,25 @@
         [((half, wide), f32), ((half, wide), bf16)],
         scalars,
         [h_one, d_qkv16, mixed16, dy_seq, norm_sum, qkv_sum, up_sum, cot_sum],
-        size * (QKV + OUT),
+        4,
         "terms",
         [pltpu.VMEM((LANES, D), f32), pltpu.VMEM((OUT, D), f32)],
     )
-    qkv_parts = sum_rep(qkv_keep.reshape(4, LANES, wide), qkv_sent.reshape(4, LANES, wide))
+    qkv_got = hop(qkv_sent.reshape(4, LANES, wide), "rep", N_REP, 1)
+    qkv_parts = sum_rep(qkv_keep.reshape(4, LANES, wide), qkv_got, *up_parts[1:])
     narrow = (rows, QKV + UP + LANES)
     g_own, g1, g2, g3, out_sum = single(
         fold_body,
         [(narrow, f32), (narrow, bf16), (narrow, bf16), (narrow, bf16), ((rows, D), f32)],
         scalars,
         [*up_parts, *qkv_parts],
-        0,
+        1,
         "fold",
         [pltpu.VMEM((LANES, UP), f32), pltpu.VMEM((LANES, wide), f32)],
     )
     g_got = to_shards([g1, g2, g3])
     grad_out = lax.ppermute(out_sum, ("rep", "shard"), [(b, a) for a, b in moves])
-    block_out = out_own + out_got[0].astype(f32) + out_got[1].astype(f32) + out_got[2].astype(f32)
+    block_out = block_in + branches.astype(f32) + last[0]
     grad_down = (
         down_parts[0]
         + down_parts[1].astype(f32)
@@ -1057,12 +1085,13 @@
         [block32],
         scalars,
         [e_own, *e_got, block_in, cotangent],
-        0,
+        2,
         "finish",
         [pltpu.VMEM((tok_count, D), f32)],
     )
     qkv_shape = (qkv_weight.shape, f32)
     up_shape = (up_weight.shape, f32)
+    vec_shape = (vectors.shape, f32)
     (
         grad_qkv,
         new_qkv,
@@ -1072,26 +1101,37 @@
         new_up,
         new_first_up,
         new_second_up,
-        vec_sum,
+        grad_vec,
+        new_vec,
+        new_first_vec,
+        new_second_vec,
     ) = single(
         adam_body,
-        [qkv_shape] * 4 + [up_shape] * 4 + [((rows, LANES), f32)],
+        [qkv_shape] * 4 + [up_shape] * 4 + [vec_shape] * 4,
         scalars,
-        [g_own, *g_got, qkv_weight, first_qkv, second_qkv, up_weight, first_up, second_up],
-        0,
+        [
+            g_own,
+            *g_got,
+            qkv_weight,
+            first_qkv,
+            second_qkv,
+            up_weight,
+            first_up,
+            second_up,
+            vectors,
+            first_vec,
+            second_vec,
+        ],
+        3,
         "adam",
-        [pltpu.VMEM((N_SHARD,) + narrow, f32)],
-    )
-    grad_vec = vec_sum[:, :n_vec].T
+        [pltpu.VMEM((N_SHARD,) + narrow, f32), square],
+    )
 
     new_out, new_first_out, new_second_out = adam_update(
         out_weight, grad_out, first_out, second_out, LR_MATRIX, WEIGHT_DECAY
     )
     new_down, new_first_down, new_second_down = adam_update(
         down_weight, grad_down, first_down, second_down, LR_MATRIX, WEIGHT_DECAY
-    )
-    new_vec, new_first_vec, new_second_vec = adam_update(
-        vectors, grad_vec, first_vec, second_vec, LR_VECTOR, 0.0
     )
     return (
         block_out,

time: 248 us -> 252 us (1.016)
  waiting for transfers between devices: 98.3 us -> 54.6 us
  local copies, waits for them, and re-layouts: 19.3 us -> 34.5 us
  between operations: 12 us -> 25.4 us
  starting transfers between devices: 58.2 us -> 66.9 us
  Pallas kernels: 44 us -> 51.2 us
  other arithmetic: 9.94 us -> 13.1 us
    ppermute x44 -> x38, waiting for transfers between devices: 98.3 us -> 54.6 us  [hop(): return lax.ppermute(value, axis, [(i, i ^ mask) for i in range(size)])]
    unnamed x150 -> x197, local copies, waits for them, and re-layouts: 16.1 us -> 32 us
    pallas_call x9 -> x10, Pallas kernels: 19.2 us -> 26.9 us  [single(): pl.pallas_call(body, out_shape=shapes, grid_spec=pltpu.PrefetchScalarGrid...]
    ppermute x44 -> x38, starting transfers between devices: 56.7 us -> 64 us  [hop(): return lax.ppermute(value, axis, [(i, i ^ mask) for i in range(size)])]
    add x1 -> x2, other arithmetic: 0.93 us -> 4.1 us  [the longest x1 2.29 us: sum_rep(): parts = [keep[k] + got[k].astype(f32) for k in range(4)]]
  transfers between devices with their start and end apart: 46 -> 42, of which waited for: 9 -> 10; matrix products, arithmetic and copies ran while one was open for 7% -> 6% of each run, Pallas kernels for 16% -> 15%
where the time goes in v4:
time: 252 us; the launch traced here: 250 us
  starting transfers between devices  66.9 us (27%)
  waiting for transfers between devices  54.6 us (22%)
  Pallas kernels  51.2 us (20%)
  local copies, waits for them, and re-layouts  34.5 us (14%)
  between operations  25.4 us (10%)
  other arithmetic  13.1 us (5%)
  matrix products  4.34 us (2%)
    ppermute x38, starting transfers between devices, hop(): return lax.ppermute(value, axis, [(i, i ^ mask) for i in range(size)])  64 us
    ppermute x38, waiting for transfers between devices, hop(): return lax.ppermute(value, axis, [(i, i ^ mask) for i in range(size)])  54.6 us
    unnamed x197, local copies, waits for them, and re-layouts  32 us
    pallas_call x10, Pallas kernels, single(): pl.pallas_call(body, out_shape=shapes, grid_spec=pltpu.PrefetchScalarGrid...  26.9 us
    pallas_call x1, Pallas kernels, attend_back(): pl.pallas_call(attend_body, out_shape=(jax.ShapeDtypeStruct((tokens, QKV)...  9.09 us
    pallas_call x1, Pallas kernels, front(): pl.pallas_call(front_body, out_shape=tuple((jax.ShapeDtypeStruct(s, d) fo...  9.09 us
    pallas_call x1, Pallas kernels, mix_heads(): pl.pallas_call(mix_body, out_shape=jax.ShapeDtypeStruct((tokens, OUT), bf...  6.06 us
  transfers between devices with their start and end apart: 42, of which 10 were waited for; matrix products, arithmetic and copies ran while one was open for 6% of the time, Pallas kernels for 15%

profile of v4, /device:TPU:0, one launch (start us, length us, event | category | flops | bytes accessed | tf_op | source)
XLA Modules:
  0.0 250.1 jit_solution(15730422290882545490)
XLA Ops:
  11.5 3.1 %collective-permute-start = (bf16[32,1920]{1,0:T(8,128)(2,1)S(1)}, bf16[32,1920]{1,0:T(8,128)(2,1)S(1)}, u32[]{:S(2)}, u32[]{:S(2)}) collective-permute-start(bf16[32,1920]{1,0:T(8,128)(2,1)S(1)} %get-tuple-element.78), channel_id=1, source_target_pairs={{0,1},{1,0},{2,3},{3,2},{4,5},{5,4},{6,7},{7,6},{8,9},{9,8},{10,11... | collective-permute-start | bytes 368648 | tf_op jit(solution)/shard_map/ppermute | solution.py:132
  15.3 5.4 %collective-permute-start.7 = (bf16[128,1024]{1,0:T(8,128)(2,1)S(1)}, bf16[128,1024]{1,0:T(8,128)(2,1)}, u32[]{:S(2)}, u32[]{:S(2)}) collective-permute-start(bf16[128,1024]{1,0:T(8,128)(2,1)S(1)} %convert_element_type.127.refs_1_.refs_0_), channel_id=1, source_target_pairs={{0,8},{4,12},{8,0},{12,4},{16,24},{20,28},{24,16},{28,20},{1,9},{5... | collective-permute-start | bytes 786440 | tf_op jit(solution)/shard_map/ppermute | solution.py:132
  22.2 4.8 %collective-permute-start.2 = (bf16[32,1920]{1,0:T(8,128)(2,1)S(1)}, bf16[32,1920]{1,0:T(8,128)(2,1)S(1)}, u32[]{:S(2)}, u32[]{:S(2)}) collective-permute-start(bf16[32,1920]{1,0:T(8,128)(2,1)S(1)} %get-tuple-element.80), channel_id=1, source_target_pairs={{0,3},{1,2},{2,1},{3,0},{4,7},{5,6},{6,5},{7,4},{8,11},{9,10},{10,... | collective-permute-start | bytes 368648 | tf_op jit(solution)/shard_map/ppermute | solution.py:132
  28.5 1.9 collective-permute-done.2.refs_3_
  30.4 5.5 %collective-permute-done.1.refs_2_ = bf16[32,1920]{1,0:T(8,128)(2,1)S(1)} collective-permute-done((bf16[32,1920]{1,0:T(8,128)(2,1)S(1)}, bf16[32,1920]{1,0:T(8,128)(2,1)S(1)}, u32[]{:S(2)}, u32[]{:S(2)}) %collective-permute-start.1) | collective-permute-done | bytes 122912 | tf_op jit(solution)/shard_map/ppermute | solution.py:132
  40.1 3.2 %collective-permute-start.4 = (bf16[128,1024]{1,0:T(8,128)(2,1)}, bf16[128,1024]{1,0:T(8,128)(2,1)S(1)}, u32[]{:S(2)}, u32[]{:S(2)}) collective-permute-start(bf16[128,1024]{1,0:T(8,128)(2,1)} %norm.1.refs_0_), channel_id=1, source_target_pairs={{0,2},{1,3},{2,0},{3,1},{4,6},{5,7},{6,4},{7,5},{8,10},{9,11},{10,... | collective-permute-start | bytes 786440 | tf_op jit(solution)/shard_map/ppermute | solution.py:132
  53.8 1.9 collective-permute-done.4.refs_2_
  56.2 7.4 %collective-permute-done.10.refs_6_.refs_14_.refs_22_ = bf16[128,2176]{1,0:T(8,128)(2,1)S(1)} collective-permute-done((bf16[128,2176]{1,0:T(8,128)(2,1)S(1)}, bf16[128,2176]{1,0:T(8,128)(2,1)S(1)}, u32[]{:S(2)}, u32[]{:S(2)}) %collective-permute-start.10) | collective-permute-done | bytes 557088 | tf_op jit(solution)/shard_map/ppermute | solution.py:132
  65.5 2.8 %collective-permute-done.5.refs_3_ = bf16[128,1024]{1,0:T(8,128)(2,1)S(1)} collective-permute-done((bf16[128,1024]{1,0:T(8,128)(2,1)}, bf16[128,1024]{1,0:T(8,128)(2,1)S(1)}, u32[]{:S(2)}, u32[]{:S(2)}) %collective-permute-start.5) | collective-permute-done | bytes 262176 | tf_op jit(solution)/shard_map/ppermute | solution.py:132
  72.8 3.7 %collective-permute-done.16.refs_4_.refs_3_ = bf16[128,1024]{1,0:T(8,128)(2,1)} collective-permute-done((bf16[128,1024]{1,0:T(8,128)(2,1)S(1)}, bf16[128,1024]{1,0:T(8,128)(2,1)}, u32[]{:S(2)}, u32[]{:S(2)}) %collective-permute-start.16) | collective-permute-done | bytes 262176 | tf_op jit(solution)/shard_map/ppermute | solution.py:132
  82.0 9.1 %front.1 = (bf16[256,1024]{1,0:T(8,128)(2,1)S(1)}, bf16[512,1024]{1,0:T(8,128)(2,1)S(1)}, bf16[512,1024]{1,0:T(8,128)(2,1)S(1)}, bf16[512,768]{1,0:T(8,128)(2,1)...) custom-call(s32[21]{0:T(128)S(1)} %pad_add_fusion.1.s_ref, ...), custom_call_target="tpu_custom_call" | custom-call | flops 10350000128 | bytes 1048576 | tf_op jit(solution)/shard_map/front/pallas_call | solution.py:599
  105.2 5.0 %hidden.1 = (bf16[512,1024]{1,0:T(8,128)(2,1)S(1)}, bf16[512,256]{1,0:T(8,128)(2,1)S(1)}, bf16[512,1024]{1,0:T(8,128)(2,1)S(1)}, f32[8,1024]{1,0:T(8,128)S(1)}) custom-call(s32[21]{0:T(128)S(1)} %pad_add_fusion.1.s_ref, bf16[512,1024]{1,0:T(8,128)(2,1)S(1)} %copy-done.11, bf16[128,1024]{1,0:T(8,128)(2,1)S(1)} %convert_element_type.127.refs_1_.refs_0_, ...), custom_call_target="tpu_custom_call" | custom-call | flops 4600000000 | bytes 1048576 | tf_op jit(solution)/shard_map/hidden/pallas_call | solution.py:438
  114.2 2.1 fusion.13
  118.9 2.0 collective-permute-start.25
  120.9 6.1 %mix_heads.1.mix_ref = bf16[512,256]{1,0:T(8,128)(2,1)S(1)} custom-call(bf16[512,768]{1,0:T(8,128)(2,1)S(1)} %copy-done.82, bf16[512,768]{1,0:T(8,128)(2,1)S(1)} %copy-done.82, bf16[512,768]{1,0:T(8,128)(2,1)S(1)} %copy-done.82, f32[512,512]{1,0:T(8,128)S(1)} %and_select_fusion.mask_ref), custom_call_target="tpu_custom_call" | custom-call | flops 6899999744 | bytes 1048576 | tf_op jit(solution)/shard_map/mix_heads/pallas_call | solution.py:717
  127.0 4.2 %branch.1 = bf16[512,1024]{1,0:T(8,128)(2,1)} custom-call(s32[21]{0:T(128)S(1)} %pad_add_fusion.1.s_ref, bf16[512,256]{1,0:T(8,128)(2,1)S(1)} %mix_heads.1.mix_ref, bf16[512,1024]{1,0:T(8,128)(2,1)S(1)} %copy-done.8, bf16[256,1024]{1,0:T(8,128)(2,1)S(1)} %copy-done.72, bf16[128,1024]{1,0:T(8,128)(2,1)S(1)} %convert_element_type.127.refs_1_.refs_0_, ...), custom_call_target="tpu_custom_call" | custom-call | flops 3449999872 | bytes 1048576 | tf_op jit(solution)/shard_map/branch/pallas_call | solution.py:438
  131.9 2.3 slice_add_fusion.1
  135.9 2.0 collective-permute-start.28
  137.9 9.1 %attend_back.1 = (bf16[512,768]{1,0:T(8,128)(2,1)S(1)}, f32[1,768]{1,0:T(1,128)S(1)}) custom-call(bf16[512,768]{1,0:T(8,128)(2,1)S(1)} %copy-done.83, bf16[512,768]{1,0:T(8,128)(2,1)S(1)} %copy-done.83, bf16[512,768]{1,0:T(8,128)(2,1)S(1)} %copy-done.83, bf16[512,256]{1,0:T(8,128)(2,1)S(1)} %copy-done.80, bf16[512,256]{1,0:T(8,128)(2,1)S(1)} %copy-done.76, ...), custom_call_target="tpu_custom_call" | custom-call | flops 12650000384 | bytes 1048576 | tf_op jit(solution)/shard_map/attend_back/pallas_call | solution.py:732
  148.2 5.2 %back.1 = (f32[128,1024]{1,0:T(8,128)S(1)}, bf16[128,1024]{1,0:T(8,128)(2,1)S(1)}, bf16[128,1024]{1,0:T(8,128)(2,1)S(1)}, bf16[128,1024]{1,0:T(8,128)(2,1)S(1)}, f32[8,1024]{1,0:T(8,128)S(1)}) custom-call(s32[21]{0:T(128)S(1)} %pad_add_fusion.1.s_ref, bf16[512,768]{1,0:T(8,128)(2,1)} %copy-done.77, bf16[512,1024]{1,0:T(8,128)(2,1)} %copy-done, ...), custom_call_target="tpu_custom_call" | custom-call | flops 5750000128 | bytes 1048576 | tf_op jit(solution)/shard_map/back/pallas_call | solution.py:438
  153.5 3.3 %terms.1 = (f32[512,1152]{1,0:T(8,128)}, bf16[512,1152]{1,0:T(8,128)(2,1)S(1)}) custom-call(s32[21]{0:T(128)S(1)} %pad_add_fusion.1.s_ref, bf16[512,1024]{1,0:T(8,128)(2,1)S(1)} %copy-done.74, bf16[512,768]{1,0:T(8,128)(2,1)S(1)} %copy-done.78, bf16[512,256]{1,0:T(8,128)(2,1)S(1)} %copy-done.76, bf16[512,1024]{1,0:T(8,128)(2,1)S(1)} %get-tuple-element.91.dy_ref, ...), custom_call_target="tpu_custom_call" | custom-call | flops 4600000000 | bytes 1048576 | tf_op jit(solution)/shard_map/terms/pallas_call | solution.py:438
  156.9 12.5 %collective-permute-start.29 = (bf16[128,1024]{1,0:T(8,128)(2,1)}, bf16[128,1024]{1,0:T(8,128)(2,1)S(1)}, u32[]{:S(2)}, u32[]{:S(2)}) collective-permute-start(bf16[128,1024]{1,0:T(8,128)(2,1)} %copy-done.57), channel_id=1, source_target_pairs={{0,1},{1,0},{2,3},{3,2},{4,5},{5,4},{6,7},{7,6},{8,9},{9,8},{10,11... | collective-permute-start | bytes 786440 | tf_op jit(solution)/shard_map/ppermute | solution.py:132
  169.5 2.4 collective-permute-start.31
  171.9 2.3 fusion
  176.1 10.5 %collective-permute-done.29.r1_ref = bf16[128,1024]{1,0:T(8,128)(2,1)S(1)} collective-permute-done((bf16[128,1024]{1,0:T(8,128)(2,1)}, bf16[128,1024]{1,0:T(8,128)(2,1)S(1)}, u32[]{:S(2)}, u32[]{:S(2)}) %collective-permute-start.29) | collective-permute-done | bytes 262176 | tf_op jit(solution)/shard_map/ppermute | solution.py:132
  188.3 2.8 %multiply_subtract_fusion = (f32[128,1024]{1,0:T(8,128)}, f32[128,1024]{1,0:T(8,128)}, f32[128,1024]{1,0:T(8,128)}, f32[128,1024]{1,0:T(8,128)}) fusion(f32[128,1024]{1,0:T(8,128)S(1)} %copy-done.86, f32[128,1024]{1,0:T(8,128)S(1)} %copy-done.89, f32[128,1024]{1,0:T(8,128)S(1)} %copy-done.90, bf16[128,1024]{1,0:T(8,128)(2,1)} %collective-permute-done.25, ...), kind=kLoop, calls=%fused_computation.30 | loop fusion | flops 3014656 | bytes 5242880 | tf_op jit(solution)/shard_map/sub | solution.py:40
  191.1 12.6 %collective-permute-done.30.r2_ref = bf16[128,1024]{1,0:T(8,128)(2,1)S(1)} collective-permute-done((bf16[128,1024]{1,0:T(8,128)(2,1)}, bf16[128,1024]{1,0:T(8,128)(2,1)S(1)}, u32[]{:S(2)}, u32[]{:S(2)}) %collective-permute-start.30) | collective-permute-done | bytes 262176 | tf_op jit(solution)/shard_map/ppermute | solution.py:132
  208.3 9.6 %collective-permute-start.36 = (bf16[32,1920]{1,0:T(8,128)(2,1)}, bf16[32,1920]{1,0:T(8,128)(2,1)S(1)}, u32[]{:S(2)}, u32[]{:S(2)}) collective-permute-start(bf16[32,1920]{1,0:T(8,128)(2,1)} %get-tuple-element.118), channel_id=1, source_target_pairs={{0,1},{1,0},{2,3},{3,2},{4,5},{5,4},{6,7},{7,6},{8,9},{9,8},{10,11... | collective-permute-start | bytes 368648 | tf_op jit(solution)/shard_map/ppermute | solution.py:132
  217.9 2.4 collective-permute-start.38
  220.2 2.1 collective-permute-start.39
  224.2 7.9 %collective-permute-done.37.refs_2_ = bf16[32,1920]{1,0:T(8,128)(2,1)S(1)} collective-permute-done((bf16[32,1920]{1,0:T(8,128)(2,1)}, bf16[32,1920]{1,0:T(8,128)(2,1)S(1)}, u32[]{:S(2)}, u32[]{:S(2)}) %collective-permute-start.37) | collective-permute-done | bytes 122912 | tf_op jit(solution)/shard_map/ppermute | solution.py:132
  237.2 2.7 %adam.1 = (f32[32,3072]{1,0:T(8,128)}, f32[32,3072]{1,0:T(8,128)}, f32[32,3072]{1,0:T(8,128)}, f32[32,3072]{1,0:T(8,128)}, f32[32,4096]{1,0:T(8,128)}, /*index=5...) custom-call(s32[21]{0:T(128)S(1)} %pad_add_fusion.1.s_ref, ...), custom_call_target="tpu_custom_call" | custom-call | flops 3449999872 | bytes 1048576 | tf_op jit(solution)/shard_map/adam/pallas_call | solution.py:438
  (289 shorter events, 66.6 us)
Async XLA Ops:
  7.2 91.9 %all-gather.2.cloned.1.call-start = ((), (), s32[]{:S(2)}) async-start(), calls=%async_computation.1 | async-start | bytes 1310720 | tf_op jit(solution)/shard_map/all_gather | solution.py:990
  15.3 21.2 %collective-permute-start.7 = (bf16[128,1024]{1,0:T(8,128)(2,1)S(1)}, bf16[128,1024]{1,0:T(8,128)(2,1)}, u32[]{:S(2)}, u32[]{:S(2)}) collective-permute-start(bf16[128,1024]{1,0:T(8,128)(2,1)S(1)} %convert_element_type.127.refs_1_.refs_0_), channel_id=1, source_target_pairs={{0,8},{4,12},{8,0},{12,4},{16,24},{20,28},{24,16},{28,20},{1,9},{5... | collective-permute-start | bytes 786440 | tf_op jit(solution)/shard_map/ppermute | solution.py:132
  20.6 15.9 %collective-permute-start.8 = (bf16[128,1024]{1,0:T(8,128)(2,1)S(1)}, bf16[128,1024]{1,0:T(8,128)(2,1)}, u32[]{:S(2)}, u32[]{:S(2)}) collective-permute-start(bf16[128,1024]{1,0:T(8,128)(2,1)S(1)} %convert_element_type.127.refs_1_.refs_0_), channel_id=1, source_target_pairs={{0,16},{4,20},{8,24},{12,28},{16,0},{20,4},{24,8},{28,12},{1,17},{... | collective-permute-start | bytes 786440 | tf_op jit(solution)/shard_map/ppermute | solution.py:132
  36.5 19.2 %collective-permute-start.9 = (bf16[128,2176]{1,0:T(8,128)(2,1)S(1)}, bf16[128,2176]{1,0:T(8,128)(2,1)S(1)}, u32[]{:S(2)}, u32[]{:S(2)}) collective-permute-start(bf16[128,2176]{1,0:T(8,128)(2,1)S(1)} %join.1.refs_4_.refs_12_.refs_20_), channel_id=1, source_target_pairs={{0,8},{4,12},{8,0},{12,4},{16,24},{20,28},{24,16},{28,20},{1,9},{5... | collective-permute-start | bytes 1671176 | tf_op jit(solution)/shard_map/ppermute | solution.py:132
  38.2 25.5 %collective-permute-start.10 = (bf16[128,2176]{1,0:T(8,128)(2,1)S(1)}, bf16[128,2176]{1,0:T(8,128)(2,1)S(1)}, u32[]{:S(2)}, u32[]{:S(2)}) collective-permute-start(bf16[128,2176]{1,0:T(8,128)(2,1)S(1)} %join.1.refs_4_.refs_12_.refs_20_), channel_id=1, source_target_pairs={{0,16},{4,20},{8,24},{12,28},{16,0},{20,4},{24,8},{28,12},{1,17},{... | collective-permute-start | bytes 1671176 | tf_op jit(solution)/shard_map/ppermute | solution.py:132
  38.7 25.0 %collective-permute-start.11 = (bf16[128,2176]{1,0:T(8,128)(2,1)S(1)}, bf16[128,2176]{1,0:T(8,128)(2,1)S(1)}, u32[]{:S(2)}, u32[]{:S(2)}) collective-permute-start(bf16[128,2176]{1,0:T(8,128)(2,1)S(1)} %join.1.refs_4_.refs_12_.refs_20_), channel_id=1, source_target_pairs={{0,24},{4,28},{8,16},{12,20},{16,8},{20,12},{24,0},{28,4},{1,25},{... | collective-permute-start | bytes 1671176 | tf_op jit(solution)/shard_map/ppermute | solution.py:132
  40.1 15.6 %collective-permute-start.4 = (bf16[128,1024]{1,0:T(8,128)(2,1)}, bf16[128,1024]{1,0:T(8,128)(2,1)S(1)}, u32[]{:S(2)}, u32[]{:S(2)}) collective-permute-start(bf16[128,1024]{1,0:T(8,128)(2,1)} %norm.1.refs_0_), channel_id=1, source_target_pairs={{0,2},{1,3},{2,0},{3,1},{4,6},{5,7},{6,4},{7,5},{8,10},{9,11},{10,... | collective-permute-start | bytes 786440 | tf_op jit(solution)/shard_map/ppermute | solution.py:132
  44.1 178.3 %reduce-scatter.2.cloned.1.call-start = ((), (), s32[]{:S(2)}) async-start(), calls=%async_computation.2 | async-start | bytes 1310720 | tf_op jit(solution)/shard_map/reduce_scatter | solution.py:1038
  52.5 15.8 %collective-permute-start.5 = (bf16[128,1024]{1,0:T(8,128)(2,1)}, bf16[128,1024]{1,0:T(8,128)(2,1)S(1)}, u32[]{:S(2)}, u32[]{:S(2)}) collective-permute-start(bf16[128,1024]{1,0:T(8,128)(2,1)} %norm.1.refs_0_), channel_id=1, source_target_pairs={{0,3},{1,2},{2,1},{3,0},{4,7},{5,6},{6,5},{7,4},{8,11},{9,10},{10,... | collective-permute-start | bytes 786440 | tf_op jit(solution)/shard_map/ppermute | solution.py:132
  55.7 17.0 %collective-permute-start.12 = (bf16[128,2176]{1,0:T(8,128)(2,1)S(1)}, bf16[128,2176]{1,0:T(8,128)(2,1)}, u32[]{:S(2)}, u32[]{:S(2)}) collective-permute-start(bf16[128,2176]{1,0:T(8,128)(2,1)S(1)} %join.1.refs_4_.refs_12_.refs_20_), channel_id=1, source_target_pairs={{0,4},{4,0},{8,12},{12,8},{16,20},{20,16},{24,28},{28,24},{1,5},{5... | collective-permute-start | bytes 1671176 | tf_op jit(solution)/shard_map/ppermute | solution.py:132
  55.7 20.7 %collective-permute-start.13 = (bf16[128,2176]{1,0:T(8,128)(2,1)S(1)}, bf16[128,2176]{1,0:T(8,128)(2,1)}, u32[]{:S(2)}, u32[]{:S(2)}) collective-permute-start(bf16[128,2176]{1,0:T(8,128)(2,1)S(1)} %collective-permute-done.9.refs_5_.refs_13_.refs_21_), channel_id=1, source_target_pairs={{0,4},{4,0},{8,12},{12,8},{16,20},{20,16},{24,28},{28,24},{1,5},{5... | collective-permute-start | bytes 1671176 | tf_op jit(solution)/shard_map/ppermute | solution.py:132
  63.7 13.3 %collective-permute-start.14 = (bf16[128,2176]{1,0:T(8,128)(2,1)S(1)}, bf16[128,2176]{1,0:T(8,128)(2,1)}, u32[]{:S(2)}, u32[]{:S(2)}) collective-permute-start(bf16[128,2176]{1,0:T(8,128)(2,1)S(1)} %collective-permute-done.10.refs_6_.refs_14_.refs_22_), channel_id=1, source_target_pairs={{0,4},{4,0},{8,12},{12,8},{16,20},{20,16},{24,28},{28,24},{1,5},{5... | collective-permute-start | bytes 1671176 | tf_op jit(solution)/shard_map/ppermute | solution.py:132
  63.7 13.4 %collective-permute-start.15 = (bf16[128,2176]{1,0:T(8,128)(2,1)S(1)}, bf16[128,2176]{1,0:T(8,128)(2,1)}, u32[]{:S(2)}, u32[]{:S(2)}) collective-permute-start(bf16[128,2176]{1,0:T(8,128)(2,1)S(1)} %collective-permute-done.11.refs_7_.refs_15_.refs_23_), channel_id=1, source_target_pairs={{0,4},{4,0},{8,12},{12,8},{16,20},{20,16},{24,28},{28,24},{1,5},{5... | collective-permute-start | bytes 1671176 | tf_op jit(solution)/shard_map/ppermute | solution.py:132
  72.7 23.5 %collective-permute-start.17 = (bf16[128,1024]{1,0:T(8,128)(2,1)S(1)}, bf16[128,1024]{1,0:T(8,128)(2,1)S(1)}, u32[]{:S(2)}, u32[]{:S(2)}) collective-permute-start(bf16[128,1024]{1,0:T(8,128)(2,1)S(1)} %convert_element_type.127.refs_1_.refs_0_), channel_id=1, source_target_pairs={{0,4},{4,0},{8,12},{12,8},{16,20},{20,16},{24,28},{28,24},{1,5},{5... | collective-permute-start | bytes 786440 | tf_op jit(solution)/shard_map/ppermute | solution.py:132
  76.4 20.5 %collective-permute-start.18 = (bf16[128,1024]{1,0:T(8,128)(2,1)}, bf16[128,1024]{1,0:T(8,128)(2,1)S(1)}, u32[]{:S(2)}, u32[]{:S(2)}) collective-permute-start(bf16[128,1024]{1,0:T(8,128)(2,1)} %collective-permute-done.7.refs_2_.refs_1_), channel_id=1, source_target_pairs={{0,4},{4,0},{8,12},{12,8},{16,20},{20,16},{24,28},{28,24},{1,5},{5... | collective-permute-start | bytes 786440 | tf_op jit(solution)/shard_map/ppermute | solution.py:132
  76.4 21.2 %collective-permute-start.19 = (bf16[128,1024]{1,0:T(8,128)(2,1)}, bf16[128,1024]{1,0:T(8,128)(2,1)S(1)}, u32[]{:S(2)}, u32[]{:S(2)}) collective-permute-start(bf16[128,1024]{1,0:T(8,128)(2,1)} %collective-permute-done.8.refs_3_.refs_2_), channel_id=1, source_target_pairs={{0,4},{4,0},{8,12},{12,8},{16,20},{20,16},{24,28},{28,24},{1,5},{5... | collective-permute-start | bytes 786440 | tf_op jit(solution)/shard_map/ppermute | solution.py:132
  77.0 21.4 %collective-permute-start.20 = (bf16[128,1024]{1,0:T(8,128)(2,1)}, bf16[128,1024]{1,0:T(8,128)(2,1)S(1)}, u32[]{:S(2)}, u32[]{:S(2)}) collective-permute-start(bf16[128,1024]{1,0:T(8,128)(2,1)} %collective-permute-done.16.refs_4_.refs_3_), channel_id=1, source_target_pairs={{0,4},{4,0},{8,12},{12,8},{16,20},{20,16},{24,28},{28,24},{1,5},{5... | collective-permute-start | bytes 786440 | tf_op jit(solution)/shard_map/ppermute | solution.py:132
  117.3 16.8 %collective-permute-start.23 = (bf16[128,1024]{1,0:T(8,128)(2,1)}, bf16[128,1024]{1,0:T(8,128)(2,1)S(1)}, u32[]{:S(2)}, u32[]{:S(2)}) collective-permute-start(bf16[128,1024]{1,0:T(8,128)(2,1)} %get-tuple-element.151), channel_id=1, source_target_pairs={{0,8},{4,12},{8,0},{12,4},{16,24},{20,28},{24,16},{28,20},{1,9},{5... | collective-permute-start | bytes 786440 | tf_op jit(solution)/shard_map/ppermute | solution.py:132
  118.4 15.8 %collective-permute-start.24 = (bf16[128,1024]{1,0:T(8,128)(2,1)}, bf16[128,1024]{1,0:T(8,128)(2,1)}, u32[]{:S(2)}, u32[]{:S(2)}) collective-permute-start(bf16[128,1024]{1,0:T(8,128)(2,1)} %get-tuple-element.150), channel_id=1, source_target_pairs={{0,16},{4,20},{8,24},{12,28},{16,0},{20,4},{24,8},{28,12},{1,17},{... | collective-permute-start | bytes 786440 | tf_op jit(solution)/shard_map/ppermute | solution.py:132
  118.9 15.3 %collective-permute-start.25 = (bf16[128,1024]{1,0:T(8,128)(2,1)}, bf16[128,1024]{1,0:T(8,128)(2,1)}, u32[]{:S(2)}, u32[]{:S(2)}) collective-permute-start(bf16[128,1024]{1,0:T(8,128)(2,1)} %get-tuple-element.149), channel_id=1, source_target_pairs={{0,24},{4,28},{8,16},{12,20},{16,8},{20,12},{24,0},{28,4},{1,25},{... | collective-permute-start | bytes 786440 | tf_op jit(solution)/shard_map/ppermute | solution.py:132
  134.2 13.7 %collective-permute-start.26 = (bf16[128,1024]{1,0:T(8,128)(2,1)S(1)}, bf16[128,1024]{1,0:T(8,128)(2,1)S(1)}, u32[]{:S(2)}, u32[]{:S(2)}) collective-permute-start(bf16[128,1024]{1,0:T(8,128)(2,1)S(1)} %get-tuple-element.99), channel_id=1, source_target_pairs={{0,8},{4,12},{8,0},{12,4},{16,24},{20,28},{24,16},{28,20},{1,9},{5... | collective-permute-start | bytes 786440 | tf_op jit(solution)/shard_map/ppermute | solution.py:132
  156.8 15.1 %collective-permute-start.32 = (bf16[4,128,1152]{2,1,0:T(8,128)(2,1)S(1)}, bf16[4,128,1152]{2,1,0:T(8,128)(2,1)}, u32[]{:S(2)}, u32[]{:S(2)}) collective-permute-start(bf16[4,128,1152]{2,1,0:T(8,128)(2,1)S(1)} %bitcast.96), channel_id=1, source_target_pairs={{0,4},{4,0},{8,12},{12,8},{16,20},{20,16},{24,28},{28,24},{1,5},{5... | collective-permute-start | bytes 3538952 | tf_op jit(solution)/shard_map/ppermute | solution.py:132
  156.9 29.7 %collective-permute-start.29 = (bf16[128,1024]{1,0:T(8,128)(2,1)}, bf16[128,1024]{1,0:T(8,128)(2,1)S(1)}, u32[]{:S(2)}, u32[]{:S(2)}) collective-permute-start(bf16[128,1024]{1,0:T(8,128)(2,1)} %copy-done.57), channel_id=1, source_target_pairs={{0,1},{1,0},{2,3},{3,2},{4,5},{5,4},{6,7},{7,6},{8,9},{9,8},{10,11... | collective-permute-start | bytes 786440 | tf_op jit(solution)/shard_map/ppermute | solution.py:132
  169.5 34.2 %collective-permute-start.30 = (bf16[128,1024]{1,0:T(8,128)(2,1)}, bf16[128,1024]{1,0:T(8,128)(2,1)S(1)}, u32[]{:S(2)}, u32[]{:S(2)}) collective-permute-start(bf16[128,1024]{1,0:T(8,128)(2,1)} %copy-done.56), channel_id=1, source_target_pairs={{0,2},{1,3},{2,0},{3,1},{4,6},{5,7},{6,4},{7,5},{8,10},{9,11},{10,... | collective-permute-start | bytes 786440 | tf_op jit(solution)/shard_map/ppermute | solution.py:132
  169.5 34.2 %collective-permute-start.31 = (bf16[128,1024]{1,0:T(8,128)(2,1)S(1)}, bf16[128,1024]{1,0:T(8,128)(2,1)S(1)}, u32[]{:S(2)}, u32[]{:S(2)}) collective-permute-start(bf16[128,1024]{1,0:T(8,128)(2,1)S(1)} %get-tuple-element.107), channel_id=1, source_target_pairs={{0,3},{1,2},{2,1},{3,0},{4,7},{5,6},{6,5},{7,4},{8,11},{9,10},{10,... | collective-permute-start | bytes 786440 | tf_op jit(solution)/shard_map/ppermute | solution.py:132
  174.2 31.5 %collective-permute-start.33 = (bf16[128,1152]{1,0:T(8,128)(2,1)S(1)}, bf16[128,1152]{1,0:T(8,128)(2,1)S(1)}, u32[]{:S(2)}, u32[]{:S(2)}) collective-permute-start(bf16[128,1152]{1,0:T(8,128)(2,1)S(1)} %get-tuple-element.114), channel_id=1, source_target_pairs={{0,8},{4,12},{8,0},{12,4},{16,24},{20,28},{24,16},{28,20},{1,9},{5... | collective-permute-start | bytes 884744 | tf_op jit(solution)/shard_map/ppermute | solution.py:132
  175.3 30.4 %collective-permute-start.34 = (bf16[128,1152]{1,0:T(8,128)(2,1)S(1)}, bf16[128,1152]{1,0:T(8,128)(2,1)S(1)}, u32[]{:S(2)}, u32[]{:S(2)}) collective-permute-start(bf16[128,1152]{1,0:T(8,128)(2,1)S(1)} %get-tuple-element.115), channel_id=1, source_target_pairs={{0,16},{4,20},{8,24},{12,28},{16,0},{20,4},{24,8},{28,12},{1,17},{... | collective-permute-start | bytes 884744 | tf_op jit(solution)/shard_map/ppermute | solution.py:132
  186.6 19.1 %collective-permute-start.35 = (bf16[128,1152]{1,0:T(8,128)(2,1)S(1)}, bf16[128,1152]{1,0:T(8,128)(2,1)S(1)}, u32[]{:S(2)}, u32[]{:S(2)}) collective-permute-start(bf16[128,1152]{1,0:T(8,128)(2,1)S(1)} %get-tuple-element.116), channel_id=1, source_target_pairs={{0,24},{4,28},{8,16},{12,20},{16,8},{20,12},{24,0},{28,4},{1,25},{... | collective-permute-start | bytes 884744 | tf_op jit(solution)/shard_map/ppermute | solution.py:132
  208.3 15.9 %collective-permute-start.36 = (bf16[32,1920]{1,0:T(8,128)(2,1)}, bf16[32,1920]{1,0:T(8,128)(2,1)S(1)}, u32[]{:S(2)}, u32[]{:S(2)}) collective-permute-start(bf16[32,1920]{1,0:T(8,128)(2,1)} %get-tuple-element.118), channel_id=1, source_target_pairs={{0,1},{1,0},{2,3},{3,2},{4,5},{5,4},{6,7},{7,6},{8,9},{9,8},{10,11... | collective-permute-start | bytes 368648 | tf_op jit(solution)/shard_map/ppermute | solution.py:132
  217.9 14.2 %collective-permute-start.37 = (bf16[32,1920]{1,0:T(8,128)(2,1)}, bf16[32,1920]{1,0:T(8,128)(2,1)S(1)}, u32[]{:S(2)}, u32[]{:S(2)}) collective-permute-start(bf16[32,1920]{1,0:T(8,128)(2,1)} %get-tuple-element.119), channel_id=1, source_target_pairs={{0,2},{1,3},{2,0},{3,1},{4,6},{5,7},{6,4},{7,5},{8,10},{9,11},{10,... | collective-permute-start | bytes 368648 | tf_op jit(solution)/shard_map/ppermute | solution.py:132
  217.9 14.9 %collective-permute-start.38 = (bf16[32,1920]{1,0:T(8,128)(2,1)}, bf16[32,1920]{1,0:T(8,128)(2,1)S(1)}, u32[]{:S(2)}, u32[]{:S(2)}) collective-permute-start(bf16[32,1920]{1,0:T(8,128)(2,1)} %get-tuple-element.120), channel_id=1, source_target_pairs={{0,3},{1,2},{2,1},{3,0},{4,7},{5,6},{6,5},{7,4},{8,11},{9,10},{10,... | collective-permute-start | bytes 368648 | tf_op jit(solution)/shard_map/ppermute | solution.py:132
  220.2 19.7 %collective-permute-start.39 = (f32[32,1024]{1,0:T(8,128)}, f32[32,1024]{1,0:T(8,128)}, u32[]{:S(2)}, u32[]{:S(2)}) collective-permute-start(f32[32,1024]{1,0:T(8,128)} %get-tuple-element.122), channel_id=1, source_target_pairs={{0,0},{4,1},{8,2},{12,3},{1,4},{5,5},{9,6},{13,7},{2,8},{6,9},{10,... | collective-permute-start | bytes 393224 | tf_op jit(solution)/shard_map/ppermute | solution.py:1075
  (108 other events, 903.1 us)
Sparse Core Ops, SparseCore 0:
  44.2 37.6 all-gather.1
  157.1 52.1 reduce-scatter.1

commit v5 on v4

--- a/solution.py
+++ b/solution.py
@@ -433,7 +433,22 @@
     )
 
 
-def single(body, outs, prefetch, ins, micros, name, scratch=(), mib=48):
+ROOM = {
+    "pack": 6,
+    "norm": 4,
+    "join": 4,
+    "branch": 16,
+    "hidden": 22,
+    "back": 28,
+    "terms": 20,
+    "mlp": 28,
+    "fold": 16,
+    "finish": 10,
+    "adam": 22,
+}
+
+
+def single(body, outs, prefetch, ins, micros, name, scratch=()):
     shapes = tuple(jax.ShapeDtypeStruct(s, d) for s, d in outs)
     return pl.pallas_call(
         body,
@@ -445,7 +460,7 @@
             out_specs=tuple(whole_spec(s.shape) for s in shapes),
             scratch_shapes=list(scratch),
         ),
-        compiler_params=params(mib),
+        compiler_params=params(ROOM[name]),
         cost_estimate=cost(micros),
         name=name,
     )(prefetch, *ins)
@@ -610,7 +625,7 @@
             out_specs=tuple(specs),
             scratch_shapes=[pltpu.VMEM(((QKV + UP) // TILE, 8, TILE), f32)],
         ),
-        compiler_params=params(40),
+        compiler_params=params(24),
         cost_estimate=cost(9),
         name="front",
     )(scalars, *normed, *pieces, *pieces, *pieces, rope)
@@ -720,7 +735,7 @@
         grid=(pairs,),
         in_specs=[pair_spec(tokens, i * pairs) for i in range(3)] + [whole_spec(mask.shape)],
         out_specs=pair_spec(tokens, 0),
-        compiler_params=params(24),
+        compiler_params=params(10),
         cost_estimate=cost(6),
         name="mix_heads",
     )(qkv, qkv, qkv, mask)
@@ -740,8 +755,8 @@
         + [pair_spec(tokens, 0), pair_spec(tokens, 0), whole_spec(mask.shape), whole_spec(rope.shape)],
         out_specs=(whole_spec((tokens, QKV)), whole_spec((1, QKV))),
         scratch_shapes=[pltpu.VMEM((tokens, LANES), f32), pltpu.VMEM((tokens, LANES), f32)],
-        compiler_params=params(32),
-        cost_estimate=cost(11),
+        compiler_params=params(12),
+        cost_estimate=cost(4),
         name="attend_back",
     )(qkv, qkv, qkv, d_mix, mixed, mask, rope)
 
@@ -775,16 +790,17 @@
         sum_ref[3:4, cols] = sums[1]
 
 
-def branch_body(s_ref, mix_ref, act_ref, out_ref, *refs):
-    down_refs, total_ref = refs[:N_REP], refs[N_REP]
+def branch_body(s_ref, mix_ref, act_ref, out_ref, last_ref, x_ref, *refs):
+    down_refs, refs = refs[:N_REP], refs[N_REP:]
+    own_ref, sent_refs = refs[0], refs[1:]
+    rows = x_ref.shape[0]
     total = plain_dot(mix_ref[...], out_ref[...])
     for i in range(0, N_REP, 2):
         weights = jnp.concatenate([down_refs[i][...], down_refs[i + 1][...]], axis=0)
         total = total + plain_dot(act_ref[:, i * LANES : (i + 2) * LANES], weights)
-    rows = total.shape[0] // N_SHARD
-    for k in range(N_SHARD):
-        at = row_block(s_ref[NEAR + k], rows)
-        total_ref[at, :] = total[k * rows : (k + 1) * rows].astype(bf16)
+    own_ref[...] = x_ref[...] + total[:rows] + last_ref[0:1, :]
+    for k in range(1, N_SHARD):
+        sent_refs[k - 1][...] = total[k * rows : (k + 1) * rows].astype(bf16)
 
 
 def terms_body(
@@ -815,12 +831,20 @@
         ref[base : base + LANES, QKV + OUT :] = vec_ref[:, here].T.astype(ref.dtype)
 
 
+def mlp_body(s_ref, act_ref, dy_ref, h_ref, du_ref, keep_ref, sent_ref):
+    half = keep_ref.shape[0]
+    for left, right, at in ((act_ref, dy_ref, 0), (h_ref, du_ref, D)):
+        cols = slice(at, at + right.shape[1])
+        sent_ref[:, cols] = contract_rows(left[:, half:], right[...]).astype(bf16)
+        keep_ref[:, cols] = contract_rows(left[:, :half], right[...])
+
+
 def fold_body(s_ref, *refs):
     up_refs, refs = refs[:4], refs[4:]
     qkv_refs, refs = refs[:4], refs[4:]
     own_ref, sent_refs, out_ref, up_sum, qkv_sum = refs[0], refs[1:4], refs[4], refs[5], refs[6]
-    for some, total in ((up_refs, up_sum), (qkv_refs, qkv_sum)):
-        total[...] = some[0][...] + some[1][...].astype(f32) + some[2][...].astype(f32) + some[3][...].astype(f32)
+    for some, total, first in ((up_refs, up_sum, D), (qkv_refs, qkv_sum, 0)):
+        total[...] = sum(ref[:, first:].astype(f32) for ref in some)
     rows = own_ref.shape[0]
     for k in range(N_SHARD):
         at = row_block(s_ref[NEAR + k], rows)
@@ -881,6 +905,11 @@
 
 def to_shards(values):
     return [hop(values[k - 1], "shard", N_SHARD, k) for k in range(1, N_SHARD)]
+
+
+def to_shards_late(values):
+    got = [hop(values[k - 1], "shard", N_SHARD, k) for k in (1, 2)]
+    return got + [hop(after(values[2], got[0]), "shard", N_SHARD, 3)]
 
 
 def to_chips(values):
@@ -959,12 +988,6 @@
     got_cols = to_shards(packed[1:])
     out_rows = lax.ppermute(out_weight.astype(bf16), ("rep", "shard"), moves)
     down_own = down_weight.astype(bf16)
-    late_down = after(down_own, out_rows, got_cols[0])
-    downs = [
-        down_own,
-        hop(down_own, "rep", N_REP, 2),
-        hop(late_down, "rep", N_REP, 4),
-    ]
     (normed_own,) = single(
         norm_body,
         [((tok_count, D), bf16)],
@@ -982,11 +1005,10 @@
         1,
         "join",
     )
-    in_rows = after(in_rows, *downs[1:])
     normed = [normed_own] + to_shards([after(normed_own, *got_cols)] * 3)
     pieces = gather_chips(in_rows)
-    downs.append(hop(after(down_own, *pieces[1:4]), "rep", N_REP, 6))
-    downs = downs + [hop(piece, "rep", N_REP, 1) for piece in downs]
+    downs = gather_chips(after(down_own, *pieces[1:4]))
+    downs[0] = down_own
     dy_all = lax.all_gather(cotangent.astype(bf16), "shard", axis=0, tiled=True)
 
     rope_parts = jnp.asarray(rope_lanes(seq_len)).reshape(N_SHARD, tok_count, 3 * LANES)
@@ -1006,48 +1028,50 @@
     block16 = ((tok_count, D), bf16)
     block32 = ((tok_count, D), f32)
     half = D // 2
+    mixed16 = mix_heads(qkv16, mask)
+    out_own, *out_sent = single(
+        branch_body,
+        [block32, block16, block16, block16],
+        scalars,
+        [mixed16, act16, out_whole, last, block_in, *downs],
+        3,
+        "branch",
+    )
+    out_got = to_shards_late(out_sent)
+
     dy_seq, d_mixed16, d_up16, up_sum = single(
         hidden_body,
         [((seq_len, D), bf16), ((seq_len, OUT), bf16), ((seq_len, UP), bf16), ((8, UP), f32)],
         scalars,
-        [dy_all, *downs, slope, out_whole],
-        4,
+        [after(dy_all, out_own), *downs, slope, out_whole],
+        1,
         "hidden",
     )
 
-    def split_terms(left, right):
-        sent = contract_rows(left[:, half:], right).astype(bf16).reshape(4, LANES, D)
-        got = hop(sent, "rep", N_REP, 1)
-        keep = contract_rows(left[:, :half], right).reshape(4, LANES, D)
-        return keep, got
-
-    down_keep, down_got = split_terms(act16, dy_seq)
-    up_keep, up_got = split_terms(h_two, d_up16)
-    down_parts = sum_rep(down_keep, down_got)
-    up_parts = sum_rep(up_keep, up_got, *down_parts[1:])
-    mixed16 = mix_heads(after(qkv16, down_got, up_got), mask)
-    (branches,) = single(
-        branch_body,
-        [((seq_len, D), bf16)],
+    mlp_keep, mlp_sent = single(
+        mlp_body,
+        [((half, D + UP), f32), ((half, D + UP), bf16)],
         scalars,
-        [mixed16, act16, out_whole, *downs],
-        3,
-        "branch",
-    )
-    d_mixed16 = after(d_mixed16, branches, *down_parts[1:])
-    branches = lax.psum_scatter(branches, "shard", scatter_dimension=0, tiled=True)
+        [act16, dy_seq, h_two, d_up16],
+        1,
+        "mlp",
+    )
+    mlp_got = hop(mlp_sent.reshape(4, LANES, D + UP), "rep", N_REP, 1)
+    mlp_parts = sum_rep(mlp_keep.reshape(4, LANES, D + UP), mlp_got)
+    d_mixed16 = after(d_mixed16, mlp_got)
     d_qkv16, qkv_sum = attend_back(qkv16, d_mixed16, mixed16, mask, rope)
-    d_qkv16 = after(d_qkv16, *up_parts[1:])
+    d_qkv16 = after(d_qkv16, *out_got)
+    h_one = after(h_one, *mlp_parts[1:])
 
     e_own, *e_sent, norm_sum = single(
         back_body,
         [block32, block16, block16, block16, ((8, D), f32)],
         scalars,
         [d_qkv16, d_up16, vec_rel, *normed, *pieces],
-        5,
+        1,
         "back",
     )
-    e_got = to_shards(e_sent)
+    e_got = to_shards_late(e_sent)
     cot_sum = jnp.sum(cotangent, axis=0, keepdims=True)
     wide = QKV + OUT + LANES
     qkv_keep, qkv_sent = single(
@@ -1060,26 +1084,21 @@
         [pltpu.VMEM((LANES, D), f32), pltpu.VMEM((OUT, D), f32)],
     )
     qkv_got = hop(qkv_sent.reshape(4, LANES, wide), "rep", N_REP, 1)
-    qkv_parts = sum_rep(qkv_keep.reshape(4, LANES, wide), qkv_got, *up_parts[1:])
+    qkv_parts = sum_rep(qkv_keep.reshape(4, LANES, wide), qkv_got, *mlp_parts[1:])
     narrow = (rows, QKV + UP + LANES)
     g_own, g1, g2, g3, out_sum = single(
         fold_body,
         [(narrow, f32), (narrow, bf16), (narrow, bf16), (narrow, bf16), ((rows, D), f32)],
         scalars,
-        [*up_parts, *qkv_parts],
+        [*mlp_parts, *qkv_parts],
         1,
         "fold",
         [pltpu.VMEM((LANES, UP), f32), pltpu.VMEM((LANES, wide), f32)],
     )
     g_got = to_shards([g1, g2, g3])
     grad_out = lax.ppermute(out_sum, ("rep", "shard"), [(b, a) for a, b in moves])
-    block_out = block_in + branches.astype(f32) + last[0]
-    grad_down = (
-        down_parts[0]
-        + down_parts[1].astype(f32)
-        + down_parts[2].astype(f32)
-        + down_parts[3].astype(f32)
-    )
+    block_out = out_own + out_got[0].astype(f32) + out_got[1].astype(f32) + out_got[2].astype(f32)
+    grad_down = sum(part[:, :D].astype(f32) for part in mlp_parts)
     (grad_input,) = single(
         finish_body,
         [block32],

time: 252 us -> 244 us (0.968)
  waiting for transfers between devices: 54.6 us -> 96.5 us
  starting transfers between devices: 66.9 us -> 44.6 us
  local copies, waits for them, and re-layouts: 34.5 us -> 24.7 us
  other arithmetic: 13.1 us -> 5.53 us
  Pallas kernels: 51.2 us -> 46 us
  matrix products: 4.34 us -> 0 us
    ppermute x38 -> x37, waiting for transfers between devices: 54.6 us -> 96.5 us  [hop(): return lax.ppermute(value, axis, [(i, i ^ mask) for i in range(size)])]
    ppermute x38 -> x37, starting transfers between devices: 64 us -> 43.2 us  [hop(): return lax.ppermute(value, axis, [(i, i ^ mask) for i in range(size)])]
    unnamed x197 -> x179, local copies, waits for them, and re-layouts: 32 us -> 22.2 us
    pallas_call x10 -> x11, Pallas kernels: 26.9 us -> 21.9 us  [single(): pl.pallas_call(body, out_shape=shapes, grid_spec=pltpu.PrefetchScalarGrid...]
    dot_general x4 -> x0, matrix products: 4.34 us -> none  [contract_rows(): lax.dot_general(left, right, (((0,), (0,)), ((), ())), preferred_element_...]
    add x2 -> x1, other arithmetic: 4.1 us -> 0.93 us  [shards(): out_own + out_got[0].astype(f32) + out_got[1].astype(f32)]
  transfers between devices with their start and end apart: 42 -> 40, of which waited for: 10 -> 16; matrix products, arithmetic and copies ran while one was open for 6% -> 3% of each run, Pallas kernels for 15% -> 15%
where the time goes in v5:
time: 244 us; the launch traced here: 243 us
  waiting for transfers between devices  96.5 us (40%)
  Pallas kernels  46 us (19%)
  starting transfers between devices  44.6 us (18%)
  between operations  25.4 us (10%)
  local copies, waits for them, and re-layouts  24.7 us (10%)
  other arithmetic  5.53 us (2%)
    ppermute x37, waiting for transfers between devices, hop(): return lax.ppermute(value, axis, [(i, i ^ mask) for i in range(size)])  96.5 us
    ppermute x37, starting transfers between devices, hop(): return lax.ppermute(value, axis, [(i, i ^ mask) for i in range(size)])  43.2 us
    unnamed x179, local copies, waits for them, and re-layouts  22.2 us
    pallas_call x11, Pallas kernels, single(): pl.pallas_call(body, out_shape=shapes, grid_spec=pltpu.PrefetchScalarGrid...  21.9 us
    pallas_call x1, Pallas kernels, attend_back(): pl.pallas_call(attend_body, out_shape=(jax.ShapeDtypeStruct((tokens, QKV)...  9.08 us
    pallas_call x1, Pallas kernels, front(): pl.pallas_call(front_body, out_shape=tuple((jax.ShapeDtypeStruct(s, d) fo...  8.94 us
    pallas_call x1, Pallas kernels, mix_heads(): pl.pallas_call(mix_body, out_shape=jax.ShapeDtypeStruct((tokens, OUT), bf...  6.07 us
  transfers between devices with their start and end apart: 40, of which 16 were waited for; matrix products, arithmetic and copies ran while one was open for 3% of the time, Pallas kernels for 15%

profile of v5, /device:TPU:0, one launch (start us, length us, event | category | flops | bytes accessed | tf_op | source)
XLA Modules:
  0.0 242.7 jit_solution(5045038320468098959)
XLA Ops:
  11.5 5.1 %collective-permute-start.2 = (bf16[32,1920]{1,0:T(8,128)(2,1)S(1)}, bf16[32,1920]{1,0:T(8,128)(2,1)S(1)}, u32[]{:S(2)}, u32[]{:S(2)}) collective-permute-start(bf16[32,1920]{1,0:T(8,128)(2,1)S(1)} %get-tuple-element.84), channel_id=1, source_target_pairs={{0,3},{1,2},{2,1},{3,0},{4,7},{5,6},{6,5},{7,4},{8,11},{9,10},{10,... | collective-permute-start | bytes 368648 | tf_op jit(solution)/shard_map/ppermute | solution.py:132
  18.8 2.0 collective-permute-done.2.refs_3_
  20.8 2.8 %collective-permute-done.refs_1_ = bf16[32,1920]{1,0:T(8,128)(2,1)S(1)} collective-permute-done((bf16[32,1920]{1,0:T(8,128)(2,1)S(1)}, bf16[32,1920]{1,0:T(8,128)(2,1)S(1)}, u32[]{:S(2)}, u32[]{:S(2)}) %collective-permute-start) | collective-permute-done | bytes 122912 | tf_op jit(solution)/shard_map/ppermute | solution.py:132
  23.6 5.4 %collective-permute-done.1.refs_2_ = bf16[32,1920]{1,0:T(8,128)(2,1)S(1)} collective-permute-done((bf16[32,1920]{1,0:T(8,128)(2,1)S(1)}, bf16[32,1920]{1,0:T(8,128)(2,1)S(1)}, u32[]{:S(2)}, u32[]{:S(2)}) %collective-permute-start.1) | collective-permute-done | bytes 122912 | tf_op jit(solution)/shard_map/ppermute | solution.py:132
  29.7 2.2 collective-permute-start.7
  46.5 2.3 collective-permute-start.4
  48.8 2.2 collective-permute-start.5
  51.0 3.0 %collective-permute-done.8.refs_6_.refs_14_.refs_22_ = bf16[128,2176]{1,0:T(8,128)(2,1)S(1)} collective-permute-done((bf16[128,2176]{1,0:T(8,128)(2,1)S(1)}, bf16[128,2176]{1,0:T(8,128)(2,1)S(1)}, u32[]{:S(2)}, u32[]{:S(2)}) %collective-permute-start.8) | collective-permute-done | bytes 557088 | tf_op jit(solution)/shard_map/ppermute | solution.py:132
  56.6 14.8 %collective-permute-done.3.refs_1_ = bf16[128,1024]{1,0:T(8,128)(2,1)S(1)} collective-permute-done((bf16[128,1024]{1,0:T(8,128)(2,1)S(1)}, bf16[128,1024]{1,0:T(8,128)(2,1)S(1)}, u32[]{:S(2)}, u32[]{:S(2)}) %collective-permute-start.3) | collective-permute-done | bytes 262176 | tf_op jit(solution)/shard_map/ppermute | solution.py:132
  72.1 7.8 %collective-permute-done.5.refs_3_ = bf16[128,1024]{1,0:T(8,128)(2,1)S(1)} collective-permute-done((bf16[128,1024]{1,0:T(8,128)(2,1)S(1)}, bf16[128,1024]{1,0:T(8,128)(2,1)S(1)}, u32[]{:S(2)}, u32[]{:S(2)}) %collective-permute-start.5) | collective-permute-done | bytes 262176 | tf_op jit(solution)/shard_map/ppermute | solution.py:132
  83.2 11.1 %collective-permute-done.15.refs_2_.refs_3_ = bf16[128,1024]{1,0:T(8,128)(2,1)S(1)} collective-permute-done((bf16[128,1024]{1,0:T(8,128)(2,1)S(1)}, bf16[128,1024]{1,0:T(8,128)(2,1)S(1)}, u32[]{:S(2)}, u32[]{:S(2)}) %collective-permute-start.15) | collective-permute-done | bytes 262176 | tf_op jit(solution)/shard_map/ppermute | solution.py:132
  98.6 8.9 %front.1 = (bf16[256,1024]{1,0:T(8,128)(2,1)S(1)}, bf16[512,1024]{1,0:T(8,128)(2,1)S(1)}, bf16[512,1024]{1,0:T(8,128)(2,1)S(1)}, bf16[512,768]{1,0:T(8,128)(2,1)...) custom-call(s32[21]{0:T(128)S(1)} %pad_add_fusion.1.s_ref, ...), custom_call_target="tpu_custom_call" | custom-call | flops 10350000128 | bytes 1048576 | tf_op jit(solution)/shard_map/front/pallas_call | solution.py:614
  107.6 6.1 %mix_heads.1.mix_ref = bf16[512,256]{1,0:T(8,128)(2,1)S(1)} custom-call(bf16[512,768]{1,0:T(8,128)(2,1)S(1)} %get-tuple-element.88.q_ref.k_ref.v_ref, bf16[512,768]{1,0:T(8,128)(2,1)S(1)} %get-tuple-element.88.q_ref.k_ref.v_ref, bf16[512,768]{1,0:T(8,128)(2,1)S(1)} %get-tuple-element.88.q_ref.k_ref.v_ref, f32[512,512]{1,0:T(8,128)S(1)} %and_select_fusion.mask_ref), custom_call_target="tpu_custom_call" | custom-call | flops 6899999744 | bytes 1048576 | tf_op jit(solution)/shard_map/mix_heads/pallas_call | solution.py:732
  113.9 2.1 branch.1
  131.3 3.2 %hidden.1 = (bf16[512,1024]{1,0:T(8,128)(2,1)S(1)}, bf16[512,256]{1,0:T(8,128)(2,1)S(1)}, bf16[512,1024]{1,0:T(8,128)(2,1)S(1)}, f32[8,1024]{1,0:T(8,128)S(1)}) custom-call(s32[21]{0:T(128)S(1)} %pad_add_fusion.1.s_ref, bf16[512,1024]{1,0:T(8,128)(2,1)S(1)} %copy-done, bf16[128,1024]{1,0:T(8,128)(2,1)S(1)} %convert_element_type.94.refs_0_.refs_1_, ...), custom_call_target="tpu_custom_call" | custom-call | flops 1150000000 | bytes 1048576 | tf_op jit(solution)/shard_map/hidden/pallas_call | solution.py:453
  134.5 2.9 %mlp.1 = (f32[512,2048]{1,0:T(8,128)S(1)}, bf16[512,2048]{1,0:T(8,128)(2,1)S(1)}) custom-call(s32[21]{0:T(128)S(1)} %pad_add_fusion.1.s_ref, bf16[512,1024]{1,0:T(8,128)(2,1)S(1)} %copy-done.73, bf16[512,1024]{1,0:T(8,128)(2,1)S(1)} %get-tuple-element.101.dy_ref, bf16[512,1024]{1,0:T(8,128)(2,1)S(1)} %copy-done.71, ...), custom_call_target="tpu_custom_call" | custom-call | flops 1150000000 | bytes 1048576 | tf_op jit(solution)/shard_map/mlp/pallas_call | solution.py:453
  137.7 5.4 %collective-permute-start.21 = (bf16[128,1024]{1,0:T(8,128)(2,1)S(1)}, bf16[128,1024]{1,0:T(8,128)(2,1)S(1)}, u32[]{:S(2)}, u32[]{:S(2)}) collective-permute-start(bf16[128,1024]{1,0:T(8,128)(2,1)S(1)} %copy-done.65), channel_id=1, source_target_pairs={{0,1},{1,0},{2,3},{3,2},{4,5},{5,4},{6,7},{7,6},{8,9},{9,8},{10,11... | collective-permute-start | bytes 786440 | tf_op jit(solution)/shard_map/ppermute | solution.py:132
  143.2 10.8 %collective-permute-done.21 = bf16[128,1024]{1,0:T(8,128)(2,1)S(1)} collective-permute-done((bf16[128,1024]{1,0:T(8,128)(2,1)S(1)}, bf16[128,1024]{1,0:T(8,128)(2,1)S(1)}, u32[]{:S(2)}, u32[]{:S(2)}) %collective-permute-start.21) | collective-permute-done | bytes 262176 | tf_op jit(solution)/shard_map/ppermute | solution.py:132
  154.0 2.6 %collective-permute-start.23 = (bf16[128,1024]{1,0:T(8,128)(2,1)S(1)}, bf16[128,1024]{1,0:T(8,128)(2,1)S(1)}, u32[]{:S(2)}, u32[]{:S(2)}) collective-permute-start(bf16[128,1024]{1,0:T(8,128)(2,1)S(1)} %copy-done.61), channel_id=1, source_target_pairs={{0,3},{1,2},{2,1},{3,0},{4,7},{5,6},{6,5},{7,4},{8,11},{9,10},{10,... | collective-permute-start | bytes 786440 | tf_op jit(solution)/shard_map/ppermute | solution.py:132
  161.1 9.1 %attend_back.1 = (bf16[512,768]{1,0:T(8,128)(2,1)S(1)}, f32[1,768]{1,0:T(1,128)S(1)}) custom-call(bf16[512,768]{1,0:T(8,128)(2,1)S(1)} %copy-done.77, bf16[512,768]{1,0:T(8,128)(2,1)S(1)} %copy-done.77, bf16[512,768]{1,0:T(8,128)(2,1)S(1)} %copy-done.77, bf16[512,256]{1,0:T(8,128)(2,1)S(1)} %get-tuple-element.105.dm_ref, bf16[512,256]{1,0:T(8,128)(2,1)S(1)} %copy-done.79, ...), custom_call_target="tpu_custom_call" | custom-call | flops 4600000000 | bytes 1048576 | tf_op jit(solution)/shard_map/attend_back/pallas_call | solution.py:747
  170.3 4.0 %back.1 = (f32[128,1024]{1,0:T(8,128)S(1)}, bf16[128,1024]{1,0:T(8,128)(2,1)S(1)}, bf16[128,1024]{1,0:T(8,128)(2,1)S(1)}, bf16[128,1024]{1,0:T(8,128)(2,1)S(1)}, f32[8,1024]{1,0:T(8,128)S(1)}) custom-call(s32[21]{0:T(128)S(1)} %pad_add_fusion.1.s_ref, bf16[512,768]{1,0:T(8,128)(2,1)S(1)} %get-tuple-element.107.dqkv_ref, ...), custom_call_target="tpu_custom_call" | custom-call | flops 1150000000 | bytes 1048576 | tf_op jit(solution)/shard_map/back/pallas_call | solution.py:453
  174.4 9.1 %collective-permute-done.29.refs_2_ = bf16[128,2048]{1,0:T(8,128)(2,1)S(1)} collective-permute-done((bf16[128,2048]{1,0:T(8,128)(2,1)S(1)}, bf16[128,2048]{1,0:T(8,128)(2,1)S(1)}, u32[]{:S(2)}, u32[]{:S(2)}) %collective-permute-start.29) | collective-permute-done | bytes 524320 | tf_op jit(solution)/shard_map/ppermute | solution.py:132
  183.4 1.9 terms.1
  188.3 9.2 %collective-permute-done.25.r1_ref = bf16[128,1024]{1,0:T(8,128)(2,1)S(1)} collective-permute-done((bf16[128,1024]{1,0:T(8,128)(2,1)S(1)}, bf16[128,1024]{1,0:T(8,128)(2,1)S(1)}, u32[]{:S(2)}, u32[]{:S(2)}) %collective-permute-start.25) | collective-permute-done | bytes 262176 | tf_op jit(solution)/shard_map/ppermute | solution.py:132
  197.5 2.4 collective-permute-start.27
  205.3 4.9 %collective-permute-done.32.refs_5_ = bf16[128,1152]{1,0:T(8,128)(2,1)S(1)} collective-permute-done((bf16[128,1152]{1,0:T(8,128)(2,1)S(1)}, bf16[128,1152]{1,0:T(8,128)(2,1)S(1)}, u32[]{:S(2)}, u32[]{:S(2)}) %collective-permute-start.32) | collective-permute-done | bytes 294944 | tf_op jit(solution)/shard_map/ppermute | solution.py:132
  211.1 4.7 %collective-permute-done.34.refs_7_ = bf16[128,1152]{1,0:T(8,128)(2,1)S(1)} collective-permute-done((bf16[128,1152]{1,0:T(8,128)(2,1)S(1)}, bf16[128,1152]{1,0:T(8,128)(2,1)S(1)}, u32[]{:S(2)}, u32[]{:S(2)}) %collective-permute-start.34) | collective-permute-done | bytes 294944 | tf_op jit(solution)/shard_map/ppermute | solution.py:132
  216.9 2.0 collective-permute-start.36
  218.9 2.4 collective-permute-start.37
  221.4 1.9 finish.1
  224.0 7.5 %collective-permute-done.36.refs_2_ = bf16[32,1920]{1,0:T(8,128)(2,1)S(1)} collective-permute-done((bf16[32,1920]{1,0:T(8,128)(2,1)S(1)}, bf16[32,1920]{1,0:T(8,128)(2,1)S(1)}, u32[]{:S(2)}, u32[]{:S(2)}) %collective-permute-start.36) | collective-permute-done | bytes 122912 | tf_op jit(solution)/shard_map/ppermute | solution.py:132
  231.6 2.8 %adam.1 = (f32[32,3072]{1,0:T(8,128)}, f32[32,3072]{1,0:T(8,128)}, f32[32,3072]{1,0:T(8,128)}, f32[32,3072]{1,0:T(8,128)}, f32[32,4096]{1,0:T(8,128)}, /*index=5...) custom-call(s32[21]{0:T(128)S(1)} %pad_add_fusion.1.s_ref, ...), custom_call_target="tpu_custom_call" | custom-call | flops 3449999872 | bytes 1048576 | tf_op jit(solution)/shard_map/adam/pallas_call | solution.py:453
  (261 shorter events, 54.7 us)
Async XLA Ops:
  7.2 115.2 %all-gather.2.cloned.1.call-start = ((), (), s32[]{:S(2)}) async-start(), calls=%async_computation | async-start | bytes 1310720 | tf_op jit(solution)/shard_map/all_gather | solution.py:1012
  16.6 12.5 %collective-permute-start.1 = (bf16[32,1920]{1,0:T(8,128)(2,1)S(1)}, bf16[32,1920]{1,0:T(8,128)(2,1)S(1)}, u32[]{:S(2)}, u32[]{:S(2)}) collective-permute-start(bf16[32,1920]{1,0:T(8,128)(2,1)S(1)} %get-tuple-element.83), channel_id=1, source_target_pairs={{0,2},{1,3},{2,0},{3,1},{4,6},{5,7},{6,4},{7,5},{8,10},{9,11},{10,... | collective-permute-start | bytes 368648 | tf_op jit(solution)/shard_map/ppermute | solution.py:132
  29.7 19.1 %collective-permute-start.7 = (bf16[128,2176]{1,0:T(8,128)(2,1)S(1)}, bf16[128,2176]{1,0:T(8,128)(2,1)S(1)}, u32[]{:S(2)}, u32[]{:S(2)}) collective-permute-start(bf16[128,2176]{1,0:T(8,128)(2,1)S(1)} %join.1.refs_4_.refs_12_.refs_20_), channel_id=1, source_target_pairs={{0,8},{4,12},{8,0},{12,4},{16,24},{20,28},{24,16},{28,20},{1,9},{5... | collective-permute-start | bytes 1671176 | tf_op jit(solution)/shard_map/ppermute | solution.py:132
  31.9 22.0 %collective-permute-start.8 = (bf16[128,2176]{1,0:T(8,128)(2,1)S(1)}, bf16[128,2176]{1,0:T(8,128)(2,1)S(1)}, u32[]{:S(2)}, u32[]{:S(2)}) collective-permute-start(bf16[128,2176]{1,0:T(8,128)(2,1)S(1)} %join.1.refs_4_.refs_12_.refs_20_), channel_id=1, source_target_pairs={{0,16},{4,20},{8,24},{12,28},{16,0},{20,4},{24,8},{28,12},{1,17},{... | collective-permute-start | bytes 1671176 | tf_op jit(solution)/shard_map/ppermute | solution.py:132
  33.4 22.3 %collective-permute-start.9 = (bf16[128,2176]{1,0:T(8,128)(2,1)S(1)}, bf16[128,2176]{1,0:T(8,128)(2,1)}, u32[]{:S(2)}, u32[]{:S(2)}) collective-permute-start(bf16[128,2176]{1,0:T(8,128)(2,1)S(1)} %join.1.refs_4_.refs_12_.refs_20_), channel_id=1, source_target_pairs={{0,24},{4,28},{8,16},{12,20},{16,8},{20,12},{24,0},{28,4},{1,25},{... | collective-permute-start | bytes 1671176 | tf_op jit(solution)/shard_map/ppermute | solution.py:132
  46.5 24.9 %collective-permute-start.3 = (bf16[128,1024]{1,0:T(8,128)(2,1)S(1)}, bf16[128,1024]{1,0:T(8,128)(2,1)S(1)}, u32[]{:S(2)}, u32[]{:S(2)}) collective-permute-start(bf16[128,1024]{1,0:T(8,128)(2,1)S(1)} %norm.1.refs_0_), channel_id=1, source_target_pairs={{0,1},{1,0},{2,3},{3,2},{4,5},{5,4},{6,7},{7,6},{8,9},{9,8},{10,11... | collective-permute-start | bytes 786440 | tf_op jit(solution)/shard_map/ppermute | solution.py:132
  46.5 25.6 %collective-permute-start.4 = (bf16[128,1024]{1,0:T(8,128)(2,1)S(1)}, bf16[128,1024]{1,0:T(8,128)(2,1)S(1)}, u32[]{:S(2)}, u32[]{:S(2)}) collective-permute-start(bf16[128,1024]{1,0:T(8,128)(2,1)S(1)} %norm.1.refs_0_), channel_id=1, source_target_pairs={{0,2},{1,3},{2,0},{3,1},{4,6},{5,7},{6,4},{7,5},{8,10},{9,11},{10,... | collective-permute-start | bytes 786440 | tf_op jit(solution)/shard_map/ppermute | solution.py:132
  48.8 31.1 %collective-permute-start.5 = (bf16[128,1024]{1,0:T(8,128)(2,1)S(1)}, bf16[128,1024]{1,0:T(8,128)(2,1)S(1)}, u32[]{:S(2)}, u32[]{:S(2)}) collective-permute-start(bf16[128,1024]{1,0:T(8,128)(2,1)S(1)} %norm.1.refs_0_), channel_id=1, source_target_pairs={{0,3},{1,2},{2,1},{3,0},{4,7},{5,6},{6,5},{7,4},{8,11},{9,10},{10,... | collective-permute-start | bytes 786440 | tf_op jit(solution)/shard_map/ppermute | solution.py:132
  53.9 26.2 %collective-permute-start.10 = (bf16[128,2176]{1,0:T(8,128)(2,1)S(1)}, bf16[128,2176]{1,0:T(8,128)(2,1)S(1)}, u32[]{:S(2)}, u32[]{:S(2)}) collective-permute-start(bf16[128,2176]{1,0:T(8,128)(2,1)S(1)} %join.1.refs_4_.refs_12_.refs_20_), channel_id=1, source_target_pairs={{0,4},{4,0},{8,12},{12,8},{16,20},{20,16},{24,28},{28,24},{1,5},{5... | collective-permute-start | bytes 1671176 | tf_op jit(solution)/shard_map/ppermute | solution.py:132
  55.7 25.9 %collective-permute-start.14 = (bf16[128,1024]{1,0:T(8,128)(2,1)S(1)}, bf16[128,1024]{1,0:T(8,128)(2,1)S(1)}, u32[]{:S(2)}, u32[]{:S(2)}) collective-permute-start(bf16[128,1024]{1,0:T(8,128)(2,1)S(1)} %convert_element_type.94.refs_0_.refs_1_), channel_id=1, source_target_pairs={{0,8},{4,12},{8,0},{12,4},{16,24},{20,28},{24,16},{28,20},{1,9},{5... | collective-permute-start | bytes 786440 | tf_op jit(solution)/shard_map/ppermute | solution.py:132
  71.4 23.4 %collective-permute-start.11 = (bf16[128,2176]{1,0:T(8,128)(2,1)S(1)}, bf16[128,2176]{1,0:T(8,128)(2,1)S(1)}, u32[]{:S(2)}, u32[]{:S(2)}) collective-permute-start(bf16[128,2176]{1,0:T(8,128)(2,1)S(1)} %collective-permute-done.7.refs_5_.refs_13_.refs_21_), channel_id=1, source_target_pairs={{0,4},{4,0},{8,12},{12,8},{16,20},{20,16},{24,28},{28,24},{1,5},{5... | collective-permute-start | bytes 1671176 | tf_op jit(solution)/shard_map/ppermute | solution.py:132
  72.1 22.8 %collective-permute-start.12 = (bf16[128,2176]{1,0:T(8,128)(2,1)S(1)}, bf16[128,2176]{1,0:T(8,128)(2,1)S(1)}, u32[]{:S(2)}, u32[]{:S(2)}) collective-permute-start(bf16[128,2176]{1,0:T(8,128)(2,1)S(1)} %collective-permute-done.8.refs_6_.refs_14_.refs_22_), channel_id=1, source_target_pairs={{0,4},{4,0},{8,12},{12,8},{16,20},{20,16},{24,28},{28,24},{1,5},{5... | collective-permute-start | bytes 1671176 | tf_op jit(solution)/shard_map/ppermute | solution.py:132
  79.9 15.5 %collective-permute-start.13 = (bf16[128,2176]{1,0:T(8,128)(2,1)}, bf16[128,2176]{1,0:T(8,128)(2,1)S(1)}, u32[]{:S(2)}, u32[]{:S(2)}) collective-permute-start(bf16[128,2176]{1,0:T(8,128)(2,1)} %collective-permute-done.9.refs_7_.refs_15_.refs_23_), channel_id=1, source_target_pairs={{0,4},{4,0},{8,12},{12,8},{16,20},{20,16},{24,28},{28,24},{1,5},{5... | collective-permute-start | bytes 1671176 | tf_op jit(solution)/shard_map/ppermute | solution.py:132
  80.1 14.2 %collective-permute-start.15 = (bf16[128,1024]{1,0:T(8,128)(2,1)S(1)}, bf16[128,1024]{1,0:T(8,128)(2,1)S(1)}, u32[]{:S(2)}, u32[]{:S(2)}) collective-permute-start(bf16[128,1024]{1,0:T(8,128)(2,1)S(1)} %convert_element_type.94.refs_0_.refs_1_), channel_id=1, source_target_pairs={{0,16},{4,20},{8,24},{12,28},{16,0},{20,4},{24,8},{28,12},{1,17},{... | collective-permute-start | bytes 786440 | tf_op jit(solution)/shard_map/ppermute | solution.py:132
  81.6 12.7 %collective-permute-start.16 = (bf16[128,1024]{1,0:T(8,128)(2,1)S(1)}, bf16[128,1024]{1,0:T(8,128)(2,1)S(1)}, u32[]{:S(2)}, u32[]{:S(2)}) collective-permute-start(bf16[128,1024]{1,0:T(8,128)(2,1)S(1)} %convert_element_type.94.refs_0_.refs_1_), channel_id=1, source_target_pairs={{0,24},{4,28},{8,16},{12,20},{16,8},{20,12},{24,0},{28,4},{1,25},{... | collective-permute-start | bytes 786440 | tf_op jit(solution)/shard_map/ppermute | solution.py:132
  94.3 19.4 %collective-permute-start.17 = (bf16[128,1024]{1,0:T(8,128)(2,1)S(1)}, bf16[128,1024]{1,0:T(8,128)(2,1)S(1)}, u32[]{:S(2)}, u32[]{:S(2)}) collective-permute-start(bf16[128,1024]{1,0:T(8,128)(2,1)S(1)} %convert_element_type.94.refs_0_.refs_1_), channel_id=1, source_target_pairs={{0,4},{4,0},{8,12},{12,8},{16,20},{20,16},{24,28},{28,24},{1,5},{5... | collective-permute-start | bytes 786440 | tf_op jit(solution)/shard_map/ppermute | solution.py:132
  94.3 19.4 %collective-permute-start.18 = (bf16[128,1024]{1,0:T(8,128)(2,1)S(1)}, bf16[128,1024]{1,0:T(8,128)(2,1)S(1)}, u32[]{:S(2)}, u32[]{:S(2)}) collective-permute-start(bf16[128,1024]{1,0:T(8,128)(2,1)S(1)} %collective-permute-done.14.refs_1_.refs_2_), channel_id=1, source_target_pairs={{0,4},{4,0},{8,12},{12,8},{16,20},{20,16},{24,28},{28,24},{1,5},{5... | collective-permute-start | bytes 786440 | tf_op jit(solution)/shard_map/ppermute | solution.py:132
  94.8 18.9 %collective-permute-start.19 = (bf16[128,1024]{1,0:T(8,128)(2,1)S(1)}, bf16[128,1024]{1,0:T(8,128)(2,1)S(1)}, u32[]{:S(2)}, u32[]{:S(2)}) collective-permute-start(bf16[128,1024]{1,0:T(8,128)(2,1)S(1)} %collective-permute-done.15.refs_2_.refs_3_), channel_id=1, source_target_pairs={{0,4},{4,0},{8,12},{12,8},{16,20},{20,16},{24,28},{28,24},{1,5},{5... | collective-permute-start | bytes 786440 | tf_op jit(solution)/shard_map/ppermute | solution.py:132
  94.9 18.8 %collective-permute-start.20 = (bf16[128,1024]{1,0:T(8,128)(2,1)S(1)}, bf16[128,1024]{1,0:T(8,128)(2,1)S(1)}, u32[]{:S(2)}, u32[]{:S(2)}) collective-permute-start(bf16[128,1024]{1,0:T(8,128)(2,1)S(1)} %collective-permute-done.16.refs_3_.refs_4_), channel_id=1, source_target_pairs={{0,4},{4,0},{8,12},{12,8},{16,20},{20,16},{24,28},{28,24},{1,5},{5... | collective-permute-start | bytes 786440 | tf_op jit(solution)/shard_map/ppermute | solution.py:132
  137.5 19.2 %collective-permute-start.24 = (bf16[4,128,2048]{2,1,0:T(8,128)(2,1)S(1)}, bf16[4,128,2048]{2,1,0:T(8,128)(2,1)S(1)}, u32[]{:S(2)}, u32[]{:S(2)}) collective-permute-start(bf16[4,128,2048]{2,1,0:T(8,128)(2,1)S(1)} %bitcast.69), channel_id=1, source_target_pairs={{0,4},{4,0},{8,12},{12,8},{16,20},{20,16},{24,28},{28,24},{1,5},{5... | collective-permute-start | bytes 6291464 | tf_op jit(solution)/shard_map/ppermute | solution.py:132
  137.7 16.3 %collective-permute-start.21 = (bf16[128,1024]{1,0:T(8,128)(2,1)S(1)}, bf16[128,1024]{1,0:T(8,128)(2,1)S(1)}, u32[]{:S(2)}, u32[]{:S(2)}) collective-permute-start(bf16[128,1024]{1,0:T(8,128)(2,1)S(1)} %copy-done.65), channel_id=1, source_target_pairs={{0,1},{1,0},{2,3},{3,2},{4,5},{5,4},{6,7},{7,6},{8,9},{9,8},{10,11... | collective-permute-start | bytes 786440 | tf_op jit(solution)/shard_map/ppermute | solution.py:132
  143.2 27.0 %collective-permute-start.22 = (bf16[128,1024]{1,0:T(8,128)(2,1)S(1)}, bf16[128,1024]{1,0:T(8,128)(2,1)S(1)}, u32[]{:S(2)}, u32[]{:S(2)}) collective-permute-start(bf16[128,1024]{1,0:T(8,128)(2,1)S(1)} %copy-done.63), channel_id=1, source_target_pairs={{0,2},{1,3},{2,0},{3,1},{4,6},{5,7},{6,4},{7,5},{8,10},{9,11},{10,... | collective-permute-start | bytes 786440 | tf_op jit(solution)/shard_map/ppermute | solution.py:132
  154.0 16.2 %collective-permute-start.23 = (bf16[128,1024]{1,0:T(8,128)(2,1)S(1)}, bf16[128,1024]{1,0:T(8,128)(2,1)S(1)}, u32[]{:S(2)}, u32[]{:S(2)}) collective-permute-start(bf16[128,1024]{1,0:T(8,128)(2,1)S(1)} %copy-done.61), channel_id=1, source_target_pairs={{0,3},{1,2},{2,1},{3,0},{4,7},{5,6},{6,5},{7,4},{8,11},{9,10},{10,... | collective-permute-start | bytes 786440 | tf_op jit(solution)/shard_map/ppermute | solution.py:132
  157.4 16.9 %collective-permute-start.28 = (bf16[128,2048]{1,0:T(8,128)(2,1)S(1)}, bf16[128,2048]{1,0:T(8,128)(2,1)S(1)}, u32[]{:S(2)}, u32[]{:S(2)}) collective-permute-start(bf16[128,2048]{1,0:T(8,128)(2,1)S(1)} %get-tuple-element.151), channel_id=1, source_target_pairs={{0,8},{4,12},{8,0},{12,4},{16,24},{20,28},{24,16},{28,20},{1,9},{5... | collective-permute-start | bytes 1572872 | tf_op jit(solution)/shard_map/ppermute | solution.py:132
  159.1 24.3 %collective-permute-start.29 = (bf16[128,2048]{1,0:T(8,128)(2,1)S(1)}, bf16[128,2048]{1,0:T(8,128)(2,1)S(1)}, u32[]{:S(2)}, u32[]{:S(2)}) collective-permute-start(bf16[128,2048]{1,0:T(8,128)(2,1)S(1)} %get-tuple-element.150), channel_id=1, source_target_pairs={{0,16},{4,20},{8,24},{12,28},{16,0},{20,4},{24,8},{28,12},{1,17},{... | collective-permute-start | bytes 1572872 | tf_op jit(solution)/shard_map/ppermute | solution.py:132
  160.7 22.8 %collective-permute-start.30 = (bf16[128,2048]{1,0:T(8,128)(2,1)S(1)}, bf16[128,2048]{1,0:T(8,128)(2,1)S(1)}, u32[]{:S(2)}, u32[]{:S(2)}) collective-permute-start(bf16[128,2048]{1,0:T(8,128)(2,1)S(1)} %get-tuple-element.149), channel_id=1, source_target_pairs={{0,24},{4,28},{8,16},{12,20},{16,8},{20,12},{24,0},{28,4},{1,25},{... | collective-permute-start | bytes 1572872 | tf_op jit(solution)/shard_map/ppermute | solution.py:132
  185.4 14.5 %collective-permute-start.31 = (bf16[4,128,1152]{2,1,0:T(8,128)(2,1)S(1)}, bf16[4,128,1152]{2,1,0:T(8,128)(2,1)S(1)}, u32[]{:S(2)}, u32[]{:S(2)}) collective-permute-start(bf16[4,128,1152]{2,1,0:T(8,128)(2,1)S(1)} %bitcast.70), channel_id=1, source_target_pairs={{0,4},{4,0},{8,12},{12,8},{16,20},{20,16},{24,28},{28,24},{1,5},{5... | collective-permute-start | bytes 3538952 | tf_op jit(solution)/shard_map/ppermute | solution.py:132
  186.5 34.8 %collective-permute-start.26 = (bf16[128,1024]{1,0:T(8,128)(2,1)S(1)}, bf16[128,1024]{1,0:T(8,128)(2,1)S(1)}, u32[]{:S(2)}, u32[]{:S(2)}) collective-permute-start(bf16[128,1024]{1,0:T(8,128)(2,1)S(1)} %get-tuple-element.111), channel_id=1, source_target_pairs={{0,2},{1,3},{2,0},{3,1},{4,6},{5,7},{6,4},{7,5},{8,10},{9,11},{10,... | collective-permute-start | bytes 786440 | tf_op jit(solution)/shard_map/ppermute | solution.py:132
  197.5 23.7 %collective-permute-start.27 = (bf16[128,1024]{1,0:T(8,128)(2,1)S(1)}, bf16[128,1024]{1,0:T(8,128)(2,1)S(1)}, u32[]{:S(2)}, u32[]{:S(2)}) collective-permute-start(bf16[128,1024]{1,0:T(8,128)(2,1)S(1)} %get-tuple-element.113), channel_id=1, source_target_pairs={{0,3},{1,2},{2,1},{3,0},{4,7},{5,6},{6,5},{7,4},{8,11},{9,10},{10,... | collective-permute-start | bytes 786440 | tf_op jit(solution)/shard_map/ppermute | solution.py:132
  202.3 13.5 %collective-permute-start.34 = (bf16[128,1152]{1,0:T(8,128)(2,1)S(1)}, bf16[128,1152]{1,0:T(8,128)(2,1)S(1)}, u32[]{:S(2)}, u32[]{:S(2)}) collective-permute-start(bf16[128,1152]{1,0:T(8,128)(2,1)S(1)} %get-tuple-element.124), channel_id=1, source_target_pairs={{0,24},{4,28},{8,16},{12,20},{16,8},{20,12},{24,0},{28,4},{1,25},{... | collective-permute-start | bytes 884744 | tf_op jit(solution)/shard_map/ppermute | solution.py:132
  216.9 14.6 %collective-permute-start.36 = (bf16[32,1920]{1,0:T(8,128)(2,1)S(1)}, bf16[32,1920]{1,0:T(8,128)(2,1)S(1)}, u32[]{:S(2)}, u32[]{:S(2)}) collective-permute-start(bf16[32,1920]{1,0:T(8,128)(2,1)S(1)} %get-tuple-element.127), channel_id=1, source_target_pairs={{0,2},{1,3},{2,0},{3,1},{4,6},{5,7},{6,4},{7,5},{8,10},{9,11},{10,... | collective-permute-start | bytes 368648 | tf_op jit(solution)/shard_map/ppermute | solution.py:132
  218.9 12.6 %collective-permute-start.37 = (bf16[32,1920]{1,0:T(8,128)(2,1)S(1)}, bf16[32,1920]{1,0:T(8,128)(2,1)S(1)}, u32[]{:S(2)}, u32[]{:S(2)}) collective-permute-start(bf16[32,1920]{1,0:T(8,128)(2,1)S(1)} %get-tuple-element.128), channel_id=1, source_target_pairs={{0,3},{1,2},{2,1},{3,0},{4,7},{5,6},{6,5},{7,4},{8,11},{9,10},{10,... | collective-permute-start | bytes 368648 | tf_op jit(solution)/shard_map/ppermute | solution.py:132
  (97 other events, 962.8 us)
Sparse Core Ops, SparseCore 0:
  34.3 46.3 all-gather.1

commit v6 on v5

--- a/solution.py
+++ b/solution.py
@@ -437,8 +437,7 @@
     "pack": 6,
     "norm": 4,
     "join": 4,
-    "branch": 16,
-    "hidden": 22,
+    "middle": 30,
     "back": 28,
     "terms": 20,
     "mlp": 28,
@@ -790,17 +789,18 @@
         sum_ref[3:4, cols] = sums[1]
 
 
-def branch_body(s_ref, mix_ref, act_ref, out_ref, last_ref, x_ref, *refs):
+def middle_body(s_ref, mix_ref, act_ref, whole_ref, last_ref, x_ref, dy_ref, slope_ref, *refs):
     down_refs, refs = refs[:N_REP], refs[N_REP:]
-    own_ref, sent_refs = refs[0], refs[1:]
+    own_ref, sent_refs = refs[0], refs[1:N_SHARD]
     rows = x_ref.shape[0]
-    total = plain_dot(mix_ref[...], out_ref[...])
+    total = plain_dot(mix_ref[...], whole_ref[...])
     for i in range(0, N_REP, 2):
         weights = jnp.concatenate([down_refs[i][...], down_refs[i + 1][...]], axis=0)
         total = total + plain_dot(act_ref[:, i * LANES : (i + 2) * LANES], weights)
     own_ref[...] = x_ref[...] + total[:rows] + last_ref[0:1, :]
     for k in range(1, N_SHARD):
         sent_refs[k - 1][...] = total[k * rows : (k + 1) * rows].astype(bf16)
+    hidden_body(s_ref, dy_ref, *down_refs, slope_ref, whole_ref, *refs[N_SHARD:])
 
 
 def terms_body(
@@ -905,11 +905,6 @@
 
 def to_shards(values):
     return [hop(values[k - 1], "shard", N_SHARD, k) for k in range(1, N_SHARD)]
-
-
-def to_shards_late(values):
-    got = [hop(values[k - 1], "shard", N_SHARD, k) for k in (1, 2)]
-    return got + [hop(after(values[2], got[0]), "shard", N_SHARD, 3)]
 
 
 def to_chips(values):
@@ -1006,10 +1001,11 @@
         "join",
     )
     normed = [normed_own] + to_shards([after(normed_own, *got_cols)] * 3)
-    pieces = gather_chips(in_rows)
-    downs = gather_chips(after(down_own, *pieces[1:4]))
-    downs[0] = down_own
-    dy_all = lax.all_gather(cotangent.astype(bf16), "shard", axis=0, tiled=True)
+    pieces = [in_rows] + to_chips([in_rows, in_rows, after(in_rows, normed[1])])
+    pieces = pieces + [hop(after(piece, normed[2], normed[3]), "rep", N_REP, 1) for piece in pieces]
+    downs = [down_own] + to_chips([after(down_own, *pieces[1:4])] * 3)
+    dy_own = after(cotangent.astype(bf16), *normed[1:3])
+    dy_all = lax.all_gather(dy_own, "shard", axis=0, tiled=True)
 
     rope_parts = jnp.asarray(rope_lanes(seq_len)).reshape(N_SHARD, tok_count, 3 * LANES)
     rope = jnp.concatenate(
@@ -1028,25 +1024,26 @@
     block16 = ((tok_count, D), bf16)
     block32 = ((tok_count, D), f32)
     half = D // 2
+    downs = downs + [hop(after(piece, qkv16), "rep", N_REP, 1) for piece in downs]
     mixed16 = mix_heads(qkv16, mask)
-    out_own, *out_sent = single(
-        branch_body,
-        [block32, block16, block16, block16],
+    out_own, s1, s2, s3, dy_seq, d_mixed16, d_up16, up_sum = single(
+        middle_body,
+        [
+            block32,
+            block16,
+            block16,
+            block16,
+            ((seq_len, D), bf16),
+            ((seq_len, OUT), bf16),
+            ((seq_len, UP), bf16),
+            ((8, UP), f32),
+        ],
         scalars,
-        [mixed16, act16, out_whole, last, block_in, *downs],
-        3,
-        "branch",
-    )
-    out_got = to_shards_late(out_sent)
-
-    dy_seq, d_mixed16, d_up16, up_sum = single(
-        hidden_body,
-        [((seq_len, D), bf16), ((seq_len, OUT), bf16), ((seq_len, UP), bf16), ((8, UP), f32)],
-        scalars,
-        [after(dy_all, out_own), *downs, slope, out_whole],
-        1,
-        "hidden",
-    )
+        [mixed16, act16, out_whole, last, block_in, dy_all, slope, *downs],
+        2,
+        "middle",
+    )
+    out_got = [hop(s1, "shard", N_SHARD, 1), hop(s2, "shard", N_SHARD, 2)]
 
     mlp_keep, mlp_sent = single(
         mlp_body,
@@ -1060,8 +1057,9 @@
     mlp_parts = sum_rep(mlp_keep.reshape(4, LANES, D + UP), mlp_got)
     d_mixed16 = after(d_mixed16, mlp_got)
     d_qkv16, qkv_sum = attend_back(qkv16, d_mixed16, mixed16, mask, rope)
-    d_qkv16 = after(d_qkv16, *out_got)
-    h_one = after(h_one, *mlp_parts[1:])
+    out_got.append(hop(after(s3, d_qkv16), "shard", N_SHARD, 3))
+    d_qkv16 = after(d_qkv16, *out_got[:2])
+    h_one = after(h_one, out_got[2], *mlp_parts[1:])
 
     e_own, *e_sent, norm_sum = single(
         back_body,
@@ -1071,7 +1069,6 @@
         1,
         "back",
     )
-    e_got = to_shards_late(e_sent)
     cot_sum = jnp.sum(cotangent, axis=0, keepdims=True)
     wide = QKV + OUT + LANES
     qkv_keep, qkv_sent = single(
@@ -1085,12 +1082,14 @@
     )
     qkv_got = hop(qkv_sent.reshape(4, LANES, wide), "rep", N_REP, 1)
     qkv_parts = sum_rep(qkv_keep.reshape(4, LANES, wide), qkv_got, *mlp_parts[1:])
+    e_got = [hop(e_sent[0], "shard", N_SHARD, 1), hop(e_sent[1], "shard", N_SHARD, 2)]
+    e_got.append(hop(after(e_sent[2], qkv_parts[1]), "shard", N_SHARD, 3))
     narrow = (rows, QKV + UP + LANES)
     g_own, g1, g2, g3, out_sum = single(
         fold_body,
         [(narrow, f32), (narrow, bf16), (narrow, bf16), (narrow, bf16), ((rows, D), f32)],
         scalars,
-        [*mlp_parts, *qkv_parts],
+        [*mlp_parts, after(qkv_parts[0], *e_got[:2]), *qkv_parts[1:]],
         1,
         "fold",
         [pltpu.VMEM((LANES, UP), f32), pltpu.VMEM((LANES, wide), f32)],
@@ -1129,7 +1128,7 @@
         [qkv_shape] * 4 + [up_shape] * 4 + [vec_shape] * 4,
         scalars,
         [
-            g_own,
+            after(g_own, e_got[2]),
             *g_got,
             qkv_weight,
             first_qkv,

time: 244 us -> 214 us (0.88)
  waiting for transfers between devices: 96.5 us -> 63.5 us
  local copies, waits for them, and re-layouts: 24.7 us -> 28.5 us
    ppermute x37, waiting for transfers between devices: 96.5 us -> 60.3 us  [hop(): return lax.ppermute(value, axis, [(i, i ^ mask) for i in range(size)])]
    unnamed x179 -> x157, local copies, waits for them, and re-layouts: 22.2 us -> 26.3 us
    all_gather x1, waiting for transfers between devices: 0.01 us -> 3.13 us  [shards(): dy_all = lax.all_gather(dy_own, 'shard', axis=0, tiled=True)]
    pallas_call x11 -> x10, Pallas kernels: 21.9 us -> 21.8 us  [single(): pl.pallas_call(body, out_shape=shapes, grid_spec=pltpu.PrefetchScalarGrid...]
  transfers between devices with their start and end apart: 40 -> 40, of which waited for: 16 -> 13; matrix products, arithmetic and copies ran while one was open for 3% -> 3% of each run, Pallas kernels for 15% -> 15%
where the time goes in v6:
time: 214 us; the launch traced here: 213 us
  waiting for transfers between devices  63.5 us (30%)
  Pallas kernels  45.8 us (21%)
  starting transfers between devices  43.4 us (20%)
  local copies, waits for them, and re-layouts  28.5 us (13%)
  between operations  25.3 us (12%)
  other arithmetic  6.08 us (3%)
    ppermute x37, waiting for transfers between devices, hop(): return lax.ppermute(value, axis, [(i, i ^ mask) for i in range(size)])  60.3 us
    ppermute x37, starting transfers between devices, hop(): return lax.ppermute(value, axis, [(i, i ^ mask) for i in range(size)])  41.8 us
    unnamed x157, local copies, waits for them, and re-layouts  26.3 us
    pallas_call x10, Pallas kernels, single(): pl.pallas_call(body, out_shape=shapes, grid_spec=pltpu.PrefetchScalarGrid...  21.8 us
    pallas_call x1, Pallas kernels, front(): pl.pallas_call(front_body, out_shape=tuple((jax.ShapeDtypeStruct(s, d) fo...  9.05 us
    pallas_call x1, Pallas kernels, attend_back(): pl.pallas_call(attend_body, out_shape=(jax.ShapeDtypeStruct((tokens, QKV)...  8.85 us
    pallas_call x1, Pallas kernels, mix_heads(): pl.pallas_call(mix_body, out_shape=jax.ShapeDtypeStruct((tokens, OUT), bf...  6.06 us
  transfers between devices with their start and end apart: 40, of which 13 were waited for; matrix products, arithmetic and copies ran while one was open for 3% of the time, Pallas kernels for 15%

profile of v6, /device:TPU:0, one launch (start us, length us, event | category | flops | bytes accessed | tf_op | source)
XLA Modules:
  0.0 212.6 jit_solution(2592281144052568245)
XLA Ops:
  11.5 3.1 %collective-permute-start = (bf16[32,1920]{1,0:T(8,128)(2,1)S(1)}, bf16[32,1920]{1,0:T(8,128)(2,1)S(1)}, u32[]{:S(2)}, u32[]{:S(2)}) collective-permute-start(bf16[32,1920]{1,0:T(8,128)(2,1)S(1)} %get-tuple-element.93), channel_id=1, source_target_pairs={{0,1},{1,0},{2,3},{3,2},{4,5},{5,4},{6,7},{7,6},{8,9},{9,8},{10,11... | collective-permute-start | bytes 368648 | tf_op jit(solution)/shard_map/ppermute | solution.py:132
  14.5 2.6 %collective-permute-start.1 = (bf16[32,1920]{1,0:T(8,128)(2,1)S(1)}, bf16[32,1920]{1,0:T(8,128)(2,1)S(1)}, u32[]{:S(2)}, u32[]{:S(2)}) collective-permute-start(bf16[32,1920]{1,0:T(8,128)(2,1)S(1)} %get-tuple-element.94), channel_id=1, source_target_pairs={{0,2},{1,3},{2,0},{3,1},{4,6},{5,7},{6,4},{7,5},{8,10},{9,11},{10,... | collective-permute-start | bytes 368648 | tf_op jit(solution)/shard_map/ppermute | solution.py:132
  19.2 9.1 %collective-permute-done.1.refs_2_ = bf16[32,1920]{1,0:T(8,128)(2,1)S(1)} collective-permute-done((bf16[32,1920]{1,0:T(8,128)(2,1)S(1)}, bf16[32,1920]{1,0:T(8,128)(2,1)S(1)}, u32[]{:S(2)}, u32[]{:S(2)}) %collective-permute-start.1) | collective-permute-done | bytes 122912 | tf_op jit(solution)/shard_map/ppermute | solution.py:132
  28.3 2.5 %collective-permute-start.3 = (bf16[128,1024]{1,0:T(8,128)(2,1)S(1)}, bf16[128,1024]{1,0:T(8,128)(2,1)S(1)}, u32[]{:S(2)}, u32[]{:S(2)}) collective-permute-start(bf16[128,1024]{1,0:T(8,128)(2,1)S(1)} %norm.1.refs_0_), channel_id=1, source_target_pairs={{0,1},{1,0},{2,3},{3,2},{4,5},{5,4},{6,7},{7,6},{8,9},{9,8},{10,11... | collective-permute-start | bytes 786440 | tf_op jit(solution)/shard_map/ppermute | solution.py:132
  44.0 1.5 collective-permute-start.8
  48.4 1.8 collective-permute-start.5
  51.0 14.0 %collective-permute-done.4.refs_2_ = bf16[128,1024]{1,0:T(8,128)(2,1)S(1)} collective-permute-done((bf16[128,1024]{1,0:T(8,128)(2,1)S(1)}, bf16[128,1024]{1,0:T(8,128)(2,1)S(1)}, u32[]{:S(2)}, u32[]{:S(2)}) %collective-permute-start.4) | collective-permute-done | bytes 262176 | tf_op jit(solution)/shard_map/ppermute | solution.py:132
  65.6 1.6 collective-permute-done.8.refs_6_.refs_14_.refs_22_
  70.6 1.7 collective-permute-start.15
  76.9 9.1 %front.1 = (bf16[256,1024]{1,0:T(8,128)(2,1)S(1)}, bf16[512,1024]{1,0:T(8,128)(2,1)S(1)}, bf16[512,1024]{1,0:T(8,128)(2,1)S(1)}, bf16[512,768]{1,0:T(8,128)(2,1)...) custom-call(s32[21]{0:T(128)S(1)} %pad_add_fusion.1.s_ref, ...), custom_call_target="tpu_custom_call" | custom-call | flops 10350000128 | bytes 1048576 | tf_op jit(solution)/shard_map/front/pallas_call | solution.py:613
  87.1 6.1 %mix_heads.1.mix_ref = bf16[512,256]{1,0:T(8,128)(2,1)S(1)} custom-call(bf16[512,768]{1,0:T(8,128)(2,1)S(1)} %get-tuple-element.104.q_ref.k_ref.v_ref, bf16[512,768]{1,0:T(8,128)(2,1)S(1)} %get-tuple-element.104.q_ref.k_ref.v_ref, bf16[512,768]{1,0:T(8,128)(2,1)S(1)} %get-tuple-element.104.q_ref.k_ref.v_ref, f32[512,512]{1,0:T(8,128)S(1)} %and_select_fusion.mask_ref), custom_call_target="tpu_custom_call" | custom-call | flops 6899999744 | bytes 1048576 | tf_op jit(solution)/shard_map/mix_heads/pallas_call | solution.py:731
  96.8 3.1 %all-gather.2.cloned.1.call-done.dy_ref = bf16[512,1024]{1,0:T(8,128)(2,1)} async-done(((bf16[128,1024]{1,0:T(8,128)(2,1)}), bf16[512,1024]{1,0:T(8,128)(2,1)}) %all-gather.2.cloned.1.call-update) | async-done | bytes 1048592 | tf_op jit(solution)/shard_map/all_gather | solution.py:1008
  111.0 1.6 copy-done.54
  114.6 4.7 %middle.1 = (f32[128,1024]{1,0:T(8,128)S(1)}, bf16[128,1024]{1,0:T(8,128)(2,1)S(1)}, bf16[128,1024]{1,0:T(8,128)(2,1)S(1)}, bf16[128,1024]{1,0:T(8,128)(2,1)S(1)...) custom-call(s32[21]{0:T(128)S(1)} %pad_add_fusion.1.s_ref, ...), custom_call_target="tpu_custom_call" | custom-call | flops 2300000000 | bytes 1048576 | tf_op jit(solution)/shard_map/middle/pallas_call | solution.py:452
  119.3 2.9 %mlp.1 = (f32[512,2048]{1,0:T(8,128)S(1)}, bf16[512,2048]{1,0:T(8,128)(2,1)S(1)}) custom-call(s32[21]{0:T(128)S(1)} %pad_add_fusion.1.s_ref, bf16[512,1024]{1,0:T(8,128)(2,1)S(1)} %copy-done.52, bf16[512,1024]{1,0:T(8,128)(2,1)S(1)} %get-tuple-element.120.dy_ref, bf16[512,1024]{1,0:T(8,128)(2,1)S(1)} %copy-done.49, ...), custom_call_target="tpu_custom_call" | custom-call | flops 1150000000 | bytes 1048576 | tf_op jit(solution)/shard_map/mlp/pallas_call | solution.py:452
  122.3 2.2 %collective-permute-start.22 = (bf16[128,1024]{1,0:T(8,128)(2,1)S(1)}, bf16[128,1024]{1,0:T(8,128)(2,1)S(1)}, u32[]{:S(2)}, u32[]{:S(2)}) collective-permute-start(bf16[128,1024]{1,0:T(8,128)(2,1)S(1)} %get-tuple-element.117), channel_id=1, source_target_pairs={{0,2},{1,3},{2,0},{3,1},{4,6},{5,7},{6,4},{7,5},{8,10},{9,11},{10,... | collective-permute-start | bytes 786440 | tf_op jit(solution)/shard_map/ppermute | solution.py:132
  124.8 1.6 collective-permute-done.23
  130.8 8.8 %attend_back.1 = (bf16[512,768]{1,0:T(8,128)(2,1)S(1)}, f32[1,768]{1,0:T(1,128)S(1)}) custom-call(bf16[512,768]{1,0:T(8,128)(2,1)S(1)} %copy-done.63, bf16[512,768]{1,0:T(8,128)(2,1)S(1)} %copy-done.63, bf16[512,768]{1,0:T(8,128)(2,1)S(1)} %copy-done.63, bf16[512,256]{1,0:T(8,128)(2,1)S(1)} %get-tuple-element.124.dm_ref, bf16[512,256]{1,0:T(8,128)(2,1)S(1)} %copy-done.59, ...), custom_call_target="tpu_custom_call" | custom-call | flops 4600000000 | bytes 1048576 | tf_op jit(solution)/shard_map/attend_back/pallas_call | solution.py:746
  139.7 2.0 collective-permute-start.24
  141.7 4.6 %back.1 = (f32[128,1024]{1,0:T(8,128)S(1)}, bf16[128,1024]{1,0:T(8,128)(2,1)S(1)}, bf16[128,1024]{1,0:T(8,128)(2,1)S(1)}, bf16[128,1024]{1,0:T(8,128)(2,1)S(1)}, f32[8,1024]{1,0:T(8,128)S(1)}) custom-call(s32[21]{0:T(128)S(1)} %pad_add_fusion.1.s_ref, bf16[512,768]{1,0:T(8,128)(2,1)S(1)} %get-tuple-element.127.dqkv_ref, ...), custom_call_target="tpu_custom_call" | custom-call | flops 1150000000 | bytes 1048576 | tf_op jit(solution)/shard_map/back/pallas_call | solution.py:452
  146.3 2.8 %collective-permute-done.24 = bf16[128,1024]{1,0:T(8,128)(2,1)S(1)} collective-permute-done((bf16[128,1024]{1,0:T(8,128)(2,1)S(1)}, bf16[128,1024]{1,0:T(8,128)(2,1)S(1)}, u32[]{:S(2)}, u32[]{:S(2)}) %collective-permute-start.24) | collective-permute-done | bytes 262176 | tf_op jit(solution)/shard_map/ppermute | solution.py:132
  149.2 4.4 %collective-permute-done.28.refs_2_ = bf16[128,2048]{1,0:T(8,128)(2,1)S(1)} collective-permute-done((bf16[128,2048]{1,0:T(8,128)(2,1)S(1)}, bf16[128,2048]{1,0:T(8,128)(2,1)S(1)}, u32[]{:S(2)}, u32[]{:S(2)}) %collective-permute-start.28) | collective-permute-done | bytes 524320 | tf_op jit(solution)/shard_map/ppermute | solution.py:132
  153.6 1.9 terms.1
  155.6 2.8 %collective-permute-done.30 = bf16[4,128,1152]{2,1,0:T(8,128)(2,1)S(1)} collective-permute-done((bf16[4,128,1152]{2,1,0:T(8,128)(2,1)S(1)}, bf16[4,128,1152]{2,1,0:T(8,128)(2,1)S(1)}, u32[]{:S(2)}, u32[]{:S(2)}) %collective-permute-start.30) | collective-permute-done | bytes 1179680 | tf_op jit(solution)/shard_map/ppermute | solution.py:132
  165.6 9.0 %collective-permute-done.25.r1_ref = bf16[128,1024]{1,0:T(8,128)(2,1)S(1)} collective-permute-done((bf16[128,1024]{1,0:T(8,128)(2,1)S(1)}, bf16[128,1024]{1,0:T(8,128)(2,1)S(1)}, u32[]{:S(2)}, u32[]{:S(2)}) %collective-permute-start.25) | collective-permute-done | bytes 262176 | tf_op jit(solution)/shard_map/ppermute | solution.py:132
  174.6 5.6 %collective-permute-done.26.r2_ref = bf16[128,1024]{1,0:T(8,128)(2,1)S(1)} collective-permute-done((bf16[128,1024]{1,0:T(8,128)(2,1)S(1)}, bf16[128,1024]{1,0:T(8,128)(2,1)S(1)}, u32[]{:S(2)}, u32[]{:S(2)}) %collective-permute-start.26) | collective-permute-done | bytes 262176 | tf_op jit(solution)/shard_map/ppermute | solution.py:132
  180.2 1.9 collective-permute-start.32
  184.1 1.5 multiply_subtract_fusion
  185.6 4.8 %collective-permute-start.36 = (bf16[32,1920]{1,0:T(8,128)(2,1)S(1)}, bf16[32,1920]{1,0:T(8,128)(2,1)S(1)}, u32[]{:S(2)}, u32[]{:S(2)}) collective-permute-start(bf16[32,1920]{1,0:T(8,128)(2,1)S(1)} %get-tuple-element.149), channel_id=1, source_target_pairs={{0,2},{1,3},{2,0},{3,1},{4,6},{5,7},{6,4},{7,5},{8,10},{9,11},{10,... | collective-permute-start | bytes 368648 | tf_op jit(solution)/shard_map/ppermute | solution.py:132
  192.8 1.9 finish.1
  194.7 7.6 %collective-permute-done.36.refs_2_ = bf16[32,1920]{1,0:T(8,128)(2,1)S(1)} collective-permute-done((bf16[32,1920]{1,0:T(8,128)(2,1)S(1)}, bf16[32,1920]{1,0:T(8,128)(2,1)S(1)}, u32[]{:S(2)}, u32[]{:S(2)}) %collective-permute-start.36) | collective-permute-done | bytes 122912 | tf_op jit(solution)/shard_map/ppermute | solution.py:132
  202.4 2.8 %adam.1 = (f32[32,3072]{1,0:T(8,128)}, f32[32,3072]{1,0:T(8,128)}, f32[32,3072]{1,0:T(8,128)}, f32[32,3072]{1,0:T(8,128)}, f32[32,4096]{1,0:T(8,128)}, /*index=5...) custom-call(s32[21]{0:T(128)S(1)} %pad_add_fusion.1.s_ref, ...), custom_call_target="tpu_custom_call" | custom-call | flops 3449999872 | bytes 1048576 | tf_op jit(solution)/shard_map/adam/pallas_call | solution.py:452
  (238 shorter events, 55.6 us)
Async XLA Ops:
  7.2 92.7 %all-gather.2.cloned.1.call-start = ((), (), s32[]{:S(2)}) async-start(), calls=%async_computation | async-start | bytes 1310720 | tf_op jit(solution)/shard_map/all_gather | solution.py:1008
  14.5 13.8 %collective-permute-start.1 = (bf16[32,1920]{1,0:T(8,128)(2,1)S(1)}, bf16[32,1920]{1,0:T(8,128)(2,1)S(1)}, u32[]{:S(2)}, u32[]{:S(2)}) collective-permute-start(bf16[32,1920]{1,0:T(8,128)(2,1)S(1)} %get-tuple-element.94), channel_id=1, source_target_pairs={{0,2},{1,3},{2,0},{3,1},{4,6},{5,7},{6,4},{7,5},{8,10},{9,11},{10,... | collective-permute-start | bytes 368648 | tf_op jit(solution)/shard_map/ppermute | solution.py:132
  17.1 11.2 %collective-permute-start.2 = (bf16[32,1920]{1,0:T(8,128)(2,1)S(1)}, bf16[32,1920]{1,0:T(8,128)(2,1)S(1)}, u32[]{:S(2)}, u32[]{:S(2)}) collective-permute-start(bf16[32,1920]{1,0:T(8,128)(2,1)S(1)} %get-tuple-element.95), channel_id=1, source_target_pairs={{0,3},{1,2},{2,1},{3,0},{4,7},{5,6},{6,5},{7,4},{8,11},{9,10},{10,... | collective-permute-start | bytes 368648 | tf_op jit(solution)/shard_map/ppermute | solution.py:132
  17.2 25.6 %collective-permute-start.6 = (bf16[32,1024]{1,0:T(8,128)(2,1)S(1)}, bf16[32,1024]{1,0:T(8,128)(2,1)S(1)}, u32[]{:S(2)}, u32[]{:S(2)}) collective-permute-start(bf16[32,1024]{1,0:T(8,128)(2,1)S(1)} %convert_element_type.93), channel_id=1, source_target_pairs={{0,0},{1,4},{2,8},{3,12},{4,1},{5,5},{6,9},{7,13},{8,2},{9,6},{10,... | collective-permute-start | bytes 196616 | tf_op jit(solution)/shard_map/ppermute | solution.py:984
  28.3 17.3 %collective-permute-start.3 = (bf16[128,1024]{1,0:T(8,128)(2,1)S(1)}, bf16[128,1024]{1,0:T(8,128)(2,1)S(1)}, u32[]{:S(2)}, u32[]{:S(2)}) collective-permute-start(bf16[128,1024]{1,0:T(8,128)(2,1)S(1)} %norm.1.refs_0_), channel_id=1, source_target_pairs={{0,1},{1,0},{2,3},{3,2},{4,5},{5,4},{6,7},{7,6},{8,9},{9,8},{10,11... | collective-permute-start | bytes 786440 | tf_op jit(solution)/shard_map/ppermute | solution.py:132
  43.4 21.7 %collective-permute-start.7 = (bf16[128,2176]{1,0:T(8,128)(2,1)S(1)}, bf16[128,2176]{1,0:T(8,128)(2,1)S(1)}, u32[]{:S(2)}, u32[]{:S(2)}) collective-permute-start(bf16[128,2176]{1,0:T(8,128)(2,1)S(1)} %join.1.refs_4_.refs_12_.refs_20_), channel_id=1, source_target_pairs={{0,8},{4,12},{8,0},{12,4},{16,24},{20,28},{24,16},{28,20},{1,9},{5... | collective-permute-start | bytes 1671176 | tf_op jit(solution)/shard_map/ppermute | solution.py:132
  44.0 23.1 %collective-permute-start.8 = (bf16[128,2176]{1,0:T(8,128)(2,1)S(1)}, bf16[128,2176]{1,0:T(8,128)(2,1)S(1)}, u32[]{:S(2)}, u32[]{:S(2)}) collective-permute-start(bf16[128,2176]{1,0:T(8,128)(2,1)S(1)} %join.1.refs_4_.refs_12_.refs_20_), channel_id=1, source_target_pairs={{0,16},{4,20},{8,24},{12,28},{16,0},{20,4},{24,8},{28,12},{1,17},{... | collective-permute-start | bytes 1671176 | tf_op jit(solution)/shard_map/ppermute | solution.py:132
  46.3 22.2 %collective-permute-start.9 = (bf16[128,2176]{1,0:T(8,128)(2,1)S(1)}, bf16[128,2176]{1,0:T(8,128)(2,1)}, u32[]{:S(2)}, u32[]{:S(2)}) collective-permute-start(bf16[128,2176]{1,0:T(8,128)(2,1)S(1)} %join.1.refs_4_.refs_12_.refs_20_), channel_id=1, source_target_pairs={{0,24},{4,28},{8,16},{12,20},{16,8},{20,12},{24,0},{28,4},{1,25},{... | collective-permute-start | bytes 1671176 | tf_op jit(solution)/shard_map/ppermute | solution.py:132
  47.8 17.2 %collective-permute-start.4 = (bf16[128,1024]{1,0:T(8,128)(2,1)S(1)}, bf16[128,1024]{1,0:T(8,128)(2,1)S(1)}, u32[]{:S(2)}, u32[]{:S(2)}) collective-permute-start(bf16[128,1024]{1,0:T(8,128)(2,1)S(1)} %norm.1.refs_0_), channel_id=1, source_target_pairs={{0,2},{1,3},{2,0},{3,1},{4,6},{5,7},{6,4},{7,5},{8,10},{9,11},{10,... | collective-permute-start | bytes 786440 | tf_op jit(solution)/shard_map/ppermute | solution.py:132
  48.4 16.6 %collective-permute-start.5 = (bf16[128,1024]{1,0:T(8,128)(2,1)S(1)}, bf16[128,1024]{1,0:T(8,128)(2,1)S(1)}, u32[]{:S(2)}, u32[]{:S(2)}) collective-permute-start(bf16[128,1024]{1,0:T(8,128)(2,1)S(1)} %norm.1.refs_0_), channel_id=1, source_target_pairs={{0,3},{1,2},{2,1},{3,0},{4,7},{5,6},{6,5},{7,4},{8,11},{9,10},{10,... | collective-permute-start | bytes 786440 | tf_op jit(solution)/shard_map/ppermute | solution.py:132
  69.5 16.6 %collective-permute-start.14 = (bf16[128,1024]{1,0:T(8,128)(2,1)}, bf16[128,1024]{1,0:T(8,128)(2,1)S(1)}, u32[]{:S(2)}, u32[]{:S(2)}) collective-permute-start(bf16[128,1024]{1,0:T(8,128)(2,1)} %convert_element_type.95.refs_0_), channel_id=1, source_target_pairs={{0,8},{4,12},{8,0},{12,4},{16,24},{20,28},{24,16},{28,20},{1,9},{5... | collective-permute-start | bytes 786440 | tf_op jit(solution)/shard_map/ppermute | solution.py:132
  70.6 16.0 %collective-permute-start.15 = (bf16[128,1024]{1,0:T(8,128)(2,1)}, bf16[128,1024]{1,0:T(8,128)(2,1)S(1)}, u32[]{:S(2)}, u32[]{:S(2)}) collective-permute-start(bf16[128,1024]{1,0:T(8,128)(2,1)} %convert_element_type.95.refs_0_), channel_id=1, source_target_pairs={{0,16},{4,20},{8,24},{12,28},{16,0},{20,4},{24,8},{28,12},{1,17},{... | collective-permute-start | bytes 786440 | tf_op jit(solution)/shard_map/ppermute | solution.py:132
  72.3 14.4 %collective-permute-start.16 = (bf16[128,1024]{1,0:T(8,128)(2,1)}, bf16[128,1024]{1,0:T(8,128)(2,1)S(1)}, u32[]{:S(2)}, u32[]{:S(2)}) collective-permute-start(bf16[128,1024]{1,0:T(8,128)(2,1)} %convert_element_type.95.refs_0_), channel_id=1, source_target_pairs={{0,24},{4,28},{8,16},{12,20},{16,8},{20,12},{24,0},{28,4},{1,25},{... | collective-permute-start | bytes 786440 | tf_op jit(solution)/shard_map/ppermute | solution.py:132
  86.1 8.6 %collective-permute-start.18 = (bf16[128,1024]{1,0:T(8,128)(2,1)S(1)}, bf16[128,1024]{1,0:T(8,128)(2,1)S(1)}, u32[]{:S(2)}, u32[]{:S(2)}) collective-permute-start(bf16[128,1024]{1,0:T(8,128)(2,1)S(1)} %collective-permute-done.14.refs_1_), channel_id=1, source_target_pairs={{0,4},{4,0},{8,12},{12,8},{16,20},{20,16},{24,28},{28,24},{1,5},{5... | collective-permute-start | bytes 786440 | tf_op jit(solution)/shard_map/ppermute | solution.py:132
  86.6 8.8 %collective-permute-start.19 = (bf16[128,1024]{1,0:T(8,128)(2,1)S(1)}, bf16[128,1024]{1,0:T(8,128)(2,1)S(1)}, u32[]{:S(2)}, u32[]{:S(2)}) collective-permute-start(bf16[128,1024]{1,0:T(8,128)(2,1)S(1)} %collective-permute-done.15.refs_2_), channel_id=1, source_target_pairs={{0,4},{4,0},{8,12},{12,8},{16,20},{20,16},{24,28},{28,24},{1,5},{5... | collective-permute-start | bytes 786440 | tf_op jit(solution)/shard_map/ppermute | solution.py:132
  86.7 9.4 %collective-permute-start.20 = (bf16[128,1024]{1,0:T(8,128)(2,1)S(1)}, bf16[128,1024]{1,0:T(8,128)(2,1)S(1)}, u32[]{:S(2)}, u32[]{:S(2)}) collective-permute-start(bf16[128,1024]{1,0:T(8,128)(2,1)S(1)} %collective-permute-done.16.refs_3_), channel_id=1, source_target_pairs={{0,4},{4,0},{8,12},{12,8},{16,20},{20,16},{24,28},{28,24},{1,5},{5... | collective-permute-start | bytes 786440 | tf_op jit(solution)/shard_map/ppermute | solution.py:132
  122.3 17.4 %collective-permute-start.22 = (bf16[128,1024]{1,0:T(8,128)(2,1)S(1)}, bf16[128,1024]{1,0:T(8,128)(2,1)S(1)}, u32[]{:S(2)}, u32[]{:S(2)}) collective-permute-start(bf16[128,1024]{1,0:T(8,128)(2,1)S(1)} %get-tuple-element.117), channel_id=1, source_target_pairs={{0,2},{1,3},{2,0},{3,1},{4,6},{5,7},{6,4},{7,5},{8,10},{9,11},{10,... | collective-permute-start | bytes 786440 | tf_op jit(solution)/shard_map/ppermute | solution.py:132
  124.5 17.1 %collective-permute-start.21 = (bf16[128,1024]{1,0:T(8,128)(2,1)S(1)}, bf16[128,1024]{1,0:T(8,128)(2,1)S(1)}, u32[]{:S(2)}, u32[]{:S(2)}) collective-permute-start(bf16[128,1024]{1,0:T(8,128)(2,1)S(1)} %get-tuple-element.116), channel_id=1, source_target_pairs={{0,1},{1,0},{2,3},{3,2},{4,5},{5,4},{6,7},{7,6},{8,9},{9,8},{10,11... | collective-permute-start | bytes 786440 | tf_op jit(solution)/shard_map/ppermute | solution.py:132
  127.2 22.0 %collective-permute-start.27 = (bf16[128,2048]{1,0:T(8,128)(2,1)S(1)}, bf16[128,2048]{1,0:T(8,128)(2,1)S(1)}, u32[]{:S(2)}, u32[]{:S(2)}) collective-permute-start(bf16[128,2048]{1,0:T(8,128)(2,1)S(1)} %get-tuple-element.174), channel_id=1, source_target_pairs={{0,8},{4,12},{8,0},{12,4},{16,24},{20,28},{24,16},{28,20},{1,9},{5... | collective-permute-start | bytes 1572872 | tf_op jit(solution)/shard_map/ppermute | solution.py:132
  128.7 24.9 %collective-permute-start.28 = (bf16[128,2048]{1,0:T(8,128)(2,1)S(1)}, bf16[128,2048]{1,0:T(8,128)(2,1)S(1)}, u32[]{:S(2)}, u32[]{:S(2)}) collective-permute-start(bf16[128,2048]{1,0:T(8,128)(2,1)S(1)} %get-tuple-element.173), channel_id=1, source_target_pairs={{0,16},{4,20},{8,24},{12,28},{16,0},{20,4},{24,8},{28,12},{1,17},{... | collective-permute-start | bytes 1572872 | tf_op jit(solution)/shard_map/ppermute | solution.py:132
  130.2 23.4 %collective-permute-start.29 = (bf16[128,2048]{1,0:T(8,128)(2,1)S(1)}, bf16[128,2048]{1,0:T(8,128)(2,1)S(1)}, u32[]{:S(2)}, u32[]{:S(2)}) collective-permute-start(bf16[128,2048]{1,0:T(8,128)(2,1)S(1)} %get-tuple-element.172), channel_id=1, source_target_pairs={{0,24},{4,28},{8,16},{12,20},{16,8},{20,12},{24,0},{28,4},{1,25},{... | collective-permute-start | bytes 1572872 | tf_op jit(solution)/shard_map/ppermute | solution.py:132
  139.7 9.5 %collective-permute-start.24 = (bf16[128,1024]{1,0:T(8,128)(2,1)S(1)}, bf16[128,1024]{1,0:T(8,128)(2,1)S(1)}, u32[]{:S(2)}, u32[]{:S(2)}) collective-permute-start(bf16[128,1024]{1,0:T(8,128)(2,1)S(1)} %get-tuple-element.126), channel_id=1, source_target_pairs={{0,3},{1,2},{2,1},{3,0},{4,7},{5,6},{6,5},{7,4},{8,11},{9,10},{10,... | collective-permute-start | bytes 786440 | tf_op jit(solution)/shard_map/ppermute | solution.py:132
  158.6 21.6 %collective-permute-start.31 = (bf16[128,1152]{1,0:T(8,128)(2,1)S(1)}, bf16[128,1152]{1,0:T(8,128)(2,1)S(1)}, u32[]{:S(2)}, u32[]{:S(2)}) collective-permute-start(bf16[128,1152]{1,0:T(8,128)(2,1)S(1)} %get-tuple-element.141), channel_id=1, source_target_pairs={{0,8},{4,12},{8,0},{12,4},{16,24},{20,28},{24,16},{28,20},{1,9},{5... | collective-permute-start | bytes 884744 | tf_op jit(solution)/shard_map/ppermute | solution.py:132
  159.9 22.3 %collective-permute-start.33 = (bf16[128,1152]{1,0:T(8,128)(2,1)S(1)}, bf16[128,1152]{1,0:T(8,128)(2,1)S(1)}, u32[]{:S(2)}, u32[]{:S(2)}) collective-permute-start(bf16[128,1152]{1,0:T(8,128)(2,1)S(1)} %get-tuple-element.144), channel_id=1, source_target_pairs={{0,16},{4,20},{8,24},{12,28},{16,0},{20,4},{24,8},{28,12},{1,17},{... | collective-permute-start | bytes 884744 | tf_op jit(solution)/shard_map/ppermute | solution.py:132
  160.7 21.5 %collective-permute-start.34 = (bf16[128,1152]{1,0:T(8,128)(2,1)S(1)}, bf16[128,1152]{1,0:T(8,128)(2,1)S(1)}, u32[]{:S(2)}, u32[]{:S(2)}) collective-permute-start(bf16[128,1152]{1,0:T(8,128)(2,1)S(1)} %get-tuple-element.145), channel_id=1, source_target_pairs={{0,24},{4,28},{8,16},{12,20},{16,8},{20,12},{24,0},{28,4},{1,25},{... | collective-permute-start | bytes 884744 | tf_op jit(solution)/shard_map/ppermute | solution.py:132
  162.2 12.5 %collective-permute-start.25 = (bf16[128,1024]{1,0:T(8,128)(2,1)S(1)}, bf16[128,1024]{1,0:T(8,128)(2,1)S(1)}, u32[]{:S(2)}, u32[]{:S(2)}) collective-permute-start(bf16[128,1024]{1,0:T(8,128)(2,1)S(1)} %get-tuple-element.130), channel_id=1, source_target_pairs={{0,1},{1,0},{2,3},{3,2},{4,5},{5,4},{6,7},{7,6},{8,9},{9,8},{10,11... | collective-permute-start | bytes 786440 | tf_op jit(solution)/shard_map/ppermute | solution.py:132
  163.6 16.6 %collective-permute-start.26 = (bf16[128,1024]{1,0:T(8,128)(2,1)S(1)}, bf16[128,1024]{1,0:T(8,128)(2,1)S(1)}, u32[]{:S(2)}, u32[]{:S(2)}) collective-permute-start(bf16[128,1024]{1,0:T(8,128)(2,1)S(1)} %get-tuple-element.131), channel_id=1, source_target_pairs={{0,2},{1,3},{2,0},{3,1},{4,6},{5,7},{6,4},{7,5},{8,10},{9,11},{10,... | collective-permute-start | bytes 786440 | tf_op jit(solution)/shard_map/ppermute | solution.py:132
  180.2 12.4 %collective-permute-start.32 = (bf16[128,1024]{1,0:T(8,128)(2,1)S(1)}, bf16[128,1024]{1,0:T(8,128)(2,1)S(1)}, u32[]{:S(2)}, u32[]{:S(2)}) collective-permute-start(bf16[128,1024]{1,0:T(8,128)(2,1)S(1)} %get-tuple-element.142), channel_id=1, source_target_pairs={{0,3},{1,2},{2,1},{3,0},{4,7},{5,6},{6,5},{7,4},{8,11},{9,10},{10,... | collective-permute-start | bytes 786440 | tf_op jit(solution)/shard_map/ppermute | solution.py:132
  183.2 8.6 %collective-permute-start.38 = (f32[32,1024]{1,0:T(8,128)S(1)}, f32[32,1024]{1,0:T(8,128)S(1)}, u32[]{:S(2)}, u32[]{:S(2)}) collective-permute-start(f32[32,1024]{1,0:T(8,128)S(1)} %get-tuple-element.152), channel_id=1, source_target_pairs={{0,0},{4,1},{8,2},{12,3},{1,4},{5,5},{9,6},{13,7},{2,8},{6,9},{10,... | collective-permute-start | bytes 393224 | tf_op jit(solution)/shard_map/ppermute | solution.py:1098
  185.6 9.1 %collective-permute-start.35 = (bf16[32,1920]{1,0:T(8,128)(2,1)S(1)}, bf16[32,1920]{1,0:T(8,128)(2,1)S(1)}, u32[]{:S(2)}, u32[]{:S(2)}) collective-permute-start(bf16[32,1920]{1,0:T(8,128)(2,1)S(1)} %get-tuple-element.148), channel_id=1, source_target_pairs={{0,1},{1,0},{2,3},{3,2},{4,5},{5,4},{6,7},{7,6},{8,9},{9,8},{10,11... | collective-permute-start | bytes 368648 | tf_op jit(solution)/shard_map/ppermute | solution.py:132
  185.6 16.7 %collective-permute-start.36 = (bf16[32,1920]{1,0:T(8,128)(2,1)S(1)}, bf16[32,1920]{1,0:T(8,128)(2,1)S(1)}, u32[]{:S(2)}, u32[]{:S(2)}) collective-permute-start(bf16[32,1920]{1,0:T(8,128)(2,1)S(1)} %get-tuple-element.149), channel_id=1, source_target_pairs={{0,2},{1,3},{2,0},{3,1},{4,6},{5,7},{6,4},{7,5},{8,10},{9,11},{10,... | collective-permute-start | bytes 368648 | tf_op jit(solution)/shard_map/ppermute | solution.py:132
  190.4 11.9 %collective-permute-start.37 = (bf16[32,1920]{1,0:T(8,128)(2,1)S(1)}, bf16[32,1920]{1,0:T(8,128)(2,1)S(1)}, u32[]{:S(2)}, u32[]{:S(2)}) collective-permute-start(bf16[32,1920]{1,0:T(8,128)(2,1)S(1)} %get-tuple-element.150), channel_id=1, source_target_pairs={{0,3},{1,2},{2,1},{3,0},{4,7},{5,6},{6,5},{7,4},{8,11},{9,10},{10,... | collective-permute-start | bytes 368648 | tf_op jit(solution)/shard_map/ppermute | solution.py:132
  (86 other events, 514.4 us)
Sparse Core Ops, SparseCore 0:
  69.6 30.2 all-gather.1

commit v7 on v6

--- a/solution.py
+++ b/solution.py
@@ -636,7 +636,7 @@
     slope_ref, whole_ref, seq_ref, dmix_ref, du_ref, sum_ref = refs
     tokens = dy_ref.shape[0] // N_SHARD
     for k in range(N_SHARD):
-        seq_ref[k * tokens : (k + 1) * tokens, :] = dy_ref[row_block(s_ref[NEAR + k], tokens), :]
+        seq_ref[k * tokens : (k + 1) * tokens, :] = dy_ref[k * tokens : (k + 1) * tokens, :]
     dy = seq_ref[...]
     dmix_ref[...] = contract_cols(dy, whole_ref[...]).astype(bf16)
     for i in range(N_REP):
@@ -1004,8 +1004,7 @@
     pieces = [in_rows] + to_chips([in_rows, in_rows, after(in_rows, normed[1])])
     pieces = pieces + [hop(after(piece, normed[2], normed[3]), "rep", N_REP, 1) for piece in pieces]
     downs = [down_own] + to_chips([after(down_own, *pieces[1:4])] * 3)
-    dy_own = after(cotangent.astype(bf16), *normed[1:3])
-    dy_all = lax.all_gather(dy_own, "shard", axis=0, tiled=True)
+    dy_own = cotangent.astype(bf16)
 
     rope_parts = jnp.asarray(rope_lanes(seq_len)).reshape(N_SHARD, tok_count, 3 * LANES)
     rope = jnp.concatenate(
@@ -1025,6 +1024,8 @@
     block32 = ((tok_count, D), f32)
     half = D // 2
     downs = downs + [hop(after(piece, qkv16), "rep", N_REP, 1) for piece in downs]
+    dys = to_shards([after(dy_own, *pieces[4:])] * 3)
+    dy_all = jnp.concatenate([after(dy_own, qkv16)] + dys, axis=0)
     mixed16 = mix_heads(qkv16, mask)
     out_own, s1, s2, s3, dy_seq, d_mixed16, d_up16, up_sum = single(
         middle_body,

time: 214 us -> 191 us (0.89)
  local copies, waits for them, and re-layouts: 28.5 us -> 4.85 us
  between operations: 25.3 us -> 11.5 us
  waiting for transfers between devices: 63.5 us -> 72.8 us
  starting transfers between devices: 43.4 us -> 52.5 us
    unnamed x157 -> x45, local copies, waits for them, and re-layouts: 26.3 us -> 3.5 us
    ppermute x37 -> x40, waiting for transfers between devices: 60.3 us -> 72.8 us  [hop(): return lax.ppermute(value, axis, [(i, i ^ mask) for i in range(size)])]
    ppermute x37 -> x40, starting transfers between devices: 41.8 us -> 50.9 us  [hop(): return lax.ppermute(value, axis, [(i, i ^ mask) for i in range(size)])]
    all_gather x1 -> x0, waiting for transfers between devices: 3.13 us -> none  [shards(): dy_all = lax.all_gather(dy_own, 'shard', axis=0, tiled=True)]
  transfers between devices with their start and end apart: 40 -> 42, of which waited for: 13 -> 15; matrix products, arithmetic and copies ran while one was open for 3% -> 3% of each run, Pallas kernels for 15% -> 16%
where the time goes in v7:
time: 191 us; the launch traced here: 190 us
  waiting for transfers between devices  72.8 us (38%)
  starting transfers between devices  52.5 us (27%)
  Pallas kernels  43.8 us (23%)
  between operations  11.5 us (6%)
  local copies, waits for them, and re-layouts  4.85 us (3%)
  other arithmetic  4.8 us (3%)
    ppermute x40, waiting for transfers between devices, hop(): return lax.ppermute(value, axis, [(i, i ^ mask) for i in range(size)])  72.8 us
    ppermute x40, starting transfers between devices, hop(): return lax.ppermute(value, axis, [(i, i ^ mask) for i in range(size)])  50.9 us
    pallas_call x10, Pallas kernels, single(): pl.pallas_call(body, out_shape=shapes, grid_spec=pltpu.PrefetchScalarGrid...  20.3 us
    pallas_call x1, Pallas kernels, attend_back(): pl.pallas_call(attend_body, out_shape=(jax.ShapeDtypeStruct((tokens, QKV)...  8.87 us
    pallas_call x1, Pallas kernels, front(): pl.pallas_call(front_body, out_shape=tuple((jax.ShapeDtypeStruct(s, d) fo...  8.59 us
    pallas_call x1, Pallas kernels, mix_heads(): pl.pallas_call(mix_body, out_shape=jax.ShapeDtypeStruct((tokens, OUT), bf...  6.06 us
  transfers between devices with their start and end apart: 42, of which 15 were waited for; matrix products, arithmetic and copies ran while one was open for 3% of the time, Pallas kernels for 16%

profile of v7, /device:TPU:0, one launch (start us, length us, event | category | flops | bytes accessed | tf_op | source)
XLA Modules:
  0.0 190.3 jit_solution(15830276308002634259)
XLA Ops:
  4.9 3.1 %collective-permute-start = (bf16[32,1920]{1,0:T(8,128)(2,1)S(1)}, bf16[32,1920]{1,0:T(8,128)(2,1)S(1)}, u32[]{:S(2)}, u32[]{:S(2)}) collective-permute-start(bf16[32,1920]{1,0:T(8,128)(2,1)S(1)} %get-tuple-element.94), channel_id=1, source_target_pairs={{0,1},{1,0},{2,3},{3,2},{4,5},{5,4},{6,7},{7,6},{8,9},{9,8},{10,11... | collective-permute-start | bytes 368648 | tf_op jit(solution)/shard_map/ppermute | solution.py:132
  8.0 2.6 %collective-permute-start.1 = (bf16[32,1920]{1,0:T(8,128)(2,1)S(1)}, bf16[32,1920]{1,0:T(8,128)(2,1)S(1)}, u32[]{:S(2)}, u32[]{:S(2)}) collective-permute-start(bf16[32,1920]{1,0:T(8,128)(2,1)S(1)} %get-tuple-element.95), channel_id=1, source_target_pairs={{0,2},{1,3},{2,0},{3,1},{4,6},{5,7},{6,4},{7,5},{8,10},{9,11},{10,... | collective-permute-start | bytes 368648 | tf_op jit(solution)/shard_map/ppermute | solution.py:132
  12.6 9.1 %collective-permute-done.1.refs_2_ = bf16[32,1920]{1,0:T(8,128)(2,1)S(1)} collective-permute-done((bf16[32,1920]{1,0:T(8,128)(2,1)S(1)}, bf16[32,1920]{1,0:T(8,128)(2,1)S(1)}, u32[]{:S(2)}, u32[]{:S(2)}) %collective-permute-start.1) | collective-permute-done | bytes 122912 | tf_op jit(solution)/shard_map/ppermute | solution.py:132
  21.7 2.5 %collective-permute-start.3 = (bf16[128,1024]{1,0:T(8,128)(2,1)S(1)}, bf16[128,1024]{1,0:T(8,128)(2,1)S(1)}, u32[]{:S(2)}, u32[]{:S(2)}) collective-permute-start(bf16[128,1024]{1,0:T(8,128)(2,1)S(1)} %norm.1.refs_0_), channel_id=1, source_target_pairs={{0,1},{1,0},{2,3},{3,2},{4,5},{5,4},{6,7},{7,6},{8,9},{9,8},{10,11... | collective-permute-start | bytes 786440 | tf_op jit(solution)/shard_map/ppermute | solution.py:132
  36.6 1.5 collective-permute-start.8
  40.2 1.8 collective-permute-start.5
  42.1 14.7 %collective-permute-done.4.refs_2_ = bf16[128,1024]{1,0:T(8,128)(2,1)S(1)} collective-permute-done((bf16[128,1024]{1,0:T(8,128)(2,1)S(1)}, bf16[128,1024]{1,0:T(8,128)(2,1)S(1)}, u32[]{:S(2)}, u32[]{:S(2)}) %collective-permute-start.4) | collective-permute-done | bytes 262176 | tf_op jit(solution)/shard_map/ppermute | solution.py:132
  57.3 2.4 %collective-permute-done.8.refs_6_.refs_14_.refs_22_ = bf16[128,2176]{1,0:T(8,128)(2,1)S(1)} collective-permute-done((bf16[128,2176]{1,0:T(8,128)(2,1)S(1)}, bf16[128,2176]{1,0:T(8,128)(2,1)S(1)}, u32[]{:S(2)}, u32[]{:S(2)}) %collective-permute-start.8) | collective-permute-done | bytes 557088 | tf_op jit(solution)/shard_map/ppermute | solution.py:132
  62.3 1.8 collective-permute-start.18
  64.7 3.7 %collective-permute-start.16 = (bf16[128,1024]{1,0:T(8,128)(2,1)S(1)}, bf16[128,1024]{1,0:T(8,128)(2,1)S(1)}, u32[]{:S(2)}, u32[]{:S(2)}) collective-permute-start(bf16[128,1024]{1,0:T(8,128)(2,1)S(1)} %get-tuple-element.109), channel_id=1, source_target_pairs={{0,3},{1,2},{2,1},{3,0},{4,7},{5,6},{6,5},{7,4},{8,11},{9,10},{10,... | collective-permute-start | bytes 786440 | tf_op jit(solution)/shard_map/ppermute | solution.py:132
  69.2 8.6 %front.1 = (bf16[256,1024]{1,0:T(8,128)(2,1)S(1)}, bf16[512,1024]{1,0:T(8,128)(2,1)S(1)}, bf16[512,1024]{1,0:T(8,128)(2,1)S(1)}, bf16[512,768]{1,0:T(8,128)(2,1)...) custom-call(s32[21]{0:T(128)S(1)} %pad_add_fusion.1.s_ref, ...), custom_call_target="tpu_custom_call" | custom-call | flops 10350000128 | bytes 1048576 | tf_op jit(solution)/shard_map/front/pallas_call | solution.py:613
  79.0 12.3 %collective-permute-done.15 = bf16[128,1024]{1,0:T(8,128)(2,1)S(1)} collective-permute-done((bf16[128,1024]{1,0:T(8,128)(2,1)S(1)}, bf16[128,1024]{1,0:T(8,128)(2,1)S(1)}, u32[]{:S(2)}, u32[]{:S(2)}) %collective-permute-start.15) | collective-permute-done | bytes 262176 | tf_op jit(solution)/shard_map/ppermute | solution.py:132
  91.3 6.1 %mix_heads.1.mix_ref = bf16[512,256]{1,0:T(8,128)(2,1)S(1)} custom-call(bf16[512,768]{1,0:T(8,128)(2,1)S(1)} %get-tuple-element.105.q_ref.k_ref.v_ref, bf16[512,768]{1,0:T(8,128)(2,1)S(1)} %get-tuple-element.105.q_ref.k_ref.v_ref, bf16[512,768]{1,0:T(8,128)(2,1)S(1)} %get-tuple-element.105.q_ref.k_ref.v_ref, f32[512,512]{1,0:T(8,128)S(1)} %and_select_fusion.mask_ref), custom_call_target="tpu_custom_call" | custom-call | flops 6899999744 | bytes 1048576 | tf_op jit(solution)/shard_map/mix_heads/pallas_call | solution.py:731
  97.5 4.8 %middle.1 = (f32[128,1024]{1,0:T(8,128)S(1)}, bf16[128,1024]{1,0:T(8,128)(2,1)S(1)}, bf16[128,1024]{1,0:T(8,128)(2,1)S(1)}, bf16[128,1024]{1,0:T(8,128)(2,1)S(1)...) custom-call(s32[21]{0:T(128)S(1)} %pad_add_fusion.1.s_ref, ...), custom_call_target="tpu_custom_call" | custom-call | flops 2300000000 | bytes 1048576 | tf_op jit(solution)/shard_map/middle/pallas_call | solution.py:452
  102.3 2.9 %mlp.1 = (f32[512,2048]{1,0:T(8,128)S(1)}, bf16[512,2048]{1,0:T(8,128)(2,1)S(1)}) custom-call(s32[21]{0:T(128)S(1)} %pad_add_fusion.1.s_ref, bf16[512,1024]{1,0:T(8,128)(2,1)S(1)} %get-tuple-element.106.act_ref, bf16[512,1024]{1,0:T(8,128)(2,1)S(1)} %get-tuple-element.122.dy_ref, bf16[512,1024]{1,0:T(8,128)(2,1)S(1)} %get-tuple-element.123.h_ref, ...), custom_call_target="tpu_custom_call" | custom-call | flops 1150000000 | bytes 1048576 | tf_op jit(solution)/shard_map/mlp/pallas_call | solution.py:452
  105.8 3.7 %collective-permute-start.24 = (bf16[128,1024]{1,0:T(8,128)(2,1)S(1)}, bf16[128,1024]{1,0:T(8,128)(2,1)S(1)}, u32[]{:S(2)}, u32[]{:S(2)}) collective-permute-start(bf16[128,1024]{1,0:T(8,128)(2,1)S(1)} %get-tuple-element.118), channel_id=1, source_target_pairs={{0,1},{1,0},{2,3},{3,2},{4,5},{5,4},{6,7},{7,6},{8,9},{9,8},{10,11... | collective-permute-start | bytes 786440 | tf_op jit(solution)/shard_map/ppermute | solution.py:132
  113.9 8.9 %attend_back.1 = (bf16[512,768]{1,0:T(8,128)(2,1)S(1)}, f32[1,768]{1,0:T(1,128)S(1)}) custom-call(bf16[512,768]{1,0:T(8,128)(2,1)S(1)} %get-tuple-element.105.q_ref.k_ref.v_ref, bf16[512,768]{1,0:T(8,128)(2,1)S(1)} %get-tuple-element.105.q_ref.k_ref.v_ref, bf16[512,768]{1,0:T(8,128)(2,1)S(1)} %get-tuple-element.105.q_ref.k_ref.v_ref, ...), custom_call_target="tpu_custom_call" | custom-call | flops 4600000000 | bytes 1048576 | tf_op jit(solution)/shard_map/attend_back/pallas_call | solution.py:746
  122.8 3.2 %collective-permute-start.27 = (bf16[128,1024]{1,0:T(8,128)(2,1)S(1)}, bf16[128,1024]{1,0:T(8,128)(2,1)S(1)}, u32[]{:S(2)}, u32[]{:S(2)}) collective-permute-start(bf16[128,1024]{1,0:T(8,128)(2,1)S(1)} %get-tuple-element.128), channel_id=1, source_target_pairs={{0,3},{1,2},{2,1},{3,0},{4,7},{5,6},{6,5},{7,4},{8,11},{9,10},{10,... | collective-permute-start | bytes 786440 | tf_op jit(solution)/shard_map/ppermute | solution.py:132
  126.0 2.9 %back.1 = (f32[128,1024]{1,0:T(8,128)S(1)}, bf16[128,1024]{1,0:T(8,128)(2,1)S(1)}, bf16[128,1024]{1,0:T(8,128)(2,1)S(1)}, bf16[128,1024]{1,0:T(8,128)(2,1)S(1)}, f32[8,1024]{1,0:T(8,128)S(1)}) custom-call(s32[21]{0:T(128)S(1)} %pad_add_fusion.1.s_ref, bf16[512,768]{1,0:T(8,128)(2,1)S(1)} %get-tuple-element.129.dqkv_ref, ...), custom_call_target="tpu_custom_call" | custom-call | flops 1150000000 | bytes 1048576 | tf_op jit(solution)/shard_map/back/pallas_call | solution.py:452
  128.9 3.5 %collective-permute-done.27 = bf16[128,1024]{1,0:T(8,128)(2,1)S(1)} collective-permute-done((bf16[128,1024]{1,0:T(8,128)(2,1)S(1)}, bf16[128,1024]{1,0:T(8,128)(2,1)S(1)}, u32[]{:S(2)}, u32[]{:S(2)}) %collective-permute-start.27) | collective-permute-done | bytes 262176 | tf_op jit(solution)/shard_map/ppermute | solution.py:132
  132.5 3.0 %collective-permute-done.31.refs_2_ = bf16[128,2048]{1,0:T(8,128)(2,1)S(1)} collective-permute-done((bf16[128,2048]{1,0:T(8,128)(2,1)S(1)}, bf16[128,2048]{1,0:T(8,128)(2,1)S(1)}, u32[]{:S(2)}, u32[]{:S(2)}) %collective-permute-start.31) | collective-permute-done | bytes 524320 | tf_op jit(solution)/shard_map/ppermute | solution.py:132
  136.6 1.9 %terms.1 = (f32[512,1152]{1,0:T(8,128)S(1)}, bf16[512,1152]{1,0:T(8,128)(2,1)S(1)}) custom-call(s32[21]{0:T(128)S(1)} %pad_add_fusion.1.s_ref, bf16[512,1024]{1,0:T(8,128)(2,1)S(1)} %get-tuple-element.137.h_ref, bf16[512,768]{1,0:T(8,128)(2,1)S(1)} %get-tuple-element.129.dqkv_ref, bf16[512,256]{1,0:T(8,128)(2,1)S(1)} %mix_heads.1.mix_ref, ...), custom_call_target="tpu_custom_call" | custom-call | flops 4600000000 | bytes 1048576 | tf_op jit(solution)/shard_map/terms/pallas_call | solution.py:452
  138.6 2.8 %collective-permute-done.33 = bf16[4,128,1152]{2,1,0:T(8,128)(2,1)S(1)} collective-permute-done((bf16[4,128,1152]{2,1,0:T(8,128)(2,1)S(1)}, bf16[4,128,1152]{2,1,0:T(8,128)(2,1)S(1)}, u32[]{:S(2)}, u32[]{:S(2)}) %collective-permute-start.33) | collective-permute-done | bytes 1179680 | tf_op jit(solution)/shard_map/ppermute | solution.py:132
  145.7 3.4 %collective-permute-start.29 = (bf16[128,1024]{1,0:T(8,128)(2,1)S(1)}, bf16[128,1024]{1,0:T(8,128)(2,1)S(1)}, u32[]{:S(2)}, u32[]{:S(2)}) collective-permute-start(bf16[128,1024]{1,0:T(8,128)(2,1)S(1)} %get-tuple-element.133), channel_id=1, source_target_pairs={{0,2},{1,3},{2,0},{3,1},{4,6},{5,7},{6,4},{7,5},{8,10},{9,11},{10,... | collective-permute-start | bytes 786440 | tf_op jit(solution)/shard_map/ppermute | solution.py:132
  150.0 8.1 %collective-permute-done.28.r1_ref = bf16[128,1024]{1,0:T(8,128)(2,1)S(1)} collective-permute-done((bf16[128,1024]{1,0:T(8,128)(2,1)S(1)}, bf16[128,1024]{1,0:T(8,128)(2,1)S(1)}, u32[]{:S(2)}, u32[]{:S(2)}) %collective-permute-start.28) | collective-permute-done | bytes 262176 | tf_op jit(solution)/shard_map/ppermute | solution.py:132
  158.1 2.1 %collective-permute-done.29.r2_ref = bf16[128,1024]{1,0:T(8,128)(2,1)S(1)} collective-permute-done((bf16[128,1024]{1,0:T(8,128)(2,1)S(1)}, bf16[128,1024]{1,0:T(8,128)(2,1)S(1)}, u32[]{:S(2)}, u32[]{:S(2)}) %collective-permute-start.29) | collective-permute-done | bytes 262176 | tf_op jit(solution)/shard_map/ppermute | solution.py:132
  160.2 2.5 %collective-permute-start.35 = (bf16[128,1024]{1,0:T(8,128)(2,1)S(1)}, bf16[128,1024]{1,0:T(8,128)(2,1)S(1)}, u32[]{:S(2)}, u32[]{:S(2)}) collective-permute-start(bf16[128,1024]{1,0:T(8,128)(2,1)S(1)} %get-tuple-element.144), channel_id=1, source_target_pairs={{0,3},{1,2},{2,1},{3,0},{4,7},{5,6},{6,5},{7,4},{8,11},{9,10},{10,... | collective-permute-start | bytes 786440 | tf_op jit(solution)/shard_map/ppermute | solution.py:132
  164.6 1.5 multiply_subtract_fusion
  167.0 3.6 %collective-permute-start.39 = (bf16[32,1920]{1,0:T(8,128)(2,1)S(1)}, bf16[32,1920]{1,0:T(8,128)(2,1)S(1)}, u32[]{:S(2)}, u32[]{:S(2)}) collective-permute-start(bf16[32,1920]{1,0:T(8,128)(2,1)S(1)} %get-tuple-element.151), channel_id=1, source_target_pairs={{0,2},{1,3},{2,0},{3,1},{4,6},{5,7},{6,4},{7,5},{8,10},{9,11},{10,... | collective-permute-start | bytes 368648 | tf_op jit(solution)/shard_map/ppermute | solution.py:132
  172.9 1.9 %finish.1 = f32[128,1024]{1,0:T(8,128)} custom-call(s32[21]{0:T(128)S(1)} %pad_add_fusion.1.s_ref, f32[128,1024]{1,0:T(8,128)S(1)} %get-tuple-element.131.own_ref, bf16[128,1024]{1,0:T(8,128)(2,1)S(1)} %collective-permute-done.28.r1_ref, bf16[128,1024]{1,0:T(8,128)(2,1)S(1)} %collective-permute-done.29.r2_ref, ...), custom_call_target="tpu_custom_call" | custom-call | flops 2300000000 | bytes 1048576 | tf_op jit(solution)/shard_map/finish/pallas_call | solution.py:452
  175.3 11.5 %collective-permute-done.39.refs_2_ = bf16[32,1920]{1,0:T(8,128)(2,1)S(1)} collective-permute-done((bf16[32,1920]{1,0:T(8,128)(2,1)S(1)}, bf16[32,1920]{1,0:T(8,128)(2,1)S(1)}, u32[]{:S(2)}, u32[]{:S(2)}) %collective-permute-start.39) | collective-permute-done | bytes 122912 | tf_op jit(solution)/shard_map/ppermute | solution.py:132
  186.8 2.8 %adam.1 = (f32[32,3072]{1,0:T(8,128)}, f32[32,3072]{1,0:T(8,128)}, f32[32,3072]{1,0:T(8,128)}, f32[32,3072]{1,0:T(8,128)}, f32[32,4096]{1,0:T(8,128)}, /*index=5...) custom-call(s32[21]{0:T(128)S(1)} %pad_add_fusion.1.s_ref, ...), custom_call_target="tpu_custom_call" | custom-call | flops 3449999872 | bytes 1048576 | tf_op jit(solution)/shard_map/adam/pallas_call | solution.py:452
  (130 shorter events, 33.5 us)
Async XLA Ops:
  8.0 13.8 %collective-permute-start.1 = (bf16[32,1920]{1,0:T(8,128)(2,1)S(1)}, bf16[32,1920]{1,0:T(8,128)(2,1)S(1)}, u32[]{:S(2)}, u32[]{:S(2)}) collective-permute-start(bf16[32,1920]{1,0:T(8,128)(2,1)S(1)} %get-tuple-element.95), channel_id=1, source_target_pairs={{0,2},{1,3},{2,0},{3,1},{4,6},{5,7},{6,4},{7,5},{8,10},{9,11},{10,... | collective-permute-start | bytes 368648 | tf_op jit(solution)/shard_map/ppermute | solution.py:132
  10.5 11.2 %collective-permute-start.2 = (bf16[32,1920]{1,0:T(8,128)(2,1)S(1)}, bf16[32,1920]{1,0:T(8,128)(2,1)S(1)}, u32[]{:S(2)}, u32[]{:S(2)}) collective-permute-start(bf16[32,1920]{1,0:T(8,128)(2,1)S(1)} %get-tuple-element.96), channel_id=1, source_target_pairs={{0,3},{1,2},{2,1},{3,0},{4,7},{5,6},{6,5},{7,4},{8,11},{9,10},{10,... | collective-permute-start | bytes 368648 | tf_op jit(solution)/shard_map/ppermute | solution.py:132
  10.6 24.7 %collective-permute-start.6 = (bf16[32,1024]{1,0:T(8,128)(2,1)S(1)}, bf16[32,1024]{1,0:T(8,128)(2,1)S(1)}, u32[]{:S(2)}, u32[]{:S(2)}) collective-permute-start(bf16[32,1024]{1,0:T(8,128)(2,1)S(1)} %convert_element_type.93), channel_id=1, source_target_pairs={{0,0},{1,4},{2,8},{3,12},{4,1},{5,5},{6,9},{7,13},{8,2},{9,6},{10,... | collective-permute-start | bytes 196616 | tf_op jit(solution)/shard_map/ppermute | solution.py:984
  21.7 16.4 %collective-permute-start.3 = (bf16[128,1024]{1,0:T(8,128)(2,1)S(1)}, bf16[128,1024]{1,0:T(8,128)(2,1)S(1)}, u32[]{:S(2)}, u32[]{:S(2)}) collective-permute-start(bf16[128,1024]{1,0:T(8,128)(2,1)S(1)} %norm.1.refs_0_), channel_id=1, source_target_pairs={{0,1},{1,0},{2,3},{3,2},{4,5},{5,4},{6,7},{7,6},{8,9},{9,8},{10,11... | collective-permute-start | bytes 786440 | tf_op jit(solution)/shard_map/ppermute | solution.py:132
  35.9 20.9 %collective-permute-start.7 = (bf16[128,2176]{1,0:T(8,128)(2,1)S(1)}, bf16[128,2176]{1,0:T(8,128)(2,1)S(1)}, u32[]{:S(2)}, u32[]{:S(2)}) collective-permute-start(bf16[128,2176]{1,0:T(8,128)(2,1)S(1)} %join.1.refs_4_.refs_12_.refs_20_), channel_id=1, source_target_pairs={{0,8},{4,12},{8,0},{12,4},{16,24},{20,28},{24,16},{28,20},{1,9},{5... | collective-permute-start | bytes 1671176 | tf_op jit(solution)/shard_map/ppermute | solution.py:132
  36.6 23.1 %collective-permute-start.8 = (bf16[128,2176]{1,0:T(8,128)(2,1)S(1)}, bf16[128,2176]{1,0:T(8,128)(2,1)S(1)}, u32[]{:S(2)}, u32[]{:S(2)}) collective-permute-start(bf16[128,2176]{1,0:T(8,128)(2,1)S(1)} %join.1.refs_4_.refs_12_.refs_20_), channel_id=1, source_target_pairs={{0,16},{4,20},{8,24},{12,28},{16,0},{20,4},{24,8},{28,12},{1,17},{... | collective-permute-start | bytes 1671176 | tf_op jit(solution)/shard_map/ppermute | solution.py:132
  38.1 22.8 %collective-permute-start.9 = (bf16[128,2176]{1,0:T(8,128)(2,1)S(1)}, bf16[128,2176]{1,0:T(8,128)(2,1)S(1)}, u32[]{:S(2)}, u32[]{:S(2)}) collective-permute-start(bf16[128,2176]{1,0:T(8,128)(2,1)S(1)} %join.1.refs_4_.refs_12_.refs_20_), channel_id=1, source_target_pairs={{0,24},{4,28},{8,16},{12,20},{16,8},{20,12},{24,0},{28,4},{1,25},{... | collective-permute-start | bytes 1671176 | tf_op jit(solution)/shard_map/ppermute | solution.py:132
  39.6 17.2 %collective-permute-start.4 = (bf16[128,1024]{1,0:T(8,128)(2,1)S(1)}, bf16[128,1024]{1,0:T(8,128)(2,1)S(1)}, u32[]{:S(2)}, u32[]{:S(2)}) collective-permute-start(bf16[128,1024]{1,0:T(8,128)(2,1)S(1)} %norm.1.refs_0_), channel_id=1, source_target_pairs={{0,2},{1,3},{2,0},{3,1},{4,6},{5,7},{6,4},{7,5},{8,10},{9,11},{10,... | collective-permute-start | bytes 786440 | tf_op jit(solution)/shard_map/ppermute | solution.py:132
  40.2 16.6 %collective-permute-start.5 = (bf16[128,1024]{1,0:T(8,128)(2,1)S(1)}, bf16[128,1024]{1,0:T(8,128)(2,1)S(1)}, u32[]{:S(2)}, u32[]{:S(2)}) collective-permute-start(bf16[128,1024]{1,0:T(8,128)(2,1)S(1)} %norm.1.refs_0_), channel_id=1, source_target_pairs={{0,3},{1,2},{2,1},{3,0},{4,7},{5,6},{6,5},{7,4},{8,11},{9,10},{10,... | collective-permute-start | bytes 786440 | tf_op jit(solution)/shard_map/ppermute | solution.py:132
  61.2 16.7 %collective-permute-start.17 = (bf16[128,1024]{1,0:T(8,128)(2,1)S(1)}, bf16[128,1024]{1,0:T(8,128)(2,1)S(1)}, u32[]{:S(2)}, u32[]{:S(2)}) collective-permute-start(bf16[128,1024]{1,0:T(8,128)(2,1)S(1)} %convert_element_type.95.refs_0_), channel_id=1, source_target_pairs={{0,8},{4,12},{8,0},{12,4},{16,24},{20,28},{24,16},{28,20},{1,9},{5... | collective-permute-start | bytes 786440 | tf_op jit(solution)/shard_map/ppermute | solution.py:132
  62.3 16.1 %collective-permute-start.18 = (bf16[128,1024]{1,0:T(8,128)(2,1)S(1)}, bf16[128,1024]{1,0:T(8,128)(2,1)S(1)}, u32[]{:S(2)}, u32[]{:S(2)}) collective-permute-start(bf16[128,1024]{1,0:T(8,128)(2,1)S(1)} %convert_element_type.95.refs_0_), channel_id=1, source_target_pairs={{0,16},{4,20},{8,24},{12,28},{16,0},{20,4},{24,8},{28,12},{1,17},{... | collective-permute-start | bytes 786440 | tf_op jit(solution)/shard_map/ppermute | solution.py:132
  64.1 14.3 %collective-permute-start.19 = (bf16[128,1024]{1,0:T(8,128)(2,1)S(1)}, bf16[128,1024]{1,0:T(8,128)(2,1)S(1)}, u32[]{:S(2)}, u32[]{:S(2)}) collective-permute-start(bf16[128,1024]{1,0:T(8,128)(2,1)S(1)} %convert_element_type.95.refs_0_), channel_id=1, source_target_pairs={{0,24},{4,28},{8,16},{12,20},{16,8},{20,12},{24,0},{28,4},{1,25},{... | collective-permute-start | bytes 786440 | tf_op jit(solution)/shard_map/ppermute | solution.py:132
  64.7 14.2 %collective-permute-start.16 = (bf16[128,1024]{1,0:T(8,128)(2,1)S(1)}, bf16[128,1024]{1,0:T(8,128)(2,1)S(1)}, u32[]{:S(2)}, u32[]{:S(2)}) collective-permute-start(bf16[128,1024]{1,0:T(8,128)(2,1)S(1)} %get-tuple-element.109), channel_id=1, source_target_pairs={{0,3},{1,2},{2,1},{3,0},{4,7},{5,6},{6,5},{7,4},{8,11},{9,10},{10,... | collective-permute-start | bytes 786440 | tf_op jit(solution)/shard_map/ppermute | solution.py:132
  68.4 22.9 %collective-permute-start.15 = (bf16[128,1024]{1,0:T(8,128)(2,1)S(1)}, bf16[128,1024]{1,0:T(8,128)(2,1)S(1)}, u32[]{:S(2)}, u32[]{:S(2)}) collective-permute-start(bf16[128,1024]{1,0:T(8,128)(2,1)S(1)} %get-tuple-element.109), channel_id=1, source_target_pairs={{0,2},{1,3},{2,0},{3,1},{4,6},{5,7},{6,4},{7,5},{8,10},{9,11},{10,... | collective-permute-start | bytes 786440 | tf_op jit(solution)/shard_map/ppermute | solution.py:132
  77.8 19.5 %collective-permute-start.14 = (bf16[128,1024]{1,0:T(8,128)(2,1)S(1)}, bf16[128,1024]{1,0:T(8,128)(2,1)S(1)}, u32[]{:S(2)}, u32[]{:S(2)}) collective-permute-start(bf16[128,1024]{1,0:T(8,128)(2,1)S(1)} %get-tuple-element.109), channel_id=1, source_target_pairs={{0,1},{1,0},{2,3},{3,2},{4,5},{5,4},{6,7},{7,6},{8,9},{9,8},{10,11... | collective-permute-start | bytes 786440 | tf_op jit(solution)/shard_map/ppermute | solution.py:132
  78.4 19.1 %collective-permute-start.20 = (bf16[128,1024]{1,0:T(8,128)(2,1)S(1)}, bf16[128,1024]{1,0:T(8,128)(2,1)S(1)}, u32[]{:S(2)}, u32[]{:S(2)}) collective-permute-start(bf16[128,1024]{1,0:T(8,128)(2,1)S(1)} %convert_element_type.95.refs_0_), channel_id=1, source_target_pairs={{0,4},{4,0},{8,12},{12,8},{16,20},{20,16},{24,28},{28,24},{1,5},{5... | collective-permute-start | bytes 786440 | tf_op jit(solution)/shard_map/ppermute | solution.py:132
  78.4 19.1 %collective-permute-start.21 = (bf16[128,1024]{1,0:T(8,128)(2,1)S(1)}, bf16[128,1024]{1,0:T(8,128)(2,1)S(1)}, u32[]{:S(2)}, u32[]{:S(2)}) collective-permute-start(bf16[128,1024]{1,0:T(8,128)(2,1)S(1)} %collective-permute-done.17.refs_1_), channel_id=1, source_target_pairs={{0,4},{4,0},{8,12},{12,8},{16,20},{20,16},{24,28},{28,24},{1,5},{5... | collective-permute-start | bytes 786440 | tf_op jit(solution)/shard_map/ppermute | solution.py:132
  78.9 18.6 %collective-permute-start.22 = (bf16[128,1024]{1,0:T(8,128)(2,1)S(1)}, bf16[128,1024]{1,0:T(8,128)(2,1)S(1)}, u32[]{:S(2)}, u32[]{:S(2)}) collective-permute-start(bf16[128,1024]{1,0:T(8,128)(2,1)S(1)} %collective-permute-done.18.refs_2_), channel_id=1, source_target_pairs={{0,4},{4,0},{8,12},{12,8},{16,20},{20,16},{24,28},{28,24},{1,5},{5... | collective-permute-start | bytes 786440 | tf_op jit(solution)/shard_map/ppermute | solution.py:132
  105.8 17.0 %collective-permute-start.25 = (bf16[128,1024]{1,0:T(8,128)(2,1)S(1)}, bf16[128,1024]{1,0:T(8,128)(2,1)S(1)}, u32[]{:S(2)}, u32[]{:S(2)}) collective-permute-start(bf16[128,1024]{1,0:T(8,128)(2,1)S(1)} %get-tuple-element.119), channel_id=1, source_target_pairs={{0,2},{1,3},{2,0},{3,1},{4,6},{5,7},{6,4},{7,5},{8,10},{9,11},{10,... | collective-permute-start | bytes 786440 | tf_op jit(solution)/shard_map/ppermute | solution.py:132
  105.8 20.2 %collective-permute-start.24 = (bf16[128,1024]{1,0:T(8,128)(2,1)S(1)}, bf16[128,1024]{1,0:T(8,128)(2,1)S(1)}, u32[]{:S(2)}, u32[]{:S(2)}) collective-permute-start(bf16[128,1024]{1,0:T(8,128)(2,1)S(1)} %get-tuple-element.118), channel_id=1, source_target_pairs={{0,1},{1,0},{2,3},{3,2},{4,5},{5,4},{6,7},{7,6},{8,9},{9,8},{10,11... | collective-permute-start | bytes 786440 | tf_op jit(solution)/shard_map/ppermute | solution.py:132
  110.3 22.2 %collective-permute-start.30 = (bf16[128,2048]{1,0:T(8,128)(2,1)S(1)}, bf16[128,2048]{1,0:T(8,128)(2,1)S(1)}, u32[]{:S(2)}, u32[]{:S(2)}) collective-permute-start(bf16[128,2048]{1,0:T(8,128)(2,1)S(1)} %get-tuple-element.176), channel_id=1, source_target_pairs={{0,8},{4,12},{8,0},{12,4},{16,24},{20,28},{24,16},{28,20},{1,9},{5... | collective-permute-start | bytes 1572872 | tf_op jit(solution)/shard_map/ppermute | solution.py:132
  111.5 23.9 %collective-permute-start.31 = (bf16[128,2048]{1,0:T(8,128)(2,1)S(1)}, bf16[128,2048]{1,0:T(8,128)(2,1)S(1)}, u32[]{:S(2)}, u32[]{:S(2)}) collective-permute-start(bf16[128,2048]{1,0:T(8,128)(2,1)S(1)} %get-tuple-element.175), channel_id=1, source_target_pairs={{0,16},{4,20},{8,24},{12,28},{16,0},{20,4},{24,8},{28,12},{1,17},{... | collective-permute-start | bytes 1572872 | tf_op jit(solution)/shard_map/ppermute | solution.py:132
  112.7 23.8 %collective-permute-start.32 = (bf16[128,2048]{1,0:T(8,128)(2,1)S(1)}, bf16[128,2048]{1,0:T(8,128)(2,1)S(1)}, u32[]{:S(2)}, u32[]{:S(2)}) collective-permute-start(bf16[128,2048]{1,0:T(8,128)(2,1)S(1)} %get-tuple-element.174), channel_id=1, source_target_pairs={{0,24},{4,28},{8,16},{12,20},{16,8},{20,12},{24,0},{28,4},{1,25},{... | collective-permute-start | bytes 1572872 | tf_op jit(solution)/shard_map/ppermute | solution.py:132
  122.8 9.7 %collective-permute-start.27 = (bf16[128,1024]{1,0:T(8,128)(2,1)S(1)}, bf16[128,1024]{1,0:T(8,128)(2,1)S(1)}, u32[]{:S(2)}, u32[]{:S(2)}) collective-permute-start(bf16[128,1024]{1,0:T(8,128)(2,1)S(1)} %get-tuple-element.128), channel_id=1, source_target_pairs={{0,3},{1,2},{2,1},{3,0},{4,7},{5,6},{6,5},{7,4},{8,11},{9,10},{10,... | collective-permute-start | bytes 786440 | tf_op jit(solution)/shard_map/ppermute | solution.py:132
  141.6 18.6 %collective-permute-start.34 = (bf16[128,1152]{1,0:T(8,128)(2,1)S(1)}, bf16[128,1152]{1,0:T(8,128)(2,1)S(1)}, u32[]{:S(2)}, u32[]{:S(2)}) collective-permute-start(bf16[128,1152]{1,0:T(8,128)(2,1)S(1)} %get-tuple-element.143), channel_id=1, source_target_pairs={{0,8},{4,12},{8,0},{12,4},{16,24},{20,28},{24,16},{28,20},{1,9},{5... | collective-permute-start | bytes 884744 | tf_op jit(solution)/shard_map/ppermute | solution.py:132
  142.7 20.0 %collective-permute-start.36 = (bf16[128,1152]{1,0:T(8,128)(2,1)S(1)}, bf16[128,1152]{1,0:T(8,128)(2,1)S(1)}, u32[]{:S(2)}, u32[]{:S(2)}) collective-permute-start(bf16[128,1152]{1,0:T(8,128)(2,1)S(1)} %get-tuple-element.146), channel_id=1, source_target_pairs={{0,16},{4,20},{8,24},{12,28},{16,0},{20,4},{24,8},{28,12},{1,17},{... | collective-permute-start | bytes 884744 | tf_op jit(solution)/shard_map/ppermute | solution.py:132
  144.0 18.7 %collective-permute-start.37 = (bf16[128,1152]{1,0:T(8,128)(2,1)S(1)}, bf16[128,1152]{1,0:T(8,128)(2,1)S(1)}, u32[]{:S(2)}, u32[]{:S(2)}) collective-permute-start(bf16[128,1152]{1,0:T(8,128)(2,1)S(1)} %get-tuple-element.147), channel_id=1, source_target_pairs={{0,24},{4,28},{8,16},{12,20},{16,8},{20,12},{24,0},{28,4},{1,25},{... | collective-permute-start | bytes 884744 | tf_op jit(solution)/shard_map/ppermute | solution.py:132
  145.2 12.9 %collective-permute-start.28 = (bf16[128,1024]{1,0:T(8,128)(2,1)S(1)}, bf16[128,1024]{1,0:T(8,128)(2,1)S(1)}, u32[]{:S(2)}, u32[]{:S(2)}) collective-permute-start(bf16[128,1024]{1,0:T(8,128)(2,1)S(1)} %get-tuple-element.132), channel_id=1, source_target_pairs={{0,1},{1,0},{2,3},{3,2},{4,5},{5,4},{6,7},{7,6},{8,9},{9,8},{10,11... | collective-permute-start | bytes 786440 | tf_op jit(solution)/shard_map/ppermute | solution.py:132
  145.7 14.5 %collective-permute-start.29 = (bf16[128,1024]{1,0:T(8,128)(2,1)S(1)}, bf16[128,1024]{1,0:T(8,128)(2,1)S(1)}, u32[]{:S(2)}, u32[]{:S(2)}) collective-permute-start(bf16[128,1024]{1,0:T(8,128)(2,1)S(1)} %get-tuple-element.133), channel_id=1, source_target_pairs={{0,2},{1,3},{2,0},{3,1},{4,6},{5,7},{6,4},{7,5},{8,10},{9,11},{10,... | collective-permute-start | bytes 786440 | tf_op jit(solution)/shard_map/ppermute | solution.py:132
  160.2 12.6 %collective-permute-start.35 = (bf16[128,1024]{1,0:T(8,128)(2,1)S(1)}, bf16[128,1024]{1,0:T(8,128)(2,1)S(1)}, u32[]{:S(2)}, u32[]{:S(2)}) collective-permute-start(bf16[128,1024]{1,0:T(8,128)(2,1)S(1)} %get-tuple-element.144), channel_id=1, source_target_pairs={{0,3},{1,2},{2,1},{3,0},{4,7},{5,6},{6,5},{7,4},{8,11},{9,10},{10,... | collective-permute-start | bytes 786440 | tf_op jit(solution)/shard_map/ppermute | solution.py:132
  167.0 19.8 %collective-permute-start.39 = (bf16[32,1920]{1,0:T(8,128)(2,1)S(1)}, bf16[32,1920]{1,0:T(8,128)(2,1)S(1)}, u32[]{:S(2)}, u32[]{:S(2)}) collective-permute-start(bf16[32,1920]{1,0:T(8,128)(2,1)S(1)} %get-tuple-element.151), channel_id=1, source_target_pairs={{0,2},{1,3},{2,0},{3,1},{4,6},{5,7},{6,4},{7,5},{8,10},{9,11},{10,... | collective-permute-start | bytes 368648 | tf_op jit(solution)/shard_map/ppermute | solution.py:132
  170.5 16.2 %collective-permute-start.40 = (bf16[32,1920]{1,0:T(8,128)(2,1)S(1)}, bf16[32,1920]{1,0:T(8,128)(2,1)S(1)}, u32[]{:S(2)}, u32[]{:S(2)}) collective-permute-start(bf16[32,1920]{1,0:T(8,128)(2,1)S(1)} %get-tuple-element.152), channel_id=1, source_target_pairs={{0,3},{1,2},{2,1},{3,0},{4,7},{5,6},{6,5},{7,4},{8,11},{9,10},{10,... | collective-permute-start | bytes 368648 | tf_op jit(solution)/shard_map/ppermute | solution.py:132
  (32 other events, 280.2 us)

commit v8 on v7

--- a/solution.py
+++ b/solution.py
@@ -1084,7 +1084,7 @@
     qkv_got = hop(qkv_sent.reshape(4, LANES, wide), "rep", N_REP, 1)
     qkv_parts = sum_rep(qkv_keep.reshape(4, LANES, wide), qkv_got, *mlp_parts[1:])
     e_got = [hop(e_sent[0], "shard", N_SHARD, 1), hop(e_sent[1], "shard", N_SHARD, 2)]
-    e_got.append(hop(after(e_sent[2], qkv_parts[1]), "shard", N_SHARD, 3))
+    e_got.append(hop(after(e_sent[2], e_got[0]), "shard", N_SHARD, 3))
     narrow = (rows, QKV + UP + LANES)
     g_own, g1, g2, g3, out_sum = single(
         fold_body,

time: 191 us -> 191 us (level)
  waiting for transfers between devices: 72.8 us -> 75.1 us
  starting transfers between devices: 52.5 us -> 50.3 us
    ppermute x40, waiting for transfers between devices: 72.8 us -> 75.1 us  [hop(): return lax.ppermute(value, axis, [(i, i ^ mask) for i in range(size)])]
    ppermute x40, starting transfers between devices: 50.9 us -> 48.8 us  [hop(): return lax.ppermute(value, axis, [(i, i ^ mask) for i in range(size)])]
  transfers between devices with their start and end apart: 42 -> 42, of which waited for: 15 -> 15; matrix products, arithmetic and copies ran while one was open for 3% -> 2% of each run, Pallas kernels for 16% -> 18%
where the time goes in v8:
time: 191 us; the launch traced here: 190 us
  waiting for transfers between devices  75.1 us (39%)
  starting transfers between devices  50.3 us (26%)
  Pallas kernels  43.8 us (23%)
  between operations  11.5 us (6%)
  local copies, waits for them, and re-layouts  4.84 us (3%)
  other arithmetic  4.8 us (3%)
    ppermute x40, waiting for transfers between devices, hop(): return lax.ppermute(value, axis, [(i, i ^ mask) for i in range(size)])  75.1 us
    ppermute x40, starting transfers between devices, hop(): return lax.ppermute(value, axis, [(i, i ^ mask) for i in range(size)])  48.8 us
    pallas_call x10, Pallas kernels, single(): pl.pallas_call(body, out_shape=shapes, grid_spec=pltpu.PrefetchScalarGrid...  20.3 us
    pallas_call x1, Pallas kernels, attend_back(): pl.pallas_call(attend_body, out_shape=(jax.ShapeDtypeStruct((tokens, QKV)...  8.86 us
    pallas_call x1, Pallas kernels, front(): pl.pallas_call(front_body, out_shape=tuple((jax.ShapeDtypeStruct(s, d) fo...  8.59 us
    pallas_call x1, Pallas kernels, mix_heads(): pl.pallas_call(mix_body, out_shape=jax.ShapeDtypeStruct((tokens, OUT), bf...  6.06 us
  transfers between devices with their start and end apart: 42, of which 15 were waited for; matrix products, arithmetic and copies ran while one was open for 2% of the time, Pallas kernels for 18%

profile of v8, /device:TPU:0, one launch (start us, length us, event | category | flops | bytes accessed | tf_op | source)
XLA Modules:
  0.0 190.4 jit_solution(2840907662130139100)
XLA Ops:
  4.9 3.1 %collective-permute-start = (bf16[32,1920]{1,0:T(8,128)(2,1)S(1)}, bf16[32,1920]{1,0:T(8,128)(2,1)S(1)}, u32[]{:S(2)}, u32[]{:S(2)}) collective-permute-start(bf16[32,1920]{1,0:T(8,128)(2,1)S(1)} %get-tuple-element.94), channel_id=1, source_target_pairs={{0,1},{1,0},{2,3},{3,2},{4,5},{5,4},{6,7},{7,6},{8,9},{9,8},{10,11... | collective-permute-start | bytes 368648 | tf_op jit(solution)/shard_map/ppermute | solution.py:132
  8.0 2.6 %collective-permute-start.1 = (bf16[32,1920]{1,0:T(8,128)(2,1)S(1)}, bf16[32,1920]{1,0:T(8,128)(2,1)S(1)}, u32[]{:S(2)}, u32[]{:S(2)}) collective-permute-start(bf16[32,1920]{1,0:T(8,128)(2,1)S(1)} %get-tuple-element.95), channel_id=1, source_target_pairs={{0,2},{1,3},{2,0},{3,1},{4,6},{5,7},{6,4},{7,5},{8,10},{9,11},{10,... | collective-permute-start | bytes 368648 | tf_op jit(solution)/shard_map/ppermute | solution.py:132
  12.6 9.1 %collective-permute-done.1.refs_2_ = bf16[32,1920]{1,0:T(8,128)(2,1)S(1)} collective-permute-done((bf16[32,1920]{1,0:T(8,128)(2,1)S(1)}, bf16[32,1920]{1,0:T(8,128)(2,1)S(1)}, u32[]{:S(2)}, u32[]{:S(2)}) %collective-permute-start.1) | collective-permute-done | bytes 122912 | tf_op jit(solution)/shard_map/ppermute | solution.py:132
  21.7 2.5 %collective-permute-start.3 = (bf16[128,1024]{1,0:T(8,128)(2,1)S(1)}, bf16[128,1024]{1,0:T(8,128)(2,1)S(1)}, u32[]{:S(2)}, u32[]{:S(2)}) collective-permute-start(bf16[128,1024]{1,0:T(8,128)(2,1)S(1)} %norm.1.refs_0_), channel_id=1, source_target_pairs={{0,1},{1,0},{2,3},{3,2},{4,5},{5,4},{6,7},{7,6},{8,9},{9,8},{10,11... | collective-permute-start | bytes 786440 | tf_op jit(solution)/shard_map/ppermute | solution.py:132
  40.2 1.8 collective-permute-start.5
  42.1 14.7 %collective-permute-done.4.refs_2_ = bf16[128,1024]{1,0:T(8,128)(2,1)S(1)} collective-permute-done((bf16[128,1024]{1,0:T(8,128)(2,1)S(1)}, bf16[128,1024]{1,0:T(8,128)(2,1)S(1)}, u32[]{:S(2)}, u32[]{:S(2)}) %collective-permute-start.4) | collective-permute-done | bytes 262176 | tf_op jit(solution)/shard_map/ppermute | solution.py:132
  57.3 2.4 %collective-permute-done.8.refs_6_.refs_14_.refs_22_ = bf16[128,2176]{1,0:T(8,128)(2,1)S(1)} collective-permute-done((bf16[128,2176]{1,0:T(8,128)(2,1)S(1)}, bf16[128,2176]{1,0:T(8,128)(2,1)S(1)}, u32[]{:S(2)}, u32[]{:S(2)}) %collective-permute-start.8) | collective-permute-done | bytes 557088 | tf_op jit(solution)/shard_map/ppermute | solution.py:132
  62.3 1.8 collective-permute-start.18
  64.7 3.7 %collective-permute-start.16 = (bf16[128,1024]{1,0:T(8,128)(2,1)S(1)}, bf16[128,1024]{1,0:T(8,128)(2,1)S(1)}, u32[]{:S(2)}, u32[]{:S(2)}) collective-permute-start(bf16[128,1024]{1,0:T(8,128)(2,1)S(1)} %get-tuple-element.109), channel_id=1, source_target_pairs={{0,3},{1,2},{2,1},{3,0},{4,7},{5,6},{6,5},{7,4},{8,11},{9,10},{10,... | collective-permute-start | bytes 786440 | tf_op jit(solution)/shard_map/ppermute | solution.py:132
  69.2 8.6 %front.1 = (bf16[256,1024]{1,0:T(8,128)(2,1)S(1)}, bf16[512,1024]{1,0:T(8,128)(2,1)S(1)}, bf16[512,1024]{1,0:T(8,128)(2,1)S(1)}, bf16[512,768]{1,0:T(8,128)(2,1)...) custom-call(s32[21]{0:T(128)S(1)} %pad_add_fusion.1.s_ref, ...), custom_call_target="tpu_custom_call" | custom-call | flops 10350000128 | bytes 1048576 | tf_op jit(solution)/shard_map/front/pallas_call | solution.py:613
  79.0 12.3 %collective-permute-done.15 = bf16[128,1024]{1,0:T(8,128)(2,1)S(1)} collective-permute-done((bf16[128,1024]{1,0:T(8,128)(2,1)S(1)}, bf16[128,1024]{1,0:T(8,128)(2,1)S(1)}, u32[]{:S(2)}, u32[]{:S(2)}) %collective-permute-start.15) | collective-permute-done | bytes 262176 | tf_op jit(solution)/shard_map/ppermute | solution.py:132
  91.3 6.1 %mix_heads.1.mix_ref = bf16[512,256]{1,0:T(8,128)(2,1)S(1)} custom-call(bf16[512,768]{1,0:T(8,128)(2,1)S(1)} %get-tuple-element.105.q_ref.k_ref.v_ref, bf16[512,768]{1,0:T(8,128)(2,1)S(1)} %get-tuple-element.105.q_ref.k_ref.v_ref, bf16[512,768]{1,0:T(8,128)(2,1)S(1)} %get-tuple-element.105.q_ref.k_ref.v_ref, f32[512,512]{1,0:T(8,128)S(1)} %and_select_fusion.mask_ref), custom_call_target="tpu_custom_call" | custom-call | flops 6899999744 | bytes 1048576 | tf_op jit(solution)/shard_map/mix_heads/pallas_call | solution.py:731
  97.5 4.8 %middle.1 = (f32[128,1024]{1,0:T(8,128)S(1)}, bf16[128,1024]{1,0:T(8,128)(2,1)S(1)}, bf16[128,1024]{1,0:T(8,128)(2,1)S(1)}, bf16[128,1024]{1,0:T(8,128)(2,1)S(1)...) custom-call(s32[21]{0:T(128)S(1)} %pad_add_fusion.1.s_ref, ...), custom_call_target="tpu_custom_call" | custom-call | flops 2300000000 | bytes 1048576 | tf_op jit(solution)/shard_map/middle/pallas_call | solution.py:452
  102.3 2.9 %mlp.1 = (f32[512,2048]{1,0:T(8,128)S(1)}, bf16[512,2048]{1,0:T(8,128)(2,1)S(1)}) custom-call(s32[21]{0:T(128)S(1)} %pad_add_fusion.1.s_ref, bf16[512,1024]{1,0:T(8,128)(2,1)S(1)} %get-tuple-element.106.act_ref, bf16[512,1024]{1,0:T(8,128)(2,1)S(1)} %get-tuple-element.122.dy_ref, bf16[512,1024]{1,0:T(8,128)(2,1)S(1)} %get-tuple-element.123.h_ref, ...), custom_call_target="tpu_custom_call" | custom-call | flops 1150000000 | bytes 1048576 | tf_op jit(solution)/shard_map/mlp/pallas_call | solution.py:452
  105.8 3.7 %collective-permute-start.24 = (bf16[128,1024]{1,0:T(8,128)(2,1)S(1)}, bf16[128,1024]{1,0:T(8,128)(2,1)S(1)}, u32[]{:S(2)}, u32[]{:S(2)}) collective-permute-start(bf16[128,1024]{1,0:T(8,128)(2,1)S(1)} %get-tuple-element.118), channel_id=1, source_target_pairs={{0,1},{1,0},{2,3},{3,2},{4,5},{5,4},{6,7},{7,6},{8,9},{9,8},{10,11... | collective-permute-start | bytes 786440 | tf_op jit(solution)/shard_map/ppermute | solution.py:132
  113.9 8.9 %attend_back.1 = (bf16[512,768]{1,0:T(8,128)(2,1)S(1)}, f32[1,768]{1,0:T(1,128)S(1)}) custom-call(bf16[512,768]{1,0:T(8,128)(2,1)S(1)} %get-tuple-element.105.q_ref.k_ref.v_ref, bf16[512,768]{1,0:T(8,128)(2,1)S(1)} %get-tuple-element.105.q_ref.k_ref.v_ref, bf16[512,768]{1,0:T(8,128)(2,1)S(1)} %get-tuple-element.105.q_ref.k_ref.v_ref, ...), custom_call_target="tpu_custom_call" | custom-call | flops 4600000000 | bytes 1048576 | tf_op jit(solution)/shard_map/attend_back/pallas_call | solution.py:746
  122.8 3.2 %collective-permute-start.27 = (bf16[128,1024]{1,0:T(8,128)(2,1)S(1)}, bf16[128,1024]{1,0:T(8,128)(2,1)S(1)}, u32[]{:S(2)}, u32[]{:S(2)}) collective-permute-start(bf16[128,1024]{1,0:T(8,128)(2,1)S(1)} %get-tuple-element.128), channel_id=1, source_target_pairs={{0,3},{1,2},{2,1},{3,0},{4,7},{5,6},{6,5},{7,4},{8,11},{9,10},{10,... | collective-permute-start | bytes 786440 | tf_op jit(solution)/shard_map/ppermute | solution.py:132
  126.0 2.9 %back.1 = (f32[128,1024]{1,0:T(8,128)S(1)}, bf16[128,1024]{1,0:T(8,128)(2,1)S(1)}, bf16[128,1024]{1,0:T(8,128)(2,1)S(1)}, bf16[128,1024]{1,0:T(8,128)(2,1)S(1)}, f32[8,1024]{1,0:T(8,128)S(1)}) custom-call(s32[21]{0:T(128)S(1)} %pad_add_fusion.1.s_ref, bf16[512,768]{1,0:T(8,128)(2,1)S(1)} %get-tuple-element.129.dqkv_ref, ...), custom_call_target="tpu_custom_call" | custom-call | flops 1150000000 | bytes 1048576 | tf_op jit(solution)/shard_map/back/pallas_call | solution.py:452
  128.9 3.5 %collective-permute-done.27 = bf16[128,1024]{1,0:T(8,128)(2,1)S(1)} collective-permute-done((bf16[128,1024]{1,0:T(8,128)(2,1)S(1)}, bf16[128,1024]{1,0:T(8,128)(2,1)S(1)}, u32[]{:S(2)}, u32[]{:S(2)}) %collective-permute-start.27) | collective-permute-done | bytes 262176 | tf_op jit(solution)/shard_map/ppermute | solution.py:132
  132.5 3.0 %collective-permute-done.32.refs_2_ = bf16[128,2048]{1,0:T(8,128)(2,1)S(1)} collective-permute-done((bf16[128,2048]{1,0:T(8,128)(2,1)S(1)}, bf16[128,2048]{1,0:T(8,128)(2,1)S(1)}, u32[]{:S(2)}, u32[]{:S(2)}) %collective-permute-start.32) | collective-permute-done | bytes 524320 | tf_op jit(solution)/shard_map/ppermute | solution.py:132
  136.6 1.9 %terms.1 = (f32[512,1152]{1,0:T(8,128)S(1)}, bf16[512,1152]{1,0:T(8,128)(2,1)S(1)}) custom-call(s32[21]{0:T(128)S(1)} %pad_add_fusion.1.s_ref, bf16[512,1024]{1,0:T(8,128)(2,1)S(1)} %get-tuple-element.138.h_ref, bf16[512,768]{1,0:T(8,128)(2,1)S(1)} %get-tuple-element.129.dqkv_ref, bf16[512,256]{1,0:T(8,128)(2,1)S(1)} %mix_heads.1.mix_ref, ...), custom_call_target="tpu_custom_call" | custom-call | flops 4600000000 | bytes 1048576 | tf_op jit(solution)/shard_map/terms/pallas_call | solution.py:452
  139.2 3.4 %collective-permute-start.29 = (bf16[128,1024]{1,0:T(8,128)(2,1)S(1)}, bf16[128,1024]{1,0:T(8,128)(2,1)S(1)}, u32[]{:S(2)}, u32[]{:S(2)}) collective-permute-start(bf16[128,1024]{1,0:T(8,128)(2,1)S(1)} %get-tuple-element.133), channel_id=1, source_target_pairs={{0,2},{1,3},{2,0},{3,1},{4,6},{5,7},{6,4},{7,5},{8,10},{9,11},{10,... | collective-permute-start | bytes 786440 | tf_op jit(solution)/shard_map/ppermute | solution.py:132
  142.5 10.1 %collective-permute-done.28.r1_ref = bf16[128,1024]{1,0:T(8,128)(2,1)S(1)} collective-permute-done((bf16[128,1024]{1,0:T(8,128)(2,1)S(1)}, bf16[128,1024]{1,0:T(8,128)(2,1)S(1)}, u32[]{:S(2)}, u32[]{:S(2)}) %collective-permute-start.28) | collective-permute-done | bytes 262176 | tf_op jit(solution)/shard_map/ppermute | solution.py:132
  152.7 1.7 collective-permute-start.30
  159.1 1.5 multiply_subtract_fusion
  160.7 4.9 %collective-permute-done.35.refs_5_ = bf16[128,1152]{1,0:T(8,128)(2,1)S(1)} collective-permute-done((bf16[128,1152]{1,0:T(8,128)(2,1)S(1)}, bf16[128,1152]{1,0:T(8,128)(2,1)S(1)}, u32[]{:S(2)}, u32[]{:S(2)}) %collective-permute-start.35) | collective-permute-done | bytes 294944 | tf_op jit(solution)/shard_map/ppermute | solution.py:132
  165.6 4.2 %collective-permute-done.36.refs_6_ = bf16[128,1152]{1,0:T(8,128)(2,1)S(1)} collective-permute-done((bf16[128,1152]{1,0:T(8,128)(2,1)S(1)}, bf16[128,1152]{1,0:T(8,128)(2,1)S(1)}, u32[]{:S(2)}, u32[]{:S(2)}) %collective-permute-start.36) | collective-permute-done | bytes 294944 | tf_op jit(solution)/shard_map/ppermute | solution.py:132
  171.8 2.9 %collective-permute-start.39 = (bf16[32,1920]{1,0:T(8,128)(2,1)S(1)}, bf16[32,1920]{1,0:T(8,128)(2,1)S(1)}, u32[]{:S(2)}, u32[]{:S(2)}) collective-permute-start(bf16[32,1920]{1,0:T(8,128)(2,1)S(1)} %get-tuple-element.151), channel_id=1, source_target_pairs={{0,2},{1,3},{2,0},{3,1},{4,6},{5,7},{6,4},{7,5},{8,10},{9,11},{10,... | collective-permute-start | bytes 368648 | tf_op jit(solution)/shard_map/ppermute | solution.py:132
  174.7 1.5 collective-permute-start.40
  176.3 1.9 %finish.1 = f32[128,1024]{1,0:T(8,128)} custom-call(s32[21]{0:T(128)S(1)} %pad_add_fusion.1.s_ref, f32[128,1024]{1,0:T(8,128)S(1)} %get-tuple-element.131.own_ref, bf16[128,1024]{1,0:T(8,128)(2,1)S(1)} %collective-permute-done.28.r1_ref, bf16[128,1024]{1,0:T(8,128)(2,1)S(1)} %collective-permute-done.29.r2_ref, ...), custom_call_target="tpu_custom_call" | custom-call | flops 2300000000 | bytes 1048576 | tf_op jit(solution)/shard_map/finish/pallas_call | solution.py:452
  179.0 7.0 %collective-permute-done.39.refs_2_ = bf16[32,1920]{1,0:T(8,128)(2,1)S(1)} collective-permute-done((bf16[32,1920]{1,0:T(8,128)(2,1)S(1)}, bf16[32,1920]{1,0:T(8,128)(2,1)S(1)}, u32[]{:S(2)}, u32[]{:S(2)}) %collective-permute-start.39) | collective-permute-done | bytes 122912 | tf_op jit(solution)/shard_map/ppermute | solution.py:132
  186.1 2.8 %adam.1 = (f32[32,3072]{1,0:T(8,128)}, f32[32,3072]{1,0:T(8,128)}, f32[32,3072]{1,0:T(8,128)}, f32[32,3072]{1,0:T(8,128)}, f32[32,4096]{1,0:T(8,128)}, /*index=5...) custom-call(s32[21]{0:T(128)S(1)} %pad_add_fusion.1.s_ref, ...), custom_call_target="tpu_custom_call" | custom-call | flops 3449999872 | bytes 1048576 | tf_op jit(solution)/shard_map/adam/pallas_call | solution.py:452
  (130 shorter events, 33.4 us)
Async XLA Ops:
  8.0 13.8 %collective-permute-start.1 = (bf16[32,1920]{1,0:T(8,128)(2,1)S(1)}, bf16[32,1920]{1,0:T(8,128)(2,1)S(1)}, u32[]{:S(2)}, u32[]{:S(2)}) collective-permute-start(bf16[32,1920]{1,0:T(8,128)(2,1)S(1)} %get-tuple-element.95), channel_id=1, source_target_pairs={{0,2},{1,3},{2,0},{3,1},{4,6},{5,7},{6,4},{7,5},{8,10},{9,11},{10,... | collective-permute-start | bytes 368648 | tf_op jit(solution)/shard_map/ppermute | solution.py:132
  10.5 11.2 %collective-permute-start.2 = (bf16[32,1920]{1,0:T(8,128)(2,1)S(1)}, bf16[32,1920]{1,0:T(8,128)(2,1)S(1)}, u32[]{:S(2)}, u32[]{:S(2)}) collective-permute-start(bf16[32,1920]{1,0:T(8,128)(2,1)S(1)} %get-tuple-element.96), channel_id=1, source_target_pairs={{0,3},{1,2},{2,1},{3,0},{4,7},{5,6},{6,5},{7,4},{8,11},{9,10},{10,... | collective-permute-start | bytes 368648 | tf_op jit(solution)/shard_map/ppermute | solution.py:132
  10.6 24.7 %collective-permute-start.6 = (bf16[32,1024]{1,0:T(8,128)(2,1)S(1)}, bf16[32,1024]{1,0:T(8,128)(2,1)S(1)}, u32[]{:S(2)}, u32[]{:S(2)}) collective-permute-start(bf16[32,1024]{1,0:T(8,128)(2,1)S(1)} %convert_element_type.93), channel_id=1, source_target_pairs={{0,0},{1,4},{2,8},{3,12},{4,1},{5,5},{6,9},{7,13},{8,2},{9,6},{10,... | collective-permute-start | bytes 196616 | tf_op jit(solution)/shard_map/ppermute | solution.py:984
  21.7 16.4 %collective-permute-start.3 = (bf16[128,1024]{1,0:T(8,128)(2,1)S(1)}, bf16[128,1024]{1,0:T(8,128)(2,1)S(1)}, u32[]{:S(2)}, u32[]{:S(2)}) collective-permute-start(bf16[128,1024]{1,0:T(8,128)(2,1)S(1)} %norm.1.refs_0_), channel_id=1, source_target_pairs={{0,1},{1,0},{2,3},{3,2},{4,5},{5,4},{6,7},{7,6},{8,9},{9,8},{10,11... | collective-permute-start | bytes 786440 | tf_op jit(solution)/shard_map/ppermute | solution.py:132
  35.9 20.9 %collective-permute-start.7 = (bf16[128,2176]{1,0:T(8,128)(2,1)S(1)}, bf16[128,2176]{1,0:T(8,128)(2,1)S(1)}, u32[]{:S(2)}, u32[]{:S(2)}) collective-permute-start(bf16[128,2176]{1,0:T(8,128)(2,1)S(1)} %join.1.refs_4_.refs_12_.refs_20_), channel_id=1, source_target_pairs={{0,8},{4,12},{8,0},{12,4},{16,24},{20,28},{24,16},{28,20},{1,9},{5... | collective-permute-start | bytes 1671176 | tf_op jit(solution)/shard_map/ppermute | solution.py:132
  36.6 23.1 %collective-permute-start.8 = (bf16[128,2176]{1,0:T(8,128)(2,1)S(1)}, bf16[128,2176]{1,0:T(8,128)(2,1)S(1)}, u32[]{:S(2)}, u32[]{:S(2)}) collective-permute-start(bf16[128,2176]{1,0:T(8,128)(2,1)S(1)} %join.1.refs_4_.refs_12_.refs_20_), channel_id=1, source_target_pairs={{0,16},{4,20},{8,24},{12,28},{16,0},{20,4},{24,8},{28,12},{1,17},{... | collective-permute-start | bytes 1671176 | tf_op jit(solution)/shard_map/ppermute | solution.py:132
  38.1 22.8 %collective-permute-start.9 = (bf16[128,2176]{1,0:T(8,128)(2,1)S(1)}, bf16[128,2176]{1,0:T(8,128)(2,1)S(1)}, u32[]{:S(2)}, u32[]{:S(2)}) collective-permute-start(bf16[128,2176]{1,0:T(8,128)(2,1)S(1)} %join.1.refs_4_.refs_12_.refs_20_), channel_id=1, source_target_pairs={{0,24},{4,28},{8,16},{12,20},{16,8},{20,12},{24,0},{28,4},{1,25},{... | collective-permute-start | bytes 1671176 | tf_op jit(solution)/shard_map/ppermute | solution.py:132
  39.6 17.2 %collective-permute-start.4 = (bf16[128,1024]{1,0:T(8,128)(2,1)S(1)}, bf16[128,1024]{1,0:T(8,128)(2,1)S(1)}, u32[]{:S(2)}, u32[]{:S(2)}) collective-permute-start(bf16[128,1024]{1,0:T(8,128)(2,1)S(1)} %norm.1.refs_0_), channel_id=1, source_target_pairs={{0,2},{1,3},{2,0},{3,1},{4,6},{5,7},{6,4},{7,5},{8,10},{9,11},{10,... | collective-permute-start | bytes 786440 | tf_op jit(solution)/shard_map/ppermute | solution.py:132
  40.2 16.6 %collective-permute-start.5 = (bf16[128,1024]{1,0:T(8,128)(2,1)S(1)}, bf16[128,1024]{1,0:T(8,128)(2,1)S(1)}, u32[]{:S(2)}, u32[]{:S(2)}) collective-permute-start(bf16[128,1024]{1,0:T(8,128)(2,1)S(1)} %norm.1.refs_0_), channel_id=1, source_target_pairs={{0,3},{1,2},{2,1},{3,0},{4,7},{5,6},{6,5},{7,4},{8,11},{9,10},{10,... | collective-permute-start | bytes 786440 | tf_op jit(solution)/shard_map/ppermute | solution.py:132
  61.2 16.7 %collective-permute-start.17 = (bf16[128,1024]{1,0:T(8,128)(2,1)S(1)}, bf16[128,1024]{1,0:T(8,128)(2,1)S(1)}, u32[]{:S(2)}, u32[]{:S(2)}) collective-permute-start(bf16[128,1024]{1,0:T(8,128)(2,1)S(1)} %convert_element_type.95.refs_0_), channel_id=1, source_target_pairs={{0,8},{4,12},{8,0},{12,4},{16,24},{20,28},{24,16},{28,20},{1,9},{5... | collective-permute-start | bytes 786440 | tf_op jit(solution)/shard_map/ppermute | solution.py:132
  62.3 16.1 %collective-permute-start.18 = (bf16[128,1024]{1,0:T(8,128)(2,1)S(1)}, bf16[128,1024]{1,0:T(8,128)(2,1)S(1)}, u32[]{:S(2)}, u32[]{:S(2)}) collective-permute-start(bf16[128,1024]{1,0:T(8,128)(2,1)S(1)} %convert_element_type.95.refs_0_), channel_id=1, source_target_pairs={{0,16},{4,20},{8,24},{12,28},{16,0},{20,4},{24,8},{28,12},{1,17},{... | collective-permute-start | bytes 786440 | tf_op jit(solution)/shard_map/ppermute | solution.py:132
  64.1 14.3 %collective-permute-start.19 = (bf16[128,1024]{1,0:T(8,128)(2,1)S(1)}, bf16[128,1024]{1,0:T(8,128)(2,1)S(1)}, u32[]{:S(2)}, u32[]{:S(2)}) collective-permute-start(bf16[128,1024]{1,0:T(8,128)(2,1)S(1)} %convert_element_type.95.refs_0_), channel_id=1, source_target_pairs={{0,24},{4,28},{8,16},{12,20},{16,8},{20,12},{24,0},{28,4},{1,25},{... | collective-permute-start | bytes 786440 | tf_op jit(solution)/shard_map/ppermute | solution.py:132
  64.7 14.2 %collective-permute-start.16 = (bf16[128,1024]{1,0:T(8,128)(2,1)S(1)}, bf16[128,1024]{1,0:T(8,128)(2,1)S(1)}, u32[]{:S(2)}, u32[]{:S(2)}) collective-permute-start(bf16[128,1024]{1,0:T(8,128)(2,1)S(1)} %get-tuple-element.109), channel_id=1, source_target_pairs={{0,3},{1,2},{2,1},{3,0},{4,7},{5,6},{6,5},{7,4},{8,11},{9,10},{10,... | collective-permute-start | bytes 786440 | tf_op jit(solution)/shard_map/ppermute | solution.py:132
  68.4 22.9 %collective-permute-start.15 = (bf16[128,1024]{1,0:T(8,128)(2,1)S(1)}, bf16[128,1024]{1,0:T(8,128)(2,1)S(1)}, u32[]{:S(2)}, u32[]{:S(2)}) collective-permute-start(bf16[128,1024]{1,0:T(8,128)(2,1)S(1)} %get-tuple-element.109), channel_id=1, source_target_pairs={{0,2},{1,3},{2,0},{3,1},{4,6},{5,7},{6,4},{7,5},{8,10},{9,11},{10,... | collective-permute-start | bytes 786440 | tf_op jit(solution)/shard_map/ppermute | solution.py:132
  77.8 19.5 %collective-permute-start.14 = (bf16[128,1024]{1,0:T(8,128)(2,1)S(1)}, bf16[128,1024]{1,0:T(8,128)(2,1)S(1)}, u32[]{:S(2)}, u32[]{:S(2)}) collective-permute-start(bf16[128,1024]{1,0:T(8,128)(2,1)S(1)} %get-tuple-element.109), channel_id=1, source_target_pairs={{0,1},{1,0},{2,3},{3,2},{4,5},{5,4},{6,7},{7,6},{8,9},{9,8},{10,11... | collective-permute-start | bytes 786440 | tf_op jit(solution)/shard_map/ppermute | solution.py:132
  78.4 19.1 %collective-permute-start.20 = (bf16[128,1024]{1,0:T(8,128)(2,1)S(1)}, bf16[128,1024]{1,0:T(8,128)(2,1)S(1)}, u32[]{:S(2)}, u32[]{:S(2)}) collective-permute-start(bf16[128,1024]{1,0:T(8,128)(2,1)S(1)} %convert_element_type.95.refs_0_), channel_id=1, source_target_pairs={{0,4},{4,0},{8,12},{12,8},{16,20},{20,16},{24,28},{28,24},{1,5},{5... | collective-permute-start | bytes 786440 | tf_op jit(solution)/shard_map/ppermute | solution.py:132
  78.4 19.1 %collective-permute-start.21 = (bf16[128,1024]{1,0:T(8,128)(2,1)S(1)}, bf16[128,1024]{1,0:T(8,128)(2,1)S(1)}, u32[]{:S(2)}, u32[]{:S(2)}) collective-permute-start(bf16[128,1024]{1,0:T(8,128)(2,1)S(1)} %collective-permute-done.17.refs_1_), channel_id=1, source_target_pairs={{0,4},{4,0},{8,12},{12,8},{16,20},{20,16},{24,28},{28,24},{1,5},{5... | collective-permute-start | bytes 786440 | tf_op jit(solution)/shard_map/ppermute | solution.py:132
  78.9 18.6 %collective-permute-start.22 = (bf16[128,1024]{1,0:T(8,128)(2,1)S(1)}, bf16[128,1024]{1,0:T(8,128)(2,1)S(1)}, u32[]{:S(2)}, u32[]{:S(2)}) collective-permute-start(bf16[128,1024]{1,0:T(8,128)(2,1)S(1)} %collective-permute-done.18.refs_2_), channel_id=1, source_target_pairs={{0,4},{4,0},{8,12},{12,8},{16,20},{20,16},{24,28},{28,24},{1,5},{5... | collective-permute-start | bytes 786440 | tf_op jit(solution)/shard_map/ppermute | solution.py:132
  105.8 17.0 %collective-permute-start.25 = (bf16[128,1024]{1,0:T(8,128)(2,1)S(1)}, bf16[128,1024]{1,0:T(8,128)(2,1)S(1)}, u32[]{:S(2)}, u32[]{:S(2)}) collective-permute-start(bf16[128,1024]{1,0:T(8,128)(2,1)S(1)} %get-tuple-element.119), channel_id=1, source_target_pairs={{0,2},{1,3},{2,0},{3,1},{4,6},{5,7},{6,4},{7,5},{8,10},{9,11},{10,... | collective-permute-start | bytes 786440 | tf_op jit(solution)/shard_map/ppermute | solution.py:132
  105.8 20.2 %collective-permute-start.24 = (bf16[128,1024]{1,0:T(8,128)(2,1)S(1)}, bf16[128,1024]{1,0:T(8,128)(2,1)S(1)}, u32[]{:S(2)}, u32[]{:S(2)}) collective-permute-start(bf16[128,1024]{1,0:T(8,128)(2,1)S(1)} %get-tuple-element.118), channel_id=1, source_target_pairs={{0,1},{1,0},{2,3},{3,2},{4,5},{5,4},{6,7},{7,6},{8,9},{9,8},{10,11... | collective-permute-start | bytes 786440 | tf_op jit(solution)/shard_map/ppermute | solution.py:132
  110.3 22.2 %collective-permute-start.31 = (bf16[128,2048]{1,0:T(8,128)(2,1)S(1)}, bf16[128,2048]{1,0:T(8,128)(2,1)S(1)}, u32[]{:S(2)}, u32[]{:S(2)}) collective-permute-start(bf16[128,2048]{1,0:T(8,128)(2,1)S(1)} %get-tuple-element.175), channel_id=1, source_target_pairs={{0,8},{4,12},{8,0},{12,4},{16,24},{20,28},{24,16},{28,20},{1,9},{5... | collective-permute-start | bytes 1572872 | tf_op jit(solution)/shard_map/ppermute | solution.py:132
  111.5 23.9 %collective-permute-start.32 = (bf16[128,2048]{1,0:T(8,128)(2,1)S(1)}, bf16[128,2048]{1,0:T(8,128)(2,1)S(1)}, u32[]{:S(2)}, u32[]{:S(2)}) collective-permute-start(bf16[128,2048]{1,0:T(8,128)(2,1)S(1)} %get-tuple-element.174), channel_id=1, source_target_pairs={{0,16},{4,20},{8,24},{12,28},{16,0},{20,4},{24,8},{28,12},{1,17},{... | collective-permute-start | bytes 1572872 | tf_op jit(solution)/shard_map/ppermute | solution.py:132
  112.8 23.8 %collective-permute-start.33 = (bf16[128,2048]{1,0:T(8,128)(2,1)S(1)}, bf16[128,2048]{1,0:T(8,128)(2,1)S(1)}, u32[]{:S(2)}, u32[]{:S(2)}) collective-permute-start(bf16[128,2048]{1,0:T(8,128)(2,1)S(1)} %get-tuple-element.173), channel_id=1, source_target_pairs={{0,24},{4,28},{8,16},{12,20},{16,8},{20,12},{24,0},{28,4},{1,25},{... | collective-permute-start | bytes 1572872 | tf_op jit(solution)/shard_map/ppermute | solution.py:132
  138.5 16.9 %collective-permute-start.34 = (bf16[4,128,1152]{2,1,0:T(8,128)(2,1)S(1)}, bf16[4,128,1152]{2,1,0:T(8,128)(2,1)S(1)}, u32[]{:S(2)}, u32[]{:S(2)}) collective-permute-start(bf16[4,128,1152]{2,1,0:T(8,128)(2,1)S(1)} %bitcast.70), channel_id=1, source_target_pairs={{0,4},{4,0},{8,12},{12,8},{16,20},{20,16},{24,28},{28,24},{1,5},{5... | collective-permute-start | bytes 3538952 | tf_op jit(solution)/shard_map/ppermute | solution.py:132
  138.6 14.1 %collective-permute-start.28 = (bf16[128,1024]{1,0:T(8,128)(2,1)S(1)}, bf16[128,1024]{1,0:T(8,128)(2,1)S(1)}, u32[]{:S(2)}, u32[]{:S(2)}) collective-permute-start(bf16[128,1024]{1,0:T(8,128)(2,1)S(1)} %get-tuple-element.132), channel_id=1, source_target_pairs={{0,1},{1,0},{2,3},{3,2},{4,5},{5,4},{6,7},{7,6},{8,9},{9,8},{10,11... | collective-permute-start | bytes 786440 | tf_op jit(solution)/shard_map/ppermute | solution.py:132
  139.2 21.5 %collective-permute-start.29 = (bf16[128,1024]{1,0:T(8,128)(2,1)S(1)}, bf16[128,1024]{1,0:T(8,128)(2,1)S(1)}, u32[]{:S(2)}, u32[]{:S(2)}) collective-permute-start(bf16[128,1024]{1,0:T(8,128)(2,1)S(1)} %get-tuple-element.133), channel_id=1, source_target_pairs={{0,2},{1,3},{2,0},{3,1},{4,6},{5,7},{6,4},{7,5},{8,10},{9,11},{10,... | collective-permute-start | bytes 786440 | tf_op jit(solution)/shard_map/ppermute | solution.py:132
  152.7 23.5 %collective-permute-start.30 = (bf16[128,1024]{1,0:T(8,128)(2,1)S(1)}, bf16[128,1024]{1,0:T(8,128)(2,1)S(1)}, u32[]{:S(2)}, u32[]{:S(2)}) collective-permute-start(bf16[128,1024]{1,0:T(8,128)(2,1)S(1)} %get-tuple-element.135), channel_id=1, source_target_pairs={{0,3},{1,2},{2,1},{3,0},{4,7},{5,6},{6,5},{7,4},{8,11},{9,10},{10,... | collective-permute-start | bytes 786440 | tf_op jit(solution)/shard_map/ppermute | solution.py:132
  156.4 13.4 %collective-permute-start.36 = (bf16[128,1152]{1,0:T(8,128)(2,1)S(1)}, bf16[128,1152]{1,0:T(8,128)(2,1)S(1)}, u32[]{:S(2)}, u32[]{:S(2)}) collective-permute-start(bf16[128,1152]{1,0:T(8,128)(2,1)S(1)} %get-tuple-element.146), channel_id=1, source_target_pairs={{0,16},{4,20},{8,24},{12,28},{16,0},{20,4},{24,8},{28,12},{1,17},{... | collective-permute-start | bytes 884744 | tf_op jit(solution)/shard_map/ppermute | solution.py:132
  157.9 12.9 %collective-permute-start.37 = (bf16[128,1152]{1,0:T(8,128)(2,1)S(1)}, bf16[128,1152]{1,0:T(8,128)(2,1)S(1)}, u32[]{:S(2)}, u32[]{:S(2)}) collective-permute-start(bf16[128,1152]{1,0:T(8,128)(2,1)S(1)} %get-tuple-element.147), channel_id=1, source_target_pairs={{0,24},{4,28},{8,16},{12,20},{16,8},{20,12},{24,0},{28,4},{1,25},{... | collective-permute-start | bytes 884744 | tf_op jit(solution)/shard_map/ppermute | solution.py:132
  171.8 14.2 %collective-permute-start.39 = (bf16[32,1920]{1,0:T(8,128)(2,1)S(1)}, bf16[32,1920]{1,0:T(8,128)(2,1)S(1)}, u32[]{:S(2)}, u32[]{:S(2)}) collective-permute-start(bf16[32,1920]{1,0:T(8,128)(2,1)S(1)} %get-tuple-element.151), channel_id=1, source_target_pairs={{0,2},{1,3},{2,0},{3,1},{4,6},{5,7},{6,4},{7,5},{8,10},{9,11},{10,... | collective-permute-start | bytes 368648 | tf_op jit(solution)/shard_map/ppermute | solution.py:132
  174.7 11.4 %collective-permute-start.40 = (bf16[32,1920]{1,0:T(8,128)(2,1)S(1)}, bf16[32,1920]{1,0:T(8,128)(2,1)S(1)}, u32[]{:S(2)}, u32[]{:S(2)}) collective-permute-start(bf16[32,1920]{1,0:T(8,128)(2,1)S(1)} %get-tuple-element.152), channel_id=1, source_target_pairs={{0,3},{1,2},{2,1},{3,0},{4,7},{5,6},{6,5},{7,4},{8,11},{9,10},{10,... | collective-permute-start | bytes 368648 | tf_op jit(solution)/shard_map/ppermute | solution.py:132
  178.2 10.7 %collective-permute-start.41 = (f32[32,1024]{1,0:T(8,128)S(1)}, f32[32,1024]{1,0:T(8,128)S(1)}, u32[]{:S(2)}, u32[]{:S(2)}) collective-permute-start(f32[32,1024]{1,0:T(8,128)S(1)} %get-tuple-element.154), channel_id=1, source_target_pairs={{0,0},{4,1},{8,2},{12,3},{1,4},{5,5},{9,6},{13,7},{2,8},{6,9},{10,... | collective-permute-start | bytes 393224 | tf_op jit(solution)/shard_map/ppermute | solution.py:1099
  (32 other events, 258.6 us)
